TPU v7x, 32 devices: a whole 2x2x4 slice. The times are simulated.
32 devices in a mesh: dev: 16 (over z, y, x), ta: 2 (over core).
Axes of the slice: x: 2, y: 2, z: 4, core: 2. Of those that a mesh axis runs over, the one named last changes fastest.
Arguments:
- token_ids: int32 [16384], P('dev'), may hold values from 0 to 50303
- bucket: int32 [16], P('dev'), may hold values from 256 to 1024, as said below
- seq_lengths: int32 [16, 4], P('dev'), may hold values from 0 to 1024, as said below
- loss_pos: int32 [4096], P('dev'), may hold values from 0 to 1023, as said below
- targets: int32 [4096], P('dev'), may hold values from 0 to 50303
- wte: bfloat16 [50304, 1024], P(('dev', 'ta')), may hold values from -0.359375 to 0.359375
- wpe: bfloat16 [1024, 1024], replicated, may hold values from -0.1796875 to 0.1796875
- w_qkv: bfloat16 [2, 3, 1024, 1024], P(None, None, 'dev', 'ta'), may hold values from -0.1875 to 0.1875
- w_out: bfloat16 [2, 1024, 1024], P(None, 'ta', 'dev'), may hold values from -1 to 1
- w_fc: bfloat16 [2, 1024, 4096], P(None, 'dev', 'ta'), may hold values from -0.1875 to 0.1875
- w_proj: bfloat16 [2, 4096, 1024], P(None, 'ta', 'dev'), may hold values from -0.09375 to 0.09375
- frozen_vec: float32 [2, 9, 1024], replicated
- fc_bias: float32 [2, 4096], P(None, 'ta'), may hold values from -0.6 to 0.6
- final_norm: float32 [2, 1024], replicated
- prefix_table: float32 [10, 512], replicated, may hold values from -0.6 to 0.6
- inner_weight: float32 [512, 512], P(None, 'dev'), may hold values from -0.25 to 0.25
- inner_bias: float32 [512], P('dev'), may hold values from -0.3 to 0.3
- outer_weight: float32 [512, 2, 2, 1024], P('dev', None, None, 'ta'), may hold values from -0.25 to 0.25
- outer_bias: float32 [2, 2, 1024], P(None, None, 'ta'), may hold values from -0.6 to 0.6
- moment_prefix: float32 [10, 512], replicated, may hold values from -4.172325e-07 to 4.172325e-07
- square_prefix: float32 [10, 512], replicated, may hold values from 4.2211477e-16 to 1.6884591e-15
- moment_inner: float32 [512, 512], P(None, 'dev'), may hold values from -4.172325e-07 to 4.172325e-07
- square_inner: float32 [512, 512], P(None, 'dev'), may hold values from 4.2211477e-16 to 1.6884591e-15
- moment_inner_bias: float32 [512], P('dev'), may hold values from -1.1920929e-06 to 1.1920929e-06
- square_inner_bias: float32 [512], P('dev'), may hold values from 3.799033e-15 to 1.5196132e-14
- moment_outer: float32 [512, 2, 2, 1024], P('dev', None, None, 'ta'), may hold values from -4.172325e-07 to 4.172325e-07
- square_outer: float32 [512, 2, 2, 1024], P('dev', None, None, 'ta'), may hold values from 4.2211477e-16 to 1.6884591e-15
- moment_outer_bias: float32 [2, 2, 1024], P(None, None, 'ta'), may hold values from -1.1920929e-06 to 1.1920929e-06
- square_outer_bias: float32 [2, 2, 1024], P(None, None, 'ta'), may hold values from 3.799033e-15 to 1.5196132e-14
Outputs:
- mean_loss: float32 [1], replicated
- grad_norm: float32 [1], replicated
- prefix_new: float32 [10, 512], replicated
- prefix_moment: float32 [10, 512], replicated
- prefix_square: float32 [10, 512], replicated
- inner_new: float32 [512, 512], P(None, 'dev')
- inner_moment: float32 [512, 512], P(None, 'dev')
- inner_square: float32 [512, 512], P(None, 'dev')
- inner_bias_new: float32 [512], P('dev')
- inner_bias_moment: float32 [512], P('dev')
- inner_bias_square: float32 [512], P('dev')
- outer_new: float32 [512, 2, 2, 1024], P('dev', None, None, 'ta')
- outer_moment: float32 [512, 2, 2, 1024], P('dev', None, None, 'ta')
- outer_square: float32 [512, 2, 2, 1024], P('dev', None, None, 'ta')
- outer_bias_new: float32 [2, 2, 1024], P(None, None, 'ta')
- outer_bias_moment: float32 [2, 2, 1024], P(None, None, 'ta')
- outer_bias_square: float32 [2, 2, 1024], P(None, None, 'ta')
- prefix_copy: bfloat16 [10, 512], replicated
- inner_copy: bfloat16 [512, 512], P(None, 'dev')
- inner_bias_copy: bfloat16 [512], P('dev')
- outer_copy: bfloat16 [512, 2, 2, 1024], P('dev', None, None, 'ta')
- outer_bias_copy: bfloat16 [2, 2, 1024], P(None, None, 'ta')
Inputs may be any that keep to these rules, and one draw needn't show every extreme that they name: `bucket`: each entry is 256 or 1024; both occur. `seq_lengths`: for a group of bucket 1024, entry 0 is its one sequence's length and the others are 0; for a group of bucket 256, the 4 entries are its sequences' lengths, each 1 or more. Some group of each bucket has a sequence of full length. `loss_pos`: rows within a group, all different within a group.
All inputs are finite; a program needn't handle non-finite values.
Results may differ from a plain program's by a relative error of at most 0.01.
Values may be sent and summed in bfloat16 or wider, within the bound.
No kernel may reach another device: no remote copies, remote signals or barrier semaphores. Data moves between devices by JAX's collectives and lax.ppermute only.
A program may use at most 280 MiB of HBM per device.

v0:
```python
import jax
import jax.numpy as jnp
from jax import lax
from jax.sharding import PartitionSpec as P

HEAD_DIM = 64


EPS_NORM = 1e-05
CLIP_NORM = 0.001
LEARN_RATE = 0.02
BETA_ONE = 0.9
BETA_TWO = 0.999
ADAM_EPS = 1e-08
DECAY_RATE = 0.01
adam_steps = 10.0
NEG_BIG = -1e30
HIGHEST = lax.Precision.HIGHEST
F32 = jnp.float32
B16 = jnp.bfloat16


def combined_all(array, axis, join):
    gathered = jax.tree.map(
        lambda a, kind: lax.all_gather(a.astype(kind), axis),
        array,
        jax.tree.map(lambda a: jnp.bfloat16 if a.dtype == jnp.float32 else a.dtype, array),
    )

    def take(source):
        return jax.tree.map(
            lambda a, own: lax.dynamic_index_in_dim(a, source, 0, False).astype(own.dtype),
            gathered,
            array,
        )

    return lax.fori_loop(
        1, lax.axis_size(axis), lambda source, state: join(state, take(source)), take(0)
    )


def layer_norm(stream, gain, shift):
    center = stream - jnp.mean(stream, -1, keepdims=True)
    spread = jnp.mean(center * center, -1, keepdims=True)
    return center * lax.rsqrt(spread + EPS_NORM) * gain + shift


def norm_back(gradient, stream, gain, shift):
    unused, pullback = jax.vjp(lambda operand: layer_norm(operand, gain, shift), stream)
    return pullback(gradient)[0]


def gelu_back(gradient, upward):
    unused, pullback = jax.vjp(lambda operand: jax.nn.gelu(operand, approximate=True), upward)
    return pullback(gradient)[0]


def across_heads(partial_sum):
    return lax.psum(partial_sum.astype(jnp.bfloat16), "ta").astype(jnp.float32)


def row_layout(bucket, seq_lengths, row_count):
    bucket_width = bucket[0]
    positions = jnp.arange(row_count, dtype=jnp.int32)
    segment = positions // bucket_width
    seq_pos = positions % bucket_width
    slots = jnp.arange(seq_lengths.shape[1], dtype=jnp.int32)
    seg_len = jnp.sum(jnp.where(segment[:, None] == slots[None], seq_lengths[0][None], 0), 1)
    return (positions, segment, seq_pos, seq_pos < seg_len)


def visible_rows(layout, first_row, block_rows, prefix_len):
    positions, segment, seq_pos, present = layout
    query_seg = segment[first_row : first_row + block_rows]
    query_pos = positions[first_row : first_row + block_rows]
    tokens_seen = (
        (query_seg[:, None] == segment[None])
        & (positions[None] <= query_pos[:, None])
        & present[None]
    )
    return jnp.concatenate([jnp.ones((block_rows, prefix_len), bool), tokens_seen], 1)


def scores_block(queries, keys, visible):
    scale = queries.shape[-1] ** (-0.5)
    scores = jnp.einsum("qhd,khd->hqk", queries, keys, preferred_element_type=F32) * scale
    return jnp.where(visible[None], scores, NEG_BIG)


def layer_forward(stream, weights, vectors, fc_half, prefix_kv, layout):
    w_qkv, w_fc, w_out, w_proj = weights
    half_width = w_qkv.shape[2]
    heads_local = half_width // HEAD_DIM
    prefix_len = prefix_kv.shape[1]
    qkv_bias = lax.dynamic_slice_in_dim(
        vectors[4:7], lax.axis_index("ta") * half_width, half_width, 1
    )
    normed = layer_norm(stream, vectors[0], vectors[1]).astype(B16)
    row_count = normed.shape[0]
    block_rows = min(512, row_count)
    qkv = (
        jnp.einsum("rd,cde->rce", normed, w_qkv, preferred_element_type=F32) + qkv_bias[None]
    ).astype(B16)
    queries = qkv[:, 0].reshape(row_count, heads_local, HEAD_DIM)
    keys = jnp.concatenate([prefix_kv[0], qkv[:, 1]], 0).reshape(-1, heads_local, HEAD_DIM)
    values = jnp.concatenate([prefix_kv[1], qkv[:, 2]], 0).reshape(-1, heads_local, HEAD_DIM)
    outputs = []
    log_totals = []
    for first_row in range(0, row_count, block_rows):
        visible = visible_rows(layout, first_row, block_rows, prefix_len)
        scores = scores_block(queries[first_row : first_row + block_rows], keys, visible)
        highest = jnp.max(scores, -1, keepdims=True)
        log_total = highest + jnp.log(jnp.sum(jnp.exp(scores - highest), -1, keepdims=True))
        shares = jnp.exp(scores - log_total).astype(B16)
        outputs.append(
            jnp.einsum("hqk,khd->qhd", shares, values, preferred_element_type=F32).astype(B16)
        )
        log_totals.append(log_total)
    mixed_heads = jnp.concatenate(outputs, 0).reshape(row_count, half_width)
    middle = stream + (
        across_heads(jnp.dot(mixed_heads, w_out, preferred_element_type=F32)) + vectors[7]
    )
    normed_two = layer_norm(middle, vectors[2], vectors[3]).astype(B16)
    upward = jnp.dot(normed_two, w_fc, preferred_element_type=F32) + fc_half
    active = jax.nn.gelu(upward, approximate=True).astype(B16)
    downward = across_heads(jnp.dot(active, w_proj, preferred_element_type=F32)) + vectors[8]
    return (middle + downward, (stream, queries, keys, values, log_totals, middle, upward))


def layer_backward(gradient, stored, weights, vectors, layout):
    stream, queries, keys, values, log_totals, middle, upward = stored
    w_qkv, w_fc, w_out, w_proj = weights
    row_count, heads_local, head_dim = queries.shape
    half_width = heads_local * head_dim
    prefix_len = keys.shape[0] - row_count
    block_rows = min(512, row_count)
    scale = head_dim ** (-0.5)
    grad_whole = gradient.astype(B16)
    d_active = jnp.einsum("rd,fd->rf", grad_whole, w_proj, preferred_element_type=F32)
    d_upward = gelu_back(d_active, upward).astype(B16)
    d_normed_two = across_heads(jnp.einsum("rf,df->rd", d_upward, w_fc, preferred_element_type=F32))
    grad_mid = gradient + norm_back(d_normed_two, middle, vectors[2], vectors[3])
    mid_whole = grad_mid.astype(B16)
    d_mixed = jnp.einsum("rd,ed->re", mid_whole, w_out, preferred_element_type=F32).astype(B16)
    d_mixed = d_mixed.reshape(row_count, heads_local, head_dim)
    key_grad = jnp.zeros(keys.shape, F32)
    value_grad = jnp.zeros(values.shape, F32)
    query_grads = []
    for block_id, first_row in enumerate(range(0, row_count, block_rows)):
        visible = visible_rows(layout, first_row, block_rows, prefix_len)
        block_queries = queries[first_row : first_row + block_rows]
        block_grad = d_mixed[first_row : first_row + block_rows]
        shares = jnp.exp(scores_block(block_queries, keys, visible) - log_totals[block_id])
        d_shares = jnp.einsum(
            "qhd,khd->hqk", block_grad, values, preferred_element_type=F32
        ).astype(B16)
        inner_term = jnp.sum(shares * d_shares, -1, keepdims=True)
        d_scores = (shares * (d_shares - inner_term)).astype(B16)
        query_grads.append(
            jnp.einsum("hqk,khd->qhd", d_scores, keys, preferred_element_type=F32) * scale
        )
        key_grad = (
            key_grad
            + jnp.einsum("hqk,qhd->khd", d_scores, block_queries, preferred_element_type=F32)
            * scale
        )
        value_grad = value_grad + jnp.einsum(
            "hqk,qhd->khd", shares.astype(B16), block_grad, preferred_element_type=F32
        )
    d_qkv = jnp.stack(
        [
            jnp.concatenate(query_grads, 0).reshape(row_count, half_width),
            key_grad[prefix_len:].reshape(row_count, half_width),
            value_grad[prefix_len:].reshape(row_count, half_width),
        ],
        1,
    ).astype(B16)
    d_normed = across_heads(jnp.einsum("rce,cde->rd", d_qkv, w_qkv, preferred_element_type=F32))
    grad_stream = grad_mid + norm_back(d_normed, stream, vectors[0], vectors[1])
    prefix_grad = jnp.stack(
        [
            key_grad[:prefix_len].reshape(prefix_len, half_width),
            value_grad[:prefix_len].reshape(prefix_len, half_width),
        ]
    )
    return (grad_stream, prefix_grad)


def adamw_update(weight, moment, square, gradient, corr_one, corr_two):
    moment = BETA_ONE * moment + (1.0 - BETA_ONE) * gradient
    square = BETA_TWO * square + (1.0 - BETA_TWO) * gradient * gradient
    weight = weight - LEARN_RATE * (
        moment / corr_one / (jnp.sqrt(square / corr_two) + ADAM_EPS) + DECAY_RATE * weight
    )
    return (weight, moment, square)


def combine(first, second):
    highest = jnp.maximum(first[0], second[0])
    scale_one = jnp.exp(first[0] - highest)
    scale_two = jnp.exp(second[0] - highest)
    return (
        highest,
        first[1] * scale_one + second[1] * scale_two,
        first[2] * scale_one[:, None] + second[2] * scale_two[:, None],
        first[3] + second[3],
        first[4] + second[4],
    )


def local(
    token_ids,
    bucket,
    seq_lengths,
    loss_pos,
    targets,
    wte,
    wpe,
    w_qkv,
    w_out,
    w_fc,
    w_proj,
    frozen_vec,
    fc_bias,
    final_norm,
    prefix_table,
    inner_weight,
    inner_bias,
    outer_weight,
    outer_bias,
    moment_prefix,
    square_prefix,
    moment_inner,
    square_inner,
    moment_inner_bias,
    square_inner_bias,
    moment_outer,
    square_outer,
    moment_outer_bias,
    square_outer_bias,
):
    row_count = token_ids.shape[0]
    width = wte.shape[1]
    layer_count = w_qkv.shape[0]
    layout = row_layout(bucket, seq_lengths, row_count)
    positions, segment, seq_pos, present = layout
    shard_rows = wte.shape[0]
    ta_size = lax.axis_size("ta")
    own_index = lax.axis_index("ta")

    def local_index(ids):
        block_of = ids // shard_rows
        return jnp.where(
            block_of % ta_size == own_index, block_of // ta_size * shard_rows + ids % shard_rows, -1
        )

    token_local = local_index(token_ids)
    shard_part = lax.all_gather(wte, "dev", axis=0, tiled=True)
    offset = token_local
    inside = (offset >= 0) & (offset < shard_part.shape[0])
    clipped = jnp.clip(offset, 0, shard_part.shape[0] - 1)
    found_rows = jnp.take(shard_part, clipped, axis=0).astype(F32)
    looked = jnp.where(inside[:, None], found_rows, 0.0)
    stream = across_heads(looked) + jnp.take(wpe, seq_pos, axis=0).astype(F32)
    hidden = jnp.tanh(jnp.dot(prefix_table, inner_weight, precision=HIGHEST) + inner_bias)
    partial_kv = jnp.einsum("pr,rlcd->lcpd", hidden, outer_weight, precision=HIGHEST)
    prefix_kv = (lax.psum(partial_kv, "dev") + outer_bias[:, :, None, :]).astype(B16)
    gathered = []
    stored_all = []
    for layer_id in range(layer_count):
        weights = (
            lax.all_gather(w_qkv[layer_id], "dev", axis=1, tiled=True),
            lax.all_gather(w_fc[layer_id], "dev", axis=0, tiled=True),
            lax.all_gather(w_out[layer_id], "dev", axis=1, tiled=True),
            lax.all_gather(w_proj[layer_id], "dev", axis=1, tiled=True),
        )
        gathered.append(weights)
        stream, stored = layer_forward(
            stream, weights, frozen_vec[layer_id], fc_bias[layer_id], prefix_kv[layer_id], layout
        )
        stored_all.append(stored)
    head_rows = jnp.take(stream, loss_pos, axis=0)
    head_in = layer_norm(head_rows, final_norm[0], final_norm[1]).astype(B16)
    target_local = local_index(targets)
    scored = loss_pos.shape[0]

    def vocab_block(running, shard_part, first_row):
        highest, summed, weighted, target_logit, target_row = running
        logits = jnp.einsum("qd,vd->qv", head_in, shard_part, preferred_element_type=F32)
        new_high = jnp.maximum(highest, jnp.max(logits, -1))
        rescale = jnp.exp(highest - new_high)
        exponent = jnp.exp(logits - new_high[:, None])
        summed = summed * rescale + jnp.sum(exponent, -1)
        weighted = weighted * rescale[:, None] + jnp.dot(
            exponent.astype(B16), shard_part, preferred_element_type=F32
        )
        offset = target_local - first_row
        inside = (offset >= 0) & (offset < shard_part.shape[0])
        clipped = jnp.clip(offset, 0, shard_part.shape[0] - 1)
        target_logit = target_logit + jnp.where(
            inside, jnp.take_along_axis(logits, clipped[:, None], 1)[:, 0], 0.0
        )
        target_row = target_row + jnp.where(
            inside[:, None], jnp.take(shard_part, clipped, axis=0).astype(F32), 0.0
        )
        return (new_high, summed, weighted, target_logit, target_row)

    start_state = (
        jnp.full((scored,), NEG_BIG, F32),
        jnp.zeros((scored,), F32),
        jnp.zeros((scored, width), F32),
        jnp.zeros((scored,), F32),
        jnp.zeros((scored, width), F32),
    )
    shard_part = lax.all_gather(wte, "dev", axis=0, tiled=True)
    shard_count = shard_part.shape[0] // shard_rows
    grouping = 1
    while grouping < 8 and shard_count % (grouping * 2) == 0:
        grouping = grouping * 2
    block_rows = shard_rows * grouping
    blocks = shard_part.reshape(shard_count // grouping, block_rows, width)
    offsets = jnp.arange(shard_count // grouping, dtype=jnp.int32) * block_rows

    def turn(state, element):
        return (vocab_block(state, element[0], element[1]), None)

    folded = lax.scan(turn, start_state, (blocks, offsets))[0]
    highest, summed, weighted, target_logit, target_row = combined_all(folded, "ta", combine)
    counted = jnp.take(present, loss_pos).astype(F32)
    log_total = highest + jnp.log(summed)
    count_total = float(scored * lax.axis_size("dev"))
    loss_sum = lax.psum(jnp.sum((log_total - target_logit) * counted), "dev")
    loss_value = loss_sum / count_total
    d_head = (weighted / summed[:, None] - target_row) * (counted / count_total)[:, None]
    d_rows = norm_back(d_head, head_rows, final_norm[0], final_norm[1])
    gradient = jnp.zeros((row_count, width), F32).at[loss_pos].add(d_rows)
    prefix_grads = [None] * layer_count
    for layer_id in reversed(range(layer_count)):
        weights = (
            lax.all_gather(w_qkv[layer_id], "dev", axis=1, tiled=True),
            lax.all_gather(w_fc[layer_id], "dev", axis=0, tiled=True),
            lax.all_gather(w_out[layer_id], "dev", axis=1, tiled=True),
            lax.all_gather(w_proj[layer_id], "dev", axis=1, tiled=True),
        )
        gradient, prefix_grads[layer_id] = layer_backward(
            gradient, stored_all[layer_id], weights, frozen_vec[layer_id], layout
        )
    d_prefix = lax.psum(jnp.stack(prefix_grads), "dev")
    d_outer = jnp.einsum("pr,lcpd->rlcd", hidden, d_prefix, precision=HIGHEST)
    d_outer_bias = jnp.sum(d_prefix, 2)
    d_hidden = lax.psum(
        jnp.einsum("lcpd,rlcd->pr", d_prefix, outer_weight, precision=HIGHEST), "ta"
    )
    d_pre = d_hidden * (1.0 - hidden * hidden)
    d_inner = jnp.dot(prefix_table.T, d_pre, precision=HIGHEST)
    d_inner_bias = jnp.sum(d_pre, 0)
    table_part = jnp.dot(d_pre, inner_weight.T, precision=HIGHEST)
    squares = (
        jnp.sum(d_outer * d_outer)
        + 0.5 * (jnp.sum(d_inner * d_inner) + jnp.sum(d_inner_bias * d_inner_bias))
        + jnp.sum(d_outer_bias * d_outer_bias) / lax.axis_size("dev")
    )
    d_table = lax.psum(table_part, "dev")
    square_sum = lax.psum(squares, ("dev", "ta"))
    grad_total = jnp.sqrt(square_sum + jnp.sum(d_table * d_table))
    factor = jnp.minimum(1.0, CLIP_NORM / (grad_total + 1e-06))
    corr_one = 1.0 - BETA_ONE**adam_steps
    corr_two = 1.0 - BETA_TWO**adam_steps
    prefix_out = adamw_update(
        prefix_table, moment_prefix, square_prefix, factor * d_table, corr_one, corr_two
    )
    inner_out = adamw_update(
        inner_weight, moment_inner, square_inner, factor * d_inner, corr_one, corr_two
    )
    ibias_out = adamw_update(
        inner_bias, moment_inner_bias, square_inner_bias, factor * d_inner_bias, corr_one, corr_two
    )
    outer_out = adamw_update(
        outer_weight, moment_outer, square_outer, factor * d_outer, corr_one, corr_two
    )
    obias_out = adamw_update(
        outer_bias, moment_outer_bias, square_outer_bias, factor * d_outer_bias, corr_one, corr_two
    )
    return (
        loss_value.reshape(1),
        grad_total.reshape(1),
        prefix_out[0],
        prefix_out[1],
        prefix_out[2],
        inner_out[0],
        inner_out[1],
        inner_out[2],
        ibias_out[0],
        ibias_out[1],
        ibias_out[2],
        outer_out[0],
        outer_out[1],
        outer_out[2],
        obias_out[0],
        obias_out[1],
        obias_out[2],
        prefix_out[0].astype(B16),
        inner_out[0].astype(B16),
        ibias_out[0].astype(B16),
        outer_out[0].astype(B16),
        obias_out[0].astype(B16),
    )


def solution(mesh):
    in_specs = (
        P("dev"),
        P("dev"),
        P("dev", None),
        P("dev"),
        P("dev"),
        P(("dev", "ta"), None),
        P(),
        P(None, None, "dev", "ta"),
        P(None, "ta", "dev"),
        P(None, "dev", "ta"),
        P(None, "ta", "dev"),
        P(),
        P(None, "ta"),
        P(),
        P(),
        P(None, "dev"),
        P("dev"),
        P("dev", None, None, "ta"),
        P(None, None, "ta"),
        P(),
        P(),
        P(None, "dev"),
        P(None, "dev"),
        P("dev"),
        P("dev"),
        P("dev", None, None, "ta"),
        P("dev", None, None, "ta"),
        P(None, None, "ta"),
        P(None, None, "ta"),
    )
    out_specs = (
        P(),
        P(),
        P(),
        P(),
        P(),
        P(None, "dev"),
        P(None, "dev"),
        P(None, "dev"),
        P("dev"),
        P("dev"),
        P("dev"),
        P("dev", None, None, "ta"),
        P("dev", None, None, "ta"),
        P("dev", None, None, "ta"),
        P(None, None, "ta"),
        P(None, None, "ta"),
        P(None, None, "ta"),
        P(),
        P(None, "dev"),
        P("dev"),
        P("dev", None, None, "ta"),
        P(None, None, "ta"),
    )
    return jax.shard_map(local, mesh=mesh, in_specs=in_specs, out_specs=out_specs, check_vma=False)
```

profile of v0, /device:TPU:0, one launch (start us, length us, event | category | flops | bytes accessed | tf_op | source)
XLA Modules:
  0.0 2119.7 jit_solution(17066167317457047486)
XLA Ops:
  12.4 522.9 %all-gather.49.cloned.1.call-done = bf16[16,1572,1024]{2,1,0:T(8,128)(2,1)} async-done(((bf16[1,1572,1024]{2,1,0:T(8,128)(2,1)}), bf16[16,1572,1024]{2,1,0:T(8,128)(2,1)}) %all-gather.49.cloned.1.call-update) | async-done | bytes 51511312 | tf_op jit(solution)/shard_map/all_gather | solution.py:315
  535.3 54.4 %reshape.628 = bf16[25152,1024]{1,0:T(8,128)(2,1)} reshape(bf16[16,1572,1024]{2,1,0:T(8,128)(2,1)} %all-gather.49.cloned.1.call-done) | data formatting | bytes 103022592
  589.7 30.1 %gather_fusion.3 = bf16[1024,1024]{1,0:T(8,128)(2,1)} fusion(bf16[25152,1024]{1,0:T(8,128)(2,1)} %reshape.628, s32[1024]{0:T(1024)S(1)} %fusion.267), kind=kCustom, calls=%fused_computation.3 | custom fusion | bytes 4198400 | tf_op jit(solution)/shard_map/jit(_take)/gather | solution.py:262
  635.9 7.8 all-reduce.16.cloned.1.call-done
  644.9 21.4 %all-reduce.14.cloned.1.call-done = bf16[1024,1024]{1,0:T(8,128)(2,1)} async-done(((bf16[1024,1024]{1,0:T(8,128)(2,1)}), bf16[1024,1024]{1,0:T(8,128)(2,1)}) %all-reduce.14.cloned.1.call-update) | async-done | bytes 2097168 | tf_op jit(solution)/shard_map/psum | solution.py:59
  671.2 67.5 %all-gather.29.cloned.1.call-done = bf16[1,3,1024,512]{3,2,1,0:T(8,128)(2,1)} async-done(((bf16[1,3,64,512]{3,2,1,0:T(8,128)(2,1)}), bf16[1,3,1024,512]{3,2,1,0:T(8,128)(2,1)}) %all-gather.29.cloned.1.call-update) | async-done | bytes 3145744 | tf_op jit(solution)/shard_map/all_gather | solution.py:272
  738.7 6.6 add_convert_fusion.1
  746.5 8.4 fusion.336
  754.9 8.2 exponential_reduce_fusion.2
  763.1 11.2 fusion.337
  774.3 8.2 exponential_reduce_fusion.3
  782.5 8.7 fusion.201
  805.6 16.7 all-reduce.18.cloned.1.call-done
  828.2 74.1 %all-gather.33.cloned.1.call-done = bf16[1,1024,2048]{2,1,0:T(8,128)(2,1)} async-done(((bf16[1,64,2048]{2,1,0:T(8,128)(2,1)}), bf16[1,1024,2048]{2,1,0:T(8,128)(2,1)}) %all-gather.33.cloned.1.call-update) | async-done | bytes 4194320 | tf_op jit(solution)/shard_map/all_gather | solution.py:273
  902.3 11.3 fusion.66
  913.7 66.7 %all-gather.35.cloned.1.call-done = bf16[1,2048,1024]{1,2,0:T(8,128)(2,1)} async-done(((bf16[1,2048,64]{1,2,0:T(8,128)(2,1)}), bf16[1,2048,1024]{1,2,0:T(8,128)(2,1)}) %all-gather.35.cloned.1.call-update) | async-done | bytes 4194320 | tf_op jit(solution)/shard_map/all_gather | solution.py:275
  980.4 11.3 fusion.162
  993.8 17.8 all-reduce.20.cloned.1.call-done
  1017.8 65.7 %all-gather.37.cloned.1.call-done = bf16[1,3,1024,512]{3,2,1,0:T(8,128)(2,1)} async-done(((bf16[1,3,64,512]{3,2,1,0:T(8,128)(2,1)}), bf16[1,3,1024,512]{3,2,1,0:T(8,128)(2,1)}) %all-gather.37.cloned.1.call-update) | async-done | bytes 3145744 | tf_op jit(solution)/shard_map/all_gather | solution.py:272
  1083.5 7.0 add_convert_fusion
  1091.7 8.0 fusion.338
  1099.7 8.2 exponential_reduce_fusion
  1107.9 8.2 fusion.339
  1116.1 8.2 exponential_reduce_fusion.1
  1124.3 8.8 fusion.195
  1146.9 18.8 all-reduce.22.cloned.1.call-done
  1171.8 74.6 %all-gather.41.cloned.1.call-done = bf16[1,1024,2048]{2,1,0:T(8,128)(2,1)} async-done(((bf16[1,64,2048]{2,1,0:T(8,128)(2,1)}), bf16[1,1024,2048]{2,1,0:T(8,128)(2,1)}) %all-gather.41.cloned.1.call-update) | async-done | bytes 4194320 | tf_op jit(solution)/shard_map/all_gather | solution.py:273
  1246.3 11.4 fusion.58
  1257.8 66.5 %all-gather.43.cloned.1.call-done = bf16[1,2048,1024]{1,2,0:T(8,128)(2,1)} async-done(((bf16[1,2048,64]{1,2,0:T(8,128)(2,1)}), bf16[1,2048,1024]{1,2,0:T(8,128)(2,1)}) %all-gather.43.cloned.1.call-update) | async-done | bytes 4194320 | tf_op jit(solution)/shard_map/all_gather | solution.py:275
  1324.3 11.3 fusion.170
  1339.0 55.3 %reshape.512 = bf16[2,12576,1024]{2,1,0:T(8,128)(2,1)} reshape(bf16[16,1572,1024]{2,1,0:T(8,128)(2,1)} %all-gather.49.cloned.1.call-done) | data formatting | bytes 103022592 | tf_op jit(solution)/shard_map/reshape | solution.py:321
  1405.1 162.0 %while.3 = (s32[]{:T(128)}, f32[256]{0:T(256)S(1)}, f32[256]{0:T(256)S(1)}, f32[256,1024]{1,0:T(8,128)}, f32[256]{0:T(256)S(1)}, /*index=5*/f32[256,1024]{1,0:T(...) while((s32[]{:T(128)}, f32[256]{0:T(256)S(1)}, ...), condition=%wide.region_28.29_spmd.clone, body=%wide.region_25.28_spmd.clone.sunk | while | flops 13205097472 | bytes 156382448 | solution.py:327
  1405.5 21.0 dynamic-slice_bitcast_fusion.2
  1426.5 14.5 fusion.384
  1442.3 7.6 gather_fusion
  1456.6 15.6 fusion.388
  1472.2 13.6 gather_fusion.1
  1486.1 21.0 dynamic-slice_bitcast_fusion.2
  1507.1 14.5 fusion.384
  1522.9 7.7 gather_fusion
  1537.3 15.6 fusion.388
  1553.0 13.6 gather_fusion.1
  1576.4 11.6 all-gather.45.cloned.1.call-done
  1596.0 17.6 fusion.165
  1613.6 22.5 %all-reduce.26.cloned.1.call-done = bf16[1024,1024]{1,0:T(8,128)(2,1)} async-done(((bf16[1024,1024]{1,0:T(8,128)(2,1)}), bf16[1024,1024]{1,0:T(8,128)(2,1)}) %all-reduce.26.cloned.1.call-update) | async-done | bytes 2097168 | tf_op jit(solution)/shard_map/psum | solution.py:59
  1645.0 7.4 fusion.106
  1652.4 8.1 fusion.18
  1660.5 8.0 fusion.20
  1674.5 10.1 fusion.21
  1684.6 7.8 fusion.90
  1695.7 9.9 fusion.23
  1714.2 7.3 bitcast_convert_fusion
  1721.6 22.5 %all-reduce.28.cloned.1.call-done = bf16[1024,1024]{1,0:T(8,128)(2,1)} async-done(((bf16[1024,1024]{1,0:T(8,128)(2,1)}), bf16[1024,1024]{1,0:T(8,128)(2,1)}) %all-reduce.28.cloned.1.call-update) | async-done | bytes 2097168 | tf_op jit(solution)/shard_map/psum | solution.py:59
  1755.8 17.6 fusion.157
  1773.7 22.2 %all-reduce.30.cloned.1.call-done = bf16[1024,1024]{1,0:T(8,128)(2,1)} async-done(((bf16[1024,1024]{1,0:T(8,128)(2,1)}), bf16[1024,1024]{1,0:T(8,128)(2,1)}) %all-reduce.30.cloned.1.call-update) | async-done | bytes 2097168 | tf_op jit(solution)/shard_map/psum | solution.py:59
  1805.7 7.4 fusion.113
  1813.2 10.1 fusion.24
  1823.3 10.0 fusion.27
  1833.3 7.4 fusion.91
  1841.5 10.5 fusion.34
  1852.1 11.0 fusion.86
  1864.8 105.5 %all-reduce.32.cloned.1.call-done = f32[2,2,10,512]{3,2,1,0:T(8,128)} async-done(((f32[2,2,10,512]{3,2,1,0:T(8,128)}), f32[2,2,10,512]{3,2,1,0:T(8,128)}) %all-reduce.32.cloned.1.call-update) | async-done | bytes 81936 | tf_op jit(solution)/shard_map/psum | solution.py:348
  1981.8 39.5 %psum.110 = f32[]{:T(128)} all-reduce(f32[]{:T(128)S(6)} %add.725), channel_id=1, replica_groups=mesh['dev'=16,'ta'=2] {'dev','ta'}, use_global_device_ids=true, to_apply=%region_55.56 | all-reduce | flops 1 | bytes 8 | tf_op jit(solution)/shard_map/psum | solution.py:364
  2021.3 76.7 %all-reduce.2 = (f32[]{:T(128)}, f32[10,512]{1,0:T(8,128)S(1)}) all-reduce(f32[]{:T(128)} %get-tuple-element.295, f32[10,512]{1,0:T(8,128)S(1)} %fusion.295), channel_id=1, replica_groups=mesh['dev'=16,'ta'=2] {'dev'}, use_global_device_ids=true, to_apply=%region_30.31 | all-reduce | flops 5121 | bytes 40968 | tf_op jit(solution)/shard_map/psum | solution.py:332
  (481 shorter events, 194.0 us)
Async XLA Ops:
  7.2 623.3 %copy-start = (bf16[1024,1024]{1,0:T(8,128)(2,1)S(1)}, bf16[1024,1024]{1,0:T(8,128)(2,1)}, u32[]{:S(2)}) copy-start(bf16[1024,1024]{1,0:T(8,128)(2,1)} %param.37) | copy-start | bytes 6291460
  7.2 528.1 %all-gather.49.cloned.1.call-start = ((), (), s32[]{:S(2)}) async-start(), calls=%async_computation.20 | async-start | bytes 54870016 | tf_op jit(solution)/shard_map/all_gather | solution.py:315
  7.9 635.8 %all-reduce.16.cloned.1.call-start = ((), (), s32[]{:S(2)}) async-start(), calls=%async_computation.1 | async-start | bytes 262144 | tf_op jit(solution)/shard_map/psum | solution.py:267
  11.6 654.8 %all-reduce.14.cloned.1.call-start = ((), (), s32[]{:S(2)}) async-start(), calls=%async_computation | async-start | bytes 4194304 | tf_op jit(solution)/shard_map/psum | solution.py:59
  623.0 115.7 %all-gather.29.cloned.1.call-start = ((), (), s32[]{:S(2)}) async-start(), calls=%async_computation.10 | async-start | bytes 3342336 | tf_op jit(solution)/shard_map/all_gather | solution.py:272
  623.9 173.5 %all-gather.31.cloned.1.call-start = ((), (), s32[]{:S(2)}) async-start(), calls=%async_computation.11 | async-start | bytes 1114112 | tf_op jit(solution)/shard_map/all_gather | solution.py:274
  624.6 197.6 %all-reduce.18.cloned.1.call-start = ((), (), s32[]{:S(2)}) async-start(), calls=%async_computation.2 | async-start | bytes 4194304 | tf_op jit(solution)/shard_map/psum | solution.py:59
  625.5 276.8 %copy-start.86 = (f32[1,1,1024]{2,0,1:T(1,128)}, f32[1,1,1024]{2,0,1:T(1,128)S(1)}, u32[]{:S(2)}) copy-start(f32[1,1,1024]{2,0,1:T(1,128)S(1)} %get-tuple-element.338) | copy-start | bytes 12292
  625.5 457.9 %copy-start.68 = (f32[1,1,1024]{2,0,1:T(1,128)}, f32[1,1,1024]{2,0,1:T(1,128)S(1)}, u32[]{:S(2)}) copy-start(f32[1,1,1024]{2,0,1:T(1,128)S(1)} %get-tuple-element.335) | copy-start | bytes 12292
  625.5 620.8 %copy-start.74 = (f32[1,1,1024]{2,0,1:T(1,128)}, f32[1,1,1024]{2,0,1:T(1,128)S(1)}, u32[]{:S(2)}) copy-start(f32[1,1,1024]{2,0,1:T(1,128)S(1)} %get-tuple-element.332) | copy-start | bytes 12292
  635.9 33.8 %copy-start.16 = (bf16[1024,1024]{1,0:T(8,128)(2,1)S(1)}, bf16[1024,1024]{1,0:T(8,128)(2,1)}, u32[]{:S(2)}) copy-start(bf16[1024,1024]{1,0:T(8,128)(2,1)} %gather_fusion.4) | copy-start | bytes 6291460
  644.9 146.3 %copy-start.45 = (bf16[1,1,10,512]{2,3,1,0:T(8,128)(2,1)}, bf16[1,1,10,512]{2,3,1,0:T(8,128)(2,1)S(1)}, u32[]{:S(2)}) copy-start(bf16[1,1,10,512]{2,3,1,0:T(8,128)(2,1)S(1)} %copy.154) | copy-start | bytes 30724
  746.3 44.9 %copy-start.19 = (bf16[1024,1,512]{0,2,1:T(8,128)(2,1)}, bf16[1024,1,512]{0,2,1:T(8,128)(2,1)S(1)}, u32[]{:S(2)}) copy-start(bf16[1024,1,512]{0,2,1:T(8,128)(2,1)S(1)} %get-tuple-element.317) | copy-start | bytes 3145732
  801.6 100.7 %all-gather.33.cloned.1.call-start = ((), (), s32[]{:S(2)}) async-start(), calls=%async_computation.12 | async-start | bytes 4456448 | tf_op jit(solution)/shard_map/all_gather | solution.py:273
  803.6 176.8 %all-gather.35.cloned.1.call-start = ((), (), s32[]{:S(2)}) async-start(), calls=%async_computation.13 | async-start | bytes 4456448 | tf_op jit(solution)/shard_map/all_gather | solution.py:275
  805.5 206.2 %all-reduce.20.cloned.1.call-start = ((), (), s32[]{:S(2)}) async-start(), calls=%async_computation.3 | async-start | bytes 4194304 | tf_op jit(solution)/shard_map/psum | solution.py:59
  805.6 174.8 %copy-start.107 = (f32[1,2048]{1,0:T(1,128)}, f32[1,2048]{1,0:T(1,128)S(1)}, u32[]{:S(2)}) copy-start(f32[1,2048]{1,0:T(1,128)S(1)} %get-tuple-element.350) | copy-start | bytes 24580
  805.6 518.7 %copy-start.109 = (f32[1,2048]{1,0:T(1,128)}, f32[1,2048]{1,0:T(1,128)S(1)}, u32[]{:S(2)}) copy-start(f32[1,2048]{1,0:T(1,128)S(1)} %get-tuple-element.349) | copy-start | bytes 24580
  825.6 88.0 %copy-start.72 = (f32[1024]{0:T(1024)}, f32[1024]{0:T(1024)S(1)}, u32[]{:S(2)}) copy-start(f32[1024]{0:T(1024)S(1)} %broadcast_multiply_fusion.2) | copy-start | bytes 12292
  828.2 85.5 %copy-start.80 = (f32[1024]{0:T(1024)}, f32[1024]{0:T(1024)S(1)}, u32[]{:S(2)}) copy-start(f32[1024]{0:T(1024)S(1)} %multiply_reduce_fusion.5) | copy-start | bytes 12292
  828.2 85.5 %copy-start.98 = (f32[1024]{0:T(1024)}, f32[1024]{0:T(1024)S(1)}, u32[]{:S(2)}) copy-start(f32[1024]{0:T(1024)S(1)} %fusion.264) | copy-start | bytes 12292
  991.7 91.8 %all-gather.37.cloned.1.call-start = ((), (), s32[]{:S(2)}) async-start(), calls=%async_computation.14 | async-start | bytes 3342336 | tf_op jit(solution)/shard_map/all_gather | solution.py:272
  992.3 149.3 %all-gather.39.cloned.1.call-start = ((), (), s32[]{:S(2)}) async-start(), calls=%async_computation.15 | async-start | bytes 1114112 | tf_op jit(solution)/shard_map/all_gather | solution.py:274
  993.0 172.7 %all-reduce.22.cloned.1.call-start = ((), (), s32[]{:S(2)}) async-start(), calls=%async_computation.4 | async-start | bytes 4194304 | tf_op jit(solution)/shard_map/psum | solution.py:59
  993.7 114.2 %copy-start.43 = (bf16[1,1,10,512]{2,3,1,0:T(8,128)(2,1)}, bf16[1,1,10,512]{2,3,1,0:T(8,128)(2,1)S(1)}, u32[]{:S(2)}) copy-start(bf16[1,1,10,512]{2,3,1,0:T(8,128)(2,1)S(1)} %copy.157) | copy-start | bytes 30724
  993.8 139.3 %copy-start.47 = (bf16[1,1,10,512]{2,3,1,0:T(8,128)(2,1)}, bf16[1,1,10,512]{2,3,1,0:T(8,128)(2,1)S(1)}, u32[]{:S(2)}) copy-start(bf16[1,1,10,512]{2,3,1,0:T(8,128)(2,1)S(1)} %copy.156) | copy-start | bytes 30724
  1015.2 75.3 %copy-start.65 = (f32[1024]{0:T(1024)}, f32[1024]{0:T(1024)S(1)}, u32[]{:S(2)}) copy-start(f32[1024]{0:T(1024)S(1)} %broadcast_multiply_fusion.1) | copy-start | bytes 12292
  1017.7 72.8 %copy-start.82 = (f32[1024]{0:T(1024)}, f32[1024]{0:T(1024)S(1)}, u32[]{:S(2)}) copy-start(f32[1024]{0:T(1024)S(1)} %multiply_reduce_fusion.4) | copy-start | bytes 12292
  1017.7 72.8 %copy-start.76 = (f32[1024]{0:T(1024)}, f32[1024]{0:T(1024)S(1)}, u32[]{:S(2)}) copy-start(f32[1024]{0:T(1024)S(1)} %fusion.265) | copy-start | bytes 12292
  1090.8 42.4 %copy-start.21 = (bf16[1024,1,512]{0,2,1:T(8,128)(2,1)}, bf16[1024,1,512]{0,2,1:T(8,128)(2,1)S(1)}, u32[]{:S(2)}) copy-start(bf16[1024,1,512]{0,2,1:T(8,128)(2,1)S(1)} %get-tuple-element.313) | copy-start | bytes 3145732
  1145.5 100.8 %all-gather.41.cloned.1.call-start = ((), (), s32[]{:S(2)}) async-start(), calls=%async_computation.16 | async-start | bytes 4456448 | tf_op jit(solution)/shard_map/all_gather | solution.py:273
  1146.3 178.0 %all-gather.43.cloned.1.call-start = ((), (), s32[]{:S(2)}) async-start(), calls=%async_computation.17 | async-start | bytes 4456448 | tf_op jit(solution)/shard_map/all_gather | solution.py:275
  1146.8 247.4 %all-reduce.24.cloned.1.call-start = ((), (), s32[]{:S(2)}) async-start(), calls=%async_computation.5 | async-start | bytes 4194304 | tf_op jit(solution)/shard_map/psum | solution.py:59
  1169.2 88.5 %copy-start.70 = (f32[1024]{0:T(1024)}, f32[1024]{0:T(1024)S(1)}, u32[]{:S(2)}) copy-start(f32[1024]{0:T(1024)S(1)} %broadcast_multiply_fusion) | copy-start | bytes 12292
  1171.8 86.0 %copy-start.84 = (f32[1024]{0:T(1024)}, f32[1024]{0:T(1024)S(1)}, u32[]{:S(2)}) copy-start(f32[1024]{0:T(1024)S(1)} %multiply_reduce_fusion.3) | copy-start | bytes 12292
  1171.8 86.0 %copy-start.95 = (f32[1024]{0:T(1024)}, f32[1024]{0:T(1024)S(1)}, u32[]{:S(2)}) copy-start(f32[1024]{0:T(1024)S(1)} %fusion.266) | copy-start | bytes 12292
  1335.6 240.7 %all-gather.47.cloned.1.call-start = ((), (), s32[]{:S(2)}) async-start(), calls=%async_computation.19 | async-start | bytes 1572864 | tf_op jit(solution)/shard_map/all_gather | solution.py:25
  1338.9 65.6 %copy-start.92 = (pred[256]{0:T(512)(128)(4,1)}, pred[256]{0:T(512)(128)(4,1)S(1)}, u32[]{:S(2)}) copy-start(pred[256]{0:T(512)(128)(4,1)S(1)} %get-tuple-element.294) | copy-start | bytes 772
  1338.9 65.6 %copy-start.78 = (f32[1,1024]{1,0:T(1,128)}, f32[1,1024]{1,0:T(1,128)S(1)}, u32[]{:S(2)}) copy-start(f32[1,1024]{1,0:T(1,128)S(1)} %get-tuple-element.351) | copy-start | bytes 12292
  1338.9 55.3 %copy-start.94 = (f32[1,1,1024]{2,0,1:T(1,128)S(1)}, f32[1,1,1024]{2,0,1:T(1,128)}, u32[]{:S(2)}) copy-start(f32[1,1,1024]{2,0,1:T(1,128)} %get-tuple-element.331) | copy-start | bytes 12292
  1568.1 19.9 all-gather.45.cloned.1.call-start
  1570.2 65.9 %all-reduce.26.cloned.1.call-start = ((), (), s32[]{:S(2)}) async-start(), calls=%async_computation.6 | async-start | bytes 4194304 | tf_op jit(solution)/shard_map/psum | solution.py:59
  1596.0 40.1 %copy-start.71 = (f32[1024]{0:T(1024)S(1)}, f32[1024]{0:T(1024)}, u32[]{:S(2)}) copy-start(f32[1024]{0:T(1024)} %copy-done.70) | copy-start | bytes 12292
  1596.0 40.1 %copy-start.75 = (f32[1,1,1024]{2,0,1:T(1,128)S(1)}, f32[1,1,1024]{2,0,1:T(1,128)}, u32[]{:S(2)}) copy-start(f32[1,1,1024]{2,0,1:T(1,128)} %copy-done.74) | copy-start | bytes 12292
  1613.6 26.4 %copy-start.96 = (f32[1024]{0:T(1024)S(1)}, f32[1024]{0:T(1024)}, u32[]{:S(2)}) copy-start(f32[1024]{0:T(1024)} %copy-done.95) | copy-start | bytes 12292
  1613.6 130.6 %all-reduce.28.cloned.1.call-start = ((), (), s32[]{:S(2)}) async-start(), calls=%async_computation.7 | async-start | bytes 4194304 | tf_op jit(solution)/shard_map/psum | solution.py:59
  1714.2 29.9 %copy-start.66 = (f32[1024]{0:T(1024)S(1)}, f32[1024]{0:T(1024)}, u32[]{:S(2)}) copy-start(f32[1024]{0:T(1024)} %copy-done.65) | copy-start | bytes 12292
  1714.2 29.9 %copy-start.69 = (f32[1,1,1024]{2,0,1:T(1,128)S(1)}, f32[1,1,1024]{2,0,1:T(1,128)}, u32[]{:S(2)}) copy-start(f32[1,1,1024]{2,0,1:T(1,128)} %copy-done.68) | copy-start | bytes 12292
  1721.6 26.4 %copy-start.83 = (f32[1024]{0:T(1024)S(1)}, f32[1024]{0:T(1024)}, u32[]{:S(2)}) copy-start(f32[1024]{0:T(1024)} %copy-done.82) | copy-start | bytes 12292
  1721.6 26.5 %copy-start.77 = (f32[1024]{0:T(1024)S(1)}, f32[1024]{0:T(1024)}, u32[]{:S(2)}) copy-start(f32[1024]{0:T(1024)} %copy-done.76) | copy-start | bytes 12292
  1721.6 74.3 %all-reduce.30.cloned.1.call-start = ((), (), s32[]{:S(2)}) async-start(), calls=%async_computation.8 | async-start | bytes 4194304 | tf_op jit(solution)/shard_map/psum | solution.py:59
  1755.7 40.2 %copy-start.73 = (f32[1024]{0:T(1024)S(1)}, f32[1024]{0:T(1024)}, u32[]{:S(2)}) copy-start(f32[1024]{0:T(1024)} %copy-done.72) | copy-start | bytes 12292
  1755.7 40.2 %copy-start.87 = (f32[1,1,1024]{2,0,1:T(1,128)S(1)}, f32[1,1,1024]{2,0,1:T(1,128)}, u32[]{:S(2)}) copy-start(f32[1,1,1024]{2,0,1:T(1,128)} %copy-done.86) | copy-start | bytes 12292
  1773.4 26.4 %copy-start.99 = (f32[1024]{0:T(1024)S(1)}, f32[1024]{0:T(1024)}, u32[]{:S(2)}) copy-start(f32[1024]{0:T(1024)} %copy-done.98) | copy-start | bytes 12292
  1773.4 196.9 %all-reduce.32.cloned.1.call-start = ((), (), s32[]{:S(2)}) async-start(), calls=%async_computation.9 | async-start | bytes 262144 | tf_op jit(solution)/shard_map/psum | solution.py:348
  1852.0 118.3 %copy-start.49 = (f32[32,2,2,512]{3,2,1,0:T(2,128)S(1)}, f32[32,2,2,512]{3,2,1,0:T(2,128)}, u32[]{:S(2)}) copy-start(f32[32,2,2,512]{3,2,1,0:T(2,128)} %param.48) | copy-start | bytes 786436
  1852.0 122.0 %copy-start.61 = (f32[10,32]{1,0:T(8,128)S(1)}, f32[10,32]{1,0:T(8,128)}, u32[]{:S(2)}) copy-start(f32[10,32]{1,0:T(8,128)} %copy-done.60) | copy-start | bytes 3844
  1852.0 122.0 %copy-start.62 = (f32[10,512]{1,0:T(8,128)S(1)}, f32[10,512]{1,0:T(8,128)}, u32[]{:S(2)}) copy-start(f32[10,512]{1,0:T(8,128)} %param.45) | copy-start | bytes 61444
  1852.0 129.6 %copy-start.50 = (f32[512,32]{0,1:T(8,128)S(1)}, f32[512,32]{0,1:T(8,128)}, u32[]{:S(2)}) copy-start(f32[512,32]{0,1:T(8,128)} %param.46) | copy-start | bytes 196612
  1852.0 247.9 %copy-start.63 = (f32[32,2,2,512]{3,2,1,0:T(2,128)S(1)}, f32[32,2,2,512]{3,2,1,0:T(2,128)}, u32[]{:S(2)}) copy-start(f32[32,2,2,512]{3,2,1,0:T(2,128)} %param.56) | copy-start | bytes 786436
  1852.1 258.3 %copy-start.1 = (bf16[1024,1024]{1,0:T(8,128)(2,1)S(1)}, bf16[1024,1024]{1,0:T(8,128)(2,1)}, u32[]{:S(2)}) copy-start(bf16[1024,1024]{1,0:T(8,128)(2,1)} %param.37) | copy-start | bytes 6291460
  1863.1 245.0 %copy-start.89 = (f32[2,2,512]{2,1,0:T(2,128)S(1)}, f32[2,2,512]{2,1,0:T(2,128)}, u32[]{:S(2)}) copy-start(f32[2,2,512]{2,1,0:T(2,128)} %param.49) | copy-start | bytes 24580
  1863.1 245.0 %copy-start.104 = (f32[2,2,512]{2,1,0:T(2,128)S(1)}, f32[2,2,512]{2,1,0:T(2,128)}, u32[]{:S(2)}) copy-start(f32[2,2,512]{2,1,0:T(2,128)} %param.58) | copy-start | bytes 24580
  1863.2 245.0 %copy-start.105 = (f32[2,2,512]{2,1,0:T(2,128)S(1)}, f32[2,2,512]{2,1,0:T(2,128)}, u32[]{:S(2)}) copy-start(f32[2,2,512]{2,1,0:T(2,128)} %param.59) | copy-start | bytes 24580
  (81 other events, 649.9 us)
Sparse Core Ops, SparseCore 0:
  10.8 524.4 all-gather.48
  541.3 102.3 all-reduce.15
  646.0 20.2 all-reduce.13
  669.9 68.7 all-gather.28
  742.3 54.4 all-gather.30
  801.7 20.4 all-reduce.17
  825.0 77.2 all-gather.32
  905.7 74.6 all-gather.34
  991.8 19.7 all-reduce.19
  1014.7 68.7 all-gather.36
  1087.2 54.3 all-gather.38
  1145.6 20.0 all-reduce.21
  1169.0 77.2 all-gather.40
  1249.5 74.6 all-gather.42
  1335.8 19.7 all-reduce.23
  1568.2 8.0 all-gather.46
  1577.7 10.1 all-gather.44
  1613.7 22.3 all-reduce.25
  1721.7 22.3 all-reduce.27
  1773.5 22.3 all-reduce.29
  1864.9 105.3 all-reduce.31
where the time goes:
time: 2130 us; the launch traced here: 2120 us
  waiting for transfers between devices  1210 us (57%)
  matrix products  341 us (16%)
  local copies, waits for them, and re-layouts  274 us (13%)
  other arithmetic  143 us (7%)
  blocking collectives  124 us (6%)
  between operations  24.2 us (1%)
    all_gather x1, waiting for transfers between devices, local(): shard_part = lax.all_gather(wte, 'dev', axis=0, tiled=True)  523 us
    all_gather x2, waiting for transfers between devices, local(): lax.all_gather(w_fc[layer_id], 'dev', axis=0, tiled=True)  149 us
    psum x8, waiting for transfers between devices, across_heads(): return lax.psum(partial_sum.astype(jnp.bfloat16), 'ta').astype(jnp.float32)  142 us
    all_gather x2, waiting for transfers between devices, local(): lax.all_gather(w_qkv[layer_id], 'dev', axis=1, tiled=True)  133 us
    all_gather x2, waiting for transfers between devices, local(): lax.all_gather(w_proj[layer_id], 'dev', axis=1, tiled=True)  133 us
    psum x1, waiting for transfers between devices, local(): d_prefix = lax.psum(jnp.stack(prefix_grads), 'dev')  105 us
    unnamed x246, local copies, waits for them, and re-layouts  77 us
    psum x1, blocking collectives, local(): loss_sum = lax.psum(jnp.sum((log_total - target_logit) * counted), 'dev')  76.7 us
  transfers between devices with their start and end apart: 21, of which 18 were waited for; matrix products, arithmetic and copies ran while one was open for 15% of the time, Pallas kernels for 0%

commit v1 on v0

v1 whole, which is shorter than its diff:
```python
import functools

import jax
import jax.numpy as jnp
from jax import lax
from jax.experimental import pallas as pl
from jax.experimental.pallas import tpu as pltpu
from jax.sharding import PartitionSpec as P

HEAD_DIM = 64


EPS_NORM = 1e-05
CLIP_NORM = 0.001
LEARN_RATE = 0.02
BETA_ONE = 0.9
BETA_TWO = 0.999
ADAM_EPS = 1e-08
DECAY_RATE = 0.01
adam_steps = 10.0
NEG_BIG = -1e30
HIGHEST = lax.Precision.HIGHEST
F32 = jnp.float32
B16 = jnp.bfloat16
GELU_SCALE = 0.7978845608028654
GELU_CUBE = 0.044715
SLOT_ROWS = 48
BLOCK = 256
LANES = 128
SWAP = [(0, 1), (1, 0)]


def shape(dims, dtype):
    return jax.ShapeDtypeStruct(dims, dtype)


def params(**more):
    return pltpu.CompilerParams(dimension_semantics=("arbitrary",), **more)


def flip(array, bit):
    size = lax.axis_size("dev")
    return lax.ppermute(array, "dev", [(i, i ^ bit) for i in range(size)])


def partner(array):
    return lax.ppermute(array, "ta", SWAP)


def bit_orders(size):
    bits = [1 << k for k in range(size.bit_length() - 1)]
    if size == 16:
        x, y, near, far = bits
        return ((far, y, near, x), (near, far, x, y), (far, x, y, near))
    return tuple(tuple(bits[k:] + bits[:k]) for k in range(3))


def offsets_of(order):
    found = [0]
    for bit in order[:-1]:
        found = found + [o ^ bit for o in found]
    return found


def doubling_rounds(schedule, state, orders):
    before = []
    for pairs in schedule:
        keys = [(chunk, part, stage) for chunk, stage in pairs for part in range(len(orders))]
        sends = []
        for chunk, part, stage in keys:
            held = state[chunk, part]
            sends.append(held[0] if len(held) == 1 else jnp.concatenate(held, 0))
        tied = lax.optimization_barrier(tuple(sends) + tuple(before))
        before = []
        for (chunk, part, stage), send in zip(keys, tied):
            got = flip(send, orders[part][stage])
            state[chunk, part] = [send, got]
            before.append(got)
    return state


def sum_over_dev(array):
    bit = 1
    while bit < lax.axis_size("dev"):
        array = array + flip(array, bit)
        bit = bit * 2
    return array


def norm_rows(x):
    center = x - jnp.mean(x, -1, keepdims=True)
    scale = lax.rsqrt(jnp.mean(center * center, -1, keepdims=True) + EPS_NORM)
    return center * scale, scale


def norm_rows_back(gradient, x, gain):
    xhat, scale = norm_rows(x)
    e2 = gradient * gain
    mean_one = jnp.mean(e2, -1, keepdims=True)
    mean_two = jnp.mean(e2 * xhat, -1, keepdims=True)
    return (e2 - mean_one - xhat * mean_two) * scale


def dot_nn(a, b):
    return lax.dot_general(a, b, (((1,), (0,)), ((), ())), preferred_element_type=F32)


def dot_nt(a, b):
    return lax.dot_general(a, b, (((1,), (1,)), ((), ())), preferred_element_type=F32)


def dot_tn(a, b):
    return lax.dot_general(a, b, (((0,), (0,)), ((), ())), preferred_element_type=F32)


class Gathered:
    def __init__(self, pair, order, columns=None):
        self.pair = pair
        self.order = order
        blocks, rows, width = pair[0].shape
        self.blocks, self.rows = blocks, rows
        self.columns = (0, width) if columns is None else columns
        self.scratch = [
            pltpu.VMEM((2 * blocks * rows, self.columns[1] - self.columns[0]), B16),
            pltpu.SemaphoreType.DMA((2 * blocks,)),
        ]

    def copies(self, me, held, taken, full, sems):
        first, last = self.columns
        for index, offset in enumerate(offsets_of(self.order)):
            for side, (ref, extra) in enumerate(((held, 0), (taken, self.order[-1]))):
                start = pl.multiple_of((me ^ (offset ^ extra)) * self.rows, self.rows)
                source = ref.at[index]
                if (first, last) != (0, ref.shape[2]):
                    source = source.at[:, pl.ds(first, last - first)]
                yield pltpu.make_async_copy(
                    source, full.at[pl.ds(start, self.rows)], sems.at[2 * index + side]
                )

    def start(self, *refs):
        for copy in self.copies(*refs):
            copy.start()

    def wait(self, *refs):
        for copy in self.copies(*refs):
            copy.wait()


ANY = pl.BlockSpec(memory_space=pl.ANY)


def rows_spec(width, block=BLOCK):
    return pl.BlockSpec((block, width), lambda i, *refs: (i, 0))


def whole_spec(dims):
    return pl.BlockSpec(dims, lambda i, *refs: (0,) * len(dims))


def key_bias(layout_ref, query_pos, key_count):
    shift = layout_ref[0]
    dims = (query_pos.shape[0], key_count)
    key_pos = lax.broadcasted_iota(jnp.int32, (1, key_count), 1)
    key_seg = lax.shift_right_logical(key_pos, jnp.full((1, key_count), shift, jnp.int32))
    query_seg = lax.shift_right_logical(query_pos, jnp.full(query_pos.shape, shift, jnp.int32))
    length = jnp.zeros((1, key_count), jnp.int32)
    for slot in range(layout_ref.shape[0] - 2):
        length = jnp.where(key_seg == slot, layout_ref[2 + slot], length)
    place = key_pos - key_seg * layout_ref[1]
    key_seg = jnp.where(place < length, key_seg, -1)
    seen = (jnp.broadcast_to(query_seg, dims) == jnp.broadcast_to(key_seg, dims)) & (
        jnp.broadcast_to(key_pos, dims) <= jnp.broadcast_to(query_pos, dims)
    )
    return jnp.where(seen, 0.0, NEG_BIG)


def prefix_bias(rows, prefix_rows, prefix_len):
    lane = lax.broadcasted_iota(jnp.int32, (rows, prefix_rows), 1)
    return jnp.where(lane < prefix_len, 0.0, NEG_BIG)


def attend(query, key, value, key_prefix, value_prefix, bias, bias_prefix):
    scores = dot_nt(query, key) + bias
    scores_prefix = dot_nt(query, key_prefix) + bias_prefix
    highest = jnp.maximum(
        jnp.max(scores, -1, keepdims=True), jnp.max(scores_prefix, -1, keepdims=True)
    )
    shares = jnp.exp(scores - highest)
    shares_prefix = jnp.exp(scores_prefix - highest)
    total = jnp.sum(shares, -1, keepdims=True) + jnp.sum(shares_prefix, -1, keepdims=True)
    mixed = dot_nn(shares.astype(B16), value) + dot_nn(shares_prefix.astype(B16), value_prefix)
    return mixed / total, highest + jnp.log(total)


def attend_pairs(q_ref, k_ref, v_ref, prefix_ref, mixed_ref, lse_ref, rows, key_count, bias, plen):
    prefix_rows = prefix_ref.shape[1]
    bias_prefix = prefix_bias(BLOCK, prefix_rows, plen)
    lse_ref[rows, :] = jnp.zeros((BLOCK, LANES), F32)
    lane = lax.broadcasted_iota(jnp.int32, (BLOCK, LANES), 1)

    def pair(index, carry):
        columns = pl.ds(pl.multiple_of(index * LANES, LANES), LANES)
        query = q_ref[rows, columns]
        key = k_ref[pl.ds(0, key_count), columns]
        value = v_ref[pl.ds(0, key_count), columns]
        key_prefix = prefix_ref[0, :, columns]
        value_prefix = prefix_ref[1, :, columns]
        parts = []
        for side in range(2):
            cut = slice(side * HEAD_DIM, (side + 1) * HEAD_DIM)
            mixed, lse = attend(
                query[:, cut],
                key[:, cut],
                value[:, cut],
                key_prefix[:, cut],
                value_prefix[:, cut],
                bias,
                bias_prefix,
            )
            parts.append(mixed)
            lse_ref[rows, :] = jnp.where(lane == 2 * index + side, lse, lse_ref[rows, :])
        mixed_ref[rows, columns] = jnp.concatenate(parts, 1).astype(B16)
        return carry

    lax.fori_loop(0, q_ref.shape[1] // LANES, pair, 0)


def first_attention(stream, vectors, bias_qkv, prefix, layout, me, weight, plen):
    row_count, width = stream.shape
    half = prefix.shape[2]
    scale = HEAD_DIM ** (-0.5)

    def body(me_ref, layout_ref, stream_ref, vec_ref, bias_ref, prefix_ref, held, taken,
             part_ref, q_out, mixed_out, lse_out, full, sems, q_s, k_s, v_s):
        step = pl.program_id(0)
        refs = (me_ref[0], held, taken, full, sems)

        @pl.when(step == 0)
        def _():
            weight.start(*refs)
            weight.wait(*refs)

        xhat, unused = norm_rows(stream_ref[...])
        normed = (xhat * vec_ref[0:1, :] + vec_ref[1:2, :]).astype(B16)
        qkv = dot_nn(normed, full[:, : 3 * half]) + bias_ref[...]
        rows = pl.ds(pl.multiple_of(step * BLOCK, BLOCK), BLOCK)
        q_s[...] = (qkv[:, :half].astype(B16) * scale).astype(B16)
        k_s[rows, :] = qkv[:, half : 2 * half].astype(B16)
        v_s[rows, :] = qkv[:, 2 * half :].astype(B16)
        q_out[...] = q_s[...]
        local_pos = lax.broadcasted_iota(jnp.int32, (BLOCK, 1), 0)
        for case in range(row_count // BLOCK):

            @pl.when(step == case)
            def _(case=case):
                key_count = (case + 1) * BLOCK
                bias = key_bias(layout_ref, local_pos + case * BLOCK, key_count)
                attend_pairs(
                    q_s, k_s, v_s, prefix_ref, mixed_out, lse_out,
                    pl.ds(0, BLOCK), key_count, bias, plen,
                )

        part_ref[...] = dot_nt(mixed_out[...], full[:, 3 * half :]).astype(B16)

    return pl.pallas_call(
        body,
        grid_spec=pltpu.PrefetchScalarGridSpec(
            num_scalar_prefetch=2,
            grid=(row_count // BLOCK,),
            in_specs=[
                rows_spec(width),
                whole_spec(vectors.shape),
                whole_spec(bias_qkv.shape),
                whole_spec(prefix.shape),
                ANY,
                ANY,
            ],
            out_specs=[rows_spec(width), rows_spec(half), rows_spec(half), rows_spec(LANES)],
            scratch_shapes=weight.scratch
            + [pltpu.VMEM((BLOCK, half), B16)]
            + [pltpu.VMEM((row_count, half), B16)] * 2,
        ),
        out_shape=[
            shape((row_count, width), B16),
            shape((row_count, half), B16),
            shape((row_count, half), B16),
            shape((row_count, LANES), F32),
        ],
        compiler_params=params(),
        name="first_attention",
    )(me, layout, stream, vectors, bias_qkv, prefix, *weight.pair)


def mlp(base, own, other, vectors, bias_up, me, w_up, w_down):
    row_count, width = base.shape
    hidden = bias_up.shape[1]

    def body(me_ref, base_ref, own_ref, other_ref, vec_ref, bias_ref, up_held, up_taken,
             down_held, down_taken, part_ref, middle_ref, slope_ref, up, up_sems, down, down_sems):
        step = pl.program_id(0)
        up_refs = (me_ref[0], up_held, up_taken, up, up_sems)
        down_refs = (me_ref[0], down_held, down_taken, down, down_sems)

        @pl.when(step == 0)
        def _():
            w_up.start(*up_refs)
            w_down.start(*down_refs)

        middle = base_ref[...] + (
            (own_ref[...].astype(F32) + other_ref[...].astype(F32)) + vec_ref[0:1, :]
        )
        middle_ref[...] = middle
        xhat, unused = norm_rows(middle)
        normed = (xhat * vec_ref[1:2, :] + vec_ref[2:3, :]).astype(B16)

        @pl.when(step == 0)
        def _():
            w_up.wait(*up_refs)

        u = dot_nn(normed, up[...]) + bias_ref[...]
        square = u * u
        t = jnp.tanh(GELU_SCALE * u * (1.0 + GELU_CUBE * square))
        half_one = 0.5 + 0.5 * t
        active = (u * half_one).astype(B16)
        slope = half_one + (0.5 * GELU_SCALE) * u * (1.0 - t * t) * (1.0 + 3 * GELU_CUBE * square)
        slope_ref[...] = slope.astype(B16)

        @pl.when(step == 0)
        def _():
            w_down.wait(*down_refs)

        part_ref[...] = dot_nt(active, down[...]).astype(B16)

    return pl.pallas_call(
        body,
        grid_spec=pltpu.PrefetchScalarGridSpec(
            num_scalar_prefetch=1,
            grid=(row_count // BLOCK,),
            in_specs=[
                rows_spec(width),
                rows_spec(width),
                rows_spec(width),
                whole_spec(vectors.shape),
                whole_spec(bias_up.shape),
                ANY,
                ANY,
                ANY,
                ANY,
            ],
            out_specs=[rows_spec(width), rows_spec(width), rows_spec(hidden)],
            scratch_shapes=w_up.scratch + w_down.scratch,
        ),
        out_shape=[
            shape((row_count, width), B16),
            shape((row_count, width), F32),
            shape((row_count, hidden), B16),
        ],
        compiler_params=params(),
        name="mlp",
    )(me, base, own, other, vectors, bias_up, *w_up.pair, *w_down.pair)


def last_attention(base, own, other, vectors, bias_qkv, prefix, layout, picks, picks_column, me,
                   weight, plen):
    row_count, width = base.shape
    half = prefix.shape[2]
    scored = picks.shape[0]
    steps = row_count // BLOCK
    scale = HEAD_DIM ** (-0.5)

    def body(me_ref, layout_ref, picks_ref, base_ref, own_ref, other_ref, vec_ref, bias_ref,
             prefix_ref, column_ref, held, taken, stream_out, part_ref, k_out, v_out, q_out,
             mixed_out, lse_out, chosen_out, full, sems, stream_s, k_s, v_s):
        step = pl.program_id(0)
        refs = (me_ref[0], held, taken, full, sems)

        @pl.when(step == 0)
        def _():
            weight.start(*refs)
            weight.wait(*refs)

        stream = base_ref[...] + (
            (own_ref[...].astype(F32) + other_ref[...].astype(F32)) + vec_ref[0:1, :]
        )
        stream_out[...] = stream
        rows = pl.ds(pl.multiple_of(step * BLOCK, BLOCK), BLOCK)
        stream_s[rows, :] = stream
        xhat, unused = norm_rows(stream)
        normed = (xhat * vec_ref[1:2, :] + vec_ref[2:3, :]).astype(B16)
        keys_values = (
            dot_nn(normed, full[:, half : 3 * half]) + bias_ref[:, half : 3 * half]
        ).astype(B16)
        k_out[...] = keys_values[:, :half]
        v_out[...] = keys_values[:, half:]
        k_s[rows, :] = keys_values[:, :half]
        v_s[rows, :] = keys_values[:, half:]

        @pl.when(step == steps - 1)
        def _():
            def pick(index, carry):
                chosen_out[pl.ds(index, 1), :] = stream_s[pl.ds(picks_ref[index], 1), :]
                return carry

            lax.fori_loop(0, scored, pick, 0)
            for first in range(0, scored, BLOCK):
                block = pl.ds(first, BLOCK)
                chosen_hat, unused = norm_rows(chosen_out[block, :])
                chosen = (chosen_hat * vec_ref[1:2, :] + vec_ref[2:3, :]).astype(B16)
                query = (dot_nn(chosen, full[:, :half]) + bias_ref[:, :half]).astype(B16)
                q_out[block, :] = (query * scale).astype(B16)
                bias = key_bias(layout_ref, column_ref[block, :], row_count)
                attend_pairs(
                    q_out, k_s, v_s, prefix_ref, mixed_out, lse_out, block, row_count, bias, plen
                )
                part_ref[block, :] = dot_nt(mixed_out[block, :], full[:, 3 * half :]).astype(B16)

    return pl.pallas_call(
        body,
        grid_spec=pltpu.PrefetchScalarGridSpec(
            num_scalar_prefetch=3,
            grid=(steps,),
            in_specs=[
                rows_spec(width),
                rows_spec(width),
                rows_spec(width),
                whole_spec(vectors.shape),
                whole_spec(bias_qkv.shape),
                whole_spec(prefix.shape),
                whole_spec(picks_column.shape),
                ANY,
                ANY,
            ],
            out_specs=[
                rows_spec(width),
                whole_spec((scored, width)),
                rows_spec(half),
                rows_spec(half),
                whole_spec((scored, half)),
                whole_spec((scored, half)),
                whole_spec((scored, LANES)),
                whole_spec((scored, width)),
            ],
            scratch_shapes=weight.scratch
            + [pltpu.VMEM((row_count, width), F32)]
            + [pltpu.VMEM((row_count, half), B16)] * 2,
        ),
        out_shape=[
            shape((row_count, width), F32),
            shape((scored, width), B16),
            shape((row_count, half), B16),
            shape((row_count, half), B16),
            shape((scored, half), B16),
            shape((scored, half), B16),
            shape((scored, LANES), F32),
            shape((scored, width), F32),
        ],
        compiler_params=params(),
        name="last_attention",
    )(me, layout, picks, base, own, other, vectors, bias_qkv, prefix, picks_column, *weight.pair)


def split_lse(lse, rows):
    high = lse.astype(B16).astype(F32)
    middle = (lse - high).astype(B16).astype(F32)
    low = (lse - high) - middle
    lane = lax.broadcasted_iota(jnp.int32, (rows, LANES), 1)
    packed = jnp.where(lane == 0, high, jnp.where(lane == 1, middle, jnp.where(lane == 2, low, 0.0)))
    return packed.astype(B16)


def vocabulary(rows, table, entries):
    row_count, width = rows.shape
    padded = table.shape[0]
    tail = padded - LANES

    def body(rows_ref, table_ref, out_ref):
        logits = dot_nt(rows_ref[...], table_ref[...])
        if entries < padded:
            lane = lax.broadcasted_iota(jnp.int32, (BLOCK, LANES), 1) + tail
            masked = jnp.where(lane < entries, logits[:, tail:], NEG_BIG)
            logits = jnp.concatenate([logits[:, :tail], masked], 1)
        highest = jnp.max(logits, -1, keepdims=True)
        shares = jnp.exp(logits - highest)
        total = jnp.sum(shares, -1, keepdims=True)
        mean = dot_nn(shares.astype(B16), table_ref[...]) / total
        out_ref[:, :width] = mean.astype(B16)
        out_ref[:, width:] = split_lse(highest + jnp.log(total), BLOCK)

    return pl.pallas_call(
        body,
        grid=(row_count // BLOCK,),
        in_specs=[rows_spec(width), whole_spec(table.shape)],
        out_specs=rows_spec(width + LANES),
        out_shape=shape((row_count, width + LANES), B16),
        compiler_params=params(),
        name="vocabulary",
    )(rows, table)


def joined_lse(ref, width):
    last = ref[:, width:].astype(F32)
    return jnp.sum(last[:, 0:4], -1, keepdims=True)


def merge(first, second):
    row_count, wide = first.shape
    width = wide - LANES
    block = next(b for b in (256, 128, 64, 48, 32, 16) if row_count % b == 0)

    def body(first_ref, second_ref, out_ref):
        one, two = joined_lse(first_ref, width), joined_lse(second_ref, width)
        highest = jnp.maximum(one, two)
        scale_one, scale_two = jnp.exp(one - highest), jnp.exp(two - highest)
        total = scale_one + scale_two
        mean = first_ref[:, :width].astype(F32) * (scale_one / total)
        mean = mean + second_ref[:, :width].astype(F32) * (scale_two / total)
        out_ref[:, :width] = mean.astype(B16)
        out_ref[:, width:] = split_lse(highest + jnp.log(total), block)

    return pl.pallas_call(
        body,
        grid=(row_count // block,),
        in_specs=[rows_spec(wide, block)] * 2,
        out_specs=rows_spec(wide, block),
        out_shape=shape((row_count, wide), B16),
        compiler_params=params(),
        name="merge",
    )(first, second)


def head_back(means, head_rows, head_in, target_rows, counted, final_norm, count_total):
    scored, width = head_rows.shape

    def body(mean_ref, rows_ref, in_ref, target_ref, counted_ref, norm_ref, grad_ref, loss_ref):
        lse = joined_lse(mean_ref, width)
        target = target_ref[...].astype(F32)
        logit = jnp.sum(in_ref[...].astype(F32) * target, -1, keepdims=True)
        seen = counted_ref[...]
        loss_ref[...] = jnp.broadcast_to((lse - logit) * seen, (BLOCK, LANES))
        d_head = (mean_ref[:, :width].astype(F32) - target) * (seen / count_total)
        grad_ref[...] = norm_rows_back(d_head, rows_ref[...], norm_ref[0:1, :])

    return pl.pallas_call(
        body,
        grid=(scored // BLOCK,),
        in_specs=[
            rows_spec(width + LANES),
            rows_spec(width),
            rows_spec(width),
            rows_spec(width),
            rows_spec(1),
            whole_spec(final_norm.shape),
        ],
        out_specs=[rows_spec(width), rows_spec(LANES)],
        out_shape=[shape((scored, width), F32), shape((scored, LANES), F32)],
        compiler_params=params(),
        name="head_back",
    )(means, head_rows, head_in, target_rows, counted, final_norm)


def mlp_back(gradient, slope, me, w_up, w_down, residual=None):
    row_count, width = gradient.shape
    hidden = slope.shape[1]
    extra = [] if residual is None else list(residual)

    def body(me_ref, *refs):
        grad_ref, slope_ref = refs[0], refs[1]
        extra_refs = refs[2 : 2 + len(extra)]
        up_held, up_taken, down_held, down_taken, part_ref, *rest = refs[2 + len(extra) :]
        up, up_sems, down, down_sems = rest[-4:]
        step = pl.program_id(0)
        up_refs = (me_ref[0], up_held, up_taken, up, up_sems)
        down_refs = (me_ref[0], down_held, down_taken, down, down_sems)

        @pl.when(step == 0)
        def _():
            w_down.start(*down_refs)
            w_up.start(*up_refs)

        grad = grad_ref[...]
        if extra:
            stream_ref, gain_ref, own_ref, other_ref = extra_refs
            incoming = own_ref[...].astype(F32) + other_ref[...].astype(F32)
            grad = grad + norm_rows_back(incoming, stream_ref[...], gain_ref[...])
            rest[0][...] = grad

        @pl.when(step == 0)
        def _():
            w_down.wait(*down_refs)

        d_active = dot_nn(grad.astype(B16), down[...])
        d_upward = (d_active * slope_ref[...].astype(F32)).astype(B16)

        @pl.when(step == 0)
        def _():
            w_up.wait(*up_refs)

        part_ref[...] = dot_nt(d_upward, up[...]).astype(B16)

    extra_specs = (
        [rows_spec(width), whole_spec(extra[1].shape), rows_spec(width), rows_spec(width)]
        if extra
        else []
    )
    return pl.pallas_call(
        body,
        grid_spec=pltpu.PrefetchScalarGridSpec(
            num_scalar_prefetch=1,
            grid=(row_count // BLOCK,),
            in_specs=[rows_spec(width), rows_spec(hidden)] + extra_specs + [ANY] * 4,
            out_specs=[rows_spec(width)] * (2 if extra else 1),
            scratch_shapes=w_up.scratch + w_down.scratch,
        ),
        out_shape=[shape((row_count, width), B16)]
        + ([shape((row_count, width), F32)] if extra else []),
        compiler_params=params(),
        name="mlp_back",
    )(me, gradient, slope, *extra, *w_up.pair, *w_down.pair)


def last_attention_back(gradient, own, other, middle, gain, q, k, v, mixed, lse, prefix, layout,
                        picks, picks_column, me, weight, plen):
    scored, width = gradient.shape
    row_count, half = k.shape
    prefix_rows = prefix.shape[1]
    scale = HEAD_DIM ** (-0.5)

    def body(me_ref, layout_ref, picks_ref, grad_ref, own_ref, other_ref, middle_ref, gain_ref,
             q_ref, k_ref, v_ref, mixed_ref, lse_ref, prefix_ref, column_ref, held, taken,
             part_ref, spread_ref, dprefix_ref, full, sems, dmix_s, dq_s, dk_s, dv_s, sum_s, rows_s):
        refs = (me_ref[0], held, taken, full, sems)
        weight.start(*refs)
        incoming = own_ref[...].astype(F32) + other_ref[...].astype(F32)
        grad_mid = grad_ref[...] + norm_rows_back(incoming, middle_ref[...], gain_ref[...])
        rows_s[...] = grad_mid
        spread_ref[...] = jnp.zeros((row_count, width), F32)

        def put(index, carry):
            spread_ref[pl.ds(picks_ref[index], 1), :] = rows_s[pl.ds(index, 1), :]
            return carry

        lax.fori_loop(0, scored, put, 0)
        weight.wait(*refs)
        dmix_s[...] = dot_nn(grad_mid.astype(B16), full[:, 3 * half :]).astype(B16)
        bias = key_bias(layout_ref, column_ref[...], row_count)
        bias_prefix = prefix_bias(scored, prefix_rows, plen)
        lane = lax.broadcasted_iota(jnp.int32, (scored, LANES), 1)

        def pair(index, carry):
            columns = pl.ds(pl.multiple_of(index * LANES, LANES), LANES)
            query, key, value = q_ref[:, columns], k_ref[:, columns], v_ref[:, columns]
            d_mixed = dmix_s[:, columns]
            key_p, value_p = prefix_ref[0, :, columns], prefix_ref[1, :, columns]
            found = [[], [], [], [], []]
            for side in range(2):
                cut = slice(side * HEAD_DIM, (side + 1) * HEAD_DIM)
                log_total = jnp.sum(
                    jnp.where(lane == 2 * index + side, lse_ref[...], 0.0), -1, keepdims=True
                )
                qh, dh = query[:, cut], d_mixed[:, cut]
                shares = jnp.exp(dot_nt(qh, key[:, cut]) + bias - log_total)
                shares_p = jnp.exp(dot_nt(qh, key_p[:, cut]) + bias_prefix - log_total)
                d_shares = dot_nt(dh, value[:, cut]).astype(B16).astype(F32)
                d_shares_p = dot_nt(dh, value_p[:, cut]).astype(B16).astype(F32)
                inner = jnp.sum(shares * d_shares, -1, keepdims=True) + jnp.sum(
                    shares_p * d_shares_p, -1, keepdims=True
                )
                d_scores = (shares * (d_shares - inner)).astype(B16)
                d_scores_p = (shares_p * (d_shares_p - inner)).astype(B16)
                found[0].append(
                    (dot_nn(d_scores, key[:, cut]) + dot_nn(d_scores_p, key_p[:, cut])) * scale
                )
                found[1].append(dot_tn(d_scores, qh))
                found[2].append(dot_tn(shares.astype(B16), dh))
                found[3].append(dot_tn(d_scores_p, qh))
                found[4].append(dot_tn(shares_p.astype(B16), dh))
            joined = [jnp.concatenate(f, 1) for f in found]
            dq_s[:, columns] = joined[0].astype(B16)
            dk_s[:, columns] = joined[1].astype(B16)
            dv_s[:, columns] = joined[2].astype(B16)
            dprefix_ref[0, :, columns] = joined[3]
            dprefix_ref[1, :, columns] = joined[4]
            return carry

        lax.fori_loop(0, half // LANES, pair, 0)
        sum_s[...] = dot_nt(dk_s[...], full[:, half : 2 * half]) + dot_nt(
            dv_s[...], full[:, 2 * half : 3 * half]
        )
        rows_s[...] = dot_nt(dq_s[...], full[:, :half])

        def add(index, carry):
            place = pl.ds(picks_ref[index], 1)
            sum_s[place, :] = sum_s[place, :] + rows_s[pl.ds(index, 1), :]
            return carry

        lax.fori_loop(0, scored, add, 0)
        part_ref[...] = sum_s[...].astype(B16)

    inputs = [gradient, own, other, middle, gain, q, k, v, mixed, lse, prefix, picks_column]
    return pl.pallas_call(
        body,
        grid_spec=pltpu.PrefetchScalarGridSpec(
            num_scalar_prefetch=3,
            grid=(1,),
            in_specs=[whole_spec(a.shape) for a in inputs] + [ANY, ANY],
            out_specs=[
                whole_spec((row_count, width)),
                whole_spec((row_count, width)),
                whole_spec(prefix.shape),
            ],
            scratch_shapes=weight.scratch
            + [
                pltpu.VMEM((scored, half), B16),
                pltpu.VMEM((scored, half), B16),
                pltpu.VMEM((row_count, half), B16),
                pltpu.VMEM((row_count, half), B16),
                pltpu.VMEM((row_count, width), F32),
                pltpu.VMEM((scored, width), F32),
            ],
        ),
        out_shape=[
            shape((row_count, width), B16),
            shape((row_count, width), F32),
            shape(prefix.shape, F32),
        ],
        compiler_params=params(),
        name="last_attention_back",
    )(me, layout, picks, *inputs, *weight.pair)


def first_prefix_back(gradient, own, other, middle, gain, q, mixed, lse, prefix, me, weight, plen):
    row_count, width = gradient.shape
    half = q.shape[1]
    prefix_rows = prefix.shape[1]

    def body(me_ref, grad_ref, own_ref, other_ref, middle_ref, gain_ref, q_ref, mixed_ref,
             lse_ref, prefix_ref, held, taken, dprefix_ref, full, sems):
        step = pl.program_id(0)
        refs = (me_ref[0], held, taken, full, sems)

        @pl.when(step == 0)
        def _():
            weight.start(*refs)
            dprefix_ref[...] = jnp.zeros(prefix.shape, F32)

        incoming = own_ref[...].astype(F32) + other_ref[...].astype(F32)
        grad_mid = grad_ref[...] + norm_rows_back(incoming, middle_ref[...], gain_ref[...])

        @pl.when(step == 0)
        def _():
            weight.wait(*refs)

        d_mixed = dot_nn(grad_mid.astype(B16), full[...]).astype(B16)
        product = d_mixed.astype(F32) * mixed_ref[...].astype(F32)
        bias_prefix = prefix_bias(BLOCK, prefix_rows, plen)
        d_keys = []
        d_values = []
        for head in range(half // HEAD_DIM):
            cut = slice(head * HEAD_DIM, (head + 1) * HEAD_DIM)
            qh, dh = q_ref[:, cut], d_mixed[:, cut]
            inner = jnp.sum(product[:, cut], -1, keepdims=True)
            shares = jnp.exp(
                dot_nt(qh, prefix_ref[0, :, cut]) + bias_prefix - lse_ref[:, head : head + 1]
            )
            d_shares = dot_nt(dh, prefix_ref[1, :, cut]).astype(B16).astype(F32)
            d_scores = (shares * (d_shares - inner)).astype(B16)
            d_keys.append(dot_tn(d_scores, qh))
            d_values.append(dot_tn(shares.astype(B16), dh))
        dprefix_ref[0] += jnp.concatenate(d_keys, 1)
        dprefix_ref[1] += jnp.concatenate(d_values, 1)

    return pl.pallas_call(
        body,
        grid_spec=pltpu.PrefetchScalarGridSpec(
            num_scalar_prefetch=1,
            grid=(row_count // BLOCK,),
            in_specs=[
                rows_spec(width),
                rows_spec(width),
                rows_spec(width),
                rows_spec(width),
                whole_spec(gain.shape),
                rows_spec(half),
                rows_spec(half),
                rows_spec(LANES),
                whole_spec(prefix.shape),
                ANY,
                ANY,
            ],
            out_specs=whole_spec(prefix.shape),
            scratch_shapes=weight.scratch,
        ),
        out_shape=shape(prefix.shape, F32),
        compiler_params=params(),
        name="first_prefix_back",
    )(me, gradient, own, other, middle, gain, q, mixed, lse, prefix, *weight.pair)


def table_rows(ids, table):
    count = ids.shape[0]
    shard_rows, width = table.shape
    size = lax.axis_size("dev")
    own = lax.axis_index("ta")
    ta_size = lax.axis_size("ta")
    shard = ids // shard_rows
    inside = ids % shard_rows
    order = jnp.arange(count, dtype=jnp.int32)
    same = ids[:, None] == ids[None, :]
    first = jnp.min(jnp.where(same, order[None], count), 1)
    is_first = first == order
    earlier = is_first[None] & (shard[None] == shard[:, None]) & (order[None] < first[:, None])
    rank = jnp.sum(earlier.astype(jnp.int32), 1)
    mine = shard % ta_size == own
    need = jnp.max(jnp.where(mine, rank, 0)) // SLOT_ROWS + 1
    slots = jnp.arange(size * SLOT_ROWS, dtype=jnp.int32)

    def fetch(turn, rows):
        local_rank = rank - turn * SLOT_ROWS
        used = mine & (local_rank >= 0) & (local_rank < SLOT_ROWS)
        slot = jnp.where(used, shard // ta_size * SLOT_ROWS + local_rank, -1)
        asked = jnp.max(jnp.where(slot[None] == slots[:, None], inside[None], 0), 1)
        asked = asked.reshape(size, SLOT_ROWS)
        header = jnp.broadcast_to(need, (size, 1))
        wanted = lax.all_to_all(jnp.concatenate([asked, header], 1), "dev", 0, 0)
        numbers = jnp.arange(shard_rows, dtype=jnp.int32)
        pick = (wanted[:, :SLOT_ROWS].reshape(-1, 1) == numbers[None]).astype(B16)
        sent = jnp.dot(pick, table, preferred_element_type=F32).astype(B16)
        got = lax.all_to_all(sent.reshape(size, SLOT_ROWS, width), "dev", 0, 0)
        spread = (slot[:, None] == slots[None]).astype(B16)
        found = jnp.dot(spread, got.reshape(-1, width), preferred_element_type=F32).astype(B16)
        return rows + found, jnp.max(wanted[:, SLOT_ROWS])

    rows, most = fetch(0, jnp.zeros((count, width), B16))
    most = jnp.maximum(most, partner(most.reshape(1, 1))[0, 0])

    def again(state):
        return state[0] < most

    def turn(state):
        return (state[0] + 1, fetch(state[0], state[1])[0])

    rows = lax.while_loop(again, turn, (jnp.int32(1), rows))[1]
    return rows + partner(rows)


def adamw_update(weight, moment, square, gradient, corr_one, corr_two):
    moment = BETA_ONE * moment + (1.0 - BETA_ONE) * gradient
    square = BETA_TWO * square + (1.0 - BETA_TWO) * gradient * gradient
    weight = weight - LEARN_RATE * (
        moment / corr_one / (jnp.sqrt(square / corr_two) + ADAM_EPS) + DECAY_RATE * weight
    )
    return (weight, moment, square)


def local(
    token_ids,
    bucket,
    seq_lengths,
    loss_pos,
    targets,
    wte,
    wpe,
    w_qkv,
    w_out,
    w_fc,
    w_proj,
    frozen_vec,
    fc_bias,
    final_norm,
    prefix_table,
    inner_weight,
    inner_bias,
    outer_weight,
    outer_bias,
    moment_prefix,
    square_prefix,
    moment_inner,
    square_inner,
    moment_inner_bias,
    square_inner_bias,
    moment_outer,
    square_outer,
    moment_outer_bias,
    square_outer_bias,
):
    row_count = token_ids.shape[0]
    scored = loss_pos.shape[0]
    width = wte.shape[1]
    half = w_qkv.shape[3]
    size = lax.axis_size("dev")
    own_index = lax.axis_index("ta")
    plen = prefix_table.shape[0]
    prefix_rows = 16
    me = lax.axis_index("dev").astype(jnp.int32).reshape(1)
    orders = bit_orders(size)
    stages = len(orders[0])
    bucket_width = bucket[0]
    shift = jnp.where(bucket_width == 256, 8, 10).astype(jnp.int32)
    layout = jnp.concatenate([shift.reshape(1), bucket_width.reshape(1), seq_lengths[0]])

    state = {}
    for layer_id in range(2):
        attention = jnp.concatenate(
            [w_qkv[layer_id, c] for c in range(3)] + [w_out[layer_id].T], 1
        )
        for part, rows in enumerate((attention, w_fc[layer_id], w_proj[layer_id].T)):
            state[layer_id, part] = [rows[None]]
    schedule = [[(layer_id, stage)] for layer_id in range(2) for stage in range(stages)]
    state = doubling_rounds(schedule, state, orders)

    def weight(layer_id, part, columns=None):
        return Gathered(state[layer_id, part], orders[part], columns)

    hidden = jnp.tanh(jnp.dot(prefix_table, inner_weight, precision=HIGHEST) + inner_bias)
    partial_kv = jnp.einsum("pr,rlcd->lcpd", hidden, outer_weight, precision=HIGHEST)
    prefix_kv = (sum_over_dev(partial_kv) + outer_bias[:, :, None, :]).astype(B16)
    prefix_kv = jnp.pad(prefix_kv, ((0, 0), (0, 0), (0, prefix_rows - plen), (0, 0)))

    rows = table_rows(jnp.concatenate([token_ids, targets]), wte)
    target_rows = rows[row_count:]
    repeat = row_count // 256
    places = jnp.where(bucket_width == 256, jnp.tile(wpe[:256], (repeat, 1)), wpe[:row_count])
    stream = rows[:row_count].astype(F32) + places.astype(F32)

    def head_bias(layer_id):
        part = lax.dynamic_slice_in_dim(frozen_vec[layer_id, 4:7], own_index * half, half, 1)
        return part.reshape(1, 3 * half)

    part, q0, mixed0, lse0 = first_attention(
        stream, frozen_vec[0, 0:2], head_bias(0), prefix_kv[0], layout, me, weight(0, 0), plen
    )
    vec = frozen_vec[0]
    part_two, middle0, slope0 = mlp(
        stream,
        part,
        partner(part),
        jnp.stack([vec[7], vec[2], vec[3]]),
        fc_bias[0:1],
        me,
        weight(0, 1),
        weight(0, 2),
    )

    vec_last = frozen_vec[1]
    picks_column = loss_pos.reshape(scored, 1)
    stream1, part, k1, v1, q1, mixed1, lse1, chosen = last_attention(
        middle0,
        part_two,
        partner(part_two),
        jnp.stack([vec[8], vec_last[0], vec_last[1]]),
        head_bias(1),
        prefix_kv[1],
        layout,
        loss_pos,
        picks_column,
        me,
        weight(1, 0),
        plen,
    )
    part_two, middle1, slope1 = mlp(
        chosen,
        part,
        partner(part),
        jnp.stack([vec_last[7], vec_last[2], vec_last[3]]),
        fc_bias[1:2],
        me,
        weight(1, 1),
        weight(1, 2),
    )
    both = part_two.astype(F32) + partner(part_two).astype(F32)
    head_rows = middle1 + (both + vec_last[8])
    center = head_rows - jnp.mean(head_rows, -1, keepdims=True)
    spread = jnp.mean(center * center, -1, keepdims=True)
    head_in = (center * lax.rsqrt(spread + EPS_NORM) * final_norm[0] + final_norm[1]).astype(B16)

    entries = 2 * wte.shape[0]
    padded = -(-entries // LANES) * LANES
    table = jnp.concatenate(
        [wte, partner(wte), jnp.zeros((padded - entries, width), B16)], 0
    )
    core_rows = scored // 2
    mine = lax.dynamic_slice_in_dim(head_in, own_index * core_rows, core_rows, 0)
    cuts = (0, 48, 96, core_rows)
    head = {(0, p): [mine[None, cuts[p] : cuts[p + 1]]] for p in range(3)}
    head = doubling_rounds([[(0, stage)] for stage in range(stages)], head, orders)
    results = []
    for side in range(2):
        stacks = [head[0, p][side].reshape(-1, width) for p in range(3)]
        answer = vocabulary(jnp.concatenate(stacks, 0), table, entries)
        ends = [0]
        for stack in stacks:
            ends.append(ends[-1] + stack.shape[0])
        results.append([answer[ends[p] : ends[p + 1]] for p in range(3)])
    keep, send = results
    for stage in reversed(range(stages)):
        if stage < stages - 1:
            split = [a.shape[0] // 2 for a in keep]
            send = [a[s:] for a, s in zip(keep, split)]
            keep = [a[:s] for a, s in zip(keep, split)]
        send = lax.optimization_barrier(tuple(send))
        keep = [merge(a, flip(b, orders[p][stage])) for p, (a, b) in enumerate(zip(keep, send))]
    own_means = jnp.concatenate(keep, 0)
    other_means = partner(own_means)
    means = jnp.where(
        own_index == 0,
        jnp.concatenate([own_means, other_means], 0),
        jnp.concatenate([other_means, own_means], 0),
    )
    place = loss_pos % bucket_width
    slot = loss_pos // bucket_width
    lengths = jnp.sum(
        jnp.where(
            slot[:, None] == jnp.arange(seq_lengths.shape[1], dtype=jnp.int32)[None],
            seq_lengths[0][None],
            0,
        ),
        1,
    )
    counted = (place < lengths).astype(F32).reshape(scored, 1)
    count_total = float(scored * size)
    grad_rows, loss_terms = head_back(
        means, head_rows, head_in, target_rows, counted, final_norm, count_total
    )
    loss_part = jnp.sum(loss_terms[:, 0])

    (part,) = mlp_back(grad_rows, slope1, me, weight(1, 1), weight(1, 2))
    part, spread_grad, d_prefix1 = last_attention_back(
        grad_rows,
        part,
        partner(part),
        middle1,
        vec_last[2:3],
        q1,
        k1,
        v1,
        mixed1,
        lse1,
        prefix_kv[1],
        layout,
        loss_pos,
        picks_column,
        me,
        weight(1, 0),
        plen,
    )
    d_prefix1 = sum_over_dev(d_prefix1[:, :plen])
    part, grad_stream = mlp_back(
        spread_grad,
        slope0,
        me,
        weight(0, 1),
        weight(0, 2),
        (stream1, vec_last[0:1], part, partner(part)),
    )
    d_prefix0 = first_prefix_back(
        grad_stream,
        part,
        partner(part),
        middle0,
        vec[2:3],
        q0,
        mixed0,
        lse0,
        prefix_kv[0],
        me,
        weight(0, 0, (3 * half, 4 * half)),
        plen,
    )
    d_prefix0 = sum_over_dev(d_prefix0[:, :plen])
    d_prefix = jnp.stack([d_prefix0, d_prefix1])

    d_outer = jnp.einsum("pr,lcpd->rlcd", hidden, d_prefix, precision=HIGHEST)
    d_outer_bias = jnp.sum(d_prefix, 2)
    hidden_part = jnp.einsum("lcpd,rlcd->pr", d_prefix, outer_weight, precision=HIGHEST)
    outer_square = jnp.sum(d_outer * d_outer) + jnp.sum(d_outer_bias * d_outer_bias) / size
    over_ta = jnp.concatenate(
        [hidden_part, jnp.broadcast_to(outer_square, (1, hidden_part.shape[1]))], 0
    )
    over_ta = over_ta + partner(over_ta)
    d_hidden = over_ta[:plen]
    d_pre = d_hidden * (1.0 - hidden * hidden)
    d_inner = jnp.dot(prefix_table.T, d_pre, precision=HIGHEST)
    d_inner_bias = jnp.sum(d_pre, 0)
    table_part = jnp.dot(d_pre, inner_weight.T, precision=HIGHEST)
    squares = over_ta[plen, 0] + jnp.sum(d_inner * d_inner) + jnp.sum(d_inner_bias * d_inner_bias)
    lane = jnp.arange(table_part.shape[1], dtype=jnp.int32)
    last_row = jnp.where(lane == 0, squares, jnp.where(lane == 1, loss_part, 0.0))
    totals = sum_over_dev(jnp.concatenate([table_part, last_row[None]], 0))
    d_table = totals[:plen]
    square_sum = totals[plen, 0]
    loss_value = totals[plen, 1] / count_total
    grad_total = jnp.sqrt(square_sum + jnp.sum(d_table * d_table))
    factor = jnp.minimum(1.0, CLIP_NORM / (grad_total + 1e-06))
    corr_one = 1.0 - BETA_ONE**adam_steps
    corr_two = 1.0 - BETA_TWO**adam_steps
    prefix_out = adamw_update(
        prefix_table, moment_prefix, square_prefix, factor * d_table, corr_one, corr_two
    )
    inner_out = adamw_update(
        inner_weight, moment_inner, square_inner, factor * d_inner, corr_one, corr_two
    )
    ibias_out = adamw_update(
        inner_bias, moment_inner_bias, square_inner_bias, factor * d_inner_bias, corr_one, corr_two
    )
    outer_out = adamw_update(
        outer_weight, moment_outer, square_outer, factor * d_outer, corr_one, corr_two
    )
    obias_out = adamw_update(
        outer_bias, moment_outer_bias, square_outer_bias, factor * d_outer_bias, corr_one, corr_two
    )
    return (
        loss_value.reshape(1),
        grad_total.reshape(1),
        prefix_out[0],
        prefix_out[1],
        prefix_out[2],
        inner_out[0],
        inner_out[1],
        inner_out[2],
        ibias_out[0],
        ibias_out[1],
        ibias_out[2],
        outer_out[0],
        outer_out[1],
        outer_out[2],
        obias_out[0],
        obias_out[1],
        obias_out[2],
        prefix_out[0].astype(B16),
        inner_out[0].astype(B16),
        ibias_out[0].astype(B16),
        outer_out[0].astype(B16),
        obias_out[0].astype(B16),
    )


def solution(mesh):
    in_specs = (
        P("dev"),
        P("dev"),
        P("dev", None),
        P("dev"),
        P("dev"),
        P(("dev", "ta"), None),
        P(),
        P(None, None, "dev", "ta"),
        P(None, "ta", "dev"),
        P(None, "dev", "ta"),
        P(None, "ta", "dev"),
        P(),
        P(None, "ta"),
        P(),
        P(),
        P(None, "dev"),
        P("dev"),
        P("dev", None, None, "ta"),
        P(None, None, "ta"),
        P(),
        P(),
        P(None, "dev"),
        P(None, "dev"),
        P("dev"),
        P("dev"),
        P("dev", None, None, "ta"),
        P("dev", None, None, "ta"),
        P(None, None, "ta"),
        P(None, None, "ta"),
    )
    out_specs = (
        P(),
        P(),
        P(),
        P(),
        P(),
        P(None, "dev"),
        P(None, "dev"),
        P(None, "dev"),
        P("dev"),
        P("dev"),
        P("dev"),
        P("dev", None, None, "ta"),
        P("dev", None, None, "ta"),
        P("dev", None, None, "ta"),
        P(None, None, "ta"),
        P(None, None, "ta"),
        P(None, None, "ta"),
        P(),
        P(None, "dev"),
        P("dev"),
        P("dev", None, None, "ta"),
        P(None, None, "ta"),
    )
    return jax.shard_map(local, mesh=mesh, in_specs=in_specs, out_specs=out_specs, check_vma=False)
```

time: 2130 us -> 773 us (0.36)
  waiting for transfers between devices: 1210 us -> 281 us
  matrix products: 341 us -> 14.3 us
  Pallas kernels: 0 us -> 231 us
  local copies, waits for them, and re-layouts: 274 us -> 88.3 us
  blocking collectives: 124 us -> 0 us
  other arithmetic: 143 us -> 47.3 us
  starting transfers between devices: 1.47 us -> 86.9 us
    all_gather x11 -> x0, waiting for transfers between devices: 953 us -> none  [the longest x1 523 us: local(): shard_part = lax.all_gather(wte, 'dev', axis=0, tiled=True)]
    dot_general x39 -> x2, matrix products: 334 us -> 11.4 us  [the longest x1 6.18 us: fetch(): sent = jnp.dot(pick, table, preferred_element_type=F32).astype(B16)]
    ppermute x0 -> x76, waiting for transfers between devices: none -> 272 us  [the longest x64 260 us: flip(): return lax.ppermute(array, 'dev', [(i, i ^ bit) for i in range(size)])]
    psum x10 -> x0, waiting for transfers between devices: 255 us -> none  [the longest x8 142 us: across_heads(): return lax.psum(partial_sum.astype(jnp.bfloat16), 'ta').astype(jnp.float32)]
    pallas_call x0 -> x23, Pallas kernels: none -> 231 us  [the longest x2 42.1 us: vocabulary(): pl.pallas_call(body, grid=(row_count // BLOCK,), in_specs=[rows_spec(widt...]
    psum x3 -> x0, blocking collectives: 119 us -> none  [the longest x1 76.7 us: local(): loss_sum = lax.psum(jnp.sum((log_total - target_logit) * counted), 'dev')]
    gather x8 -> x0, local copies, waits for them, and re-layouts: 83.6 us -> none  [the longest x1 30.1 us: local(): found_rows = jnp.take(shard_part, clipped, axis=0).astype(F32)]
    reduce_sum x27 -> x6, other arithmetic: 83.5 us -> 5.43 us  [the longest x1 2.21 us: table_rows(): rank = jnp.sum(earlier.astype(jnp.int32), 1)]
  transfers between devices with their start and end apart: 21 -> 78, of which waited for: 18 -> 45; matrix products, arithmetic and copies ran while one was open for 15% -> 14% of each run, Pallas kernels for 0% -> 18%
where the time goes in v1:
time: 773 us; the launch traced here: 763 us
  waiting for transfers between devices  281 us (36%)
  Pallas kernels  231 us (30%)
  local copies, waits for them, and re-layouts  88.3 us (11%)
  starting transfers between devices  86.9 us (11%)
  other arithmetic  47.3 us (6%)
  matrix products  14.3 us (2%)
  between operations  13.8 us (2%)
    ppermute x64, waiting for transfers between devices, flip(): return lax.ppermute(array, 'dev', [(i, i ^ bit) for i in range(size)])  260 us
    ppermute x64, starting transfers between devices, flip(): return lax.ppermute(array, 'dev', [(i, i ^ bit) for i in range(size)])  75.1 us
    pallas_call x2, Pallas kernels, vocabulary(): pl.pallas_call(body, grid=(row_count // BLOCK,), in_specs=[rows_spec(widt...  42.1 us
    pallas_call x2, Pallas kernels, mlp(): pl.pallas_call(body, grid_spec=pltpu.PrefetchScalarGridSpec(num_scalar_pr...  32.2 us
    concatenate x1, local copies, waits for them, and re-layouts, local(): jnp.concatenate([wte, partner(wte), jnp.zeros((padded - entries, width),...  31.1 us
    pallas_call x1, Pallas kernels, first_attention(): pl.pallas_call(body, grid_spec=pltpu.PrefetchScalarGridSpec(num_scalar_pr...  30.9 us
    pallas_call x2, Pallas kernels, mlp_back(): pl.pallas_call(body, grid_spec=pltpu.PrefetchScalarGridSpec(num_scalar_pr...  28.8 us
    pallas_call x12, Pallas kernels, merge(): pl.pallas_call(body, grid=(row_count // block,), in_specs=[rows_spec(wide...  28.5 us
  transfers between devices with their start and end apart: 78, of which 45 were waited for; matrix products, arithmetic and copies ran while one was open for 14% of the time, Pallas kernels for 18%

profile of v1, /device:TPU:0, one launch (start us, length us, event | category | flops | bytes accessed | tf_op | source)
XLA Modules:
  0.0 762.7 jit_solution(11010947853577659229)
XLA Ops:
  6.5 4.1 collective-permute-start.6
  19.5 3.8 all-to-all-start.2
  23.3 2.8 collective-permute-start.8
  26.1 8.3 %all-to-all-done.2 = s32[16,1,49]{2,1,0:T(1,128)S(1)} async-done(((s32[16,1,49]{2,1,0:T(1,128)}), s32[16,1,49]{2,1,0:T(1,128)S(1)}, u32[]{:S(2)}, u32[]{:S(2)}) %all-to-all-start.2) | async-done | bytes 3168 | tf_op jit(solution)/shard_map/all_to_all | solution.py:824
  34.6 2.6 collective-permute-done.8
  38.9 6.2 fusion.25
  45.1 5.5 all-to-all-start.3
  50.7 2.8 collective-permute-start.10
  55.0 54.9 %collective-permute-done.10 = bf16[2,64,2048]{2,1,0:T(8,128)(2,1)S(1)} collective-permute-done((bf16[2,64,2048]{2,1,0:T(8,128)(2,1)S(1)}, bf16[2,64,2048]{2,1,0:T(8,128)(2,1)S(1)}, u32[]{:S(2)}, u32[]{:S(2)}) %collective-permute-start.10) | collective-permute-done | bytes 524320 | tf_op jit(solution)/shard_map/ppermute | solution.py:43
  111.8 2.2 collective-permute-start.14
  118.0 16.5 %collective-permute-done.12 = bf16[4,64,2048]{2,1,0:T(8,128)(2,1)} collective-permute-done((bf16[4,64,2048]{2,1,0:T(8,128)(2,1)S(1)}, bf16[4,64,2048]{2,1,0:T(8,128)(2,1)}, u32[]{:S(2)}, u32[]{:S(2)}) %collective-permute-start.12) | collective-permute-done | bytes 1048608 | tf_op jit(solution)/shard_map/ppermute | solution.py:43
  134.5 2.7 pad_maximum_fusion.held
  137.2 2.8 pad_maximum_fusion.1.up_held.refs_6_
  139.9 2.8 pad_maximum_fusion.2.down_held.refs_8_
  146.7 5.2 fusion.22
  154.3 35.8 %collective-permute-done.15.taken = bf16[8,64,2048]{2,1,0:T(8,128)(2,1)} collective-permute-done((bf16[8,64,2048]{2,1,0:T(8,128)(2,1)}, bf16[8,64,2048]{2,1,0:T(8,128)(2,1)}, u32[]{:S(2)}, u32[]{:S(2)}) %collective-permute-start.15) | collective-permute-done | bytes 2097184 | tf_op jit(solution)/shard_map/ppermute | solution.py:43
  199.0 2.4 collective-permute-start.22
  201.3 6.3 collective-permute-done.20
  207.8 21.0 %collective-permute-done.22 = bf16[1,64,2048]{2,1,0:T(8,128)(2,1)S(1)} collective-permute-done((bf16[1,64,2048]{2,1,0:T(8,128)(2,1)S(1)}, bf16[1,64,2048]{2,1,0:T(8,128)(2,1)S(1)}, u32[]{:S(2)}, u32[]{:S(2)}) %collective-permute-start.22) | collective-permute-done | bytes 262176 | tf_op jit(solution)/shard_map/ppermute | solution.py:43
  230.3 2.9 collective-permute-start.24
  233.2 3.8 collective-permute-done.5
  238.7 3.9 collective-permute-done.24
  243.7 3.1 add.355
  246.9 3.1 convert_add_fusion.stream_ref.base_ref
  250.0 30.9 %first_attention.1 = (bf16[1024,1024]{1,0:T(8,128)(2,1)}, bf16[1024,512]{1,0:T(8,128)(2,1)}, bf16[1024,512]{1,0:T(8,128)(2,1)}, f32[1024,128]{1,0:T(8,128)}) custom-call(s32[1]{0:T(128)} %bitcast.me_ref, s32[6]{0:T(128)} %pad_add_fusion.2.layout_ref, f32[1024,1024]{1,0:T(8,128)} %convert_add_fusion.stream_ref.base_ref, f32[2,1024]{1,0:T(2,128)} %bitcast.177, ...), custom_call_target="tpu_custom_call" | custom-call | tf_op jit(solution)/shard_map/first_attention/pallas_call | solution.py:265
  284.7 22.1 %collective-permute-done.26 = bf16[4,64,2048]{2,1,0:T(8,128)(2,1)S(1)} collective-permute-done((bf16[4,64,2048]{2,1,0:T(8,128)(2,1)S(1)}, bf16[4,64,2048]{2,1,0:T(8,128)(2,1)S(1)}, u32[]{:S(2)}, u32[]{:S(2)}) %collective-permute-start.26) | collective-permute-done | bytes 1048608 | tf_op jit(solution)/shard_map/ppermute | solution.py:43
  307.0 3.4 pad_maximum_fusion.4.up_held.refs_2_
  312.9 22.6 %mlp.2 = (bf16[1024,1024]{1,0:T(8,128)(2,1)}, f32[1024,1024]{1,0:T(8,128)}, bf16[1024,2048]{1,0:T(8,128)(2,1)}) custom-call(s32[1]{0:T(128)} %bitcast.me_ref, f32[1024,1024]{1,0:T(8,128)} %convert_add_fusion.stream_ref.base_ref, bf16[1024,1024]{1,0:T(8,128)(2,1)} %get-tuple-element.299.own_ref, bf16[1024,1024]{1,0:T(8,128)(2,1)} %collective-permute-done.16.other_ref, ...), custom_call_target="tpu_custom_call" | custom-call | tf_op jit(solution)/shard_map/mlp/pallas_call | solution.py:334
  339.2 20.1 %collective-permute-done.29.taken = bf16[8,64,2048]{2,1,0:T(8,128)(2,1)} collective-permute-done((bf16[8,64,2048]{2,1,0:T(8,128)(2,1)S(1)}, bf16[8,64,2048]{2,1,0:T(8,128)(2,1)}, u32[]{:S(2)}, u32[]{:S(2)}) %collective-permute-start.29) | collective-permute-done | bytes 2097184 | tf_op jit(solution)/shard_map/ppermute | solution.py:43
  359.3 21.8 %last_attention.1 = (f32[1024,1024]{1,0:T(8,128)}, bf16[256,1024]{1,0:T(8,128)(2,1)}, bf16[1024,512]{1,0:T(8,128)(2,1)}, bf16[1024,512]{1,0:T(8,128)(2,1)}, bf16...) custom-call(s32[1]{0:T(128)} %bitcast.me_ref, ...), custom_call_target="tpu_custom_call" | custom-call | tf_op jit(solution)/shard_map/last_attention/pallas_call | solution.py:417
  385.0 9.6 %mlp.3 = (bf16[256,1024]{1,0:T(8,128)(2,1)}, f32[256,1024]{1,0:T(8,128)}, bf16[256,2048]{1,0:T(8,128)(2,1)}) custom-call(s32[1]{0:T(128)} %bitcast.me_ref, f32[256,1024]{1,0:T(8,128)} %get-tuple-element.314.base_ref, bf16[256,1024]{1,0:T(8,128)(2,1)} %get-tuple-element.315.own_ref, bf16[256,1024]{1,0:T(8,128)(2,1)} %copy-done.18, ...), custom_call_target="tpu_custom_call" | custom-call | tf_op jit(solution)/shard_map/mlp/pallas_call | solution.py:334
  403.1 5.0 collective-permute-done.36
  412.5 2.4 collective-permute-done.39
  417.2 5.0 collective-permute-done.38
  425.0 5.6 collective-permute-done.42
  430.6 2.7 collective-permute-done.40
  437.9 31.1 %concatenate.253.table_ref = bf16[3200,1024]{1,0:T(8,128)(2,1)} concatenate(bf16[1572,1024]{1,0:T(8,128)(2,1)} %param.36, bf16[1572,1024]{1,0:T(8,128)(2,1)} %collective-permute-done.43, bf16[56,1024]{1,0:T(8,128)(2,1)S(1)} %broadcast_in_dim.141), dimensions={0} | concatenate | bytes 13107200 | tf_op jit(solution)/shard_map/concatenate | solution.py:978
  469.0 2.8 pad_maximum_fusion.7.rows_ref
  471.8 21.1 %vocabulary.3 = bf16[1024,1152]{1,0:T(8,128)(2,1)} custom-call(bf16[1024,1024]{1,0:T(8,128)(2,1)} %pad_maximum_fusion.7.rows_ref, bf16[3200,1024]{1,0:T(8,128)(2,1)} %concatenate.253.table_ref), custom_call_target="tpu_custom_call" | custom-call | tf_op jit(solution)/shard_map/vocabulary/pallas_call | solution.py:489
  494.9 2.5 fusion.70
  499.4 21.0 %vocabulary.2 = bf16[1024,1152]{1,0:T(8,128)(2,1)} custom-call(bf16[1024,1024]{1,0:T(8,128)(2,1)} %pad_maximum_fusion.6.rows_ref, bf16[3200,1024]{1,0:T(8,128)(2,1)} %concatenate.253.table_ref), custom_call_target="tpu_custom_call" | custom-call | tf_op jit(solution)/shard_map/vocabulary/pallas_call | solution.py:489
  523.4 2.8 fusion.69
  527.9 2.5 merge.14
  532.3 9.6 %collective-permute-done.47.second_ref = bf16[384,1152]{1,0:T(8,128)(2,1)} collective-permute-done((bf16[384,1152]{1,0:T(8,128)(2,1)S(1)}, bf16[384,1152]{1,0:T(8,128)(2,1)}, u32[]{:S(2)}, u32[]{:S(2)}) %collective-permute-start.47) | collective-permute-done | bytes 884768 | tf_op jit(solution)/shard_map/ppermute | solution.py:43
  541.9 3.4 merge.12
  548.3 3.5 merge.13
  557.7 2.8 collective-permute-done.52.second_ref
  565.7 3.0 merge.15
  571.3 3.0 merge.16
  613.5 3.7 head_back.1
  617.2 8.5 %mlp_back.2.own_ref = bf16[256,1024]{1,0:T(8,128)(2,1)} custom-call(s32[1]{0:T(128)} %bitcast.me_ref, f32[256,1024]{1,0:T(8,128)} %get-tuple-element.344.refs_0_.grad_ref, bf16[256,2048]{1,0:T(8,128)(2,1)} %get-tuple-element.345.refs_1_, bf16[8,64,2048]{2,1,0:T(8,128)(2,1)} %pad_maximum_fusion.4.up_held.refs_2_, ...), custom_call_target="tpu_custom_call" | custom-call | tf_op jit(solution)/shard_map/mlp_back/pallas_call | solution.py:605
  628.8 23.9 %last_attention_back.1 = (bf16[1024,1024]{1,0:T(8,128)(2,1)}, f32[1024,1024]{1,0:T(8,128)}, f32[2,16,512]{2,1,0:T(8,128)}) custom-call(s32[1]{0:T(128)} %bitcast.me_ref, s32[6]{0:T(128)} %pad_add_fusion.2.layout_ref, s32[256]{0:T(256)} %picks_ref.3, f32[256,1024]{1,0:T(8,128)} %get-tuple-element.344.refs_0_.grad_ref, bf16[256,1024]{1,0:T(8,128)(2,1)} %mlp_back.2.own_ref, ...), custom_call_target="tpu_custom_call" | custom-call | tf_op jit(solution)/shard_map/last_attention_back/pallas_call | solution.py:700
  653.2 4.0 collective-permute-done.61.refs_5_
  658.5 20.3 %mlp_back.3 = (bf16[1024,1024]{1,0:T(8,128)(2,1)}, f32[1024,1024]{1,0:T(8,128)}) custom-call(s32[1]{0:T(128)} %bitcast.me_ref, f32[1024,1024]{1,0:T(8,128)} %get-tuple-element.351.refs_0_, bf16[1024,2048]{1,0:T(8,128)(2,1)} %get-tuple-element.352.refs_1_, f32[1024,1024]{1,0:T(8,128)} %get-tuple-element.353.refs_2_, f32[1,1024]{1,0:T(1,128)} %copy-done.47, ...), custom_call_target="tpu_custom_call" | custom-call | tf_op jit(solution)/shard_map/mlp_back/pallas_call | solution.py:605
  680.4 2.9 collective-permute-done.62.other_ref
  684.7 19.4 %first_prefix_back.1 = f32[2,16,512]{2,1,0:T(8,128)} custom-call(s32[1]{0:T(128)} %bitcast.me_ref, f32[1024,1024]{1,0:T(8,128)} %get-tuple-element.355.grad_ref, bf16[1024,1024]{1,0:T(8,128)(2,1)} %get-tuple-element.356.own_ref, bf16[1024,1024]{1,0:T(8,128)(2,1)} %copy-done.7, f32[1024,1024]{1,0:T(8,128)} %get-tuple-element.302.base_ref.middle_ref, ...), custom_call_target="tpu_custom_call" | custom-call | tf_op jit(solution)/shard_map/first_prefix_back/pallas_call | solution.py:772
  706.4 2.3 collective-permute-done.63
  711.2 2.7 collective-permute-done.64
  716.5 2.3 collective-permute-done.65
  719.2 2.6 collective-permute-done.70
  734.6 2.8 collective-permute-done.72
  738.8 2.7 collective-permute-done.73
  741.5 3.9 collective-permute-done.74
  746.0 4.2 collective-permute-done.75
  (400 shorter events, 176.7 us)
Async XLA Ops:
  6.5 28.0 %collective-permute-start.6 = (bf16[1,64,2048]{2,1,0:T(8,128)(2,1)S(1)}, bf16[1,64,2048]{2,1,0:T(8,128)(2,1)S(1)}, u32[]{:S(2)}, u32[]{:S(2)}) collective-permute-start(bf16[1,64,2048]{2,1,0:T(8,128)(2,1)S(1)} %maximum_bitcast_fusion), channel_id=1, source_target_pairs={{0,16},{2,18},{4,20},{6,22},{8,24},{10,26},{12,28},{14,30},{16,0},... | collective-permute-start | bytes 786440 | tf_op jit(solution)/shard_map/ppermute | solution.py:43
  10.6 24.0 %collective-permute-start.7 = (bf16[1,64,2048]{2,1,0:T(8,128)(2,1)S(1)}, bf16[1,64,2048]{2,1,0:T(8,128)(2,1)S(1)}, u32[]{:S(2)}, u32[]{:S(2)}) collective-permute-start(bf16[1,64,2048]{2,1,0:T(8,128)(2,1)S(1)} %get-tuple-element.290), channel_id=1, source_target_pairs={{0,8},{2,10},{4,12},{6,14},{8,0},{10,2},{12,4},{14,6},{16,24},{18,... | collective-permute-start | bytes 786440 | tf_op jit(solution)/shard_map/ppermute | solution.py:43
  19.5 15.0 %all-to-all-start.2 = ((s32[16,1,49]{2,1,0:T(1,128)}), s32[16,1,49]{2,1,0:T(1,128)S(1)}, u32[]{:S(2)}, u32[]{:S(2)}) async-start(s32[16,1,49]{2,1,0:T(1,128)} %bitcast.4), calls=%async_computation.2 | async-start | bytes 16384 | tf_op jit(solution)/shard_map/all_to_all | solution.py:824
  23.3 13.9 %collective-permute-start.8 = (bf16[1,64,2048]{2,1,0:T(8,128)(2,1)S(1)}, bf16[1,64,2048]{2,1,0:T(8,128)(2,1)S(1)}, u32[]{:S(2)}, u32[]{:S(2)}) collective-permute-start(bf16[1,64,2048]{2,1,0:T(8,128)(2,1)S(1)} %get-tuple-element.291), channel_id=1, source_target_pairs={{0,16},{2,18},{4,20},{6,22},{8,24},{10,26},{12,28},{14,30},{16,0},... | collective-permute-start | bytes 786440 | tf_op jit(solution)/shard_map/ppermute | solution.py:43
  37.3 17.6 %collective-permute-start.9 = (bf16[2,64,2048]{2,1,0:T(8,128)(2,1)S(1)}, bf16[2,64,2048]{2,1,0:T(8,128)(2,1)S(1)}, u32[]{:S(2)}, u32[]{:S(2)}) collective-permute-start(bf16[2,64,2048]{2,1,0:T(8,128)(2,1)S(1)} %pad_maximum_fusion.16), channel_id=1, source_target_pairs={{0,4},{2,6},{4,0},{6,2},{8,12},{10,14},{12,8},{14,10},{16,20},{18,... | collective-permute-start | bytes 1572872 | tf_op jit(solution)/shard_map/ppermute | solution.py:43
  45.1 101.6 %all-to-all-start.3 = ((bf16[16,48,1024]{2,1,0:T(8,128)(2,1)}), bf16[16,48,1024]{2,1,0:T(8,128)(2,1)}, u32[]{:S(2)}, u32[]{:S(2)}) async-start(bf16[16,48,1024]{2,1,0:T(8,128)(2,1)} %bitcast.167), calls=%async_computation.3 | async-start | bytes 3145728 | tf_op jit(solution)/shard_map/all_to_all | solution.py:828
  50.7 59.3 %collective-permute-start.10 = (bf16[2,64,2048]{2,1,0:T(8,128)(2,1)S(1)}, bf16[2,64,2048]{2,1,0:T(8,128)(2,1)S(1)}, u32[]{:S(2)}, u32[]{:S(2)}) collective-permute-start(bf16[2,64,2048]{2,1,0:T(8,128)(2,1)S(1)} %pad_maximum_fusion.17), channel_id=1, source_target_pairs={{0,16},{2,18},{4,20},{6,22},{8,24},{10,26},{12,28},{14,30},{16,0},... | collective-permute-start | bytes 1572872 | tf_op jit(solution)/shard_map/ppermute | solution.py:43
  53.5 56.6 %collective-permute-start.11 = (bf16[2,64,2048]{2,1,0:T(8,128)(2,1)S(1)}, bf16[2,64,2048]{2,1,0:T(8,128)(2,1)S(1)}, u32[]{:S(2)}, u32[]{:S(2)}) collective-permute-start(bf16[2,64,2048]{2,1,0:T(8,128)(2,1)S(1)} %pad_maximum_fusion.18), channel_id=1, source_target_pairs={{0,2},{2,0},{4,6},{6,4},{8,10},{10,8},{12,14},{14,12},{16,18},{18,... | collective-permute-start | bytes 1572872 | tf_op jit(solution)/shard_map/ppermute | solution.py:43
  110.2 24.3 %collective-permute-start.12 = (bf16[4,64,2048]{2,1,0:T(8,128)(2,1)S(1)}, bf16[4,64,2048]{2,1,0:T(8,128)(2,1)}, u32[]{:S(2)}, u32[]{:S(2)}) collective-permute-start(bf16[4,64,2048]{2,1,0:T(8,128)(2,1)S(1)} %pad_maximum_fusion.8), channel_id=1, source_target_pairs={{0,8},{2,10},{4,12},{6,14},{8,0},{10,2},{12,4},{14,6},{16,24},{18,... | collective-permute-start | bytes 3145736 | tf_op jit(solution)/shard_map/ppermute | solution.py:43
  110.3 26.9 %collective-permute-start.13 = (bf16[4,64,2048]{2,1,0:T(8,128)(2,1)S(1)}, bf16[4,64,2048]{2,1,0:T(8,128)(2,1)}, u32[]{:S(2)}, u32[]{:S(2)}) collective-permute-start(bf16[4,64,2048]{2,1,0:T(8,128)(2,1)S(1)} %pad_maximum_fusion.9), channel_id=1, source_target_pairs={{0,2},{2,0},{4,6},{6,4},{8,10},{10,8},{12,14},{14,12},{16,18},{18,... | collective-permute-start | bytes 3145736 | tf_op jit(solution)/shard_map/ppermute | solution.py:43
  111.8 28.2 %collective-permute-start.14 = (bf16[4,64,2048]{2,1,0:T(8,128)(2,1)S(1)}, bf16[4,64,2048]{2,1,0:T(8,128)(2,1)}, u32[]{:S(2)}, u32[]{:S(2)}) collective-permute-start(bf16[4,64,2048]{2,1,0:T(8,128)(2,1)S(1)} %pad_maximum_fusion.10), channel_id=1, source_target_pairs={{0,4},{2,6},{4,0},{6,2},{8,12},{10,14},{12,8},{14,10},{16,20},{18,... | collective-permute-start | bytes 3145736 | tf_op jit(solution)/shard_map/ppermute | solution.py:43
  142.7 47.4 %collective-permute-start.15 = (bf16[8,64,2048]{2,1,0:T(8,128)(2,1)}, bf16[8,64,2048]{2,1,0:T(8,128)(2,1)}, u32[]{:S(2)}, u32[]{:S(2)}) collective-permute-start(bf16[8,64,2048]{2,1,0:T(8,128)(2,1)} %pad_maximum_fusion.held), channel_id=1, source_target_pairs={{0,2},{2,0},{4,6},{6,4},{8,10},{10,8},{12,14},{14,12},{16,18},{18,... | collective-permute-start | bytes 6291464 | tf_op jit(solution)/shard_map/ppermute | solution.py:43
  144.2 46.2 %collective-permute-start.17 = (bf16[8,64,2048]{2,1,0:T(8,128)(2,1)}, bf16[8,64,2048]{2,1,0:T(8,128)(2,1)}, u32[]{:S(2)}, u32[]{:S(2)}) collective-permute-start(bf16[8,64,2048]{2,1,0:T(8,128)(2,1)} %pad_maximum_fusion.1.up_held.refs_6_), channel_id=1, source_target_pairs={{0,4},{2,6},{4,0},{6,2},{8,12},{10,14},{12,8},{14,10},{16,20},{18,... | collective-permute-start | bytes 6291464 | tf_op jit(solution)/shard_map/ppermute | solution.py:43
  146.4 45.4 %collective-permute-start.18 = (bf16[8,64,2048]{2,1,0:T(8,128)(2,1)}, bf16[8,64,2048]{2,1,0:T(8,128)(2,1)}, u32[]{:S(2)}, u32[]{:S(2)}) collective-permute-start(bf16[8,64,2048]{2,1,0:T(8,128)(2,1)} %pad_maximum_fusion.2.down_held.refs_8_), channel_id=1, source_target_pairs={{0,8},{2,10},{4,12},{6,14},{8,0},{10,2},{12,4},{14,6},{16,24},{18,... | collective-permute-start | bytes 6291464 | tf_op jit(solution)/shard_map/ppermute | solution.py:43
  152.2 91.5 %collective-permute-start.1 = (bf16[1280,1024]{1,0:T(8,128)(2,1)}, bf16[1280,1024]{1,0:T(8,128)(2,1)}, u32[]{:S(2)}, u32[]{:S(2)}) collective-permute-start(bf16[1280,1024]{1,0:T(8,128)(2,1)} %get-tuple-element.288), channel_id=1, source_target_pairs={{0,1},{1,0},{2,3},{3,2},{4,5},{5,4},{6,7},{7,6},{8,9},{9,8},{10,11... | collective-permute-start | bytes 7864328 | tf_op jit(solution)/shard_map/ppermute | solution.py:47
  153.3 38.6 %collective-permute-start.2 = (f32[2,2,10,512]{3,2,1,0:T(8,128)S(1)}, f32[2,2,10,512]{3,2,1,0:T(8,128)S(1)}, u32[]{:S(2)}, u32[]{:S(2)}) collective-permute-start(f32[2,2,10,512]{3,2,1,0:T(8,128)S(1)} %convolution_bitcast_fusion), channel_id=1, source_target_pairs={{0,2},{2,0},{4,6},{6,4},{8,10},{10,8},{12,14},{14,12},{16,18},{18,... | collective-permute-start | bytes 245768 | tf_op jit(solution)/shard_map/ppermute | solution.py:43
  191.8 15.9 %collective-permute-start.20 = (bf16[1,64,2048]{2,1,0:T(8,128)(2,1)S(1)}, bf16[1,64,2048]{2,1,0:T(8,128)(2,1)S(1)}, u32[]{:S(2)}, u32[]{:S(2)}) collective-permute-start(bf16[1,64,2048]{2,1,0:T(8,128)(2,1)S(1)} %maximum_bitcast_fusion.1), channel_id=1, source_target_pairs={{0,16},{2,18},{4,20},{6,22},{8,24},{10,26},{12,28},{14,30},{16,0},... | collective-permute-start | bytes 786440 | tf_op jit(solution)/shard_map/ppermute | solution.py:43
  191.9 5.6 collective-permute-start.3
  194.0 13.7 %collective-permute-start.21 = (bf16[1,64,2048]{2,1,0:T(8,128)(2,1)S(1)}, bf16[1,64,2048]{2,1,0:T(8,128)(2,1)S(1)}, u32[]{:S(2)}, u32[]{:S(2)}) collective-permute-start(bf16[1,64,2048]{2,1,0:T(8,128)(2,1)S(1)} %copy-done.12), channel_id=1, source_target_pairs={{0,8},{2,10},{4,12},{6,14},{8,0},{10,2},{12,4},{14,6},{16,24},{18,... | collective-permute-start | bytes 786440 | tf_op jit(solution)/shard_map/ppermute | solution.py:43
  197.4 32.1 %collective-permute-start.4 = (f32[2,2,10,512]{3,2,1,0:T(8,128)S(1)}, f32[2,2,10,512]{3,2,1,0:T(8,128)S(1)}, u32[]{:S(2)}, u32[]{:S(2)}) collective-permute-start(f32[2,2,10,512]{3,2,1,0:T(8,128)S(1)} %add.361), channel_id=1, source_target_pairs={{0,8},{2,10},{4,12},{6,14},{8,0},{10,2},{12,4},{14,6},{16,24},{18,... | collective-permute-start | bytes 245768 | tf_op jit(solution)/shard_map/ppermute | solution.py:43
  199.0 29.9 %collective-permute-start.22 = (bf16[1,64,2048]{2,1,0:T(8,128)(2,1)S(1)}, bf16[1,64,2048]{2,1,0:T(8,128)(2,1)S(1)}, u32[]{:S(2)}, u32[]{:S(2)}) collective-permute-start(bf16[1,64,2048]{2,1,0:T(8,128)(2,1)S(1)} %copy-done.11), channel_id=1, source_target_pairs={{0,16},{2,18},{4,20},{6,22},{8,24},{10,26},{12,28},{14,30},{16,0},... | collective-permute-start | bytes 786440 | tf_op jit(solution)/shard_map/ppermute | solution.py:43
  228.9 9.7 %collective-permute-start.23 = (bf16[2,64,2048]{2,1,0:T(8,128)(2,1)S(1)}, bf16[2,64,2048]{2,1,0:T(8,128)(2,1)S(1)}, u32[]{:S(2)}, u32[]{:S(2)}) collective-permute-start(bf16[2,64,2048]{2,1,0:T(8,128)(2,1)S(1)} %pad_maximum_fusion.19), channel_id=1, source_target_pairs={{0,4},{2,6},{4,0},{6,2},{8,12},{10,14},{12,8},{14,10},{16,20},{18,... | collective-permute-start | bytes 1572872 | tf_op jit(solution)/shard_map/ppermute | solution.py:43
  229.6 7.4 collective-permute-start.5
  230.3 12.3 %collective-permute-start.24 = (bf16[2,64,2048]{2,1,0:T(8,128)(2,1)S(1)}, bf16[2,64,2048]{2,1,0:T(8,128)(2,1)S(1)}, u32[]{:S(2)}, u32[]{:S(2)}) collective-permute-start(bf16[2,64,2048]{2,1,0:T(8,128)(2,1)S(1)} %pad_maximum_fusion.20), channel_id=1, source_target_pairs={{0,16},{2,18},{4,20},{6,22},{8,24},{10,26},{12,28},{14,30},{16,0},... | collective-permute-start | bytes 1572872 | tf_op jit(solution)/shard_map/ppermute | solution.py:43
  237.0 44.0 %collective-permute-start.25 = (bf16[2,64,2048]{2,1,0:T(8,128)(2,1)S(1)}, bf16[2,64,2048]{2,1,0:T(8,128)(2,1)S(1)}, u32[]{:S(2)}, u32[]{:S(2)}) collective-permute-start(bf16[2,64,2048]{2,1,0:T(8,128)(2,1)S(1)} %pad_maximum_fusion.21), channel_id=1, source_target_pairs={{0,2},{2,0},{4,6},{6,4},{8,10},{10,8},{12,14},{14,12},{16,18},{18,... | collective-permute-start | bytes 1572872 | tf_op jit(solution)/shard_map/ppermute | solution.py:43
  280.9 31.9 %collective-permute-start.16 = (bf16[1024,1024]{1,0:T(8,128)(2,1)}, bf16[1024,1024]{1,0:T(8,128)(2,1)}, u32[]{:S(2)}, u32[]{:S(2)}) collective-permute-start(bf16[1024,1024]{1,0:T(8,128)(2,1)} %get-tuple-element.299.own_ref), channel_id=1, source_target_pairs={{0,1},{1,0},{2,3},{3,2},{4,5},{5,4},{6,7},{7,6},{8,9},{9,8},{10,11... | collective-permute-start | bytes 6291464 | tf_op jit(solution)/shard_map/ppermute | solution.py:47
  281.1 25.6 %collective-permute-start.26 = (bf16[4,64,2048]{2,1,0:T(8,128)(2,1)S(1)}, bf16[4,64,2048]{2,1,0:T(8,128)(2,1)S(1)}, u32[]{:S(2)}, u32[]{:S(2)}) collective-permute-start(bf16[4,64,2048]{2,1,0:T(8,128)(2,1)S(1)} %pad_maximum_fusion.11), channel_id=1, source_target_pairs={{0,8},{2,10},{4,12},{6,14},{8,0},{10,2},{12,4},{14,6},{16,24},{18,... | collective-permute-start | bytes 3145736 | tf_op jit(solution)/shard_map/ppermute | solution.py:43
  281.2 25.8 %collective-permute-start.27 = (bf16[4,64,2048]{2,1,0:T(8,128)(2,1)}, bf16[4,64,2048]{2,1,0:T(8,128)(2,1)S(1)}, u32[]{:S(2)}, u32[]{:S(2)}) collective-permute-start(bf16[4,64,2048]{2,1,0:T(8,128)(2,1)} %pad_maximum_fusion.12), channel_id=1, source_target_pairs={{0,2},{2,0},{4,6},{6,4},{8,10},{10,8},{12,14},{14,12},{16,18},{18,... | collective-permute-start | bytes 3145736 | tf_op jit(solution)/shard_map/ppermute | solution.py:43
  282.8 27.6 %collective-permute-start.28 = (bf16[4,64,2048]{2,1,0:T(8,128)(2,1)S(1)}, bf16[4,64,2048]{2,1,0:T(8,128)(2,1)S(1)}, u32[]{:S(2)}, u32[]{:S(2)}) collective-permute-start(bf16[4,64,2048]{2,1,0:T(8,128)(2,1)S(1)} %pad_maximum_fusion.13), channel_id=1, source_target_pairs={{0,4},{2,6},{4,0},{6,2},{8,12},{10,14},{12,8},{14,10},{16,20},{18,... | collective-permute-start | bytes 3145736 | tf_op jit(solution)/shard_map/ppermute | solution.py:43
  311.9 47.3 %collective-permute-start.29 = (bf16[8,64,2048]{2,1,0:T(8,128)(2,1)S(1)}, bf16[8,64,2048]{2,1,0:T(8,128)(2,1)}, u32[]{:S(2)}, u32[]{:S(2)}) collective-permute-start(bf16[8,64,2048]{2,1,0:T(8,128)(2,1)S(1)} %pad_maximum_fusion.3.held), channel_id=1, source_target_pairs={{0,2},{2,0},{4,6},{6,4},{8,10},{10,8},{12,14},{14,12},{16,18},{18,... | collective-permute-start | bytes 6291464 | tf_op jit(solution)/shard_map/ppermute | solution.py:43
  335.5 23.8 %collective-permute-start.19 = (bf16[1024,1024]{1,0:T(8,128)(2,1)}, bf16[1024,1024]{1,0:T(8,128)(2,1)}, u32[]{:S(2)}, u32[]{:S(2)}) collective-permute-start(bf16[1024,1024]{1,0:T(8,128)(2,1)} %get-tuple-element.303.own_ref), channel_id=1, source_target_pairs={{0,1},{1,0},{2,3},{3,2},{4,5},{5,4},{6,7},{7,6},{8,9},{9,8},{10,11... | collective-permute-start | bytes 6291464 | tf_op jit(solution)/shard_map/ppermute | solution.py:47
  335.5 48.4 %collective-permute-start.31 = (bf16[8,64,2048]{2,1,0:T(8,128)(2,1)}, bf16[8,64,2048]{2,1,0:T(8,128)(2,1)}, u32[]{:S(2)}, u32[]{:S(2)}) collective-permute-start(bf16[8,64,2048]{2,1,0:T(8,128)(2,1)} %pad_maximum_fusion.4.up_held.refs_2_), channel_id=1, source_target_pairs={{0,4},{2,6},{4,0},{6,2},{8,12},{10,14},{12,8},{14,10},{16,20},{18,... | collective-permute-start | bytes 6291464 | tf_op jit(solution)/shard_map/ppermute | solution.py:43
  336.2 48.0 %collective-permute-start.32 = (bf16[8,64,2048]{2,1,0:T(8,128)(2,1)}, bf16[8,64,2048]{2,1,0:T(8,128)(2,1)}, u32[]{:S(2)}, u32[]{:S(2)}) collective-permute-start(bf16[8,64,2048]{2,1,0:T(8,128)(2,1)} %pad_maximum_fusion.5.down_held.refs_4_), channel_id=1, source_target_pairs={{0,8},{2,10},{4,12},{6,14},{8,0},{10,2},{12,4},{14,6},{16,24},{18,... | collective-permute-start | bytes 6291464 | tf_op jit(solution)/shard_map/ppermute | solution.py:43
  394.7 43.1 %collective-permute-start.43 = (bf16[1572,1024]{1,0:T(8,128)(2,1)}, bf16[1572,1024]{1,0:T(8,128)(2,1)}, u32[]{:S(2)}, u32[]{:S(2)}) collective-permute-start(bf16[1572,1024]{1,0:T(8,128)(2,1)} %param.36), channel_id=1, source_target_pairs={{0,1},{1,0},{2,3},{3,2},{4,5},{5,4},{6,7},{7,6},{8,9},{9,8},{10,11... | collective-permute-start | bytes 9658376 | tf_op jit(solution)/shard_map/ppermute | solution.py:47
  399.1 9.0 %collective-permute-start.36 = (bf16[1,32,1024]{2,1,0:T(8,128)(2,1)S(1)}, bf16[1,32,1024]{2,1,0:T(8,128)(2,1)S(1)}, u32[]{:S(2)}, u32[]{:S(2)}) collective-permute-start(bf16[1,32,1024]{2,1,0:T(8,128)(2,1)S(1)} %dynamic-slice_bitcast_fusion.2), channel_id=1, source_target_pairs={{0,16},{2,18},{4,20},{6,22},{8,24},{10,26},{12,28},{14,30},{16,0},... | collective-permute-start | bytes 196616 | tf_op jit(solution)/shard_map/ppermute | solution.py:43
  401.2 8.5 %collective-permute-start.34 = (bf16[1,48,1024]{2,1,0:T(8,128)(2,1)S(1)}, bf16[1,48,1024]{2,1,0:T(8,128)(2,1)S(1)}, u32[]{:S(2)}, u32[]{:S(2)}) collective-permute-start(bf16[1,48,1024]{2,1,0:T(8,128)(2,1)S(1)} %get-tuple-element.320), channel_id=1, source_target_pairs={{0,16},{2,18},{4,20},{6,22},{8,24},{10,26},{12,28},{14,30},{16,0},... | collective-permute-start | bytes 294920 | tf_op jit(solution)/shard_map/ppermute | solution.py:43
  402.1 7.8 %collective-permute-start.35 = (bf16[1,48,1024]{2,1,0:T(8,128)(2,1)S(1)}, bf16[1,48,1024]{2,1,0:T(8,128)(2,1)S(1)}, u32[]{:S(2)}, u32[]{:S(2)}) collective-permute-start(bf16[1,48,1024]{2,1,0:T(8,128)(2,1)S(1)} %get-tuple-element.321), channel_id=1, source_target_pairs={{0,8},{2,10},{4,12},{6,14},{8,0},{10,2},{12,4},{14,6},{16,24},{18,... | collective-permute-start | bytes 294920 | tf_op jit(solution)/shard_map/ppermute | solution.py:43
  409.9 5.1 collective-permute-start.39
  411.0 6.1 collective-permute-start.37
  412.5 9.6 %collective-permute-start.38 = (bf16[2,48,1024]{2,1,0:T(8,128)(2,1)S(1)}, bf16[2,48,1024]{2,1,0:T(8,128)(2,1)S(1)}, u32[]{:S(2)}, u32[]{:S(2)}) collective-permute-start(bf16[2,48,1024]{2,1,0:T(8,128)(2,1)S(1)} %pad_maximum_fusion.28), channel_id=1, source_target_pairs={{0,16},{2,18},{4,20},{6,22},{8,24},{10,26},{12,28},{14,30},{16,0},... | collective-permute-start | bytes 589832 | tf_op jit(solution)/shard_map/ppermute | solution.py:43
  422.2 11.1 %collective-permute-start.40 = (bf16[4,48,1024]{2,1,0:T(8,128)(2,1)S(1)}, bf16[4,48,1024]{2,1,0:T(8,128)(2,1)S(1)}, u32[]{:S(2)}, u32[]{:S(2)}) collective-permute-start(bf16[4,48,1024]{2,1,0:T(8,128)(2,1)S(1)} %pad_maximum_fusion.23), channel_id=1, source_target_pairs={{0,8},{2,10},{4,12},{6,14},{8,0},{10,2},{12,4},{14,6},{16,24},{18,... | collective-permute-start | bytes 1179656 | tf_op jit(solution)/shard_map/ppermute | solution.py:43
  422.3 8.3 %collective-permute-start.42 = (bf16[4,32,1024]{2,1,0:T(8,128)(2,1)S(1)}, bf16[4,32,1024]{2,1,0:T(8,128)(2,1)S(1)}, u32[]{:S(2)}, u32[]{:S(2)}) collective-permute-start(bf16[4,32,1024]{2,1,0:T(8,128)(2,1)S(1)} %pad_maximum_fusion.26), channel_id=1, source_target_pairs={{0,4},{2,6},{4,0},{6,2},{8,12},{10,14},{12,8},{14,10},{16,20},{18,... | collective-permute-start | bytes 786440 | tf_op jit(solution)/shard_map/ppermute | solution.py:43
  424.1 10.8 %collective-permute-start.41 = (bf16[4,48,1024]{2,1,0:T(8,128)(2,1)S(1)}, bf16[4,48,1024]{2,1,0:T(8,128)(2,1)S(1)}, u32[]{:S(2)}, u32[]{:S(2)}) collective-permute-start(bf16[4,48,1024]{2,1,0:T(8,128)(2,1)S(1)} %pad_maximum_fusion.24), channel_id=1, source_target_pairs={{0,2},{2,0},{4,6},{6,4},{8,10},{10,8},{12,14},{14,12},{16,18},{18,... | collective-permute-start | bytes 1179656 | tf_op jit(solution)/shard_map/ppermute | solution.py:43
  434.9 34.0 %collective-permute-start.44 = (bf16[8,48,1024]{2,1,0:T(8,128)(2,1)S(1)}, bf16[8,48,1024]{2,1,0:T(8,128)(2,1)S(1)}, u32[]{:S(2)}, u32[]{:S(2)}) collective-permute-start(bf16[8,48,1024]{2,1,0:T(8,128)(2,1)S(1)} %pad_maximum_fusion.14), channel_id=1, source_target_pairs={{0,2},{2,0},{4,6},{6,4},{8,10},{10,8},{12,14},{14,12},{16,18},{18,... | collective-permute-start | bytes 2359304 | tf_op jit(solution)/shard_map/ppermute | solution.py:43
  435.9 33.1 %collective-permute-start.45 = (bf16[8,48,1024]{2,1,0:T(8,128)(2,1)S(1)}, bf16[8,48,1024]{2,1,0:T(8,128)(2,1)}, u32[]{:S(2)}, u32[]{:S(2)}) collective-permute-start(bf16[8,48,1024]{2,1,0:T(8,128)(2,1)S(1)} %pad_maximum_fusion.15), channel_id=1, source_target_pairs={{0,4},{2,6},{4,0},{6,2},{8,12},{10,14},{12,8},{14,10},{16,20},{18,... | collective-permute-start | bytes 2359304 | tf_op jit(solution)/shard_map/ppermute | solution.py:43
  436.2 32.7 %collective-permute-start.46 = (bf16[8,32,1024]{2,1,0:T(8,128)(2,1)S(1)}, bf16[8,32,1024]{2,1,0:T(8,128)(2,1)}, u32[]{:S(2)}, u32[]{:S(2)}) collective-permute-start(bf16[8,32,1024]{2,1,0:T(8,128)(2,1)S(1)} %pad_maximum_fusion.22), channel_id=1, source_target_pairs={{0,8},{2,10},{4,12},{6,14},{8,0},{10,2},{12,4},{14,6},{16,24},{18,... | collective-permute-start | bytes 1572872 | tf_op jit(solution)/shard_map/ppermute | solution.py:43
  497.4 30.5 %collective-permute-start.49 = (bf16[256,1152]{1,0:T(8,128)(2,1)}, bf16[256,1152]{1,0:T(8,128)(2,1)}, u32[]{:S(2)}, u32[]{:S(2)}) collective-permute-start(bf16[256,1152]{1,0:T(8,128)(2,1)} %slice.354), channel_id=1, source_target_pairs={{0,8},{2,10},{4,12},{6,14},{8,0},{10,2},{12,4},{14,6},{16,24},{18,... | collective-permute-start | bytes 1769480 | tf_op jit(solution)/shard_map/ppermute | solution.py:43
  522.3 19.7 %collective-permute-start.47 = (bf16[384,1152]{1,0:T(8,128)(2,1)S(1)}, bf16[384,1152]{1,0:T(8,128)(2,1)}, u32[]{:S(2)}, u32[]{:S(2)}) collective-permute-start(bf16[384,1152]{1,0:T(8,128)(2,1)S(1)} %copy-done.14), channel_id=1, source_target_pairs={{0,2},{2,0},{4,6},{6,4},{8,10},{10,8},{12,14},{14,12},{16,18},{18,... | collective-permute-start | bytes 2654216 | tf_op jit(solution)/shard_map/ppermute | solution.py:43
  526.2 21.2 %collective-permute-start.48 = (bf16[384,1152]{1,0:T(8,128)(2,1)S(1)}, bf16[384,1152]{1,0:T(8,128)(2,1)S(1)}, u32[]{:S(2)}, u32[]{:S(2)}) collective-permute-start(bf16[384,1152]{1,0:T(8,128)(2,1)S(1)} %get-tuple-element.333), channel_id=1, source_target_pairs={{0,4},{2,6},{4,0},{6,2},{8,12},{10,14},{12,8},{14,10},{16,20},{18,... | collective-permute-start | bytes 2654216 | tf_op jit(solution)/shard_map/ppermute | solution.py:43
  553.8 6.7 collective-permute-start.52
  555.2 9.7 %collective-permute-start.50 = (bf16[192,1152]{1,0:T(8,128)(2,1)S(1)}, bf16[192,1152]{1,0:T(8,128)(2,1)S(1)}, u32[]{:S(2)}, u32[]{:S(2)}) collective-permute-start(bf16[192,1152]{1,0:T(8,128)(2,1)S(1)} %get-tuple-element.335), channel_id=1, source_target_pairs={{0,8},{2,10},{4,12},{6,14},{8,0},{10,2},{12,4},{14,6},{16,24},{18,... | collective-permute-start | bytes 1327112 | tf_op jit(solution)/shard_map/ppermute | solution.py:43
  556.6 13.9 %collective-permute-start.51 = (bf16[192,1152]{1,0:T(8,128)(2,1)S(1)}, bf16[192,1152]{1,0:T(8,128)(2,1)S(1)}, u32[]{:S(2)}, u32[]{:S(2)}) collective-permute-start(bf16[192,1152]{1,0:T(8,128)(2,1)S(1)} %get-tuple-element.336), channel_id=1, source_target_pairs={{0,2},{2,0},{4,6},{6,4},{8,10},{10,8},{12,14},{14,12},{16,18},{18,... | collective-permute-start | bytes 1327112 | tf_op jit(solution)/shard_map/ppermute | solution.py:43
  576.1 5.1 collective-permute-start.55
  577.2 8.1 %collective-permute-start.53 = (bf16[96,1152]{1,0:T(8,128)(2,1)S(1)}, bf16[96,1152]{1,0:T(8,128)(2,1)S(1)}, u32[]{:S(2)}, u32[]{:S(2)}) collective-permute-start(bf16[96,1152]{1,0:T(8,128)(2,1)S(1)} %get-tuple-element.338), channel_id=1, source_target_pairs={{0,4},{2,6},{4,0},{6,2},{8,12},{10,14},{12,8},{14,10},{16,20},{18,... | collective-permute-start | bytes 663560 | tf_op jit(solution)/shard_map/ppermute | solution.py:43
  578.6 10.9 %collective-permute-start.54 = (bf16[96,1152]{1,0:T(8,128)(2,1)S(1)}, bf16[96,1152]{1,0:T(8,128)(2,1)S(1)}, u32[]{:S(2)}, u32[]{:S(2)}) collective-permute-start(bf16[96,1152]{1,0:T(8,128)(2,1)S(1)} %get-tuple-element.339), channel_id=1, source_target_pairs={{0,16},{2,18},{4,20},{6,22},{8,24},{10,26},{12,28},{14,30},{16,0},... | collective-permute-start | bytes 663560 | tf_op jit(solution)/shard_map/ppermute | solution.py:43
  593.9 6.0 collective-permute-start.58
  596.0 6.8 collective-permute-start.56
  596.9 8.4 %collective-permute-start.57 = (bf16[48,1152]{1,0:T(8,128)(2,1)S(1)}, bf16[48,1152]{1,0:T(8,128)(2,1)S(1)}, u32[]{:S(2)}, u32[]{:S(2)}) collective-permute-start(bf16[48,1152]{1,0:T(8,128)(2,1)S(1)} %get-tuple-element.342), channel_id=1, source_target_pairs={{0,8},{2,10},{4,12},{6,14},{8,0},{10,2},{12,4},{14,6},{16,24},{18,... | collective-permute-start | bytes 331784 | tf_op jit(solution)/shard_map/ppermute | solution.py:43
  679.3 26.0 %collective-permute-start.67 = (f32[2,10,512]{2,1,0:T(8,128)S(1)}, f32[2,10,512]{2,1,0:T(8,128)S(1)}, u32[]{:S(2)}, u32[]{:S(2)}) collective-permute-start(f32[2,10,512]{2,1,0:T(8,128)S(1)} %bitcast.174), channel_id=1, source_target_pairs={{0,2},{2,0},{4,6},{6,4},{8,10},{10,8},{12,14},{14,12},{16,18},{18,... | collective-permute-start | bytes 122888 | tf_op jit(solution)/shard_map/ppermute | solution.py:43
  705.3 5.4 collective-permute-start.68
  713.9 4.8 collective-permute-start.65
  715.1 6.7 collective-permute-start.70
  718.7 5.2 collective-permute-start.66
  745.4 4.8 collective-permute-start.75
  (85 other events, 1115.5 us)

commit v2 on v1

--- a/solution.py
+++ b/solution.py
@@ -38,6 +38,12 @@
     return pltpu.CompilerParams(dimension_semantics=("arbitrary",), **more)
 
 
+def cost(microseconds):
+    return pl.CostEstimate(
+        flops=int(microseconds * 1.15e9), transcendentals=0, bytes_accessed=1024
+    )
+
+
 def flip(array, bit):
     size = lax.axis_size("dev")
     return lax.ppermute(array, "dev", [(i, i ^ bit) for i in range(size)])
@@ -47,43 +53,106 @@
     return lax.ppermute(array, "ta", SWAP)
 
 
-def bit_orders(size):
+def bit_orders(size, parts):
     bits = [1 << k for k in range(size.bit_length() - 1)]
     if size == 16:
         x, y, near, far = bits
-        return ((far, y, near, x), (near, far, x, y), (far, x, y, near))
-    return tuple(tuple(bits[k:] + bits[:k]) for k in range(3))
-
-
-def offsets_of(order):
-    found = [0]
-    for bit in order[:-1]:
-        found = found + [o ^ bit for o in found]
-    return found
-
-
-def doubling_rounds(schedule, state, orders):
-    before = []
-    for pairs in schedule:
-        keys = [(chunk, part, stage) for chunk, stage in pairs for part in range(len(orders))]
-        sends = []
-        for chunk, part, stage in keys:
-            held = state[chunk, part]
-            sends.append(held[0] if len(held) == 1 else jnp.concatenate(held, 0))
-        tied = lax.optimization_barrier(tuple(sends) + tuple(before))
-        before = []
-        for (chunk, part, stage), send in zip(keys, tied):
-            got = flip(send, orders[part][stage])
-            state[chunk, part] = [send, got]
-            before.append(got)
-    return state
+        if parts == 3:
+            return ((far, y, near, x), (near, far, x, y), (far, x, y, near))
+        return (
+            (x, y, near, far),
+            (x, y, far, near),
+            (near, far, x, y),
+            (far, near, y, x),
+        )
+    return tuple(tuple(bits[k:] + bits[:k]) for k in range(parts))
+
+
+def cuts_of(total, unit, parts):
+    sixths = (0, 2, 4) if parts == 3 else (0, 1, 2, 4)
+    return [total * k // 6 // unit * unit for k in sixths] + [total]
+
+
+def pack(groups):
+    arrays = [array for group, unused, unused in groups for array in group]
+    outs = []
+    moves = []
+    for number, (group, first, last) in enumerate(groups):
+        total = 0
+        for array in group:
+            moves.append((number, total, array.shape[0], first, last - first))
+            total += array.shape[0]
+        outs.append(shape((total, group[0].shape[1], last - first), group[0].dtype))
+
+    def body(*refs):
+        sems = refs[-1]
+        copies = [
+            pltpu.make_async_copy(
+                refs[index].at[:, :, pl.ds(first, wide)],
+                refs[len(arrays) + number].at[pl.ds(begin, count)],
+                sems.at[index],
+            )
+            for index, (number, begin, count, first, wide) in enumerate(moves)
+        ]
+        for copy in copies:
+            copy.start()
+        for copy in copies:
+            copy.wait()
+
+    return pl.pallas_call(
+        body,
+        in_specs=[pl.BlockSpec(memory_space=pl.ANY)] * len(arrays),
+        out_specs=[pl.BlockSpec(memory_space=pltpu.VMEM)] * len(outs),
+        out_shape=outs,
+        scratch_shapes=[pltpu.SemaphoreType.DMA((len(arrays),))],
+        cost_estimate=cost(2),
+        name="pack",
+    )(*arrays)
+
+
+class Rounds:
+    def __init__(self):
+        self.orders = {}
+        self.held = {}
+        self.split = {}
+        self.before = []
+
+    def add(self, chunk, orders, arrays, splits=None):
+        self.orders[chunk] = orders
+        for part, array in enumerate(arrays):
+            self.held[chunk, part] = [array[None]]
+            self.split[chunk, part] = splits[part] if splits else None
+
+    def step(self, chunk, stage, side=None, through=()):
+        parts = range(len(self.orders[chunk]))
+        held = [self.held[chunk, part] for part in parts]
+        if stage == 0:
+            sends = [arrays[0] for arrays in held]
+        else:
+            spans = []
+            for part, arrays in zip(parts, held):
+                cut, width = self.split[chunk, part], arrays[0].shape[2]
+                spans.append((cut if side == 1 else 0, cut if side == 0 else width))
+            sends = pack([(arrays, *span) for arrays, span in zip(held, spans)])
+        through, sends, unused = lax.optimization_barrier((through, sends, self.before))
+        self.before = []
+        for part, send in enumerate(sends):
+            got = flip(send, self.orders[chunk][part][stage])
+            self.held[(chunk, part) if side is None else (chunk, part, side)] = [send, got]
+            self.before.append(got)
+        return through
 
 
 def sum_over_dev(array):
+    size = lax.axis_size("dev")
     bit = 1
-    while bit < lax.axis_size("dev"):
-        array = array + flip(array, bit)
-        bit = bit * 2
+    while bit < size:
+        if bit * 2 < size:
+            near, far, both = flip(array, bit), flip(array, bit * 2), flip(array, bit * 3)
+            array = (array + near) + (far + both)
+        else:
+            array = array + flip(array, bit)
+        bit = bit * 4
     return array
 
 
@@ -114,39 +183,47 @@
 
 
 class Gathered:
-    def __init__(self, pair, order, columns=None):
-        self.pair = pair
-        self.order = order
-        blocks, rows, width = pair[0].shape
-        self.blocks, self.rows = blocks, rows
-        self.columns = (0, width) if columns is None else columns
+    def __init__(self, segments, first, last):
+        self.pieces = []
+        for stacks, order, begin, end, skip in segments:
+            low, high = max(first, begin), min(last, end)
+            if low < high:
+                self.pieces.append((stacks, order, low - begin + skip, high - low, low - first))
+        stacks, order, *unused = self.pieces[0]
+        self.rows = stacks[0].shape[1]
+        self.blocks = 1 << len(order)
         self.scratch = [
-            pltpu.VMEM((2 * blocks * rows, self.columns[1] - self.columns[0]), B16),
-            pltpu.SemaphoreType.DMA((2 * blocks,)),
+            pltpu.VMEM((self.blocks * self.rows, last - first), B16),
+            pltpu.SemaphoreType.DMA((len(self.pieces) * self.blocks,)),
         ]
-
-    def copies(self, me, held, taken, full, sems):
-        first, last = self.columns
-        for index, offset in enumerate(offsets_of(self.order)):
-            for side, (ref, extra) in enumerate(((held, 0), (taken, self.order[-1]))):
-                start = pl.multiple_of((me ^ (offset ^ extra)) * self.rows, self.rows)
-                source = ref.at[index]
-                if (first, last) != (0, ref.shape[2]):
-                    source = source.at[:, pl.ds(first, last - first)]
-                yield pltpu.make_async_copy(
-                    source, full.at[pl.ds(start, self.rows)], sems.at[2 * index + side]
-                )
+        self.operands = [array for piece in self.pieces for array in piece[0]]
+        self.specs = [pl.BlockSpec(memory_space=pl.ANY)] * len(self.operands)
+
+    def each(self, act, me, refs, full, sems):
+        for number, (stacks, order, source, wide, target) in enumerate(self.pieces):
+            blocks = self.blocks // len(stacks)
+            for side, ref in enumerate(refs[number * len(stacks) : (number + 1) * len(stacks)]):
+
+                def one(index, carry, side=side, ref=ref):
+                    place = me ^ (order[-1] if side else 0)
+                    for k, bit in enumerate(order[:-1]):
+                        place = place ^ jnp.where((index >> k) % 2 == 1, bit, 0)
+                    start = pl.multiple_of(place * self.rows, self.rows)
+                    copy = pltpu.make_async_copy(
+                        ref.at[index, :, pl.ds(source, wide)],
+                        full.at[pl.ds(start, self.rows), pl.ds(target, wide)],
+                        sems.at[number * self.blocks + side * blocks + index],
+                    )
+                    act(copy)
+                    return carry
+
+                lax.fori_loop(0, blocks, one, 0)
 
     def start(self, *refs):
-        for copy in self.copies(*refs):
-            copy.start()
+        self.each(lambda copy: copy.start(), *refs)
 
     def wait(self, *refs):
-        for copy in self.copies(*refs):
-            copy.wait()
-
-
-ANY = pl.BlockSpec(memory_space=pl.ANY)
+        self.each(lambda copy: copy.wait(), *refs)
 
 
 def rows_spec(width, block=BLOCK):
@@ -218,7 +295,9 @@
                 bias_prefix,
             )
             parts.append(mixed)
-            lse_ref[rows, :] = jnp.where(lane == 2 * index + side, lse, lse_ref[rows, :])
+            lse_ref[rows, :] = jnp.where(
+                lane // prefix_rows == 2 * index + side, lse, lse_ref[rows, :]
+            )
         mixed_ref[rows, columns] = jnp.concatenate(parts, 1).astype(B16)
         return carry
 
@@ -230,10 +309,12 @@
     half = prefix.shape[2]
     scale = HEAD_DIM ** (-0.5)
 
-    def body(me_ref, layout_ref, stream_ref, vec_ref, bias_ref, prefix_ref, held, taken,
-             part_ref, q_out, mixed_out, lse_out, full, sems, q_s, k_s, v_s):
+    stacks = len(weight.operands)
+
+    def body(me_ref, layout_ref, stream_ref, vec_ref, bias_ref, prefix_ref, *refs):
+        part_ref, q_out, mixed_out, lse_out, full, sems, q_s, k_s, v_s = refs[stacks:]
         step = pl.program_id(0)
-        refs = (me_ref[0], held, taken, full, sems)
+        refs = (me_ref[0], refs[:stacks], full, sems)
 
         @pl.when(step == 0)
         def _():
@@ -272,8 +353,7 @@
                 whole_spec(vectors.shape),
                 whole_spec(bias_qkv.shape),
                 whole_spec(prefix.shape),
-                ANY,
-                ANY,
+                *weight.specs,
             ],
             out_specs=[rows_spec(width), rows_spec(half), rows_spec(half), rows_spec(LANES)],
             scratch_shapes=weight.scratch
@@ -287,19 +367,22 @@
             shape((row_count, LANES), F32),
         ],
         compiler_params=params(),
+        cost_estimate=cost(30 * row_count // 1024),
         name="first_attention",
-    )(me, layout, stream, vectors, bias_qkv, prefix, *weight.pair)
+    )(me, layout, stream, vectors, bias_qkv, prefix, *weight.operands)
 
 
 def mlp(base, own, other, vectors, bias_up, me, w_up, w_down):
     row_count, width = base.shape
     hidden = bias_up.shape[1]
 
-    def body(me_ref, base_ref, own_ref, other_ref, vec_ref, bias_ref, up_held, up_taken,
-             down_held, down_taken, part_ref, middle_ref, slope_ref, up, up_sems, down, down_sems):
+    ups, downs = len(w_up.operands), len(w_down.operands)
+
+    def body(me_ref, base_ref, own_ref, other_ref, vec_ref, bias_ref, *refs):
+        part_ref, middle_ref, slope_ref, up, up_sems, down, down_sems = refs[ups + downs :]
         step = pl.program_id(0)
-        up_refs = (me_ref[0], up_held, up_taken, up, up_sems)
-        down_refs = (me_ref[0], down_held, down_taken, down, down_sems)
+        up_refs = (me_ref[0], refs[:ups], up, up_sems)
+        down_refs = (me_ref[0], refs[ups : ups + downs], down, down_sems)
 
         @pl.when(step == 0)
         def _():
@@ -342,10 +425,8 @@
                 rows_spec(width),
                 whole_spec(vectors.shape),
                 whole_spec(bias_up.shape),
-                ANY,
-                ANY,
-                ANY,
-                ANY,
+                *w_up.specs,
+                *w_down.specs,
             ],
             out_specs=[rows_spec(width), rows_spec(width), rows_spec(hidden)],
             scratch_shapes=w_up.scratch + w_down.scratch,
@@ -356,8 +437,9 @@
             shape((row_count, hidden), B16),
         ],
         compiler_params=params(),
+        cost_estimate=cost(23 * row_count // 1024),
         name="mlp",
-    )(me, base, own, other, vectors, bias_up, *w_up.pair, *w_down.pair)
+    )(me, base, own, other, vectors, bias_up, *w_up.operands, *w_down.operands)
 
 
 def last_attention(base, own, other, vectors, bias_qkv, prefix, layout, picks, picks_column, me,
@@ -368,11 +450,14 @@
     steps = row_count // BLOCK
     scale = HEAD_DIM ** (-0.5)
 
+    stacks = len(weight.operands)
+
     def body(me_ref, layout_ref, picks_ref, base_ref, own_ref, other_ref, vec_ref, bias_ref,
-             prefix_ref, column_ref, held, taken, stream_out, part_ref, k_out, v_out, q_out,
-             mixed_out, lse_out, chosen_out, full, sems, stream_s, k_s, v_s):
+             prefix_ref, column_ref, *refs):
+        (stream_out, part_ref, k_out, v_out, q_out, mixed_out, lse_out, chosen_out,
+         full, sems, stream_s, k_s, v_s) = refs[stacks:]
         step = pl.program_id(0)
-        refs = (me_ref[0], held, taken, full, sems)
+        refs = (me_ref[0], refs[:stacks], full, sems)
 
         @pl.when(step == 0)
         def _():
@@ -401,7 +486,7 @@
                 chosen_out[pl.ds(index, 1), :] = stream_s[pl.ds(picks_ref[index], 1), :]
                 return carry
 
-            lax.fori_loop(0, scored, pick, 0)
+            lax.fori_loop(0, scored, pick, 0, unroll=8)
             for first in range(0, scored, BLOCK):
                 block = pl.ds(first, BLOCK)
                 chosen_hat, unused = norm_rows(chosen_out[block, :])
@@ -427,8 +512,7 @@
                 whole_spec(bias_qkv.shape),
                 whole_spec(prefix.shape),
                 whole_spec(picks_column.shape),
-                ANY,
-                ANY,
+                *weight.specs,
             ],
             out_specs=[
                 rows_spec(width),
@@ -455,8 +539,9 @@
             shape((scored, width), F32),
         ],
         compiler_params=params(),
+        cost_estimate=cost(22),
         name="last_attention",
-    )(me, layout, picks, base, own, other, vectors, bias_qkv, prefix, picks_column, *weight.pair)
+    )(me, layout, picks, base, own, other, vectors, bias_qkv, prefix, picks_column, *weight.operands)
 
 
 def split_lse(lse, rows):
@@ -468,71 +553,106 @@
     return packed.astype(B16)
 
 
-def vocabulary(rows, table, entries):
-    row_count, width = rows.shape
+VMEM = pl.BlockSpec(memory_space=pltpu.VMEM)
+
+
+def vocabulary(stacks, table, entries):
+    width = table.shape[1]
     padded = table.shape[0]
-    tail = padded - LANES
-
-    def body(rows_ref, table_ref, out_ref):
-        logits = dot_nt(rows_ref[...], table_ref[...])
-        if entries < padded:
-            lane = lax.broadcasted_iota(jnp.int32, (BLOCK, LANES), 1) + tail
-            masked = jnp.where(lane < entries, logits[:, tail:], NEG_BIG)
-            logits = jnp.concatenate([logits[:, :tail], masked], 1)
-        highest = jnp.max(logits, -1, keepdims=True)
-        shares = jnp.exp(logits - highest)
-        total = jnp.sum(shares, -1, keepdims=True)
-        mean = dot_nn(shares.astype(B16), table_ref[...]) / total
-        out_ref[:, :width] = mean.astype(B16)
-        out_ref[:, width:] = split_lse(highest + jnp.log(total), BLOCK)
+    half = padded // 2
+    ends = [0]
+    for stack in stacks:
+        ends.append(ends[-1] + stack.shape[0])
+    block = max(b for b in range(16, 400, 16) if ends[-1] % b == 0)
+
+    def body(*refs):
+        table_ref = refs[len(stacks)]
+        outs = refs[len(stacks) + 1 : -2]
+        rows_s, mean_s = refs[-2:]
+        for ref, first, last in zip(refs, ends[:-1], ends[1:]):
+            rows_s[first:last, :] = ref[...]
+
+        def turn(index, carry):
+            rows = pl.ds(pl.multiple_of(index * block, block), block)
+            logits = dot_nt(rows_s[rows, :], table_ref[...])
+            pieces = []
+            for first in range(0, padded, LANES):
+                piece = logits[:, first : first + LANES]
+                if any(c % half >= entries for c in range(first, first + LANES)):
+                    lane = lax.broadcasted_iota(jnp.int32, piece.shape, 1) + first
+                    piece = jnp.where(lane % half < entries, piece, NEG_BIG)
+                pieces.append(piece)
+            logits = jnp.concatenate(pieces, 1)
+            highest = jnp.max(logits, -1, keepdims=True)
+            shares = jnp.exp(logits - highest)
+            total = jnp.sum(shares, -1, keepdims=True)
+            mean = dot_nn(shares.astype(B16), table_ref[...]) / total
+            mean_s[rows, :width] = mean.astype(B16)
+            mean_s[rows, width:] = split_lse(highest + jnp.log(total), block)
+            return carry
+
+        lax.fori_loop(0, ends[-1] // block, turn, 0)
+        for out, first, last in zip(outs, ends[:-1], ends[1:]):
+            out[...] = mean_s[first:last, :]
 
     return pl.pallas_call(
         body,
-        grid=(row_count // BLOCK,),
-        in_specs=[rows_spec(width), whole_spec(table.shape)],
-        out_specs=rows_spec(width + LANES),
-        out_shape=shape((row_count, width + LANES), B16),
-        compiler_params=params(),
+        in_specs=[VMEM] * (len(stacks) + 1),
+        out_specs=[VMEM] * len(stacks),
+        out_shape=[shape((stack.shape[0], width + LANES), B16) for stack in stacks],
+        scratch_shapes=[
+            pltpu.VMEM((ends[-1], width), B16),
+            pltpu.VMEM((ends[-1], width + LANES), B16),
+        ],
+        cost_estimate=cost(10 * ends[-1] // 384),
         name="vocabulary",
-    )(rows, table)
-
-
-def joined_lse(ref, width):
-    last = ref[:, width:].astype(F32)
-    return jnp.sum(last[:, 0:4], -1, keepdims=True)
-
-
-def merge(first, second):
-    row_count, wide = first.shape
+    )(*stacks, table)
+
+
+def joined_lse(block, width):
+    return jnp.sum(block[:, width:].astype(F32)[:, 0:4], -1, keepdims=True)
+
+
+def merge(firsts, seconds, last):
+    wide = firsts[0].shape[1]
     width = wide - LANES
-    block = next(b for b in (256, 128, 64, 48, 32, 16) if row_count % b == 0)
-
-    def body(first_ref, second_ref, out_ref):
-        one, two = joined_lse(first_ref, width), joined_lse(second_ref, width)
-        highest = jnp.maximum(one, two)
-        scale_one, scale_two = jnp.exp(one - highest), jnp.exp(two - highest)
-        total = scale_one + scale_two
-        mean = first_ref[:, :width].astype(F32) * (scale_one / total)
-        mean = mean + second_ref[:, :width].astype(F32) * (scale_two / total)
-        out_ref[:, :width] = mean.astype(B16)
-        out_ref[:, width:] = split_lse(highest + jnp.log(total), block)
-
-    return pl.pallas_call(
+    count = len(firsts)
+    pieces = 1 if last else 2
+
+    def body(*refs):
+        outs = refs[2 * count :]
+        for part in range(count):
+            first_ref, second_ref = refs[part], refs[count + part]
+            rows = first_ref.shape[0] // pieces
+            for piece in range(pieces):
+                one = first_ref[piece * rows : (piece + 1) * rows, :]
+                two = second_ref[piece * rows : (piece + 1) * rows, :]
+                lse_one, lse_two = joined_lse(one, width), joined_lse(two, width)
+                highest = jnp.maximum(lse_one, lse_two)
+                scale_one, scale_two = jnp.exp(lse_one - highest), jnp.exp(lse_two - highest)
+                total = scale_one + scale_two
+                mean = one[:, :width].astype(F32) * (scale_one / total)
+                mean = mean + two[:, :width].astype(F32) * (scale_two / total)
+                out_ref = outs[piece * count + part]
+                out_ref[:, :width] = mean.astype(B16)
+                out_ref[:, width:] = split_lse(highest + jnp.log(total), rows)
+
+    outs = pl.pallas_call(
         body,
-        grid=(row_count // block,),
-        in_specs=[rows_spec(wide, block)] * 2,
-        out_specs=rows_spec(wide, block),
-        out_shape=shape((row_count, wide), B16),
-        compiler_params=params(),
+        in_specs=[VMEM] * (2 * count),
+        out_specs=[VMEM] * (pieces * count),
+        out_shape=[shape((a.shape[0] // pieces, wide), B16) for a in firsts] * pieces,
+        cost_estimate=cost(3),
         name="merge",
-    )(first, second)
+    )(*firsts, *seconds)
+    return outs[:count], outs[count:]
 
 
 def head_back(means, head_rows, head_in, target_rows, counted, final_norm, count_total):
     scored, width = head_rows.shape
 
     def body(mean_ref, rows_ref, in_ref, target_ref, counted_ref, norm_ref, grad_ref, loss_ref):
-        lse = joined_lse(mean_ref, width)
+        lse = joined_lse(mean_ref[...], width)
         target = target_ref[...].astype(F32)
         logit = jnp.sum(in_ref[...].astype(F32) * target, -1, keepdims=True)
         seen = counted_ref[...]
@@ -554,6 +674,7 @@
         out_specs=[rows_spec(width), rows_spec(LANES)],
         out_shape=[shape((scored, width), F32), shape((scored, LANES), F32)],
         compiler_params=params(),
+        cost_estimate=cost(4),
         name="head_back",
     )(means, head_rows, head_in, target_rows, counted, final_norm)
 
@@ -562,15 +683,17 @@
     row_count, width = gradient.shape
     hidden = slope.shape[1]
     extra = [] if residual is None else list(residual)
+    ups, downs = len(w_up.operands), len(w_down.operands)
 
     def body(me_ref, *refs):
         grad_ref, slope_ref = refs[0], refs[1]
         extra_refs = refs[2 : 2 + len(extra)]
-        up_held, up_taken, down_held, down_taken, part_ref, *rest = refs[2 + len(extra) :]
+        refs = refs[2 + len(extra) :]
+        part_ref, *rest = refs[ups + downs :]
         up, up_sems, down, down_sems = rest[-4:]
         step = pl.program_id(0)
-        up_refs = (me_ref[0], up_held, up_taken, up, up_sems)
-        down_refs = (me_ref[0], down_held, down_taken, down, down_sems)
+        up_refs = (me_ref[0], refs[:ups], up, up_sems)
+        down_refs = (me_ref[0], refs[ups : ups + downs], down, down_sems)
 
         @pl.when(step == 0)
         def _():
@@ -607,28 +730,32 @@
         grid_spec=pltpu.PrefetchScalarGridSpec(
             num_scalar_prefetch=1,
             grid=(row_count // BLOCK,),
-            in_specs=[rows_spec(width), rows_spec(hidden)] + extra_specs + [ANY] * 4,
+            in_specs=[rows_spec(width), rows_spec(hidden)] + extra_specs + w_up.specs + w_down.specs,
             out_specs=[rows_spec(width)] * (2 if extra else 1),
             scratch_shapes=w_up.scratch + w_down.scratch,
         ),
         out_shape=[shape((row_count, width), B16)]
         + ([shape((row_count, width), F32)] if extra else []),
         compiler_params=params(),
+        cost_estimate=cost(20 * row_count // 1024),
         name="mlp_back",
-    )(me, gradient, slope, *extra, *w_up.pair, *w_down.pair)
-
-
-def last_attention_back(gradient, own, other, middle, gain, q, k, v, mixed, lse, prefix, layout,
-                        picks, picks_column, me, weight, plen):
+    )(me, gradient, slope, *extra, *w_up.operands, *w_down.operands)
+
+
+def last_attention_back(gradient, own, other, middle, gain, q, k, v, lse, prefix, layout, picks,
+                        picks_column, me, weight, plen):
     scored, width = gradient.shape
     row_count, half = k.shape
     prefix_rows = prefix.shape[1]
     scale = HEAD_DIM ** (-0.5)
 
+    stacks = len(weight.operands)
+
     def body(me_ref, layout_ref, picks_ref, grad_ref, own_ref, other_ref, middle_ref, gain_ref,
-             q_ref, k_ref, v_ref, mixed_ref, lse_ref, prefix_ref, column_ref, held, taken,
-             part_ref, spread_ref, dprefix_ref, full, sems, dmix_s, dq_s, dk_s, dv_s, sum_s, rows_s):
-        refs = (me_ref[0], held, taken, full, sems)
+             q_ref, k_ref, v_ref, lse_ref, prefix_ref, column_ref, *refs):
+        (part_ref, spread_ref, dprefix_ref, full, sems,
+         dmix_s, dq_s, dk_s, dv_s, sum_s, rows_s) = refs[stacks:]
+        refs = (me_ref[0], refs[:stacks], full, sems)
         weight.start(*refs)
         incoming = own_ref[...].astype(F32) + other_ref[...].astype(F32)
         grad_mid = grad_ref[...] + norm_rows_back(incoming, middle_ref[...], gain_ref[...])
@@ -639,7 +766,7 @@
             spread_ref[pl.ds(picks_ref[index], 1), :] = rows_s[pl.ds(index, 1), :]
             return carry
 
-        lax.fori_loop(0, scored, put, 0)
+        lax.fori_loop(0, scored, put, 0, unroll=8)
         weight.wait(*refs)
         dmix_s[...] = dot_nn(grad_mid.astype(B16), full[:, 3 * half :]).astype(B16)
         bias = key_bias(layout_ref, column_ref[...], row_count)
@@ -655,7 +782,9 @@
             for side in range(2):
                 cut = slice(side * HEAD_DIM, (side + 1) * HEAD_DIM)
                 log_total = jnp.sum(
-                    jnp.where(lane == 2 * index + side, lse_ref[...], 0.0), -1, keepdims=True
+                    jnp.where(lane == prefix_rows * (2 * index + side), lse_ref[...], 0.0),
+                    -1,
+                    keepdims=True,
                 )
                 qh, dh = query[:, cut], d_mixed[:, cut]
                 shares = jnp.exp(dot_nt(qh, key[:, cut]) + bias - log_total)
@@ -693,16 +822,16 @@
             sum_s[place, :] = sum_s[place, :] + rows_s[pl.ds(index, 1), :]
             return carry
 
-        lax.fori_loop(0, scored, add, 0)
+        lax.fori_loop(0, scored, add, 0, unroll=8)
         part_ref[...] = sum_s[...].astype(B16)
 
-    inputs = [gradient, own, other, middle, gain, q, k, v, mixed, lse, prefix, picks_column]
+    inputs = [gradient, own, other, middle, gain, q, k, v, lse, prefix, picks_column]
     return pl.pallas_call(
         body,
         grid_spec=pltpu.PrefetchScalarGridSpec(
             num_scalar_prefetch=3,
             grid=(1,),
-            in_specs=[whole_spec(a.shape) for a in inputs] + [ANY, ANY],
+            in_specs=[whole_spec(a.shape) for a in inputs] + weight.specs,
             out_specs=[
                 whole_spec((row_count, width)),
                 whole_spec((row_count, width)),
@@ -724,24 +853,39 @@
             shape(prefix.shape, F32),
         ],
         compiler_params=params(),
+        cost_estimate=cost(24),
         name="last_attention_back",
-    )(me, layout, picks, *inputs, *weight.pair)
+    )(me, layout, picks, *inputs, *weight.operands)
 
 
 def first_prefix_back(gradient, own, other, middle, gain, q, mixed, lse, prefix, me, weight, plen):
     row_count, width = gradient.shape
     half = q.shape[1]
     prefix_rows = prefix.shape[1]
+    lanes = half // HEAD_DIM * prefix_rows
+    stacks = len(weight.operands)
+
+    def own_head(dims, lane_axis):
+        lane = lax.broadcasted_iota(jnp.int32, dims, lane_axis)
+        column = lax.broadcasted_iota(jnp.int32, dims, 1 - lane_axis)
+        return lane // prefix_rows == column // HEAD_DIM
 
     def body(me_ref, grad_ref, own_ref, other_ref, middle_ref, gain_ref, q_ref, mixed_ref,
-             lse_ref, prefix_ref, held, taken, dprefix_ref, full, sems):
+             lse_ref, prefix_ref, *refs):
+        dprefix_ref, full, sems, spread_s, sum_s = refs[stacks:]
         step = pl.program_id(0)
-        refs = (me_ref[0], held, taken, full, sems)
+        refs = (me_ref[0], refs[:stacks], full, sems)
 
         @pl.when(step == 0)
         def _():
             weight.start(*refs)
-            dprefix_ref[...] = jnp.zeros(prefix.shape, F32)
+            sum_s[...] = jnp.zeros(sum_s.shape, F32)
+            for c in range(2):
+                tiled = jnp.concatenate([prefix_ref[c]] * (lanes // prefix_rows), 0)
+                spread_s[c] = jnp.where(
+                    own_head((lanes, half), 0), tiled.astype(F32), 0.0
+                ).astype(B16)
+            spread_s[2] = jnp.where(own_head((lanes, half), 0), 1.0, 0.0).astype(B16)
 
         incoming = own_ref[...].astype(F32) + other_ref[...].astype(F32)
         grad_mid = grad_ref[...] + norm_rows_back(incoming, middle_ref[...], gain_ref[...])
@@ -752,22 +896,25 @@
 
         d_mixed = dot_nn(grad_mid.astype(B16), full[...]).astype(B16)
         product = d_mixed.astype(F32) * mixed_ref[...].astype(F32)
-        bias_prefix = prefix_bias(BLOCK, prefix_rows, plen)
-        d_keys = []
-        d_values = []
-        for head in range(half // HEAD_DIM):
-            cut = slice(head * HEAD_DIM, (head + 1) * HEAD_DIM)
-            qh, dh = q_ref[:, cut], d_mixed[:, cut]
-            inner = jnp.sum(product[:, cut], -1, keepdims=True)
-            shares = jnp.exp(
-                dot_nt(qh, prefix_ref[0, :, cut]) + bias_prefix - lse_ref[:, head : head + 1]
-            )
-            d_shares = dot_nt(dh, prefix_ref[1, :, cut]).astype(B16).astype(F32)
-            d_scores = (shares * (d_shares - inner)).astype(B16)
-            d_keys.append(dot_tn(d_scores, qh))
-            d_values.append(dot_tn(shares.astype(B16), dh))
-        dprefix_ref[0] += jnp.concatenate(d_keys, 1)
-        dprefix_ref[1] += jnp.concatenate(d_values, 1)
+        high = product.astype(B16)
+        low = (product - high.astype(F32)).astype(B16)
+        inner = dot_nt(high, spread_s[2]) + dot_nt(low, spread_s[2])
+        lane = lax.broadcasted_iota(jnp.int32, (BLOCK, lanes), 1)
+        shares = jnp.exp(dot_nt(q_ref[...], spread_s[0]) - lse_ref[:, :lanes])
+        shares = jnp.where(lane % prefix_rows < plen, shares, 0.0)
+        d_shares = dot_nt(d_mixed, spread_s[1]).astype(B16).astype(F32)
+        d_scores = (shares * (d_shares - inner)).astype(B16)
+        sum_s[0] += dot_tn(d_scores, q_ref[...])
+        sum_s[1] += dot_tn(shares.astype(B16), d_mixed)
+
+        @pl.when(step == row_count // BLOCK - 1)
+        def _():
+            for c in range(2):
+                held = jnp.where(own_head((lanes, half), 0), sum_s[c], 0.0)
+                total = held[:prefix_rows]
+                for first in range(prefix_rows, lanes, prefix_rows):
+                    total = total + held[first : first + prefix_rows]
+                dprefix_ref[c] = total
 
     return pl.pallas_call(
         body,
@@ -784,63 +931,79 @@
                 rows_spec(half),
                 rows_spec(LANES),
                 whole_spec(prefix.shape),
-                ANY,
-                ANY,
+                *weight.specs,
             ],
             out_specs=whole_spec(prefix.shape),
-            scratch_shapes=weight.scratch,
+            scratch_shapes=weight.scratch
+            + [pltpu.VMEM((3, lanes, half), B16), pltpu.VMEM((2, lanes, half), F32)],
         ),
         out_shape=shape(prefix.shape, F32),
         compiler_params=params(),
+        cost_estimate=cost(11),
         name="first_prefix_back",
-    )(me, gradient, own, other, middle, gain, q, mixed, lse, prefix, *weight.pair)
-
-
-def table_rows(ids, table):
-    count = ids.shape[0]
-    shard_rows, width = table.shape
-    size = lax.axis_size("dev")
-    own = lax.axis_index("ta")
-    ta_size = lax.axis_size("ta")
-    shard = ids // shard_rows
-    inside = ids % shard_rows
-    order = jnp.arange(count, dtype=jnp.int32)
-    same = ids[:, None] == ids[None, :]
-    first = jnp.min(jnp.where(same, order[None], count), 1)
-    is_first = first == order
-    earlier = is_first[None] & (shard[None] == shard[:, None]) & (order[None] < first[:, None])
-    rank = jnp.sum(earlier.astype(jnp.int32), 1)
-    mine = shard % ta_size == own
-    need = jnp.max(jnp.where(mine, rank, 0)) // SLOT_ROWS + 1
-    slots = jnp.arange(size * SLOT_ROWS, dtype=jnp.int32)
-
-    def fetch(turn, rows):
-        local_rank = rank - turn * SLOT_ROWS
-        used = mine & (local_rank >= 0) & (local_rank < SLOT_ROWS)
-        slot = jnp.where(used, shard // ta_size * SLOT_ROWS + local_rank, -1)
-        asked = jnp.max(jnp.where(slot[None] == slots[:, None], inside[None], 0), 1)
-        asked = asked.reshape(size, SLOT_ROWS)
-        header = jnp.broadcast_to(need, (size, 1))
-        wanted = lax.all_to_all(jnp.concatenate([asked, header], 1), "dev", 0, 0)
-        numbers = jnp.arange(shard_rows, dtype=jnp.int32)
+    )(me, gradient, own, other, middle, gain, q, mixed, lse, prefix, *weight.operands)
+
+
+class TableRows:
+    def __init__(self, ids, table):
+        count = ids.shape[0]
+        shard_rows = table.shape[0]
+        ta_size = lax.axis_size("ta")
+        shard = ids // shard_rows
+        self.table = table
+        self.inside = ids % shard_rows
+        self.owner = shard // ta_size
+        order = jnp.arange(count, dtype=jnp.int32)
+        same = ids[:, None] == ids[None, :]
+        first = jnp.min(jnp.where(same, order[None], count), 1)
+        is_first = first == order
+        earlier = is_first[None] & (shard[None] == shard[:, None]) & (order[None] < first[:, None])
+        self.rank = jnp.sum(earlier.astype(jnp.int32), 1)
+        self.mine = shard % ta_size == lax.axis_index("ta")
+        self.need = jnp.max(jnp.where(self.mine, self.rank, 0)) // SLOT_ROWS + 1
+        self.per_core = lax.axis_size("dev") * SLOT_ROWS
+
+    def slot(self, turn):
+        rank = self.rank - turn * SLOT_ROWS
+        used = (rank >= 0) & (rank < SLOT_ROWS)
+        slot = self.owner * SLOT_ROWS + rank + jnp.where(self.mine, 0, self.per_core)
+        return jnp.where(used, slot, -1)
+
+    def ask(self, turn):
+        slots = jnp.arange(self.per_core, dtype=jnp.int32)
+        found = self.slot(turn)[None] == slots[:, None]
+        asked = jnp.max(jnp.where(found, self.inside[None], 0), 1).reshape(-1, SLOT_ROWS)
+        header = jnp.broadcast_to(self.need, (asked.shape[0], 1))
+        return lax.all_to_all(jnp.concatenate([asked, header], 1), "dev", 0, 0)
+
+    def answer(self, wanted):
+        numbers = jnp.arange(self.table.shape[0], dtype=jnp.int32)
         pick = (wanted[:, :SLOT_ROWS].reshape(-1, 1) == numbers[None]).astype(B16)
-        sent = jnp.dot(pick, table, preferred_element_type=F32).astype(B16)
-        got = lax.all_to_all(sent.reshape(size, SLOT_ROWS, width), "dev", 0, 0)
-        spread = (slot[:, None] == slots[None]).astype(B16)
-        found = jnp.dot(spread, got.reshape(-1, width), preferred_element_type=F32).astype(B16)
-        return rows + found, jnp.max(wanted[:, SLOT_ROWS])
-
-    rows, most = fetch(0, jnp.zeros((count, width), B16))
-    most = jnp.maximum(most, partner(most.reshape(1, 1))[0, 0])
-
-    def again(state):
-        return state[0] < most
-
-    def turn(state):
-        return (state[0] + 1, fetch(state[0], state[1])[0])
-
-    rows = lax.while_loop(again, turn, (jnp.int32(1), rows))[1]
-    return rows + partner(rows)
+        sent = jnp.dot(pick, self.table, preferred_element_type=F32).astype(B16)
+        return sent.reshape(-1, SLOT_ROWS, self.table.shape[1])
+
+    def fetch(self, sent):
+        got = lax.all_to_all(sent, "dev", 0, 0)
+        return got.reshape(self.per_core, self.table.shape[1])
+
+    def place(self, turn, got):
+        slots = jnp.arange(2 * self.per_core, dtype=jnp.int32)
+        spread = (self.slot(turn)[:, None] == slots[None]).astype(B16)
+        both = jnp.concatenate([got, partner(got)], 0)
+        return jnp.dot(spread, both, preferred_element_type=F32)
+
+    def finish(self, base, wanted, got):
+        most = jnp.max(wanted[:, SLOT_ROWS])
+        most = jnp.maximum(most, partner(most.reshape(1, 1))[0, 0])
+
+        def again(state):
+            return state[0] < most
+
+        def turn(state):
+            got = self.fetch(self.answer(self.ask(state[0])))
+            return (state[0] + 1, state[1] + self.place(state[0], got))
+
+        return lax.while_loop(again, turn, (jnp.int32(1), base + self.place(0, got)))[1]
 
 
 def adamw_update(weight, moment, square, gradient, corr_one, corr_two):
@@ -892,61 +1055,140 @@
     plen = prefix_table.shape[0]
     prefix_rows = 16
     me = lax.axis_index("dev").astype(jnp.int32).reshape(1)
-    orders = bit_orders(size)
-    stages = len(orders[0])
+    orders = (bit_orders(size, 3), bit_orders(size, 4))
+    stages = len(orders[0][0])
     bucket_width = bucket[0]
     shift = jnp.where(bucket_width == 256, 8, 10).astype(jnp.int32)
     layout = jnp.concatenate([shift.reshape(1), bucket_width.reshape(1), seq_lengths[0]])
 
-    state = {}
-    for layer_id in range(2):
-        attention = jnp.concatenate(
-            [w_qkv[layer_id, c] for c in range(3)] + [w_out[layer_id].T], 1
+    rounds = Rounds()
+    ff = w_fc.shape[2]
+    totals = (4 * half, 2 * ff)
+    cuts = [[cuts_of(total, LANES, len(order)) for total in totals] for order in orders]
+
+    def add_layer(layer_id, qkv, out, fc, proj):
+        sides = (
+            jnp.concatenate([qkv[c] for c in range(3)] + [out.T], 1),
+            jnp.concatenate([fc, proj.T], 1),
         )
-        for part, rows in enumerate((attention, w_fc[layer_id], w_proj[layer_id].T)):
-            state[layer_id, part] = [rows[None]]
-    schedule = [[(layer_id, stage)] for layer_id in range(2) for stage in range(stages)]
-    state = doubling_rounds(schedule, state, orders)
-
-    def weight(layer_id, part, columns=None):
-        return Gathered(state[layer_id, part], orders[part], columns)
-
-    hidden = jnp.tanh(jnp.dot(prefix_table, inner_weight, precision=HIGHEST) + inner_bias)
-    partial_kv = jnp.einsum("pr,rlcd->lcpd", hidden, outer_weight, precision=HIGHEST)
-    prefix_kv = (sum_over_dev(partial_kv) + outer_bias[:, :, None, :]).astype(B16)
-    prefix_kv = jnp.pad(prefix_kv, ((0, 0), (0, 0), (0, prefix_rows - plen), (0, 0)))
-
-    rows = table_rows(jnp.concatenate([token_ids, targets]), wte)
-    target_rows = rows[row_count:]
-    repeat = row_count // 256
-    places = jnp.where(bucket_width == 256, jnp.tile(wpe[:256], (repeat, 1)), wpe[:row_count])
-    stream = rows[:row_count].astype(F32) + places.astype(F32)
+        parts = [
+            [
+                rows[:, c[p] : c[p + 1]]
+                for rows, c in zip(sides, cuts[layer_id])
+            ]
+            for p in range(len(orders[layer_id]))
+        ]
+        rounds.add(
+            layer_id,
+            orders[layer_id],
+            [jnp.concatenate(part, 1) for part in parts],
+            [part[0].shape[1] for part in parts],
+        )
+
+    def weight(layer_id, side, first, last):
+        segments = []
+        for p, order in enumerate(orders[layer_id]):
+            if layer_id == 0:
+                stacks, skip = rounds.held[0, p], cuts[0][0][p + 1] - cuts[0][0][p]
+                begin = cuts[0][side][p]
+                end = cuts[0][side][p + 1]
+                segments.append((stacks, order, begin, end, skip if side else 0))
+            else:
+                stacks = rounds.held[1, p, side]
+                segments.append((stacks, order, cuts[1][side][p], cuts[1][side][p + 1], 0))
+        return Gathered(segments, first, last)
+
+    def attention_weight(layer_id, first=0):
+        return weight(layer_id, 0, first * half, 4 * half)
+
+    def mlp_weights(layer_id):
+        return weight(layer_id, 1, 0, ff), weight(layer_id, 1, ff, 2 * ff)
 
     def head_bias(layer_id):
         part = lax.dynamic_slice_in_dim(frozen_vec[layer_id, 4:7], own_index * half, half, 1)
         return part.reshape(1, 3 * half)
 
+    add_layer(0, w_qkv[0], w_out[0], w_fc[0], w_proj[0])
+    ids, prefix_in = rounds.step(
+        0,
+        0,
+        through=(
+            (token_ids, targets),
+            (prefix_table, inner_weight, inner_bias, outer_weight),
+        ),
+    )
+    lookup = TableRows(jnp.concatenate(ids), wte)
+    wanted = lookup.ask(0)
+    hidden = jnp.tanh(jnp.dot(prefix_in[0], prefix_in[1], precision=HIGHEST) + prefix_in[2])
+    sums = jnp.einsum("pr,rlcd->lcpd", hidden, prefix_in[3], precision=HIGHEST)
+
+    wanted, sums, last_layer = rounds.step(
+        0, 1, through=(wanted, sums, (w_qkv[1], w_out[1], w_fc[1], w_proj[1]))
+    )
+    sent = lookup.answer(wanted)
+    for stage in range(stages):
+        sums = sums + flip(sums, 1 << stage)
+    prefix_kv = (sums + outer_bias[:, :, None, :]).astype(B16)
+    prefix_kv = jnp.pad(prefix_kv, ((0, 0), (0, 0), (0, prefix_rows - plen), (0, 0)))
+    add_layer(1, *last_layer)
+    for stage in range(2, stages - 2):
+        rounds.step(0, stage)
+
+    sent, wanted, prefix_kv, next_rows = rounds.step(
+        0,
+        stages - 2,
+        through=(sent, wanted, prefix_kv, [rounds.held[1, p][0] for p in range(len(orders[1]))]),
+    )
+    for part, array in enumerate(next_rows):
+        rounds.held[1, part] = [array]
+    got = lookup.fetch(sent)
+
+    got, wanted, places = rounds.step(0, stages - 1, through=(got, wanted, wpe))
+    repeat = row_count // 256
+    places = jnp.where(bucket_width == 256, jnp.tile(places[:256], (repeat, 1)), places[:row_count])
+    places = jnp.concatenate([places, jnp.zeros((scored, width), places.dtype)], 0)
+    rows = lookup.finish(places.astype(F32), wanted, got)
+    stream = rows[:row_count]
+    target_rows = rows[row_count:].astype(B16)
+
+    stream, target_rows = rounds.step(1, 0, through=(stream, target_rows))
     part, q0, mixed0, lse0 = first_attention(
-        stream, frozen_vec[0, 0:2], head_bias(0), prefix_kv[0], layout, me, weight(0, 0), plen
-    )
+        stream, frozen_vec[0, 0:2], head_bias(0), prefix_kv[0], layout, me, attention_weight(0), plen
+    )
+
+    part, table = rounds.step(1, 1, through=(part, wte))
+    other = partner(part)
+    entries = wte.shape[0]
+    table_half = -(-entries // 64) * 64
+    table = jnp.pad(table, ((0, table_half - entries), (0, 0)))
+
+    part, other, table = rounds.step(1, 2, through=(part, other, table))
     vec = frozen_vec[0]
     part_two, middle0, slope0 = mlp(
         stream,
         part,
-        partner(part),
+        other,
         jnp.stack([vec[7], vec[2], vec[3]]),
         fc_bias[0:1],
         me,
-        weight(0, 1),
-        weight(0, 2),
-    )
+        *mlp_weights(0),
+    )
+
+    for stage in range(3, stages - 1):
+        rounds.step(1, stage)
+
+    table, part_two = rounds.step(1, stages - 1, 0, through=(table, part_two))
+    other = partner(part_two)
+    table = jnp.concatenate([table, partner(table)], 0)
+
+    part_two, other, table = rounds.step(1, stages - 1, 1, through=(part_two, other, table))
 
     vec_last = frozen_vec[1]
     picks_column = loss_pos.reshape(scored, 1)
     stream1, part, k1, v1, q1, mixed1, lse1, chosen = last_attention(
         middle0,
         part_two,
-        partner(part_two),
+        other,
         jnp.stack([vec[8], vec_last[0], vec_last[1]]),
         head_bias(1),
         prefix_kv[1],
@@ -954,7 +1196,7 @@
         loss_pos,
         picks_column,
         me,
-        weight(1, 0),
+        attention_weight(1),
         plen,
     )
     part_two, middle1, slope1 = mlp(
@@ -964,8 +1206,7 @@
         jnp.stack([vec_last[7], vec_last[2], vec_last[3]]),
         fc_bias[1:2],
         me,
-        weight(1, 1),
-        weight(1, 2),
+        *mlp_weights(1),
     )
     both = part_two.astype(F32) + partner(part_two).astype(F32)
     head_rows = middle1 + (both + vec_last[8])
@@ -973,32 +1214,25 @@
     spread = jnp.mean(center * center, -1, keepdims=True)
     head_in = (center * lax.rsqrt(spread + EPS_NORM) * final_norm[0] + final_norm[1]).astype(B16)
 
-    entries = 2 * wte.shape[0]
-    padded = -(-entries // LANES) * LANES
-    table = jnp.concatenate(
-        [wte, partner(wte), jnp.zeros((padded - entries, width), B16)], 0
-    )
     core_rows = scored // 2
     mine = lax.dynamic_slice_in_dim(head_in, own_index * core_rows, core_rows, 0)
-    cuts = (0, 48, 96, core_rows)
-    head = {(0, p): [mine[None, cuts[p] : cuts[p + 1]]] for p in range(3)}
-    head = doubling_rounds([[(0, stage)] for stage in range(stages)], head, orders)
-    results = []
-    for side in range(2):
-        stacks = [head[0, p][side].reshape(-1, width) for p in range(3)]
-        answer = vocabulary(jnp.concatenate(stacks, 0), table, entries)
-        ends = [0]
-        for stack in stacks:
-            ends.append(ends[-1] + stack.shape[0])
-        results.append([answer[ends[p] : ends[p + 1]] for p in range(3)])
-    keep, send = results
+    cuts_head = (0, 48, 96, core_rows)
+    head_order = bit_orders(size, 3)
+    head = Rounds()
+    head.add(0, head_order, [mine[a:b] for a, b in zip(cuts_head[:-1], cuts_head[1:])])
+    for stage in range(stages):
+        head.step(0, stage)
+    near, far = [
+        [head.held[0, p][side].reshape(-1, width) for p in range(len(head_order))]
+        for side in range(2)
+    ]
+    keep = vocabulary(near[:1], table, entries)
+    far, keep, near = lax.optimization_barrier((far, keep, near))
+    send = vocabulary(far, table, entries)
+    keep = list(keep) + list(vocabulary(near[1:], table, entries))
     for stage in reversed(range(stages)):
-        if stage < stages - 1:
-            split = [a.shape[0] // 2 for a in keep]
-            send = [a[s:] for a, s in zip(keep, split)]
-            keep = [a[:s] for a, s in zip(keep, split)]
-        send = lax.optimization_barrier(tuple(send))
-        keep = [merge(a, flip(b, orders[p][stage])) for p, (a, b) in enumerate(zip(keep, send))]
+        got = [flip(array, head_order[p][stage]) for p, array in enumerate(send)]
+        keep, send = merge(keep, got, stage == 0)
     own_means = jnp.concatenate(keep, 0)
     other_means = partner(own_means)
     means = jnp.where(
@@ -1023,7 +1257,7 @@
     )
     loss_part = jnp.sum(loss_terms[:, 0])
 
-    (part,) = mlp_back(grad_rows, slope1, me, weight(1, 1), weight(1, 2))
+    (part,) = mlp_back(grad_rows, slope1, me, *mlp_weights(1))
     part, spread_grad, d_prefix1 = last_attention_back(
         grad_rows,
         part,
@@ -1033,23 +1267,20 @@
         q1,
         k1,
         v1,
-        mixed1,
         lse1,
         prefix_kv[1],
         layout,
         loss_pos,
         picks_column,
         me,
-        weight(1, 0),
+        attention_weight(1),
         plen,
     )
-    d_prefix1 = sum_over_dev(d_prefix1[:, :plen])
     part, grad_stream = mlp_back(
         spread_grad,
         slope0,
         me,
-        weight(0, 1),
-        weight(0, 2),
+        *mlp_weights(0),
         (stream1, vec_last[0:1], part, partner(part)),
     )
     d_prefix0 = first_prefix_back(
@@ -1063,11 +1294,10 @@
         lse0,
         prefix_kv[0],
         me,
-        weight(0, 0, (3 * half, 4 * half)),
+        attention_weight(0, 3),
         plen,
     )
-    d_prefix0 = sum_over_dev(d_prefix0[:, :plen])
-    d_prefix = jnp.stack([d_prefix0, d_prefix1])
+    d_prefix = sum_over_dev(jnp.stack([d_prefix0, d_prefix1])[:, :, :plen])
 
     d_outer = jnp.einsum("pr,lcpd->rlcd", hidden, d_prefix, precision=HIGHEST)
     d_outer_bias = jnp.sum(d_prefix, 2)

time: 773 us -> 677 us (0.88)
  waiting for transfers between devices: 281 us -> 228 us
  local copies, waits for them, and re-layouts: 88.3 us -> 41.9 us
  other arithmetic: 47.3 us -> 28.7 us
  Pallas kernels: 231 us -> 242 us
  starting transfers between devices: 86.9 us -> 96.8 us
    ppermute x64 -> x72, waiting for transfers between devices: 260 us -> 213 us  [flip(): return lax.ppermute(array, 'dev', [(i, i ^ bit) for i in range(size)])]
    concatenate x3 -> x2, local copies, waits for them, and re-layouts: 31.7 us -> 0.61 us  [the longest x1 0.61 us: ask(): return lax.all_to_all(jnp.concatenate([asked, header], 1), 'dev', 0, 0)]
    slice x17 -> x9, local copies, waits for them, and re-layouts: 28.7 us -> 6.97 us  [the longest x1 4.76 us: local(): stream = rows[:row_count]]
    pallas_call x14 -> x17, Pallas kernels: 70.6 us -> 91.9 us  [the longest x3 47.6 us: vocabulary(): pl.pallas_call(body, in_specs=[VMEM] * (len(stacks) + 1), out_specs=[VMEM...]
    concatenate x29 -> x1, other arithmetic: 19.9 us -> 5.42 us  [local(): table = jnp.concatenate([table, partner(table)], 0)]
    ppermute x64 -> x72, starting transfers between devices: 75.1 us -> 84.3 us  [flip(): return lax.ppermute(array, 'dev', [(i, i ^ bit) for i in range(size)])]
    all_to_all x2, waiting for transfers between devices: 8.3 us -> 0.01 us  [the longest x1 0.01 us: ask(): return lax.all_to_all(jnp.concatenate([asked, header], 1), 'dev', 0, 0)]
    pallas_call x1, Pallas kernels: 19.4 us -> 11.6 us  [first_prefix_back(): pl.pallas_call(body, grid_spec=pltpu.PrefetchScalarGridSpec(num_scalar_pr...]
  transfers between devices with their start and end apart: 78 -> 86, of which waited for: 45 -> 49; matrix products, arithmetic and copies ran while one was open for 14% -> 7% of each run, Pallas kernels for 18% -> 17%
where the time goes in v2:
time: 677 us; the launch traced here: 670 us
  Pallas kernels  242 us (36%)
  waiting for transfers between devices  228 us (34%)
  starting transfers between devices  96.8 us (14%)
  local copies, waits for them, and re-layouts  41.9 us (6%)
  other arithmetic  28.7 us (4%)
  matrix products  18.3 us (3%)
  between operations  13.6 us (2%)
    ppermute x72, waiting for transfers between devices, flip(): return lax.ppermute(array, 'dev', [(i, i ^ bit) for i in range(size)])  213 us
    ppermute x72, starting transfers between devices, flip(): return lax.ppermute(array, 'dev', [(i, i ^ bit) for i in range(size)])  84.3 us
    pallas_call x3, Pallas kernels, vocabulary(): pl.pallas_call(body, in_specs=[VMEM] * (len(stacks) + 1), out_specs=[VMEM...  47.6 us
    pallas_call x10, Pallas kernels, pack(): pl.pallas_call(body, in_specs=[pl.BlockSpec(memory_space=pl.ANY)] * len(a...  32.5 us
    pallas_call x2, Pallas kernels, mlp(): pl.pallas_call(body, grid_spec=pltpu.PrefetchScalarGridSpec(num_scalar_pr...  31.7 us
    pallas_call x1, Pallas kernels, first_attention(): pl.pallas_call(body, grid_spec=pltpu.PrefetchScalarGridSpec(num_scalar_pr...  31.1 us
    pallas_call x2, Pallas kernels, mlp_back(): pl.pallas_call(body, grid_spec=pltpu.PrefetchScalarGridSpec(num_scalar_pr...  27.8 us
    pallas_call x1, Pallas kernels, last_attention_back(): pl.pallas_call(body, grid_spec=pltpu.PrefetchScalarGridSpec(num_scalar_pr...  24 us
  transfers between devices with their start and end apart: 86, of which 49 were waited for; matrix products, arithmetic and copies ran while one was open for 7% of the time, Pallas kernels for 17%

profile of v2, /device:TPU:0, one launch (start us, length us, event | category | flops | bytes accessed | tf_op | source)
XLA Modules:
  0.0 669.7 jit_solution(8413679193564491892)
XLA Ops:
  4.1 4.1 collective-permute-start.3
  18.1 5.9 all-to-all-start.2
  23.9 7.6 %collective-permute-done.1.refs_1_ = bf16[1,64,1920]{2,1,0:T(8,128)(2,1)S(1)} collective-permute-done((bf16[1,64,1920]{2,1,0:T(8,128)(2,1)S(1)}, bf16[1,64,1920]{2,1,0:T(8,128)(2,1)S(1)}, u32[]{:S(2)}, u32[]{:S(2)}) %collective-permute-start.1) | collective-permute-done | bytes 245792 | tf_op jit(solution)/shard_map/ppermute | solution.py:49
  33.0 2.7 pack.10
  39.6 6.2 fusion.18
  45.8 6.7 %collective-permute-done.4 = f32[2,2,10,512]{3,2,1,0:T(8,128)S(1)} collective-permute-done((f32[2,2,10,512]{3,2,1,0:T(8,128)S(1)}, f32[2,2,10,512]{3,2,1,0:T(8,128)S(1)}, u32[]{:S(2)}, u32[]{:S(2)}) %collective-permute-start.4) | collective-permute-done | bytes 81952 | tf_op jit(solution)/shard_map/ppermute | solution.py:49
  54.0 3.7 collective-permute-done.5
  59.2 5.8 collective-permute-done.6
  65.6 7.6 %collective-permute-done.7 = f32[2,2,10,512]{3,2,1,0:T(8,128)S(1)} collective-permute-done((f32[2,2,10,512]{3,2,1,0:T(8,128)S(1)}, f32[2,2,10,512]{3,2,1,0:T(8,128)S(1)}, u32[]{:S(2)}, u32[]{:S(2)}) %collective-permute-start.7) | collective-permute-done | bytes 81952 | tf_op jit(solution)/shard_map/ppermute | solution.py:49
  74.1 3.5 pack.11
  77.6 4.6 all-to-all-start.3
  87.1 44.1 %collective-permute-done.11.refs_1_ = bf16[4,64,1920]{2,1,0:T(8,128)(2,1)} collective-permute-done((bf16[4,64,1920]{2,1,0:T(8,128)(2,1)}, bf16[4,64,1920]{2,1,0:T(8,128)(2,1)}, u32[]{:S(2)}, u32[]{:S(2)}) %collective-permute-start.11) | collective-permute-done | bytes 983072 | tf_op jit(solution)/shard_map/ppermute | solution.py:49
  131.2 5.4 pack.12
  149.7 9.2 %convert_add_fusion = f32[1280,1024]{1,0:T(8,128)} fusion(s32[1280]{0:T(1024)S(1)} %add_select_fusion.5, bf16[768,1024]{1,0:T(8,128)(2,1)} %collective-permute-done.14, bf16[768,1024]{1,0:T(8,128)(2,1)} %bitcast.39, bf16[1024,1024]{1,0:T(8,128)(2,1)} %bitcast_select_fusion), kind=kOutput, calls=%fused_computation.22 | convolution fusion | flops 4037410816 | bytes 10490880 | tf_op jit(solution)/shard_map/dot_general | solution.py:993
  159.1 4.8 slice.275.stream_ref.base_ref
  166.0 26.1 %collective-permute-done.16.refs_1_.refs_7_ = bf16[8,64,1920]{2,1,0:T(8,128)(2,1)} collective-permute-done((bf16[8,64,1920]{2,1,0:T(8,128)(2,1)}, bf16[8,64,1920]{2,1,0:T(8,128)(2,1)}, u32[]{:S(2)}, u32[]{:S(2)}) %collective-permute-start.16) | collective-permute-done | bytes 1966112 | tf_op jit(solution)/shard_map/ppermute | solution.py:49
  195.5 2.5 collective-permute-start.22
  200.5 31.1 %first_attention.1 = (bf16[1024,1024]{1,0:T(8,128)(2,1)}, bf16[1024,512]{1,0:T(8,128)(2,1)}, bf16[1024,512]{1,0:T(8,128)(2,1)}, f32[1024,128]{1,0:T(8,128)}) custom-call(s32[1]{0:T(128)} %bitcast.4.me_ref, s32[6]{0:T(128)} %pad_add_fusion.layout_ref, f32[1024,1024]{1,0:T(8,128)} %slice.275.stream_ref.base_ref, f32[2,1024]{1,0:T(2,128)} %bitcast.178, ...), custom_call_target="tpu_custom_call" | custom-call | flops 34500001792 | bytes 1024 | tf_op jit(solution)/shard_map/first_attention/pallas_call | solution.py:346
  233.1 2.6 pack.13
  238.5 2.5 collective-permute-start.25
  242.3 2.3 pad.13
  244.5 8.1 %collective-permute-done.24.refs_1_ = bf16[2,64,896]{2,1,0:T(8,128)(2,1)S(1)} collective-permute-done((bf16[2,64,896]{2,1,0:T(8,128)(2,1)}, bf16[2,64,896]{2,1,0:T(8,128)(2,1)S(1)}, u32[]{:S(2)}, u32[]{:S(2)}) %collective-permute-start.24) | collective-permute-done | bytes 229408 | tf_op jit(solution)/shard_map/ppermute | solution.py:49
  252.6 11.4 %collective-permute-done.26.refs_5_ = bf16[2,64,2048]{2,1,0:T(8,128)(2,1)} collective-permute-done((bf16[2,64,2048]{2,1,0:T(8,128)(2,1)}, bf16[2,64,2048]{2,1,0:T(8,128)(2,1)}, u32[]{:S(2)}, u32[]{:S(2)}) %collective-permute-start.26) | collective-permute-done | bytes 524320 | tf_op jit(solution)/shard_map/ppermute | solution.py:49
  264.0 3.6 pack.14
  267.7 2.8 collective-permute-start.31
  272.1 22.2 %mlp.2 = (bf16[1024,1024]{1,0:T(8,128)(2,1)}, f32[1024,1024]{1,0:T(8,128)}, bf16[1024,2048]{1,0:T(8,128)(2,1)}) custom-call(s32[1]{0:T(128)} %bitcast.4.me_ref, f32[1024,1024]{1,0:T(8,128)} %slice.275.stream_ref.base_ref, bf16[1024,1024]{1,0:T(8,128)(2,1)} %get-tuple-element.302.own_ref, bf16[1024,1024]{1,0:T(8,128)(2,1)} %collective-permute-done.23.other_ref, ...), custom_call_target="tpu_custom_call" | custom-call | flops 26449999872 | bytes 1024 | tf_op jit(solution)/shard_map/mlp/pallas_call | solution.py:417
  294.9 3.1 pack.15
  303.4 4.3 pack.16
  309.8 5.4 pad_maximum_fusion.refs_1_.refs_2_.refs_3_
  315.2 7.0 %collective-permute-done.34.refs_1_ = bf16[8,64,256]{2,1,0:T(8,128)(2,1)S(1)} collective-permute-done((bf16[8,64,256]{2,1,0:T(8,128)(2,1)}, bf16[8,64,256]{2,1,0:T(8,128)(2,1)S(1)}, u32[]{:S(2)}, u32[]{:S(2)}) %collective-permute-start.34) | collective-permute-done | bytes 262176 | tf_op jit(solution)/shard_map/ppermute | solution.py:49
  325.4 2.3 collective-permute-start.40
  327.7 20.6 %last_attention.1 = (f32[1024,1024]{1,0:T(8,128)}, bf16[256,1024]{1,0:T(8,128)(2,1)}, bf16[1024,512]{1,0:T(8,128)(2,1)}, bf16[1024,512]{1,0:T(8,128)(2,1)}, bf16...) custom-call(s32[1]{0:T(128)} %bitcast.4.me_ref, ...), custom_call_target="tpu_custom_call" | custom-call | flops 25300000768 | bytes 1024 | tf_op jit(solution)/shard_map/last_attention/pallas_call | solution.py:502
  350.5 4.7 collective-permute-done.39.refs_1_.refs_3_
  357.6 9.5 %mlp.3 = (bf16[256,1024]{1,0:T(8,128)(2,1)}, f32[256,1024]{1,0:T(8,128)}, bf16[256,2048]{1,0:T(8,128)(2,1)}) custom-call(s32[1]{0:T(128)} %bitcast.4.me_ref, f32[256,1024]{1,0:T(8,128)} %get-tuple-element.327.base_ref, bf16[256,1024]{1,0:T(8,128)(2,1)} %get-tuple-element.328.own_ref, bf16[256,1024]{1,0:T(8,128)(2,1)} %copy-done.62, ...), custom_call_target="tpu_custom_call" | custom-call | flops 5750000128 | bytes 1024 | tf_op jit(solution)/shard_map/mlp/pallas_call | solution.py:417
  371.7 3.2 collective-permute-start.45
  374.9 7.4 %collective-permute-done.46.refs_5_ = bf16[1,32,1024]{2,1,0:T(8,128)(2,1)S(1)} collective-permute-done((bf16[1,32,1024]{2,1,0:T(8,128)(2,1)S(1)}, bf16[1,32,1024]{2,1,0:T(8,128)(2,1)S(1)}, u32[]{:S(2)}, u32[]{:S(2)}) %collective-permute-start.46) | collective-permute-done | bytes 65568 | tf_op jit(solution)/shard_map/ppermute | solution.py:49
  387.8 3.7 collective-permute-done.49.refs_5_
  392.6 4.4 collective-permute-done.48.refs_3_
  397.8 2.4 pack.18
  402.2 7.4 %collective-permute-done.52.refs_5_ = bf16[4,32,1024]{2,1,0:T(8,128)(2,1)S(1)} collective-permute-done((bf16[4,32,1024]{2,1,0:T(8,128)(2,1)}, bf16[4,32,1024]{2,1,0:T(8,128)(2,1)S(1)}, u32[]{:S(2)}, u32[]{:S(2)}) %collective-permute-start.52) | collective-permute-done | bytes 262176 | tf_op jit(solution)/shard_map/ppermute | solution.py:49
  413.0 2.9 pack.19
  418.8 10.3 %vocabulary.3.refs_0_ = bf16[384,1152]{1,0:T(8,128)(2,1)} custom-call(bf16[384,1024]{1,0:T(8,128)(2,1)} %bitcast.185, bf16[3200,1024]{1,0:T(8,128)(2,1)} %pad_maximum_fusion.refs_1_.refs_2_.refs_3_), custom_call_target="tpu_custom_call" | custom-call | flops 11500000256 | bytes 1024 | tf_op jit(solution)/shard_map/vocabulary/pallas_call | solution.py:598
  430.4 4.3 collective-permute-done.53
  436.5 22.3 %vocabulary.5 = (bf16[384,1152]{1,0:T(8,128)(2,1)}, bf16[384,1152]{1,0:T(8,128)(2,1)}, bf16[256,1152]{1,0:T(8,128)(2,1)}) custom-call(bf16[384,1024]{1,0:T(8,128)(2,1)} %bitcast.186, bf16[384,1024]{1,0:T(8,128)(2,1)} %bitcast.187, bf16[256,1024]{1,0:T(8,128)(2,1)} %bitcast.189, bf16[3200,1024]{1,0:T(8,128)(2,1)} %pad_maximum_fusion.refs_1_.refs_2_.refs_3_), custom_call_target="tpu_custom_call" | custom-call | flops 29899999232 | bytes 1024 | tf_op jit(solution)/shard_map/vocabulary/pallas_call | solution.py:598
  461.3 15.0 %vocabulary.4 = (bf16[384,1152]{1,0:T(8,128)(2,1)}, bf16[256,1152]{1,0:T(8,128)(2,1)}) custom-call(bf16[384,1024]{1,0:T(8,128)(2,1)} %bitcast.184, bf16[256,1024]{1,0:T(8,128)(2,1)} %bitcast.188, bf16[3200,1024]{1,0:T(8,128)(2,1)} %pad_maximum_fusion.refs_1_.refs_2_.refs_3_), custom_call_target="tpu_custom_call" | custom-call | flops 18400000000 | bytes 1024 | tf_op jit(solution)/shard_map/vocabulary/pallas_call | solution.py:598
  480.1 4.5 merge.4
  486.8 6.2 collective-permute-done.61.refs_5_
  494.6 3.0 merge.5
  498.4 2.6 collective-permute-start.63
  502.2 4.2 collective-permute-done.64.refs_5_
  508.5 2.4 merge.6
  511.3 2.7 collective-permute-start.66
  514.2 5.7 collective-permute-done.67.refs_5_
  527.4 3.7 head_back.1
  531.1 8.6 %mlp_back.2.own_ref = bf16[256,1024]{1,0:T(8,128)(2,1)} custom-call(s32[1]{0:T(128)} %bitcast.4.me_ref, f32[256,1024]{1,0:T(8,128)} %get-tuple-element.390.refs_0_.grad_ref, bf16[256,2048]{1,0:T(8,128)(2,1)} %get-tuple-element.391.refs_1_, bf16[8,64,640]{2,1,0:T(8,128)(2,1)} %get-tuple-element.329.refs_0_.refs_2_, ...), custom_call_target="tpu_custom_call" | custom-call | flops 5750000128 | bytes 1024 | tf_op jit(solution)/shard_map/mlp_back/pallas_call | solution.py:728
  542.7 24.0 %last_attention_back.1 = (bf16[1024,1024]{1,0:T(8,128)(2,1)}, f32[1024,1024]{1,0:T(8,128)}, f32[2,16,512]{2,1,0:T(8,128)}) custom-call(s32[1]{0:T(128)} %bitcast.4.me_ref, s32[6]{0:T(128)} %pad_add_fusion.layout_ref, s32[256]{0:T(256)} %picks_ref.3, f32[256,1024]{1,0:T(8,128)} %get-tuple-element.390.refs_0_.grad_ref, bf16[256,1024]{1,0:T(8,128)(2,1)} %mlp_back.2.own_ref, ...), custom_call_target="tpu_custom_call" | custom-call | flops 27599998976 | bytes 1024 | tf_op jit(solution)/shard_map/last_attention_back/pallas_call | solution.py:829
  566.9 4.2 collective-permute-done.70.refs_5_
  572.5 19.1 %mlp_back.3 = (bf16[1024,1024]{1,0:T(8,128)(2,1)}, f32[1024,1024]{1,0:T(8,128)}) custom-call(s32[1]{0:T(128)} %bitcast.4.me_ref, f32[1024,1024]{1,0:T(8,128)} %get-tuple-element.396.refs_0_, bf16[1024,2048]{1,0:T(8,128)(2,1)} %get-tuple-element.397.refs_1_, f32[1024,1024]{1,0:T(8,128)} %get-tuple-element.398.refs_2_, f32[1,1024]{1,0:T(1,128)} %copy-done.36, ...), custom_call_target="tpu_custom_call" | custom-call | flops 23000000512 | bytes 1024 | tf_op jit(solution)/shard_map/mlp_back/pallas_call | solution.py:728
  591.8 4.2 collective-permute-done.71.other_ref
  597.4 11.6 %first_prefix_back.1 = f32[2,16,512]{2,1,0:T(8,128)} custom-call(s32[1]{0:T(128)} %bitcast.4.me_ref, f32[1024,1024]{1,0:T(8,128)} %get-tuple-element.400.grad_ref, bf16[1024,1024]{1,0:T(8,128)(2,1)} %get-tuple-element.401.own_ref, bf16[1024,1024]{1,0:T(8,128)(2,1)} %copy-done.53, f32[1024,1024]{1,0:T(8,128)} %get-tuple-element.304.base_ref.middle_ref, ...), custom_call_target="tpu_custom_call" | custom-call | flops 12650000384 | bytes 1024 | tf_op jit(solution)/shard_map/first_prefix_back/pallas_call | solution.py:919
  613.5 2.9 collective-permute-done.72
  616.4 2.7 collective-permute-done.73
  626.5 6.2 collective-permute-done.76
  653.6 2.4 collective-permute-done.83
  (422 shorter events, 158.0 us)
Async XLA Ops:
  4.1 27.4 %collective-permute-start.3 = (bf16[1,64,2176]{2,1,0:T(8,128)(2,1)S(1)}, bf16[1,64,2176]{2,1,0:T(8,128)(2,1)S(1)}, u32[]{:S(2)}, u32[]{:S(2)}) collective-permute-start(bf16[1,64,2176]{2,1,0:T(8,128)(2,1)S(1)} %fusion.28.refs_4_), channel_id=1, source_target_pairs={{0,16},{2,18},{4,20},{6,22},{8,24},{10,26},{12,28},{14,30},{16,0},... | collective-permute-start | bytes 835592 | tf_op jit(solution)/shard_map/ppermute | solution.py:49
  8.2 23.3 %collective-permute-start.2 = (bf16[1,64,2048]{2,1,0:T(8,128)(2,1)S(1)}, bf16[1,64,2048]{2,1,0:T(8,128)(2,1)S(1)}, u32[]{:S(2)}, u32[]{:S(2)}) collective-permute-start(bf16[1,64,2048]{2,1,0:T(8,128)(2,1)S(1)} %fusion.32.refs_2_), channel_id=1, source_target_pairs={{0,8},{2,10},{4,12},{6,14},{8,0},{10,2},{12,4},{14,6},{16,24},{18,... | collective-permute-start | bytes 786440 | tf_op jit(solution)/shard_map/ppermute | solution.py:49
  9.8 21.7 %collective-permute-start.1 = (bf16[1,64,1920]{2,1,0:T(8,128)(2,1)S(1)}, bf16[1,64,1920]{2,1,0:T(8,128)(2,1)S(1)}, u32[]{:S(2)}, u32[]{:S(2)}) collective-permute-start(bf16[1,64,1920]{2,1,0:T(8,128)(2,1)S(1)} %fusion.44.refs_0_), channel_id=1, source_target_pairs={{0,16},{2,18},{4,20},{6,22},{8,24},{10,26},{12,28},{14,30},{16,0},... | collective-permute-start | bytes 737288 | tf_op jit(solution)/shard_map/ppermute | solution.py:49
  18.1 17.6 %all-to-all-start.2 = ((s32[16,1,49]{2,1,0:T(1,128)}), s32[16,1,49]{2,1,0:T(1,128)S(1)}, u32[]{:S(2)}, u32[]{:S(2)}) async-start(s32[16,1,49]{2,1,0:T(1,128)} %bitcast.20), calls=%async_computation.2 | async-start | bytes 16384 | tf_op jit(solution)/shard_map/all_to_all | solution.py:977
  35.7 37.5 %collective-permute-start.10 = (bf16[2,64,2176]{2,1,0:T(8,128)(2,1)}, bf16[2,64,2176]{2,1,0:T(8,128)(2,1)S(1)}, u32[]{:S(2)}, u32[]{:S(2)}) collective-permute-start(bf16[2,64,2176]{2,1,0:T(8,128)(2,1)} %get-tuple-element.258.refs_4_), channel_id=1, source_target_pairs={{0,2},{2,0},{4,6},{6,4},{8,10},{10,8},{12,14},{14,12},{16,18},{18,... | collective-permute-start | bytes 1671176 | tf_op jit(solution)/shard_map/ppermute | solution.py:49
  37.3 35.9 %collective-permute-start.9 = (bf16[2,64,2048]{2,1,0:T(8,128)(2,1)}, bf16[2,64,2048]{2,1,0:T(8,128)(2,1)}, u32[]{:S(2)}, u32[]{:S(2)}) collective-permute-start(bf16[2,64,2048]{2,1,0:T(8,128)(2,1)} %get-tuple-element.257.refs_2_), channel_id=1, source_target_pairs={{0,16},{2,18},{4,20},{6,22},{8,24},{10,26},{12,28},{14,30},{16,0},... | collective-permute-start | bytes 1572872 | tf_op jit(solution)/shard_map/ppermute | solution.py:49
  37.3 35.9 %collective-permute-start.8 = (bf16[2,64,1920]{2,1,0:T(8,128)(2,1)}, bf16[2,64,1920]{2,1,0:T(8,128)(2,1)}, u32[]{:S(2)}, u32[]{:S(2)}) collective-permute-start(bf16[2,64,1920]{2,1,0:T(8,128)(2,1)} %get-tuple-element.256.refs_0_), channel_id=1, source_target_pairs={{0,4},{2,6},{4,0},{6,2},{8,12},{10,14},{12,8},{14,10},{16,20},{18,... | collective-permute-start | bytes 1474568 | tf_op jit(solution)/shard_map/ppermute | solution.py:49
  38.9 13.7 %collective-permute-start.4 = (f32[2,2,10,512]{3,2,1,0:T(8,128)S(1)}, f32[2,2,10,512]{3,2,1,0:T(8,128)S(1)}, u32[]{:S(2)}, u32[]{:S(2)}) collective-permute-start(f32[2,2,10,512]{3,2,1,0:T(8,128)S(1)} %convolution_bitcast_fusion), channel_id=1, source_target_pairs={{0,2},{2,0},{4,6},{6,4},{8,10},{10,8},{12,14},{14,12},{16,18},{18,... | collective-permute-start | bytes 245768 | tf_op jit(solution)/shard_map/ppermute | solution.py:49
  57.6 7.3 %collective-permute-start.6 = (f32[2,2,10,512]{3,2,1,0:T(8,128)S(1)}, f32[2,2,10,512]{3,2,1,0:T(8,128)S(1)}, u32[]{:S(2)}, u32[]{:S(2)}) collective-permute-start(f32[2,2,10,512]{3,2,1,0:T(8,128)S(1)} %add.335), channel_id=1, source_target_pairs={{0,8},{2,10},{4,12},{6,14},{8,0},{10,2},{12,4},{14,6},{16,24},{18,... | collective-permute-start | bytes 245768 | tf_op jit(solution)/shard_map/ppermute | solution.py:49
  65.0 8.2 %collective-permute-start.7 = (f32[2,2,10,512]{3,2,1,0:T(8,128)S(1)}, f32[2,2,10,512]{3,2,1,0:T(8,128)S(1)}, u32[]{:S(2)}, u32[]{:S(2)}) collective-permute-start(f32[2,2,10,512]{3,2,1,0:T(8,128)S(1)} %add.336), channel_id=1, source_target_pairs={{0,16},{2,18},{4,20},{6,22},{8,24},{10,26},{12,28},{14,30},{16,0},... | collective-permute-start | bytes 245768 | tf_op jit(solution)/shard_map/ppermute | solution.py:49
  77.6 59.1 %all-to-all-start.3 = ((bf16[16,48,1024]{2,1,0:T(8,128)(2,1)}), bf16[16,48,1024]{2,1,0:T(8,128)(2,1)}, u32[]{:S(2)}, u32[]{:S(2)}) async-start(bf16[16,48,1024]{2,1,0:T(8,128)(2,1)} %bitcast.29), calls=%async_computation.3 | async-start | bytes 3145728 | tf_op jit(solution)/shard_map/all_to_all | solution.py:986
  82.2 49.0 %collective-permute-start.13 = (bf16[4,64,2176]{2,1,0:T(8,128)(2,1)}, bf16[4,64,2176]{2,1,0:T(8,128)(2,1)}, u32[]{:S(2)}, u32[]{:S(2)}) collective-permute-start(bf16[4,64,2176]{2,1,0:T(8,128)(2,1)} %get-tuple-element.266.refs_4_), channel_id=1, source_target_pairs={{0,4},{2,6},{4,0},{6,2},{8,12},{10,14},{12,8},{14,10},{16,20},{18,... | collective-permute-start | bytes 3342344 | tf_op jit(solution)/shard_map/ppermute | solution.py:49
  84.2 47.0 %collective-permute-start.12 = (bf16[4,64,2048]{2,1,0:T(8,128)(2,1)}, bf16[4,64,2048]{2,1,0:T(8,128)(2,1)}, u32[]{:S(2)}, u32[]{:S(2)}) collective-permute-start(bf16[4,64,2048]{2,1,0:T(8,128)(2,1)} %get-tuple-element.265.refs_2_), channel_id=1, source_target_pairs={{0,2},{2,0},{4,6},{6,4},{8,10},{10,8},{12,14},{14,12},{16,18},{18,... | collective-permute-start | bytes 3145736 | tf_op jit(solution)/shard_map/ppermute | solution.py:49
  85.7 45.6 %collective-permute-start.11 = (bf16[4,64,1920]{2,1,0:T(8,128)(2,1)}, bf16[4,64,1920]{2,1,0:T(8,128)(2,1)}, u32[]{:S(2)}, u32[]{:S(2)}) collective-permute-start(bf16[4,64,1920]{2,1,0:T(8,128)(2,1)} %get-tuple-element.264.refs_0_), channel_id=1, source_target_pairs={{0,8},{2,10},{4,12},{6,14},{8,0},{10,2},{12,4},{14,6},{16,24},{18,... | collective-permute-start | bytes 2949128 | tf_op jit(solution)/shard_map/ppermute | solution.py:49
  136.7 13.0 %collective-permute-start.14 = (bf16[768,1024]{1,0:T(8,128)(2,1)}, bf16[768,1024]{1,0:T(8,128)(2,1)}, u32[]{:S(2)}, u32[]{:S(2)}) collective-permute-start(bf16[768,1024]{1,0:T(8,128)(2,1)} %bitcast.39), channel_id=1, source_target_pairs={{0,1},{1,0},{2,3},{3,2},{4,5},{5,4},{6,7},{7,6},{8,9},{9,8},{10,11... | collective-permute-start | bytes 4718600 | tf_op jit(solution)/shard_map/ppermute | solution.py:53
  144.8 50.7 %collective-permute-start.18 = (bf16[8,64,2176]{2,1,0:T(8,128)(2,1)}, bf16[8,64,2176]{2,1,0:T(8,128)(2,1)}, u32[]{:S(2)}, u32[]{:S(2)}) collective-permute-start(bf16[8,64,2176]{2,1,0:T(8,128)(2,1)} %get-tuple-element.280.refs_4_.refs_6_.refs_12_.refs_0_), channel_id=1, source_target_pairs={{0,8},{2,10},{4,12},{6,14},{8,0},{10,2},{12,4},{14,6},{16,24},{18,... | collective-permute-start | bytes 6684680 | tf_op jit(solution)/shard_map/ppermute | solution.py:49
  145.8 47.6 %collective-permute-start.17 = (bf16[8,64,2048]{2,1,0:T(8,128)(2,1)}, bf16[8,64,2048]{2,1,0:T(8,128)(2,1)}, u32[]{:S(2)}, u32[]{:S(2)}) collective-permute-start(bf16[8,64,2048]{2,1,0:T(8,128)(2,1)} %get-tuple-element.279.refs_2_.refs_4_.refs_8_.refs_10_), channel_id=1, source_target_pairs={{0,4},{2,6},{4,0},{6,2},{8,12},{10,14},{12,8},{14,10},{16,20},{18,... | collective-permute-start | bytes 6291464 | tf_op jit(solution)/shard_map/ppermute | solution.py:49
  147.3 44.8 %collective-permute-start.16 = (bf16[8,64,1920]{2,1,0:T(8,128)(2,1)}, bf16[8,64,1920]{2,1,0:T(8,128)(2,1)}, u32[]{:S(2)}, u32[]{:S(2)}) collective-permute-start(bf16[8,64,1920]{2,1,0:T(8,128)(2,1)} %get-tuple-element.278.refs_0_.refs_6_), channel_id=1, source_target_pairs={{0,2},{2,0},{4,6},{6,4},{8,10},{10,8},{12,14},{14,12},{16,18},{18,... | collective-permute-start | bytes 5898248 | tf_op jit(solution)/shard_map/ppermute | solution.py:49
  195.5 36.2 %collective-permute-start.22 = (bf16[1,64,2176]{2,1,0:T(8,128)(2,1)S(1)}, bf16[1,64,2176]{2,1,0:T(8,128)(2,1)S(1)}, u32[]{:S(2)}, u32[]{:S(2)}) collective-permute-start(bf16[1,64,2176]{2,1,0:T(8,128)(2,1)S(1)} %fusion.26.refs_6_), channel_id=1, source_target_pairs={{0,16},{2,18},{4,20},{6,22},{8,24},{10,26},{12,28},{14,30},{16,0},... | collective-permute-start | bytes 835592 | tf_op jit(solution)/shard_map/ppermute | solution.py:49
  198.0 33.6 %collective-permute-start.21 = (bf16[1,64,2048]{2,1,0:T(8,128)(2,1)S(1)}, bf16[1,64,2048]{2,1,0:T(8,128)(2,1)S(1)}, u32[]{:S(2)}, u32[]{:S(2)}) collective-permute-start(bf16[1,64,2048]{2,1,0:T(8,128)(2,1)S(1)} %fusion.35.refs_4_), channel_id=1, source_target_pairs={{0,8},{2,10},{4,12},{6,14},{8,0},{10,2},{12,4},{14,6},{16,24},{18,... | collective-permute-start | bytes 786440 | tf_op jit(solution)/shard_map/ppermute | solution.py:49
  198.5 33.2 %collective-permute-start.20 = (bf16[1,64,1024]{2,1,0:T(8,128)(2,1)S(1)}, bf16[1,64,1024]{2,1,0:T(8,128)(2,1)S(1)}, u32[]{:S(2)}, u32[]{:S(2)}) collective-permute-start(bf16[1,64,1024]{2,1,0:T(8,128)(2,1)S(1)} %fusion.47.refs_2_), channel_id=1, source_target_pairs={{0,2},{2,0},{4,6},{6,4},{8,10},{10,8},{12,14},{14,12},{16,18},{18,... | collective-permute-start | bytes 393224 | tf_op jit(solution)/shard_map/ppermute | solution.py:49
  199.9 31.7 %collective-permute-start.19 = (bf16[1,64,896]{2,1,0:T(8,128)(2,1)S(1)}, bf16[1,64,896]{2,1,0:T(8,128)(2,1)S(1)}, u32[]{:S(2)}, u32[]{:S(2)}) collective-permute-start(bf16[1,64,896]{2,1,0:T(8,128)(2,1)S(1)} %maximum_bitcast_fusion.refs_0_), channel_id=1, source_target_pairs={{0,2},{2,0},{4,6},{6,4},{8,10},{10,8},{12,14},{14,12},{16,18},{18,... | collective-permute-start | bytes 344072 | tf_op jit(solution)/shard_map/ppermute | solution.py:49
  235.8 31.9 %collective-permute-start.23 = (bf16[1024,1024]{1,0:T(8,128)(2,1)}, bf16[1024,1024]{1,0:T(8,128)(2,1)}, u32[]{:S(2)}, u32[]{:S(2)}) collective-permute-start(bf16[1024,1024]{1,0:T(8,128)(2,1)} %get-tuple-element.302.own_ref), channel_id=1, source_target_pairs={{0,1},{1,0},{2,3},{3,2},{4,5},{5,4},{6,7},{7,6},{8,9},{9,8},{10,11... | collective-permute-start | bytes 6291464 | tf_op jit(solution)/shard_map/ppermute | solution.py:53
  235.9 28.1 %collective-permute-start.27 = (bf16[2,64,2176]{2,1,0:T(8,128)(2,1)}, bf16[2,64,2176]{2,1,0:T(8,128)(2,1)}, u32[]{:S(2)}, u32[]{:S(2)}) collective-permute-start(bf16[2,64,2176]{2,1,0:T(8,128)(2,1)} %get-tuple-element.297.refs_6_), channel_id=1, source_target_pairs={{0,8},{2,10},{4,12},{6,14},{8,0},{10,2},{12,4},{14,6},{16,24},{18,... | collective-permute-start | bytes 1671176 | tf_op jit(solution)/shard_map/ppermute | solution.py:49
  237.5 26.5 %collective-permute-start.26 = (bf16[2,64,2048]{2,1,0:T(8,128)(2,1)}, bf16[2,64,2048]{2,1,0:T(8,128)(2,1)}, u32[]{:S(2)}, u32[]{:S(2)}) collective-permute-start(bf16[2,64,2048]{2,1,0:T(8,128)(2,1)} %get-tuple-element.296.refs_4_), channel_id=1, source_target_pairs={{0,16},{2,18},{4,20},{6,22},{8,24},{10,26},{12,28},{14,30},{16,0},... | collective-permute-start | bytes 1572872 | tf_op jit(solution)/shard_map/ppermute | solution.py:49
  238.5 14.1 %collective-permute-start.25 = (bf16[2,64,1024]{2,1,0:T(8,128)(2,1)}, bf16[2,64,1024]{2,1,0:T(8,128)(2,1)}, u32[]{:S(2)}, u32[]{:S(2)}) collective-permute-start(bf16[2,64,1024]{2,1,0:T(8,128)(2,1)} %get-tuple-element.295.refs_2_), channel_id=1, source_target_pairs={{0,4},{2,6},{4,0},{6,2},{8,12},{10,14},{12,8},{14,10},{16,20},{18,... | collective-permute-start | bytes 786440 | tf_op jit(solution)/shard_map/ppermute | solution.py:49
  241.0 11.6 %collective-permute-start.24 = (bf16[2,64,896]{2,1,0:T(8,128)(2,1)}, bf16[2,64,896]{2,1,0:T(8,128)(2,1)S(1)}, u32[]{:S(2)}, u32[]{:S(2)}) collective-permute-start(bf16[2,64,896]{2,1,0:T(8,128)(2,1)} %get-tuple-element.294.refs_0_), channel_id=1, source_target_pairs={{0,4},{2,6},{4,0},{6,2},{8,12},{10,14},{12,8},{14,10},{16,20},{18,... | collective-permute-start | bytes 688136 | tf_op jit(solution)/shard_map/ppermute | solution.py:49
  267.7 27.3 %collective-permute-start.31 = (bf16[4,64,2176]{2,1,0:T(8,128)(2,1)}, bf16[4,64,2176]{2,1,0:T(8,128)(2,1)}, u32[]{:S(2)}, u32[]{:S(2)}) collective-permute-start(bf16[4,64,2176]{2,1,0:T(8,128)(2,1)} %get-tuple-element.310.refs_6_), channel_id=1, source_target_pairs={{0,4},{2,6},{4,0},{6,2},{8,12},{10,14},{12,8},{14,10},{16,20},{18,... | collective-permute-start | bytes 3342344 | tf_op jit(solution)/shard_map/ppermute | solution.py:49
  270.4 24.5 %collective-permute-start.30 = (bf16[4,64,2048]{2,1,0:T(8,128)(2,1)}, bf16[4,64,2048]{2,1,0:T(8,128)(2,1)}, u32[]{:S(2)}, u32[]{:S(2)}) collective-permute-start(bf16[4,64,2048]{2,1,0:T(8,128)(2,1)} %get-tuple-element.309.refs_4_), channel_id=1, source_target_pairs={{0,2},{2,0},{4,6},{6,4},{8,10},{10,8},{12,14},{14,12},{16,18},{18,... | collective-permute-start | bytes 3145736 | tf_op jit(solution)/shard_map/ppermute | solution.py:49
  271.2 23.7 %collective-permute-start.29 = (bf16[4,64,1024]{2,1,0:T(8,128)(2,1)}, bf16[4,64,1024]{2,1,0:T(8,128)(2,1)}, u32[]{:S(2)}, u32[]{:S(2)}) collective-permute-start(bf16[4,64,1024]{2,1,0:T(8,128)(2,1)} %get-tuple-element.308.refs_2_), channel_id=1, source_target_pairs={{0,16},{2,18},{4,20},{6,22},{8,24},{10,26},{12,28},{14,30},{16,0},... | collective-permute-start | bytes 1572872 | tf_op jit(solution)/shard_map/ppermute | solution.py:49
  272.1 22.8 %collective-permute-start.28 = (bf16[4,64,896]{2,1,0:T(8,128)(2,1)}, bf16[4,64,896]{2,1,0:T(8,128)(2,1)}, u32[]{:S(2)}, u32[]{:S(2)}) collective-permute-start(bf16[4,64,896]{2,1,0:T(8,128)(2,1)} %get-tuple-element.307.refs_0_), channel_id=1, source_target_pairs={{0,8},{2,10},{4,12},{6,14},{8,0},{10,2},{12,4},{14,6},{16,24},{18,... | collective-permute-start | bytes 1376264 | tf_op jit(solution)/shard_map/ppermute | solution.py:49
  298.0 9.7 %collective-permute-start.33 = (bf16[1600,1024]{1,0:T(8,128)(2,1)S(1)}, bf16[1600,1024]{1,0:T(8,128)(2,1)}, u32[]{:S(2)}, u32[]{:S(2)}) collective-permute-start(bf16[1600,1024]{1,0:T(8,128)(2,1)S(1)} %pad.13), channel_id=1, source_target_pairs={{0,1},{1,0},{2,3},{3,2},{4,5},{5,4},{6,7},{7,6},{8,9},{9,8},{10,11... | collective-permute-start | bytes 9830408 | tf_op jit(solution)/shard_map/ppermute | solution.py:53
  298.1 24.1 %collective-permute-start.32 = (bf16[1024,1024]{1,0:T(8,128)(2,1)}, bf16[1024,1024]{1,0:T(8,128)(2,1)}, u32[]{:S(2)}, u32[]{:S(2)}) collective-permute-start(bf16[1024,1024]{1,0:T(8,128)(2,1)} %get-tuple-element.325.own_ref), channel_id=1, source_target_pairs={{0,1},{1,0},{2,3},{3,2},{4,5},{5,4},{6,7},{7,6},{8,9},{9,8},{10,11... | collective-permute-start | bytes 6291464 | tf_op jit(solution)/shard_map/ppermute | solution.py:53
  300.6 21.6 %collective-permute-start.37 = (bf16[8,64,768]{2,1,0:T(8,128)(2,1)}, bf16[8,64,768]{2,1,0:T(8,128)(2,1)}, u32[]{:S(2)}, u32[]{:S(2)}) collective-permute-start(bf16[8,64,768]{2,1,0:T(8,128)(2,1)} %get-tuple-element.324.refs_6_), channel_id=1, source_target_pairs={{0,2},{2,0},{4,6},{6,4},{8,10},{10,8},{12,14},{14,12},{16,18},{18,... | collective-permute-start | bytes 2359304 | tf_op jit(solution)/shard_map/ppermute | solution.py:49
  301.9 20.3 %collective-permute-start.36 = (bf16[8,64,640]{2,1,0:T(8,128)(2,1)}, bf16[8,64,640]{2,1,0:T(8,128)(2,1)}, u32[]{:S(2)}, u32[]{:S(2)}) collective-permute-start(bf16[8,64,640]{2,1,0:T(8,128)(2,1)} %get-tuple-element.323.refs_4_), channel_id=1, source_target_pairs={{0,4},{2,6},{4,0},{6,2},{8,12},{10,14},{12,8},{14,10},{16,20},{18,... | collective-permute-start | bytes 1966088 | tf_op jit(solution)/shard_map/ppermute | solution.py:49
  303.0 19.2 %collective-permute-start.35 = (bf16[8,64,384]{2,1,0:T(8,128)(2,1)}, bf16[8,64,384]{2,1,0:T(8,128)(2,1)}, u32[]{:S(2)}, u32[]{:S(2)}) collective-permute-start(bf16[8,64,384]{2,1,0:T(8,128)(2,1)} %get-tuple-element.322.refs_2_), channel_id=1, source_target_pairs={{0,8},{2,10},{4,12},{6,14},{8,0},{10,2},{12,4},{14,6},{16,24},{18,... | collective-permute-start | bytes 1179656 | tf_op jit(solution)/shard_map/ppermute | solution.py:49
  307.7 14.5 %collective-permute-start.34 = (bf16[8,64,256]{2,1,0:T(8,128)(2,1)}, bf16[8,64,256]{2,1,0:T(8,128)(2,1)S(1)}, u32[]{:S(2)}, u32[]{:S(2)}) collective-permute-start(bf16[8,64,256]{2,1,0:T(8,128)(2,1)} %get-tuple-element.321.refs_0_), channel_id=1, source_target_pairs={{0,16},{2,18},{4,20},{6,22},{8,24},{10,26},{12,28},{14,30},{16,0},... | collective-permute-start | bytes 786440 | tf_op jit(solution)/shard_map/ppermute | solution.py:49
  322.9 32.4 %collective-permute-start.41 = (bf16[8,64,1408]{2,1,0:T(8,128)(2,1)}, bf16[8,64,1408]{2,1,0:T(8,128)(2,1)S(1)}, u32[]{:S(2)}, u32[]{:S(2)}) collective-permute-start(bf16[8,64,1408]{2,1,0:T(8,128)(2,1)} %get-tuple-element.331.refs_4_.refs_6_.refs_8_), channel_id=1, source_target_pairs={{0,4},{2,6},{4,0},{6,2},{8,12},{10,14},{12,8},{14,10},{16,20},{18,... | collective-permute-start | bytes 4325384 | tf_op jit(solution)/shard_map/ppermute | solution.py:49
  324.7 31.8 %collective-permute-start.42 = (bf16[8,64,1408]{2,1,0:T(8,128)(2,1)}, bf16[8,64,1408]{2,1,0:T(8,128)(2,1)S(1)}, u32[]{:S(2)}, u32[]{:S(2)}) collective-permute-start(bf16[8,64,1408]{2,1,0:T(8,128)(2,1)} %get-tuple-element.332.refs_8_.refs_10_), channel_id=1, source_target_pairs={{0,2},{2,0},{4,6},{6,4},{8,10},{10,8},{12,14},{14,12},{16,18},{18,... | collective-permute-start | bytes 4325384 | tf_op jit(solution)/shard_map/ppermute | solution.py:49
  325.4 29.8 %collective-permute-start.39 = (bf16[8,64,640]{2,1,0:T(8,128)(2,1)}, bf16[8,64,640]{2,1,0:T(8,128)(2,1)}, u32[]{:S(2)}, u32[]{:S(2)}) collective-permute-start(bf16[8,64,640]{2,1,0:T(8,128)(2,1)} %get-tuple-element.329.refs_0_.refs_2_), channel_id=1, source_target_pairs={{0,16},{2,18},{4,20},{6,22},{8,24},{10,26},{12,28},{14,30},{16,0},... | collective-permute-start | bytes 1966088 | tf_op jit(solution)/shard_map/ppermute | solution.py:49
  325.4 29.9 %collective-permute-start.40 = (bf16[8,64,640]{2,1,0:T(8,128)(2,1)}, bf16[8,64,640]{2,1,0:T(8,128)(2,1)}, u32[]{:S(2)}, u32[]{:S(2)}) collective-permute-start(bf16[8,64,640]{2,1,0:T(8,128)(2,1)} %get-tuple-element.330.refs_2_.refs_4_), channel_id=1, source_target_pairs={{0,8},{2,10},{4,12},{6,14},{8,0},{10,2},{12,4},{14,6},{16,24},{18,... | collective-permute-start | bytes 1966088 | tf_op jit(solution)/shard_map/ppermute | solution.py:49
  371.6 10.7 %collective-permute-start.44 = (bf16[1,48,1024]{2,1,0:T(8,128)(2,1)S(1)}, bf16[1,48,1024]{2,1,0:T(8,128)(2,1)S(1)}, u32[]{:S(2)}, u32[]{:S(2)}) collective-permute-start(bf16[1,48,1024]{2,1,0:T(8,128)(2,1)S(1)} %get-tuple-element.335.refs_0_), channel_id=1, source_target_pairs={{0,16},{2,18},{4,20},{6,22},{8,24},{10,26},{12,28},{14,30},{16,0},... | collective-permute-start | bytes 294920 | tf_op jit(solution)/shard_map/ppermute | solution.py:49
  371.7 10.7 %collective-permute-start.45 = (bf16[1,48,1024]{2,1,0:T(8,128)(2,1)S(1)}, bf16[1,48,1024]{2,1,0:T(8,128)(2,1)S(1)}, u32[]{:S(2)}, u32[]{:S(2)}) collective-permute-start(bf16[1,48,1024]{2,1,0:T(8,128)(2,1)S(1)} %get-tuple-element.336.refs_2_), channel_id=1, source_target_pairs={{0,8},{2,10},{4,12},{6,14},{8,0},{10,2},{12,4},{14,6},{16,24},{18,... | collective-permute-start | bytes 294920 | tf_op jit(solution)/shard_map/ppermute | solution.py:49
  374.8 7.5 %collective-permute-start.46 = (bf16[1,32,1024]{2,1,0:T(8,128)(2,1)S(1)}, bf16[1,32,1024]{2,1,0:T(8,128)(2,1)S(1)}, u32[]{:S(2)}, u32[]{:S(2)}) collective-permute-start(bf16[1,32,1024]{2,1,0:T(8,128)(2,1)S(1)} %dynamic-slice_bitcast_fusion.2.refs_4_), channel_id=1, source_target_pairs={{0,16},{2,18},{4,20},{6,22},{8,24},{10,26},{12,28},{14,30},{16,0},... | collective-permute-start | bytes 196616 | tf_op jit(solution)/shard_map/ppermute | solution.py:49
  385.5 7.1 %collective-permute-start.47 = (bf16[2,48,1024]{2,1,0:T(8,128)(2,1)}, bf16[2,48,1024]{2,1,0:T(8,128)(2,1)S(1)}, u32[]{:S(2)}, u32[]{:S(2)}) collective-permute-start(bf16[2,48,1024]{2,1,0:T(8,128)(2,1)} %get-tuple-element.341.refs_0_), channel_id=1, source_target_pairs={{0,4},{2,6},{4,0},{6,2},{8,12},{10,14},{12,8},{14,10},{16,20},{18,... | collective-permute-start | bytes 589832 | tf_op jit(solution)/shard_map/ppermute | solution.py:49
  386.3 10.8 %collective-permute-start.48 = (bf16[2,48,1024]{2,1,0:T(8,128)(2,1)}, bf16[2,48,1024]{2,1,0:T(8,128)(2,1)S(1)}, u32[]{:S(2)}, u32[]{:S(2)}) collective-permute-start(bf16[2,48,1024]{2,1,0:T(8,128)(2,1)} %get-tuple-element.342.refs_2_), channel_id=1, source_target_pairs={{0,16},{2,18},{4,20},{6,22},{8,24},{10,26},{12,28},{14,30},{16,0},... | collective-permute-start | bytes 589832 | tf_op jit(solution)/shard_map/ppermute | solution.py:49
  400.2 11.3 %collective-permute-start.50 = (bf16[4,48,1024]{2,1,0:T(8,128)(2,1)}, bf16[4,48,1024]{2,1,0:T(8,128)(2,1)S(1)}, u32[]{:S(2)}, u32[]{:S(2)}) collective-permute-start(bf16[4,48,1024]{2,1,0:T(8,128)(2,1)} %get-tuple-element.347.refs_0_), channel_id=1, source_target_pairs={{0,8},{2,10},{4,12},{6,14},{8,0},{10,2},{12,4},{14,6},{16,24},{18,... | collective-permute-start | bytes 1179656 | tf_op jit(solution)/shard_map/ppermute | solution.py:49
  400.2 11.3 %collective-permute-start.51 = (bf16[4,48,1024]{2,1,0:T(8,128)(2,1)}, bf16[4,48,1024]{2,1,0:T(8,128)(2,1)S(1)}, u32[]{:S(2)}, u32[]{:S(2)}) collective-permute-start(bf16[4,48,1024]{2,1,0:T(8,128)(2,1)} %get-tuple-element.348.refs_2_), channel_id=1, source_target_pairs={{0,2},{2,0},{4,6},{6,4},{8,10},{10,8},{12,14},{14,12},{16,18},{18,... | collective-permute-start | bytes 1179656 | tf_op jit(solution)/shard_map/ppermute | solution.py:49
  401.4 8.2 %collective-permute-start.52 = (bf16[4,32,1024]{2,1,0:T(8,128)(2,1)}, bf16[4,32,1024]{2,1,0:T(8,128)(2,1)S(1)}, u32[]{:S(2)}, u32[]{:S(2)}) collective-permute-start(bf16[4,32,1024]{2,1,0:T(8,128)(2,1)} %get-tuple-element.349.refs_4_), channel_id=1, source_target_pairs={{0,4},{2,6},{4,0},{6,2},{8,12},{10,14},{12,8},{14,10},{16,20},{18,... | collective-permute-start | bytes 786440 | tf_op jit(solution)/shard_map/ppermute | solution.py:49
  415.9 18.9 %collective-permute-start.53 = (bf16[8,48,1024]{2,1,0:T(8,128)(2,1)}, bf16[8,48,1024]{2,1,0:T(8,128)(2,1)S(1)}, u32[]{:S(2)}, u32[]{:S(2)}) collective-permute-start(bf16[8,48,1024]{2,1,0:T(8,128)(2,1)} %get-tuple-element.353), channel_id=1, source_target_pairs={{0,2},{2,0},{4,6},{6,4},{8,10},{10,8},{12,14},{14,12},{16,18},{18,... | collective-permute-start | bytes 2359304 | tf_op jit(solution)/shard_map/ppermute | solution.py:49
  417.1 18.5 %collective-permute-start.54 = (bf16[8,48,1024]{2,1,0:T(8,128)(2,1)}, bf16[8,48,1024]{2,1,0:T(8,128)(2,1)S(1)}, u32[]{:S(2)}, u32[]{:S(2)}) collective-permute-start(bf16[8,48,1024]{2,1,0:T(8,128)(2,1)} %get-tuple-element.354), channel_id=1, source_target_pairs={{0,4},{2,6},{4,0},{6,2},{8,12},{10,14},{12,8},{14,10},{16,20},{18,... | collective-permute-start | bytes 2359304 | tf_op jit(solution)/shard_map/ppermute | solution.py:49
  417.8 12.7 %collective-permute-start.55 = (bf16[8,32,1024]{2,1,0:T(8,128)(2,1)}, bf16[8,32,1024]{2,1,0:T(8,128)(2,1)S(1)}, u32[]{:S(2)}, u32[]{:S(2)}) collective-permute-start(bf16[8,32,1024]{2,1,0:T(8,128)(2,1)} %get-tuple-element.355), channel_id=1, source_target_pairs={{0,8},{2,10},{4,12},{6,14},{8,0},{10,2},{12,4},{14,6},{16,24},{18,... | collective-permute-start | bytes 1572872 | tf_op jit(solution)/shard_map/ppermute | solution.py:49
  458.8 19.7 %collective-permute-start.56 = (bf16[384,1152]{1,0:T(8,128)(2,1)}, bf16[384,1152]{1,0:T(8,128)(2,1)S(1)}, u32[]{:S(2)}, u32[]{:S(2)}) collective-permute-start(bf16[384,1152]{1,0:T(8,128)(2,1)} %get-tuple-element.365), channel_id=1, source_target_pairs={{0,2},{2,0},{4,6},{6,4},{8,10},{10,8},{12,14},{14,12},{16,18},{18,... | collective-permute-start | bytes 2654216 | tf_op jit(solution)/shard_map/ppermute | solution.py:49
  459.7 19.5 %collective-permute-start.57 = (bf16[384,1152]{1,0:T(8,128)(2,1)}, bf16[384,1152]{1,0:T(8,128)(2,1)S(1)}, u32[]{:S(2)}, u32[]{:S(2)}) collective-permute-start(bf16[384,1152]{1,0:T(8,128)(2,1)} %get-tuple-element.366), channel_id=1, source_target_pairs={{0,4},{2,6},{4,0},{6,2},{8,12},{10,14},{12,8},{14,10},{16,20},{18,... | collective-permute-start | bytes 2654216 | tf_op jit(solution)/shard_map/ppermute | solution.py:49
  460.7 15.7 %collective-permute-start.58 = (bf16[256,1152]{1,0:T(8,128)(2,1)}, bf16[256,1152]{1,0:T(8,128)(2,1)S(1)}, u32[]{:S(2)}, u32[]{:S(2)}) collective-permute-start(bf16[256,1152]{1,0:T(8,128)(2,1)} %get-tuple-element.367), channel_id=1, source_target_pairs={{0,8},{2,10},{4,12},{6,14},{8,0},{10,2},{12,4},{14,6},{16,24},{18,... | collective-permute-start | bytes 1769480 | tf_op jit(solution)/shard_map/ppermute | solution.py:49
  484.6 9.1 %collective-permute-start.59 = (bf16[192,1152]{1,0:T(8,128)(2,1)}, bf16[192,1152]{1,0:T(8,128)(2,1)S(1)}, u32[]{:S(2)}, u32[]{:S(2)}) collective-permute-start(bf16[192,1152]{1,0:T(8,128)(2,1)} %get-tuple-element.371), channel_id=1, source_target_pairs={{0,8},{2,10},{4,12},{6,14},{8,0},{10,2},{12,4},{14,6},{16,24},{18,... | collective-permute-start | bytes 1327112 | tf_op jit(solution)/shard_map/ppermute | solution.py:49
  485.0 8.7 %collective-permute-start.60 = (bf16[192,1152]{1,0:T(8,128)(2,1)}, bf16[192,1152]{1,0:T(8,128)(2,1)S(1)}, u32[]{:S(2)}, u32[]{:S(2)}) collective-permute-start(bf16[192,1152]{1,0:T(8,128)(2,1)} %get-tuple-element.372), channel_id=1, source_target_pairs={{0,2},{2,0},{4,6},{6,4},{8,10},{10,8},{12,14},{14,12},{16,18},{18,... | collective-permute-start | bytes 1327112 | tf_op jit(solution)/shard_map/ppermute | solution.py:49
  497.6 8.8 %collective-permute-start.62 = (bf16[96,1152]{1,0:T(8,128)(2,1)}, bf16[96,1152]{1,0:T(8,128)(2,1)S(1)}, u32[]{:S(2)}, u32[]{:S(2)}) collective-permute-start(bf16[96,1152]{1,0:T(8,128)(2,1)} %get-tuple-element.377), channel_id=1, source_target_pairs={{0,4},{2,6},{4,0},{6,2},{8,12},{10,14},{12,8},{14,10},{16,20},{18,... | collective-permute-start | bytes 663560 | tf_op jit(solution)/shard_map/ppermute | solution.py:49
  498.4 9.4 %collective-permute-start.63 = (bf16[96,1152]{1,0:T(8,128)(2,1)}, bf16[96,1152]{1,0:T(8,128)(2,1)S(1)}, u32[]{:S(2)}, u32[]{:S(2)}) collective-permute-start(bf16[96,1152]{1,0:T(8,128)(2,1)} %get-tuple-element.378), channel_id=1, source_target_pairs={{0,16},{2,18},{4,20},{6,22},{8,24},{10,26},{12,28},{14,30},{16,0},... | collective-permute-start | bytes 663560 | tf_op jit(solution)/shard_map/ppermute | solution.py:49
  510.9 8.9 %collective-permute-start.65 = (bf16[48,1152]{1,0:T(8,128)(2,1)}, bf16[48,1152]{1,0:T(8,128)(2,1)S(1)}, u32[]{:S(2)}, u32[]{:S(2)}) collective-permute-start(bf16[48,1152]{1,0:T(8,128)(2,1)} %get-tuple-element.383), channel_id=1, source_target_pairs={{0,16},{2,18},{4,20},{6,22},{8,24},{10,26},{12,28},{14,30},{16,0},... | collective-permute-start | bytes 331784 | tf_op jit(solution)/shard_map/ppermute | solution.py:49
  511.3 8.6 %collective-permute-start.66 = (bf16[48,1152]{1,0:T(8,128)(2,1)}, bf16[48,1152]{1,0:T(8,128)(2,1)S(1)}, u32[]{:S(2)}, u32[]{:S(2)}) collective-permute-start(bf16[48,1152]{1,0:T(8,128)(2,1)} %get-tuple-element.384), channel_id=1, source_target_pairs={{0,8},{2,10},{4,12},{6,14},{8,0},{10,2},{12,4},{14,6},{16,24},{18,... | collective-permute-start | bytes 331784 | tf_op jit(solution)/shard_map/ppermute | solution.py:49
  611.0 8.1 %collective-permute-start.73 = (f32[2,2,10,512]{3,2,1,0:T(8,128)S(1)}, f32[2,2,10,512]{3,2,1,0:T(8,128)S(1)}, u32[]{:S(2)}, u32[]{:S(2)}) collective-permute-start(f32[2,2,10,512]{3,2,1,0:T(8,128)S(1)} %pad_maximum_fusion.4), channel_id=1, source_target_pairs={{0,4},{2,6},{4,0},{6,2},{8,12},{10,14},{12,8},{14,10},{16,20},{18,... | collective-permute-start | bytes 245768 | tf_op jit(solution)/shard_map/ppermute | solution.py:49
  620.2 12.5 %collective-permute-start.76 = (f32[2,2,10,512]{3,2,1,0:T(8,128)S(1)}, f32[2,2,10,512]{3,2,1,0:T(8,128)S(1)}, u32[]{:S(2)}, u32[]{:S(2)}) collective-permute-start(f32[2,2,10,512]{3,2,1,0:T(8,128)S(1)} %add_add_fusion.2), channel_id=1, source_target_pairs={{0,16},{2,18},{4,20},{6,22},{8,24},{10,26},{12,28},{14,30},{16,0},... | collective-permute-start | bytes 245768 | tf_op jit(solution)/shard_map/ppermute | solution.py:49
  622.4 10.3 %collective-permute-start.77 = (f32[2,2,10,512]{3,2,1,0:T(8,128)S(1)}, f32[2,2,10,512]{3,2,1,0:T(8,128)S(1)}, u32[]{:S(2)}, u32[]{:S(2)}) collective-permute-start(f32[2,2,10,512]{3,2,1,0:T(8,128)S(1)} %add_add_fusion.2), channel_id=1, source_target_pairs={{0,24},{2,26},{4,28},{6,30},{8,16},{10,18},{12,20},{14,22},{16,8},... | collective-permute-start | bytes 245768 | tf_op jit(solution)/shard_map/ppermute | solution.py:49
  (115 other events, 2166.0 us)

commit v3 on v2

--- a/solution.py
+++ b/solution.py
@@ -27,6 +27,7 @@
 SLOT_ROWS = 48
 BLOCK = 256
 LANES = 128
+PIECE = 2048
 SWAP = [(0, 1), (1, 0)]
 
 
@@ -185,10 +186,10 @@
 class Gathered:
     def __init__(self, segments, first, last):
         self.pieces = []
-        for stacks, order, begin, end, skip in segments:
-            low, high = max(first, begin), min(last, end)
+        for stacks, order, begin in segments:
+            low, high = max(first, begin), min(last, begin + stacks[0].shape[2])
             if low < high:
-                self.pieces.append((stacks, order, low - begin + skip, high - low, low - first))
+                self.pieces.append((stacks, order, low - begin, high - low, low - first))
         stacks, order, *unused = self.pieces[0]
         self.rows = stacks[0].shape[1]
         self.blocks = 1 << len(order)
@@ -304,8 +305,8 @@
     lax.fori_loop(0, q_ref.shape[1] // LANES, pair, 0)
 
 
-def first_attention(stream, vectors, bias_qkv, prefix, layout, me, weight, plen):
-    row_count, width = stream.shape
+def first_attention(stream, row_count, vectors, bias_qkv, prefix, layout, me, weight, plen):
+    width = stream.shape[1]
     half = prefix.shape[2]
     scale = HEAD_DIM ** (-0.5)
 
@@ -373,7 +374,7 @@
 
 
 def mlp(base, own, other, vectors, bias_up, me, w_up, w_down):
-    row_count, width = base.shape
+    row_count, width = own.shape
     hidden = bias_up.shape[1]
 
     ups, downs = len(w_up.operands), len(w_down.operands)
@@ -400,19 +401,25 @@
         def _():
             w_up.wait(*up_refs)
 
-        u = dot_nn(normed, up[...]) + bias_ref[...]
-        square = u * u
-        t = jnp.tanh(GELU_SCALE * u * (1.0 + GELU_CUBE * square))
-        half_one = 0.5 + 0.5 * t
-        active = (u * half_one).astype(B16)
-        slope = half_one + (0.5 * GELU_SCALE) * u * (1.0 - t * t) * (1.0 + 3 * GELU_CUBE * square)
-        slope_ref[...] = slope.astype(B16)
-
-        @pl.when(step == 0)
-        def _():
-            w_down.wait(*down_refs)
-
-        part_ref[...] = dot_nt(active, down[...]).astype(B16)
+        total = None
+        for first in range(0, hidden, PIECE):
+            piece = slice(first, first + PIECE)
+            u = dot_nn(normed, up[:, piece]) + bias_ref[:, piece]
+            square = u * u
+            t = jnp.tanh(GELU_SCALE * u * (1.0 + GELU_CUBE * square))
+            half_one = 0.5 + 0.5 * t
+            active = (u * half_one).astype(B16)
+            bend = (0.5 * GELU_SCALE) * u * (1.0 - t * t) * (1.0 + 3 * GELU_CUBE * square)
+            slope_ref[:, piece] = (half_one + bend).astype(B16)
+            if first == 0:
+
+                @pl.when(step == 0)
+                def _():
+                    w_down.wait(*down_refs)
+
+            product = dot_nt(active, down[:, piece])
+            total = product if total is None else total + product
+        part_ref[...] = total.astype(B16)
 
     return pl.pallas_call(
         body,
@@ -648,12 +655,12 @@
     return outs[:count], outs[count:]
 
 
-def head_back(means, head_rows, head_in, target_rows, counted, final_norm, count_total):
+def head_back(means, head_rows, head_in, rows, skip, counted, final_norm, count_total):
     scored, width = head_rows.shape
 
     def body(mean_ref, rows_ref, in_ref, target_ref, counted_ref, norm_ref, grad_ref, loss_ref):
         lse = joined_lse(mean_ref[...], width)
-        target = target_ref[...].astype(F32)
+        target = target_ref[...]
         logit = jnp.sum(in_ref[...].astype(F32) * target, -1, keepdims=True)
         seen = counted_ref[...]
         loss_ref[...] = jnp.broadcast_to((lse - logit) * seen, (BLOCK, LANES))
@@ -667,7 +674,7 @@
             rows_spec(width + LANES),
             rows_spec(width),
             rows_spec(width),
-            rows_spec(width),
+            pl.BlockSpec((BLOCK, width), lambda i: (i + skip // BLOCK, 0)),
             rows_spec(1),
             whole_spec(final_norm.shape),
         ],
@@ -676,7 +683,7 @@
         compiler_params=params(),
         cost_estimate=cost(4),
         name="head_back",
-    )(means, head_rows, head_in, target_rows, counted, final_norm)
+    )(means, head_rows, head_in, rows, counted, final_norm)
 
 
 def mlp_back(gradient, slope, me, w_up, w_down, residual=None):
@@ -711,14 +718,21 @@
         def _():
             w_down.wait(*down_refs)
 
-        d_active = dot_nn(grad.astype(B16), down[...])
-        d_upward = (d_active * slope_ref[...].astype(F32)).astype(B16)
-
-        @pl.when(step == 0)
-        def _():
-            w_up.wait(*up_refs)
-
-        part_ref[...] = dot_nt(d_upward, up[...]).astype(B16)
+        low = grad.astype(B16)
+        total = None
+        for first in range(0, hidden, PIECE):
+            piece = slice(first, first + PIECE)
+            d_active = dot_nn(low, down[:, piece])
+            d_upward = (d_active * slope_ref[:, piece].astype(F32)).astype(B16)
+            if first == 0:
+
+                @pl.when(step == 0)
+                def _():
+                    w_up.wait(*up_refs)
+
+            product = dot_nt(d_upward, up[:, piece])
+            total = product if total is None else total + product
+        part_ref[...] = total.astype(B16)
 
     extra_specs = (
         [rows_spec(width), whole_spec(extra[1].shape), rows_spec(width), rows_spec(width)]
@@ -1086,16 +1100,10 @@
         )
 
     def weight(layer_id, side, first, last):
-        segments = []
-        for p, order in enumerate(orders[layer_id]):
-            if layer_id == 0:
-                stacks, skip = rounds.held[0, p], cuts[0][0][p + 1] - cuts[0][0][p]
-                begin = cuts[0][side][p]
-                end = cuts[0][side][p + 1]
-                segments.append((stacks, order, begin, end, skip if side else 0))
-            else:
-                stacks = rounds.held[1, p, side]
-                segments.append((stacks, order, cuts[1][side][p], cuts[1][side][p + 1], 0))
+        segments = [
+            (rounds.held[layer_id, p, side], order, cuts[layer_id][side][p])
+            for p, order in enumerate(orders[layer_id])
+        ]
         return Gathered(segments, first, last)
 
     def attention_weight(layer_id, first=0):
@@ -1121,48 +1129,56 @@
     wanted = lookup.ask(0)
     hidden = jnp.tanh(jnp.dot(prefix_in[0], prefix_in[1], precision=HIGHEST) + prefix_in[2])
     sums = jnp.einsum("pr,rlcd->lcpd", hidden, prefix_in[3], precision=HIGHEST)
-
-    wanted, sums, last_layer = rounds.step(
-        0, 1, through=(wanted, sums, (w_qkv[1], w_out[1], w_fc[1], w_proj[1]))
-    )
+    for stage in range(stages - 2):
+        sums = sums + flip(sums, 1 << stage)
+
+    wanted, sums = rounds.step(0, 1, through=(wanted, sums))
     sent = lookup.answer(wanted)
-    for stage in range(stages):
-        sums = sums + flip(sums, 1 << stage)
+    sums = sums + flip(sums, 1 << (stages - 2))
+    for stage in range(2, stages - 2):
+        rounds.step(0, stage)
+
+    sent, wanted, sums, last_layer = rounds.step(
+        0,
+        stages - 2,
+        through=(sent, wanted, sums, (w_qkv[1], w_out[1], w_fc[1], w_proj[1])),
+    )
+    got = lookup.fetch(sent)
+    add_layer(1, *last_layer)
+    sums = sums + flip(sums, 1 << (stages - 1))
     prefix_kv = (sums + outer_bias[:, :, None, :]).astype(B16)
     prefix_kv = jnp.pad(prefix_kv, ((0, 0), (0, 0), (0, prefix_rows - plen), (0, 0)))
-    add_layer(1, *last_layer)
-    for stage in range(2, stages - 2):
-        rounds.step(0, stage)
-
-    sent, wanted, prefix_kv, next_rows = rounds.step(
+
+    got, wanted, places, prefix_kv, next_rows = rounds.step(
         0,
-        stages - 2,
-        through=(sent, wanted, prefix_kv, [rounds.held[1, p][0] for p in range(len(orders[1]))]),
+        stages - 1,
+        0,
+        through=(got, wanted, wpe, prefix_kv, [rounds.held[1, p][0] for p in range(len(orders[1]))]),
     )
     for part, array in enumerate(next_rows):
         rounds.held[1, part] = [array]
-    got = lookup.fetch(sent)
-
-    got, wanted, places = rounds.step(0, stages - 1, through=(got, wanted, wpe))
     repeat = row_count // 256
     places = jnp.where(bucket_width == 256, jnp.tile(places[:256], (repeat, 1)), places[:row_count])
     places = jnp.concatenate([places, jnp.zeros((scored, width), places.dtype)], 0)
-    rows = lookup.finish(places.astype(F32), wanted, got)
-    stream = rows[:row_count]
-    target_rows = rows[row_count:].astype(B16)
-
-    stream, target_rows = rounds.step(1, 0, through=(stream, target_rows))
+    stream = lookup.finish(places.astype(F32), wanted, got)
+
+    stream = rounds.step(0, stages - 1, 1, through=stream)
     part, q0, mixed0, lse0 = first_attention(
-        stream, frozen_vec[0, 0:2], head_bias(0), prefix_kv[0], layout, me, attention_weight(0), plen
-    )
-
-    part, table = rounds.step(1, 1, through=(part, wte))
+        stream,
+        row_count,
+        frozen_vec[0, 0:2],
+        head_bias(0),
+        prefix_kv[0],
+        layout,
+        me,
+        attention_weight(0),
+        plen,
+    )
+
+    part = rounds.step(1, 0, through=part)
     other = partner(part)
-    entries = wte.shape[0]
-    table_half = -(-entries // 64) * 64
-    table = jnp.pad(table, ((0, table_half - entries), (0, 0)))
-
-    part, other, table = rounds.step(1, 2, through=(part, other, table))
+
+    part, other = rounds.step(1, 1, through=(part, other))
     vec = frozen_vec[0]
     part_two, middle0, slope0 = mlp(
         stream,
@@ -1174,11 +1190,15 @@
         *mlp_weights(0),
     )
 
+    part_two, table = rounds.step(1, 2, through=(part_two, wte))
+    other = partner(part_two)
+    entries = wte.shape[0]
+    table_half = -(-entries // 64) * 64
+    table = jnp.pad(table, ((0, table_half - entries), (0, 0)))
     for stage in range(3, stages - 1):
         rounds.step(1, stage)
 
-    table, part_two = rounds.step(1, stages - 1, 0, through=(table, part_two))
-    other = partner(part_two)
+    table, part_two, other = rounds.step(1, stages - 1, 0, through=(table, part_two, other))
     table = jnp.concatenate([table, partner(table)], 0)
 
     part_two, other, table = rounds.step(1, stages - 1, 1, through=(part_two, other, table))
@@ -1253,7 +1273,7 @@
     counted = (place < lengths).astype(F32).reshape(scored, 1)
     count_total = float(scored * size)
     grad_rows, loss_terms = head_back(
-        means, head_rows, head_in, target_rows, counted, final_norm, count_total
+        means, head_rows, head_in, stream, row_count, counted, final_norm, count_total
     )
     loss_part = jnp.sum(loss_terms[:, 0])
 

time: 677 us -> 661 us (0.976)
  waiting for transfers between devices: 228 us -> 205 us
  starting transfers between devices: 96.8 us -> 104 us
    ppermute x72 -> x75, waiting for transfers between devices: 213 us -> 190 us  [flip(): return lax.ppermute(array, 'dev', [(i, i ^ bit) for i in range(size)])]
    ppermute x72 -> x75, starting transfers between devices: 84.3 us -> 92.9 us  [flip(): return lax.ppermute(array, 'dev', [(i, i ^ bit) for i in range(size)])]
    slice x2 -> x0, local copies, waits for them, and re-layouts: 6.9 us -> none  [the longest x1 4.76 us: local(): stream = rows[:row_count]]
    unnamed x190 -> x212, local copies, waits for them, and re-layouts: 21.4 us -> 26.5 us
    pallas_call x10 -> x11, Pallas kernels: 32.5 us -> 34.3 us  [pack(): pl.pallas_call(body, in_specs=[pl.BlockSpec(memory_space=pl.ANY)] * len(a...]
  transfers between devices with their start and end apart: 86 -> 89, of which waited for: 49 -> 51; matrix products, arithmetic and copies ran while one was open for 7% -> 6% of each run, Pallas kernels for 17% -> 18%
where the time goes in v3:
time: 661 us; the launch traced here: 655 us
  Pallas kernels  245 us (37%)
  waiting for transfers between devices  205 us (31%)
  starting transfers between devices  104 us (16%)
  local copies, waits for them, and re-layouts  40.1 us (6%)
  other arithmetic  28.7 us (4%)
  matrix products  18.4 us (3%)
  between operations  13.8 us (2%)
    ppermute x75, waiting for transfers between devices, flip(): return lax.ppermute(array, 'dev', [(i, i ^ bit) for i in range(size)])  190 us
    ppermute x75, starting transfers between devices, flip(): return lax.ppermute(array, 'dev', [(i, i ^ bit) for i in range(size)])  92.9 us
    pallas_call x3, Pallas kernels, vocabulary(): pl.pallas_call(body, in_specs=[VMEM] * (len(stacks) + 1), out_specs=[VMEM...  47.6 us
    pallas_call x11, Pallas kernels, pack(): pl.pallas_call(body, in_specs=[pl.BlockSpec(memory_space=pl.ANY)] * len(a...  34.3 us
    pallas_call x2, Pallas kernels, mlp(): pl.pallas_call(body, grid_spec=pltpu.PrefetchScalarGridSpec(num_scalar_pr...  31.8 us
    pallas_call x1, Pallas kernels, first_attention(): pl.pallas_call(body, grid_spec=pltpu.PrefetchScalarGridSpec(num_scalar_pr...  31.3 us
    pallas_call x2, Pallas kernels, mlp_back(): pl.pallas_call(body, grid_spec=pltpu.PrefetchScalarGridSpec(num_scalar_pr...  27.7 us
    unnamed x212, local copies, waits for them, and re-layouts  26.5 us
  transfers between devices with their start and end apart: 89, of which 51 were waited for; matrix products, arithmetic and copies ran while one was open for 6% of the time, Pallas kernels for 18%

profile of v3, /device:TPU:0, one launch (start us, length us, event | category | flops | bytes accessed | tf_op | source)
XLA Modules:
  0.0 654.9 jit_solution(13075134177747979306)
XLA Ops:
  4.7 3.0 collective-permute-start.1
  7.7 2.6 collective-permute-start.5
  21.4 4.9 all-to-all-start.2
  26.4 7.0 %collective-permute-done.3.refs_1_ = bf16[1,64,1920]{2,1,0:T(8,128)(2,1)S(1)} collective-permute-done((bf16[1,64,1920]{2,1,0:T(8,128)(2,1)S(1)}, bf16[1,64,1920]{2,1,0:T(8,128)(2,1)S(1)}, u32[]{:S(2)}, u32[]{:S(2)}) %collective-permute-start.3) | collective-permute-done | bytes 245792 | tf_op jit(solution)/shard_map/ppermute | solution.py:50
  34.8 2.6 pack.11
  39.6 4.1 collective-permute-start.6
  43.8 6.2 fusion.18
  49.9 2.2 collective-permute-done.6
  52.2 10.6 %collective-permute-done.8.refs_3_ = bf16[2,64,2048]{2,1,0:T(8,128)(2,1)S(1)} collective-permute-done((bf16[2,64,2048]{2,1,0:T(8,128)(2,1)}, bf16[2,64,2048]{2,1,0:T(8,128)(2,1)S(1)}, u32[]{:S(2)}, u32[]{:S(2)}) %collective-permute-start.8) | collective-permute-done | bytes 524320 | tf_op jit(solution)/shard_map/ppermute | solution.py:50
  64.5 3.5 pack.12
  68.0 4.8 all-to-all-start.3
  77.9 2.4 collective-permute-start.10
  80.4 41.9 %collective-permute-done.10 = f32[2,2,10,512]{3,2,1,0:T(8,128)S(1)} collective-permute-done((f32[2,2,10,512]{3,2,1,0:T(8,128)S(1)}, f32[2,2,10,512]{3,2,1,0:T(8,128)S(1)}, u32[]{:S(2)}, u32[]{:S(2)}) %collective-permute-start.10) | collective-permute-done | bytes 81952 | tf_op jit(solution)/shard_map/ppermute | solution.py:50
  124.5 3.0 pack.13
  132.2 4.3 pack.14
  139.3 2.4 collective-permute-start.18
  147.2 9.3 %convert_add_fusion = f32[1280,1024]{1,0:T(8,128)} fusion(s32[1280]{0:T(1024)S(1)} %add_select_fusion.5, bf16[768,1024]{1,0:T(8,128)(2,1)} %collective-permute-done.14, bf16[768,1024]{1,0:T(8,128)(2,1)} %bitcast.30, bf16[1024,1024]{1,0:T(8,128)(2,1)} %bitcast_select_fusion), kind=kOutput, calls=%fused_computation.22 | convolution fusion | flops 4037410816 | bytes 10490880 | tf_op jit(solution)/shard_map/dot_general | solution.py:1007
  166.2 31.3 %first_attention.1 = (bf16[1024,1024]{1,0:T(8,128)(2,1)}, bf16[1024,512]{1,0:T(8,128)(2,1)}, bf16[1024,512]{1,0:T(8,128)(2,1)}, f32[1024,128]{1,0:T(8,128)}) custom-call(s32[1]{0:T(128)} %bitcast.4.me_ref, s32[6]{0:T(128)} %pad_add_fusion.layout_ref, f32[1280,1024]{1,0:T(8,128)} %get-tuple-element.288.stream_ref.base_ref.target_ref, f32[2,1024]{1,0:T(2,128)} %bitcast.178, ...), custom_call_target="tpu_custom_call" | custom-call | flops 34500001792 | bytes 1024 | tf_op jit(solution)/shard_map/first_attention/pallas_call | solution.py:347
  202.8 5.4 collective-permute-done.23.refs_1_
  208.1 3.7 collective-permute-done.25.refs_5_
  212.5 2.7 collective-permute-done.26.refs_7_
  215.9 2.7 pack.15
  222.6 22.2 %mlp.2 = (bf16[1024,1024]{1,0:T(8,128)(2,1)}, f32[1024,1024]{1,0:T(8,128)}, bf16[1024,2048]{1,0:T(8,128)(2,1)}) custom-call(s32[1]{0:T(128)} %bitcast.4.me_ref, f32[1280,1024]{1,0:T(8,128)} %get-tuple-element.288.stream_ref.base_ref.target_ref, bf16[1024,1024]{1,0:T(8,128)(2,1)} %get-tuple-element.307.own_ref, bf16[1024,1024]{1,0:T(8,128)(2,1)} %copy-done.52, ...), custom_call_target="tpu_custom_call" | custom-call | flops 26449999872 | bytes 1024 | tf_op jit(solution)/shard_map/mlp/pallas_call | solution.py:424
  246.5 3.7 pack.16
  254.6 2.3 pad.13
  256.9 17.3 %collective-permute-done.32.refs_1_ = bf16[4,64,896]{2,1,0:T(8,128)(2,1)} collective-permute-done((bf16[4,64,896]{2,1,0:T(8,128)(2,1)}, bf16[4,64,896]{2,1,0:T(8,128)(2,1)}, u32[]{:S(2)}, u32[]{:S(2)}) %collective-permute-start.32) | collective-permute-done | bytes 458784 | tf_op jit(solution)/shard_map/ppermute | solution.py:50
  274.2 3.8 collective-permute-done.33.refs_3_
  277.9 3.0 pack.17
  284.2 4.3 pack.18
  290.1 2.6 collective-permute-start.37
  292.7 5.4 pad_maximum_fusion.refs_1_.refs_2_.refs_3_
  298.1 6.6 %collective-permute-done.37.refs_1_ = bf16[8,64,256]{2,1,0:T(8,128)(2,1)S(1)} collective-permute-done((bf16[8,64,256]{2,1,0:T(8,128)(2,1)}, bf16[8,64,256]{2,1,0:T(8,128)(2,1)S(1)}, u32[]{:S(2)}, u32[]{:S(2)}) %collective-permute-start.37) | collective-permute-done | bytes 262176 | tf_op jit(solution)/shard_map/ppermute | solution.py:50
  312.0 20.6 %last_attention.1 = (f32[1024,1024]{1,0:T(8,128)}, bf16[256,1024]{1,0:T(8,128)(2,1)}, bf16[1024,512]{1,0:T(8,128)(2,1)}, bf16[1024,512]{1,0:T(8,128)(2,1)}, bf16...) custom-call(s32[1]{0:T(128)} %bitcast.4.me_ref, ...), custom_call_target="tpu_custom_call" | custom-call | flops 25300000768 | bytes 1024 | tf_op jit(solution)/shard_map/last_attention/pallas_call | solution.py:509
  334.8 5.1 collective-permute-done.42.refs_1_.refs_3_
  342.3 9.5 %mlp.3 = (bf16[256,1024]{1,0:T(8,128)(2,1)}, f32[256,1024]{1,0:T(8,128)}, bf16[256,2048]{1,0:T(8,128)(2,1)}) custom-call(s32[1]{0:T(128)} %bitcast.4.me_ref, f32[256,1024]{1,0:T(8,128)} %get-tuple-element.342.base_ref, bf16[256,1024]{1,0:T(8,128)(2,1)} %get-tuple-element.343.own_ref, bf16[256,1024]{1,0:T(8,128)(2,1)} %copy-done.71, ...), custom_call_target="tpu_custom_call" | custom-call | flops 5750000128 | bytes 1024 | tf_op jit(solution)/shard_map/mlp/pallas_call | solution.py:424
  360.5 6.5 %collective-permute-done.49.refs_5_ = bf16[1,32,1024]{2,1,0:T(8,128)(2,1)S(1)} collective-permute-done((bf16[1,32,1024]{2,1,0:T(8,128)(2,1)S(1)}, bf16[1,32,1024]{2,1,0:T(8,128)(2,1)S(1)}, u32[]{:S(2)}, u32[]{:S(2)}) %collective-permute-start.49) | collective-permute-done | bytes 65568 | tf_op jit(solution)/shard_map/ppermute | solution.py:50
  373.0 4.0 collective-permute-done.52.refs_5_
  377.0 5.2 collective-permute-done.51.refs_3_
  382.9 2.4 pack.20
  387.3 7.4 %collective-permute-done.55.refs_5_ = bf16[4,32,1024]{2,1,0:T(8,128)(2,1)S(1)} collective-permute-done((bf16[4,32,1024]{2,1,0:T(8,128)(2,1)}, bf16[4,32,1024]{2,1,0:T(8,128)(2,1)S(1)}, u32[]{:S(2)}, u32[]{:S(2)}) %collective-permute-start.55) | collective-permute-done | bytes 262176 | tf_op jit(solution)/shard_map/ppermute | solution.py:50
  397.6 2.9 pack.21
  404.0 10.3 %vocabulary.3.refs_0_ = bf16[384,1152]{1,0:T(8,128)(2,1)} custom-call(bf16[384,1024]{1,0:T(8,128)(2,1)} %bitcast.185, bf16[3200,1024]{1,0:T(8,128)(2,1)} %pad_maximum_fusion.refs_1_.refs_2_.refs_3_), custom_call_target="tpu_custom_call" | custom-call | flops 11500000256 | bytes 1024 | tf_op jit(solution)/shard_map/vocabulary/pallas_call | solution.py:605
  415.7 3.7 collective-permute-done.56
  421.8 22.3 %vocabulary.5 = (bf16[384,1152]{1,0:T(8,128)(2,1)}, bf16[384,1152]{1,0:T(8,128)(2,1)}, bf16[256,1152]{1,0:T(8,128)(2,1)}) custom-call(bf16[384,1024]{1,0:T(8,128)(2,1)} %bitcast.186, bf16[384,1024]{1,0:T(8,128)(2,1)} %bitcast.187, bf16[256,1024]{1,0:T(8,128)(2,1)} %bitcast.189, bf16[3200,1024]{1,0:T(8,128)(2,1)} %pad_maximum_fusion.refs_1_.refs_2_.refs_3_), custom_call_target="tpu_custom_call" | custom-call | flops 29899999232 | bytes 1024 | tf_op jit(solution)/shard_map/vocabulary/pallas_call | solution.py:605
  446.0 15.0 %vocabulary.4 = (bf16[384,1152]{1,0:T(8,128)(2,1)}, bf16[256,1152]{1,0:T(8,128)(2,1)}) custom-call(bf16[384,1024]{1,0:T(8,128)(2,1)} %bitcast.184, bf16[256,1024]{1,0:T(8,128)(2,1)} %bitcast.188, bf16[3200,1024]{1,0:T(8,128)(2,1)} %pad_maximum_fusion.refs_1_.refs_2_.refs_3_), custom_call_target="tpu_custom_call" | custom-call | flops 18400000000 | bytes 1024 | tf_op jit(solution)/shard_map/vocabulary/pallas_call | solution.py:605
  461.0 2.8 collective-permute-done.59.refs_3_
  465.3 4.4 merge.4
  472.0 6.2 collective-permute-done.64.refs_5_
  480.0 3.0 merge.5
  486.8 4.4 collective-permute-done.67.refs_5_
  493.8 2.4 merge.6
  496.2 2.6 collective-permute-start.69
  499.3 5.8 collective-permute-done.70.refs_5_
  512.6 3.8 head_back.1
  516.4 8.6 %mlp_back.2.own_ref = bf16[256,1024]{1,0:T(8,128)(2,1)} custom-call(s32[1]{0:T(128)} %bitcast.4.me_ref, f32[256,1024]{1,0:T(8,128)} %get-tuple-element.404.refs_0_.grad_ref, bf16[256,2048]{1,0:T(8,128)(2,1)} %get-tuple-element.405.refs_1_, bf16[8,64,640]{2,1,0:T(8,128)(2,1)} %get-tuple-element.344.refs_0_.refs_2_, ...), custom_call_target="tpu_custom_call" | custom-call | flops 5750000128 | bytes 1024 | tf_op jit(solution)/shard_map/mlp_back/pallas_call | solution.py:742
  528.0 24.0 %last_attention_back.1 = (bf16[1024,1024]{1,0:T(8,128)(2,1)}, f32[1024,1024]{1,0:T(8,128)}, f32[2,16,512]{2,1,0:T(8,128)}) custom-call(s32[1]{0:T(128)} %bitcast.4.me_ref, s32[6]{0:T(128)} %pad_add_fusion.layout_ref, s32[256]{0:T(256)} %picks_ref.3, f32[256,1024]{1,0:T(8,128)} %get-tuple-element.404.refs_0_.grad_ref, bf16[256,1024]{1,0:T(8,128)(2,1)} %mlp_back.2.own_ref, ...), custom_call_target="tpu_custom_call" | custom-call | flops 27599998976 | bytes 1024 | tf_op jit(solution)/shard_map/last_attention_back/pallas_call | solution.py:843
  552.2 4.2 collective-permute-done.73.refs_5_
  557.8 19.1 %mlp_back.3 = (bf16[1024,1024]{1,0:T(8,128)(2,1)}, f32[1024,1024]{1,0:T(8,128)}) custom-call(s32[1]{0:T(128)} %bitcast.4.me_ref, f32[1024,1024]{1,0:T(8,128)} %get-tuple-element.410.refs_0_, bf16[1024,2048]{1,0:T(8,128)(2,1)} %get-tuple-element.411.refs_1_, f32[1024,1024]{1,0:T(8,128)} %get-tuple-element.412.refs_2_, f32[1,1024]{1,0:T(1,128)} %copy-done.36, ...), custom_call_target="tpu_custom_call" | custom-call | flops 23000000512 | bytes 1024 | tf_op jit(solution)/shard_map/mlp_back/pallas_call | solution.py:742
  577.2 4.2 collective-permute-done.74.other_ref
  582.9 11.6 %first_prefix_back.1 = f32[2,16,512]{2,1,0:T(8,128)} custom-call(s32[1]{0:T(128)} %bitcast.4.me_ref, f32[1024,1024]{1,0:T(8,128)} %get-tuple-element.414.grad_ref, bf16[1024,1024]{1,0:T(8,128)(2,1)} %get-tuple-element.415.own_ref, bf16[1024,1024]{1,0:T(8,128)(2,1)} %copy-done.54, f32[1024,1024]{1,0:T(8,128)} %get-tuple-element.309.base_ref.middle_ref, ...), custom_call_target="tpu_custom_call" | custom-call | flops 12650000384 | bytes 1024 | tf_op jit(solution)/shard_map/first_prefix_back/pallas_call | solution.py:933
  599.0 2.9 collective-permute-done.75
  605.6 2.4 collective-permute-start.79
  612.0 6.3 collective-permute-done.79
  639.0 2.4 collective-permute-done.86
  (449 shorter events, 173.4 us)
Async XLA Ops:
  4.7 11.7 %collective-permute-start.1 = (f32[2,2,10,512]{3,2,1,0:T(8,128)S(1)}, f32[2,2,10,512]{3,2,1,0:T(8,128)S(1)}, u32[]{:S(2)}, u32[]{:S(2)}) collective-permute-start(f32[2,2,10,512]{3,2,1,0:T(8,128)S(1)} %convolution_bitcast_fusion), channel_id=1, source_target_pairs={{0,2},{2,0},{4,6},{6,4},{8,10},{10,8},{12,14},{14,12},{16,18},{18,... | collective-permute-start | bytes 245768 | tf_op jit(solution)/shard_map/ppermute | solution.py:50
  7.7 25.7 %collective-permute-start.5 = (bf16[1,64,2176]{2,1,0:T(8,128)(2,1)S(1)}, bf16[1,64,2176]{2,1,0:T(8,128)(2,1)S(1)}, u32[]{:S(2)}, u32[]{:S(2)}) collective-permute-start(bf16[1,64,2176]{2,1,0:T(8,128)(2,1)S(1)} %fusion.28.refs_4_), channel_id=1, source_target_pairs={{0,16},{2,18},{4,20},{6,22},{8,24},{10,26},{12,28},{14,30},{16,0},... | collective-permute-start | bytes 835592 | tf_op jit(solution)/shard_map/ppermute | solution.py:50
  10.3 23.1 %collective-permute-start.4 = (bf16[1,64,2048]{2,1,0:T(8,128)(2,1)S(1)}, bf16[1,64,2048]{2,1,0:T(8,128)(2,1)S(1)}, u32[]{:S(2)}, u32[]{:S(2)}) collective-permute-start(bf16[1,64,2048]{2,1,0:T(8,128)(2,1)S(1)} %fusion.32.refs_2_), channel_id=1, source_target_pairs={{0,8},{2,10},{4,12},{6,14},{8,0},{10,2},{12,4},{14,6},{16,24},{18,... | collective-permute-start | bytes 786440 | tf_op jit(solution)/shard_map/ppermute | solution.py:50
  11.9 21.5 %collective-permute-start.3 = (bf16[1,64,1920]{2,1,0:T(8,128)(2,1)S(1)}, bf16[1,64,1920]{2,1,0:T(8,128)(2,1)S(1)}, u32[]{:S(2)}, u32[]{:S(2)}) collective-permute-start(bf16[1,64,1920]{2,1,0:T(8,128)(2,1)S(1)} %fusion.44.refs_0_), channel_id=1, source_target_pairs={{0,16},{2,18},{4,20},{6,22},{8,24},{10,26},{12,28},{14,30},{16,0},... | collective-permute-start | bytes 737288 | tf_op jit(solution)/shard_map/ppermute | solution.py:50
  21.4 16.1 %all-to-all-start.2 = ((s32[16,1,49]{2,1,0:T(1,128)}), s32[16,1,49]{2,1,0:T(1,128)S(1)}, u32[]{:S(2)}, u32[]{:S(2)}) async-start(s32[16,1,49]{2,1,0:T(1,128)} %bitcast.20), calls=%async_computation.2 | async-start | bytes 16384 | tf_op jit(solution)/shard_map/all_to_all | solution.py:991
  37.5 25.3 %collective-permute-start.9 = (bf16[2,64,2176]{2,1,0:T(8,128)(2,1)}, bf16[2,64,2176]{2,1,0:T(8,128)(2,1)S(1)}, u32[]{:S(2)}, u32[]{:S(2)}) collective-permute-start(bf16[2,64,2176]{2,1,0:T(8,128)(2,1)} %get-tuple-element.261.refs_4_), channel_id=1, source_target_pairs={{0,2},{2,0},{4,6},{6,4},{8,10},{10,8},{12,14},{14,12},{16,18},{18,... | collective-permute-start | bytes 1671176 | tf_op jit(solution)/shard_map/ppermute | solution.py:50
  38.1 24.8 %collective-permute-start.8 = (bf16[2,64,2048]{2,1,0:T(8,128)(2,1)}, bf16[2,64,2048]{2,1,0:T(8,128)(2,1)S(1)}, u32[]{:S(2)}, u32[]{:S(2)}) collective-permute-start(bf16[2,64,2048]{2,1,0:T(8,128)(2,1)} %get-tuple-element.260.refs_2_), channel_id=1, source_target_pairs={{0,16},{2,18},{4,20},{6,22},{8,24},{10,26},{12,28},{14,30},{16,0},... | collective-permute-start | bytes 1572872 | tf_op jit(solution)/shard_map/ppermute | solution.py:50
  38.3 13.9 %collective-permute-start.7 = (bf16[2,64,1920]{2,1,0:T(8,128)(2,1)}, bf16[2,64,1920]{2,1,0:T(8,128)(2,1)S(1)}, u32[]{:S(2)}, u32[]{:S(2)}) collective-permute-start(bf16[2,64,1920]{2,1,0:T(8,128)(2,1)} %get-tuple-element.259.refs_0_), channel_id=1, source_target_pairs={{0,4},{2,6},{4,0},{6,2},{8,12},{10,14},{12,8},{14,10},{16,20},{18,... | collective-permute-start | bytes 1474568 | tf_op jit(solution)/shard_map/ppermute | solution.py:50
  39.6 12.5 %collective-permute-start.6 = (f32[2,2,10,512]{3,2,1,0:T(8,128)S(1)}, f32[2,2,10,512]{3,2,1,0:T(8,128)S(1)}, u32[]{:S(2)}, u32[]{:S(2)}) collective-permute-start(f32[2,2,10,512]{3,2,1,0:T(8,128)S(1)} %add.335), channel_id=1, source_target_pairs={{0,8},{2,10},{4,12},{6,14},{8,0},{10,2},{12,4},{14,6},{16,24},{18,... | collective-permute-start | bytes 245768 | tf_op jit(solution)/shard_map/ppermute | solution.py:50
  68.0 59.5 %all-to-all-start.3 = ((bf16[16,48,1024]{2,1,0:T(8,128)(2,1)}), bf16[16,48,1024]{2,1,0:T(8,128)(2,1)}, u32[]{:S(2)}, u32[]{:S(2)}) async-start(bf16[16,48,1024]{2,1,0:T(8,128)(2,1)} %bitcast.25), calls=%async_computation.3 | async-start | bytes 3145728 | tf_op jit(solution)/shard_map/all_to_all | solution.py:1000
  72.8 51.7 %collective-permute-start.13 = (bf16[4,64,2176]{2,1,0:T(8,128)(2,1)}, bf16[4,64,2176]{2,1,0:T(8,128)(2,1)}, u32[]{:S(2)}, u32[]{:S(2)}) collective-permute-start(bf16[4,64,2176]{2,1,0:T(8,128)(2,1)} %get-tuple-element.274.refs_4_), channel_id=1, source_target_pairs={{0,4},{2,6},{4,0},{6,2},{8,12},{10,14},{12,8},{14,10},{16,20},{18,... | collective-permute-start | bytes 3342344 | tf_op jit(solution)/shard_map/ppermute | solution.py:50
  74.9 49.6 %collective-permute-start.12 = (bf16[4,64,2048]{2,1,0:T(8,128)(2,1)}, bf16[4,64,2048]{2,1,0:T(8,128)(2,1)}, u32[]{:S(2)}, u32[]{:S(2)}) collective-permute-start(bf16[4,64,2048]{2,1,0:T(8,128)(2,1)} %get-tuple-element.273.refs_2_), channel_id=1, source_target_pairs={{0,2},{2,0},{4,6},{6,4},{8,10},{10,8},{12,14},{14,12},{16,18},{18,... | collective-permute-start | bytes 3145736 | tf_op jit(solution)/shard_map/ppermute | solution.py:50
  76.3 48.1 %collective-permute-start.11 = (bf16[4,64,1920]{2,1,0:T(8,128)(2,1)}, bf16[4,64,1920]{2,1,0:T(8,128)(2,1)}, u32[]{:S(2)}, u32[]{:S(2)}) collective-permute-start(bf16[4,64,1920]{2,1,0:T(8,128)(2,1)} %get-tuple-element.272.refs_0_), channel_id=1, source_target_pairs={{0,8},{2,10},{4,12},{6,14},{8,0},{10,2},{12,4},{14,6},{16,24},{18,... | collective-permute-start | bytes 2949128 | tf_op jit(solution)/shard_map/ppermute | solution.py:50
  77.9 44.5 %collective-permute-start.10 = (f32[2,2,10,512]{3,2,1,0:T(8,128)S(1)}, f32[2,2,10,512]{3,2,1,0:T(8,128)S(1)}, u32[]{:S(2)}, u32[]{:S(2)}) collective-permute-start(f32[2,2,10,512]{3,2,1,0:T(8,128)S(1)} %add.336), channel_id=1, source_target_pairs={{0,16},{2,18},{4,20},{6,22},{8,24},{10,26},{12,28},{14,30},{16,0},... | collective-permute-start | bytes 245768 | tf_op jit(solution)/shard_map/ppermute | solution.py:50
  127.5 19.8 %collective-permute-start.14 = (bf16[768,1024]{1,0:T(8,128)(2,1)}, bf16[768,1024]{1,0:T(8,128)(2,1)}, u32[]{:S(2)}, u32[]{:S(2)}) collective-permute-start(bf16[768,1024]{1,0:T(8,128)(2,1)} %bitcast.30), channel_id=1, source_target_pairs={{0,1},{1,0},{2,3},{3,2},{4,5},{5,4},{6,7},{7,6},{8,9},{9,8},{10,11... | collective-permute-start | bytes 4718600 | tf_op jit(solution)/shard_map/ppermute | solution.py:54
  137.2 8.8 %collective-permute-start.15 = (s32[1,1]{1,0:T(1,128)}, s32[1,1]{1,0:T(1,128)}, u32[]{:S(2)}, u32[]{:S(2)}) collective-permute-start(s32[1,1]{1,0:T(1,128)} %bitcast.41), channel_id=1, source_target_pairs={{0,1},{1,0},{2,3},{3,2},{4,5},{5,4},{6,7},{7,6},{8,9},{9,8},{10,11... | collective-permute-start | bytes 20 | tf_op jit(solution)/shard_map/ppermute | solution.py:54
  139.3 21.3 %collective-permute-start.18 = (bf16[8,64,768]{2,1,0:T(8,128)(2,1)}, bf16[8,64,768]{2,1,0:T(8,128)(2,1)S(1)}, u32[]{:S(2)}, u32[]{:S(2)}) collective-permute-start(bf16[8,64,768]{2,1,0:T(8,128)(2,1)} %get-tuple-element.287.refs_4_.refs_0_), channel_id=1, source_target_pairs={{0,8},{2,10},{4,12},{6,14},{8,0},{10,2},{12,4},{14,6},{16,24},{18,... | collective-permute-start | bytes 2359304 | tf_op jit(solution)/shard_map/ppermute | solution.py:50
  141.7 16.6 %collective-permute-start.16 = (bf16[8,64,640]{2,1,0:T(8,128)(2,1)}, bf16[8,64,640]{2,1,0:T(8,128)(2,1)S(1)}, u32[]{:S(2)}, u32[]{:S(2)}) collective-permute-start(bf16[8,64,640]{2,1,0:T(8,128)(2,1)} %get-tuple-element.285.refs_0_), channel_id=1, source_target_pairs={{0,2},{2,0},{4,6},{6,4},{8,10},{10,8},{12,14},{14,12},{16,18},{18,... | collective-permute-start | bytes 1966088 | tf_op jit(solution)/shard_map/ppermute | solution.py:50
  143.8 16.7 %collective-permute-start.17 = (bf16[8,64,640]{2,1,0:T(8,128)(2,1)}, bf16[8,64,640]{2,1,0:T(8,128)(2,1)S(1)}, u32[]{:S(2)}, u32[]{:S(2)}) collective-permute-start(bf16[8,64,640]{2,1,0:T(8,128)(2,1)} %get-tuple-element.286.refs_2_), channel_id=1, source_target_pairs={{0,4},{2,6},{4,0},{6,2},{8,12},{10,14},{12,8},{14,10},{16,20},{18,... | collective-permute-start | bytes 1966088 | tf_op jit(solution)/shard_map/ppermute | solution.py:50
  161.9 35.6 %collective-permute-start.20 = (bf16[8,64,1408]{2,1,0:T(8,128)(2,1)}, bf16[8,64,1408]{2,1,0:T(8,128)(2,1)S(1)}, u32[]{:S(2)}, u32[]{:S(2)}) collective-permute-start(bf16[8,64,1408]{2,1,0:T(8,128)(2,1)} %get-tuple-element.296.refs_2_.refs_4_.refs_8_.refs_10_), channel_id=1, source_target_pairs={{0,4},{2,6},{4,0},{6,2},{8,12},{10,14},{12,8},{14,10},{16,20},{18,... | collective-permute-start | bytes 4325384 | tf_op jit(solution)/shard_map/ppermute | solution.py:50
  163.7 33.8 %collective-permute-start.21 = (bf16[8,64,1408]{2,1,0:T(8,128)(2,1)}, bf16[8,64,1408]{2,1,0:T(8,128)(2,1)}, u32[]{:S(2)}, u32[]{:S(2)}) collective-permute-start(bf16[8,64,1408]{2,1,0:T(8,128)(2,1)} %get-tuple-element.297.refs_6_.refs_12_), channel_id=1, source_target_pairs={{0,8},{2,10},{4,12},{6,14},{8,0},{10,2},{12,4},{14,6},{16,24},{18,... | collective-permute-start | bytes 4325384 | tf_op jit(solution)/shard_map/ppermute | solution.py:50
  165.3 32.2 %collective-permute-start.19 = (bf16[8,64,1280]{2,1,0:T(8,128)(2,1)}, bf16[8,64,1280]{2,1,0:T(8,128)(2,1)}, u32[]{:S(2)}, u32[]{:S(2)}) collective-permute-start(bf16[8,64,1280]{2,1,0:T(8,128)(2,1)} %get-tuple-element.295.refs_0_.refs_6_), channel_id=1, source_target_pairs={{0,2},{2,0},{4,6},{6,4},{8,10},{10,8},{12,14},{14,12},{16,18},{18,... | collective-permute-start | bytes 3932168 | tf_op jit(solution)/shard_map/ppermute | solution.py:50
  198.7 20.0 %collective-permute-start.22 = (bf16[1024,1024]{1,0:T(8,128)(2,1)}, bf16[1024,1024]{1,0:T(8,128)(2,1)S(1)}, u32[]{:S(2)}, u32[]{:S(2)}) collective-permute-start(bf16[1024,1024]{1,0:T(8,128)(2,1)} %get-tuple-element.307.own_ref), channel_id=1, source_target_pairs={{0,1},{1,0},{2,3},{3,2},{4,5},{5,4},{6,7},{7,6},{8,9},{9,8},{10,11... | collective-permute-start | bytes 6291464 | tf_op jit(solution)/shard_map/ppermute | solution.py:54
  199.3 15.9 %collective-permute-start.26 = (bf16[1,64,2176]{2,1,0:T(8,128)(2,1)S(1)}, bf16[1,64,2176]{2,1,0:T(8,128)(2,1)S(1)}, u32[]{:S(2)}, u32[]{:S(2)}) collective-permute-start(bf16[1,64,2176]{2,1,0:T(8,128)(2,1)S(1)} %fusion.26.refs_6_), channel_id=1, source_target_pairs={{0,16},{2,18},{4,20},{6,22},{8,24},{10,26},{12,28},{14,30},{16,0},... | collective-permute-start | bytes 835592 | tf_op jit(solution)/shard_map/ppermute | solution.py:50
  199.3 12.5 %collective-permute-start.25 = (bf16[1,64,2048]{2,1,0:T(8,128)(2,1)S(1)}, bf16[1,64,2048]{2,1,0:T(8,128)(2,1)S(1)}, u32[]{:S(2)}, u32[]{:S(2)}) collective-permute-start(bf16[1,64,2048]{2,1,0:T(8,128)(2,1)S(1)} %fusion.35.refs_4_), channel_id=1, source_target_pairs={{0,8},{2,10},{4,12},{6,14},{8,0},{10,2},{12,4},{14,6},{16,24},{18,... | collective-permute-start | bytes 786440 | tf_op jit(solution)/shard_map/ppermute | solution.py:50
  200.0 8.1 %collective-permute-start.24 = (bf16[1,64,1024]{2,1,0:T(8,128)(2,1)S(1)}, bf16[1,64,1024]{2,1,0:T(8,128)(2,1)S(1)}, u32[]{:S(2)}, u32[]{:S(2)}) collective-permute-start(bf16[1,64,1024]{2,1,0:T(8,128)(2,1)S(1)} %fusion.47.refs_2_), channel_id=1, source_target_pairs={{0,2},{2,0},{4,6},{6,4},{8,10},{10,8},{12,14},{14,12},{16,18},{18,... | collective-permute-start | bytes 393224 | tf_op jit(solution)/shard_map/ppermute | solution.py:50
  218.6 26.2 %collective-permute-start.30 = (bf16[2,64,2176]{2,1,0:T(8,128)(2,1)}, bf16[2,64,2176]{2,1,0:T(8,128)(2,1)S(1)}, u32[]{:S(2)}, u32[]{:S(2)}) collective-permute-start(bf16[2,64,2176]{2,1,0:T(8,128)(2,1)} %get-tuple-element.314.refs_6_), channel_id=1, source_target_pairs={{0,8},{2,10},{4,12},{6,14},{8,0},{10,2},{12,4},{14,6},{16,24},{18,... | collective-permute-start | bytes 1671176 | tf_op jit(solution)/shard_map/ppermute | solution.py:50
  218.7 26.1 %collective-permute-start.29 = (bf16[2,64,2048]{2,1,0:T(8,128)(2,1)}, bf16[2,64,2048]{2,1,0:T(8,128)(2,1)S(1)}, u32[]{:S(2)}, u32[]{:S(2)}) collective-permute-start(bf16[2,64,2048]{2,1,0:T(8,128)(2,1)} %get-tuple-element.313.refs_4_), channel_id=1, source_target_pairs={{0,16},{2,18},{4,20},{6,22},{8,24},{10,26},{12,28},{14,30},{16,0},... | collective-permute-start | bytes 1572872 | tf_op jit(solution)/shard_map/ppermute | solution.py:50
  220.6 24.3 %collective-permute-start.28 = (bf16[2,64,1024]{2,1,0:T(8,128)(2,1)}, bf16[2,64,1024]{2,1,0:T(8,128)(2,1)}, u32[]{:S(2)}, u32[]{:S(2)}) collective-permute-start(bf16[2,64,1024]{2,1,0:T(8,128)(2,1)} %get-tuple-element.312.refs_2_), channel_id=1, source_target_pairs={{0,4},{2,6},{4,0},{6,2},{8,12},{10,14},{12,8},{14,10},{16,20},{18,... | collective-permute-start | bytes 786440 | tf_op jit(solution)/shard_map/ppermute | solution.py:50
  221.1 23.7 %collective-permute-start.27 = (bf16[2,64,896]{2,1,0:T(8,128)(2,1)}, bf16[2,64,896]{2,1,0:T(8,128)(2,1)S(1)}, u32[]{:S(2)}, u32[]{:S(2)}) collective-permute-start(bf16[2,64,896]{2,1,0:T(8,128)(2,1)} %get-tuple-element.311.refs_0_), channel_id=1, source_target_pairs={{0,4},{2,6},{4,0},{6,2},{8,12},{10,14},{12,8},{14,10},{16,20},{18,... | collective-permute-start | bytes 688136 | tf_op jit(solution)/shard_map/ppermute | solution.py:50
  250.2 30.8 %collective-permute-start.31 = (bf16[1024,1024]{1,0:T(8,128)(2,1)}, bf16[1024,1024]{1,0:T(8,128)(2,1)}, u32[]{:S(2)}, u32[]{:S(2)}) collective-permute-start(bf16[1024,1024]{1,0:T(8,128)(2,1)} %get-tuple-element.340.own_ref), channel_id=1, source_target_pairs={{0,1},{1,0},{2,3},{3,2},{4,5},{5,4},{6,7},{7,6},{8,9},{9,8},{10,11... | collective-permute-start | bytes 6291464 | tf_op jit(solution)/shard_map/ppermute | solution.py:54
  250.3 27.7 %collective-permute-start.35 = (bf16[4,64,2176]{2,1,0:T(8,128)(2,1)}, bf16[4,64,2176]{2,1,0:T(8,128)(2,1)}, u32[]{:S(2)}, u32[]{:S(2)}) collective-permute-start(bf16[4,64,2176]{2,1,0:T(8,128)(2,1)} %get-tuple-element.324.refs_6_), channel_id=1, source_target_pairs={{0,4},{2,6},{4,0},{6,2},{8,12},{10,14},{12,8},{14,10},{16,20},{18,... | collective-permute-start | bytes 3342344 | tf_op jit(solution)/shard_map/ppermute | solution.py:50
  250.8 27.1 %collective-permute-start.34 = (bf16[4,64,2048]{2,1,0:T(8,128)(2,1)}, bf16[4,64,2048]{2,1,0:T(8,128)(2,1)}, u32[]{:S(2)}, u32[]{:S(2)}) collective-permute-start(bf16[4,64,2048]{2,1,0:T(8,128)(2,1)} %get-tuple-element.323.refs_4_), channel_id=1, source_target_pairs={{0,2},{2,0},{4,6},{6,4},{8,10},{10,8},{12,14},{14,12},{16,18},{18,... | collective-permute-start | bytes 3145736 | tf_op jit(solution)/shard_map/ppermute | solution.py:50
  251.6 26.4 %collective-permute-start.33 = (bf16[4,64,1024]{2,1,0:T(8,128)(2,1)}, bf16[4,64,1024]{2,1,0:T(8,128)(2,1)}, u32[]{:S(2)}, u32[]{:S(2)}) collective-permute-start(bf16[4,64,1024]{2,1,0:T(8,128)(2,1)} %get-tuple-element.322.refs_2_), channel_id=1, source_target_pairs={{0,16},{2,18},{4,20},{6,22},{8,24},{10,26},{12,28},{14,30},{16,0},... | collective-permute-start | bytes 1572872 | tf_op jit(solution)/shard_map/ppermute | solution.py:50
  252.7 21.5 %collective-permute-start.32 = (bf16[4,64,896]{2,1,0:T(8,128)(2,1)}, bf16[4,64,896]{2,1,0:T(8,128)(2,1)}, u32[]{:S(2)}, u32[]{:S(2)}) collective-permute-start(bf16[4,64,896]{2,1,0:T(8,128)(2,1)} %get-tuple-element.321.refs_0_), channel_id=1, source_target_pairs={{0,8},{2,10},{4,12},{6,14},{8,0},{10,2},{12,4},{14,6},{16,24},{18,... | collective-permute-start | bytes 1376264 | tf_op jit(solution)/shard_map/ppermute | solution.py:50
  281.0 11.7 %collective-permute-start.36 = (bf16[1600,1024]{1,0:T(8,128)(2,1)S(1)}, bf16[1600,1024]{1,0:T(8,128)(2,1)}, u32[]{:S(2)}, u32[]{:S(2)}) collective-permute-start(bf16[1600,1024]{1,0:T(8,128)(2,1)S(1)} %pad.13), channel_id=1, source_target_pairs={{0,1},{1,0},{2,3},{3,2},{4,5},{5,4},{6,7},{7,6},{8,9},{9,8},{10,11... | collective-permute-start | bytes 9830408 | tf_op jit(solution)/shard_map/ppermute | solution.py:54
  283.1 23.7 %collective-permute-start.40 = (bf16[8,64,768]{2,1,0:T(8,128)(2,1)}, bf16[8,64,768]{2,1,0:T(8,128)(2,1)}, u32[]{:S(2)}, u32[]{:S(2)}) collective-permute-start(bf16[8,64,768]{2,1,0:T(8,128)(2,1)} %get-tuple-element.339.refs_6_), channel_id=1, source_target_pairs={{0,2},{2,0},{4,6},{6,4},{8,10},{10,8},{12,14},{14,12},{16,18},{18,... | collective-permute-start | bytes 2359304 | tf_op jit(solution)/shard_map/ppermute | solution.py:50
  288.5 18.4 %collective-permute-start.39 = (bf16[8,64,640]{2,1,0:T(8,128)(2,1)}, bf16[8,64,640]{2,1,0:T(8,128)(2,1)S(1)}, u32[]{:S(2)}, u32[]{:S(2)}) collective-permute-start(bf16[8,64,640]{2,1,0:T(8,128)(2,1)} %get-tuple-element.338.refs_4_), channel_id=1, source_target_pairs={{0,4},{2,6},{4,0},{6,2},{8,12},{10,14},{12,8},{14,10},{16,20},{18,... | collective-permute-start | bytes 1966088 | tf_op jit(solution)/shard_map/ppermute | solution.py:50
  290.1 16.8 %collective-permute-start.38 = (bf16[8,64,384]{2,1,0:T(8,128)(2,1)}, bf16[8,64,384]{2,1,0:T(8,128)(2,1)S(1)}, u32[]{:S(2)}, u32[]{:S(2)}) collective-permute-start(bf16[8,64,384]{2,1,0:T(8,128)(2,1)} %get-tuple-element.337.refs_2_), channel_id=1, source_target_pairs={{0,8},{2,10},{4,12},{6,14},{8,0},{10,2},{12,4},{14,6},{16,24},{18,... | collective-permute-start | bytes 1179656 | tf_op jit(solution)/shard_map/ppermute | solution.py:50
  290.1 14.7 %collective-permute-start.37 = (bf16[8,64,256]{2,1,0:T(8,128)(2,1)}, bf16[8,64,256]{2,1,0:T(8,128)(2,1)S(1)}, u32[]{:S(2)}, u32[]{:S(2)}) collective-permute-start(bf16[8,64,256]{2,1,0:T(8,128)(2,1)} %get-tuple-element.336.refs_0_), channel_id=1, source_target_pairs={{0,16},{2,18},{4,20},{6,22},{8,24},{10,26},{12,28},{14,30},{16,0},... | collective-permute-start | bytes 786440 | tf_op jit(solution)/shard_map/ppermute | solution.py:50
  307.8 32.8 %collective-permute-start.44 = (bf16[8,64,1408]{2,1,0:T(8,128)(2,1)}, bf16[8,64,1408]{2,1,0:T(8,128)(2,1)S(1)}, u32[]{:S(2)}, u32[]{:S(2)}) collective-permute-start(bf16[8,64,1408]{2,1,0:T(8,128)(2,1)} %get-tuple-element.346.refs_4_.refs_6_.refs_8_), channel_id=1, source_target_pairs={{0,4},{2,6},{4,0},{6,2},{8,12},{10,14},{12,8},{14,10},{16,20},{18,... | collective-permute-start | bytes 4325384 | tf_op jit(solution)/shard_map/ppermute | solution.py:50
  308.4 32.5 %collective-permute-start.45 = (bf16[8,64,1408]{2,1,0:T(8,128)(2,1)}, bf16[8,64,1408]{2,1,0:T(8,128)(2,1)S(1)}, u32[]{:S(2)}, u32[]{:S(2)}) collective-permute-start(bf16[8,64,1408]{2,1,0:T(8,128)(2,1)} %get-tuple-element.347.refs_8_.refs_10_), channel_id=1, source_target_pairs={{0,2},{2,0},{4,6},{6,4},{8,10},{10,8},{12,14},{14,12},{16,18},{18,... | collective-permute-start | bytes 4325384 | tf_op jit(solution)/shard_map/ppermute | solution.py:50
  309.4 30.5 %collective-permute-start.42 = (bf16[8,64,640]{2,1,0:T(8,128)(2,1)}, bf16[8,64,640]{2,1,0:T(8,128)(2,1)}, u32[]{:S(2)}, u32[]{:S(2)}) collective-permute-start(bf16[8,64,640]{2,1,0:T(8,128)(2,1)} %get-tuple-element.344.refs_0_.refs_2_), channel_id=1, source_target_pairs={{0,16},{2,18},{4,20},{6,22},{8,24},{10,26},{12,28},{14,30},{16,0},... | collective-permute-start | bytes 1966088 | tf_op jit(solution)/shard_map/ppermute | solution.py:50
  311.0 28.9 %collective-permute-start.43 = (bf16[8,64,640]{2,1,0:T(8,128)(2,1)}, bf16[8,64,640]{2,1,0:T(8,128)(2,1)}, u32[]{:S(2)}, u32[]{:S(2)}) collective-permute-start(bf16[8,64,640]{2,1,0:T(8,128)(2,1)} %get-tuple-element.345.refs_2_.refs_4_), channel_id=1, source_target_pairs={{0,8},{2,10},{4,12},{6,14},{8,0},{10,2},{12,4},{14,6},{16,24},{18,... | collective-permute-start | bytes 1966088 | tf_op jit(solution)/shard_map/ppermute | solution.py:50
  356.3 10.7 %collective-permute-start.47 = (bf16[1,48,1024]{2,1,0:T(8,128)(2,1)S(1)}, bf16[1,48,1024]{2,1,0:T(8,128)(2,1)S(1)}, u32[]{:S(2)}, u32[]{:S(2)}) collective-permute-start(bf16[1,48,1024]{2,1,0:T(8,128)(2,1)S(1)} %get-tuple-element.350.refs_0_), channel_id=1, source_target_pairs={{0,16},{2,18},{4,20},{6,22},{8,24},{10,26},{12,28},{14,30},{16,0},... | collective-permute-start | bytes 294920 | tf_op jit(solution)/shard_map/ppermute | solution.py:50
  357.9 9.2 %collective-permute-start.48 = (bf16[1,48,1024]{2,1,0:T(8,128)(2,1)S(1)}, bf16[1,48,1024]{2,1,0:T(8,128)(2,1)S(1)}, u32[]{:S(2)}, u32[]{:S(2)}) collective-permute-start(bf16[1,48,1024]{2,1,0:T(8,128)(2,1)S(1)} %get-tuple-element.351.refs_2_), channel_id=1, source_target_pairs={{0,8},{2,10},{4,12},{6,14},{8,0},{10,2},{12,4},{14,6},{16,24},{18,... | collective-permute-start | bytes 294920 | tf_op jit(solution)/shard_map/ppermute | solution.py:50
  371.6 10.6 %collective-permute-start.51 = (bf16[2,48,1024]{2,1,0:T(8,128)(2,1)}, bf16[2,48,1024]{2,1,0:T(8,128)(2,1)S(1)}, u32[]{:S(2)}, u32[]{:S(2)}) collective-permute-start(bf16[2,48,1024]{2,1,0:T(8,128)(2,1)} %get-tuple-element.357.refs_2_), channel_id=1, source_target_pairs={{0,16},{2,18},{4,20},{6,22},{8,24},{10,26},{12,28},{14,30},{16,0},... | collective-permute-start | bytes 589832 | tf_op jit(solution)/shard_map/ppermute | solution.py:50
  385.2 10.9 %collective-permute-start.53 = (bf16[4,48,1024]{2,1,0:T(8,128)(2,1)}, bf16[4,48,1024]{2,1,0:T(8,128)(2,1)S(1)}, u32[]{:S(2)}, u32[]{:S(2)}) collective-permute-start(bf16[4,48,1024]{2,1,0:T(8,128)(2,1)} %get-tuple-element.362.refs_0_), channel_id=1, source_target_pairs={{0,8},{2,10},{4,12},{6,14},{8,0},{10,2},{12,4},{14,6},{16,24},{18,... | collective-permute-start | bytes 1179656 | tf_op jit(solution)/shard_map/ppermute | solution.py:50
  385.3 10.9 %collective-permute-start.54 = (bf16[4,48,1024]{2,1,0:T(8,128)(2,1)}, bf16[4,48,1024]{2,1,0:T(8,128)(2,1)S(1)}, u32[]{:S(2)}, u32[]{:S(2)}) collective-permute-start(bf16[4,48,1024]{2,1,0:T(8,128)(2,1)} %get-tuple-element.363.refs_2_), channel_id=1, source_target_pairs={{0,2},{2,0},{4,6},{6,4},{8,10},{10,8},{12,14},{14,12},{16,18},{18,... | collective-permute-start | bytes 1179656 | tf_op jit(solution)/shard_map/ppermute | solution.py:50
  386.6 8.2 %collective-permute-start.55 = (bf16[4,32,1024]{2,1,0:T(8,128)(2,1)}, bf16[4,32,1024]{2,1,0:T(8,128)(2,1)S(1)}, u32[]{:S(2)}, u32[]{:S(2)}) collective-permute-start(bf16[4,32,1024]{2,1,0:T(8,128)(2,1)} %get-tuple-element.364.refs_4_), channel_id=1, source_target_pairs={{0,4},{2,6},{4,0},{6,2},{8,12},{10,14},{12,8},{14,10},{16,20},{18,... | collective-permute-start | bytes 786440 | tf_op jit(solution)/shard_map/ppermute | solution.py:50
  400.6 18.8 %collective-permute-start.56 = (bf16[8,48,1024]{2,1,0:T(8,128)(2,1)}, bf16[8,48,1024]{2,1,0:T(8,128)(2,1)S(1)}, u32[]{:S(2)}, u32[]{:S(2)}) collective-permute-start(bf16[8,48,1024]{2,1,0:T(8,128)(2,1)} %get-tuple-element.368), channel_id=1, source_target_pairs={{0,2},{2,0},{4,6},{6,4},{8,10},{10,8},{12,14},{14,12},{16,18},{18,... | collective-permute-start | bytes 2359304 | tf_op jit(solution)/shard_map/ppermute | solution.py:50
  402.3 18.5 %collective-permute-start.57 = (bf16[8,48,1024]{2,1,0:T(8,128)(2,1)}, bf16[8,48,1024]{2,1,0:T(8,128)(2,1)S(1)}, u32[]{:S(2)}, u32[]{:S(2)}) collective-permute-start(bf16[8,48,1024]{2,1,0:T(8,128)(2,1)} %get-tuple-element.369), channel_id=1, source_target_pairs={{0,4},{2,6},{4,0},{6,2},{8,12},{10,14},{12,8},{14,10},{16,20},{18,... | collective-permute-start | bytes 2359304 | tf_op jit(solution)/shard_map/ppermute | solution.py:50
  403.0 12.7 %collective-permute-start.58 = (bf16[8,32,1024]{2,1,0:T(8,128)(2,1)}, bf16[8,32,1024]{2,1,0:T(8,128)(2,1)S(1)}, u32[]{:S(2)}, u32[]{:S(2)}) collective-permute-start(bf16[8,32,1024]{2,1,0:T(8,128)(2,1)} %get-tuple-element.370), channel_id=1, source_target_pairs={{0,8},{2,10},{4,12},{6,14},{8,0},{10,2},{12,4},{14,6},{16,24},{18,... | collective-permute-start | bytes 1572872 | tf_op jit(solution)/shard_map/ppermute | solution.py:50
  444.1 19.8 %collective-permute-start.59 = (bf16[384,1152]{1,0:T(8,128)(2,1)}, bf16[384,1152]{1,0:T(8,128)(2,1)S(1)}, u32[]{:S(2)}, u32[]{:S(2)}) collective-permute-start(bf16[384,1152]{1,0:T(8,128)(2,1)} %get-tuple-element.380), channel_id=1, source_target_pairs={{0,2},{2,0},{4,6},{6,4},{8,10},{10,8},{12,14},{14,12},{16,18},{18,... | collective-permute-start | bytes 2654216 | tf_op jit(solution)/shard_map/ppermute | solution.py:50
  444.6 19.7 %collective-permute-start.60 = (bf16[384,1152]{1,0:T(8,128)(2,1)}, bf16[384,1152]{1,0:T(8,128)(2,1)S(1)}, u32[]{:S(2)}, u32[]{:S(2)}) collective-permute-start(bf16[384,1152]{1,0:T(8,128)(2,1)} %get-tuple-element.381), channel_id=1, source_target_pairs={{0,4},{2,6},{4,0},{6,2},{8,12},{10,14},{12,8},{14,10},{16,20},{18,... | collective-permute-start | bytes 2654216 | tf_op jit(solution)/shard_map/ppermute | solution.py:50
  445.4 15.6 %collective-permute-start.61 = (bf16[256,1152]{1,0:T(8,128)(2,1)}, bf16[256,1152]{1,0:T(8,128)(2,1)S(1)}, u32[]{:S(2)}, u32[]{:S(2)}) collective-permute-start(bf16[256,1152]{1,0:T(8,128)(2,1)} %get-tuple-element.382), channel_id=1, source_target_pairs={{0,8},{2,10},{4,12},{6,14},{8,0},{10,2},{12,4},{14,6},{16,24},{18,... | collective-permute-start | bytes 1769480 | tf_op jit(solution)/shard_map/ppermute | solution.py:50
  469.7 9.3 %collective-permute-start.62 = (bf16[192,1152]{1,0:T(8,128)(2,1)}, bf16[192,1152]{1,0:T(8,128)(2,1)S(1)}, u32[]{:S(2)}, u32[]{:S(2)}) collective-permute-start(bf16[192,1152]{1,0:T(8,128)(2,1)} %get-tuple-element.386), channel_id=1, source_target_pairs={{0,8},{2,10},{4,12},{6,14},{8,0},{10,2},{12,4},{14,6},{16,24},{18,... | collective-permute-start | bytes 1327112 | tf_op jit(solution)/shard_map/ppermute | solution.py:50
  470.0 9.1 %collective-permute-start.63 = (bf16[192,1152]{1,0:T(8,128)(2,1)}, bf16[192,1152]{1,0:T(8,128)(2,1)S(1)}, u32[]{:S(2)}, u32[]{:S(2)}) collective-permute-start(bf16[192,1152]{1,0:T(8,128)(2,1)} %get-tuple-element.387), channel_id=1, source_target_pairs={{0,2},{2,0},{4,6},{6,4},{8,10},{10,8},{12,14},{14,12},{16,18},{18,... | collective-permute-start | bytes 1327112 | tf_op jit(solution)/shard_map/ppermute | solution.py:50
  483.0 8.2 %collective-permute-start.65 = (bf16[96,1152]{1,0:T(8,128)(2,1)}, bf16[96,1152]{1,0:T(8,128)(2,1)S(1)}, u32[]{:S(2)}, u32[]{:S(2)}) collective-permute-start(bf16[96,1152]{1,0:T(8,128)(2,1)} %get-tuple-element.392), channel_id=1, source_target_pairs={{0,4},{2,6},{4,0},{6,2},{8,12},{10,14},{12,8},{14,10},{16,20},{18,... | collective-permute-start | bytes 663560 | tf_op jit(solution)/shard_map/ppermute | solution.py:50
  483.7 9.4 %collective-permute-start.66 = (bf16[96,1152]{1,0:T(8,128)(2,1)}, bf16[96,1152]{1,0:T(8,128)(2,1)S(1)}, u32[]{:S(2)}, u32[]{:S(2)}) collective-permute-start(bf16[96,1152]{1,0:T(8,128)(2,1)} %get-tuple-element.393), channel_id=1, source_target_pairs={{0,16},{2,18},{4,20},{6,22},{8,24},{10,26},{12,28},{14,30},{16,0},... | collective-permute-start | bytes 663560 | tf_op jit(solution)/shard_map/ppermute | solution.py:50
  496.2 8.9 %collective-permute-start.68 = (bf16[48,1152]{1,0:T(8,128)(2,1)}, bf16[48,1152]{1,0:T(8,128)(2,1)S(1)}, u32[]{:S(2)}, u32[]{:S(2)}) collective-permute-start(bf16[48,1152]{1,0:T(8,128)(2,1)} %get-tuple-element.398), channel_id=1, source_target_pairs={{0,16},{2,18},{4,20},{6,22},{8,24},{10,26},{12,28},{14,30},{16,0},... | collective-permute-start | bytes 331784 | tf_op jit(solution)/shard_map/ppermute | solution.py:50
  496.2 8.9 %collective-permute-start.69 = (bf16[48,1152]{1,0:T(8,128)(2,1)}, bf16[48,1152]{1,0:T(8,128)(2,1)S(1)}, u32[]{:S(2)}, u32[]{:S(2)}) collective-permute-start(bf16[48,1152]{1,0:T(8,128)(2,1)} %get-tuple-element.399), channel_id=1, source_target_pairs={{0,8},{2,10},{4,12},{6,14},{8,0},{10,2},{12,4},{14,6},{16,24},{18,... | collective-permute-start | bytes 331784 | tf_op jit(solution)/shard_map/ppermute | solution.py:50
  605.6 12.7 %collective-permute-start.79 = (f32[2,2,10,512]{3,2,1,0:T(8,128)S(1)}, f32[2,2,10,512]{3,2,1,0:T(8,128)S(1)}, u32[]{:S(2)}, u32[]{:S(2)}) collective-permute-start(f32[2,2,10,512]{3,2,1,0:T(8,128)S(1)} %add_add_fusion.2), channel_id=1, source_target_pairs={{0,16},{2,18},{4,20},{6,22},{8,24},{10,26},{12,28},{14,30},{16,0},... | collective-permute-start | bytes 245768 | tf_op jit(solution)/shard_map/ppermute | solution.py:50
  608.0 10.3 %collective-permute-start.80 = (f32[2,2,10,512]{3,2,1,0:T(8,128)S(1)}, f32[2,2,10,512]{3,2,1,0:T(8,128)S(1)}, u32[]{:S(2)}, u32[]{:S(2)}) collective-permute-start(f32[2,2,10,512]{3,2,1,0:T(8,128)S(1)} %add_add_fusion.2), channel_id=1, source_target_pairs={{0,24},{2,26},{4,28},{6,30},{8,16},{10,18},{12,20},{14,22},{16,8},... | collective-permute-start | bytes 245768 | tf_op jit(solution)/shard_map/ppermute | solution.py:50
  (129 other events, 2095.2 us)

commit v4 on v3

--- a/solution.py
+++ b/solution.py
@@ -4,6 +4,7 @@
 import jax.numpy as jnp
 from jax import lax
 from jax.experimental import pallas as pl
+from jax.experimental.layout import Layout, with_layout_constraint
 from jax.experimental.pallas import tpu as pltpu
 from jax.sharding import PartitionSpec as P
 
@@ -625,6 +626,9 @@
     width = wide - LANES
     count = len(firsts)
     pieces = 1 if last else 2
+    begins = [0]
+    for array in firsts:
+        begins.append(begins[-1] + array.shape[0])
 
     def body(*refs):
         outs = refs[2 * count :]
@@ -640,50 +644,93 @@
                 total = scale_one + scale_two
                 mean = one[:, :width].astype(F32) * (scale_one / total)
                 mean = mean + two[:, :width].astype(F32) * (scale_two / total)
-                out_ref = outs[piece * count + part]
+                if last:
+                    out_ref = outs[0].at[begins[part] : begins[part + 1]]
+                else:
+                    out_ref = outs[piece * count + part]
                 out_ref[:, :width] = mean.astype(B16)
                 out_ref[:, width:] = split_lse(highest + jnp.log(total), rows)
 
     outs = pl.pallas_call(
         body,
         in_specs=[VMEM] * (2 * count),
-        out_specs=[VMEM] * (pieces * count),
-        out_shape=[shape((a.shape[0] // pieces, wide), B16) for a in firsts] * pieces,
+        out_specs=[VMEM] * (1 if last else 2 * count),
+        out_shape=[shape((begins[-1], wide), B16)]
+        if last
+        else [shape((a.shape[0] // 2, wide), B16) for a in firsts] * 2,
         cost_estimate=cost(3),
         name="merge",
     )(*firsts, *seconds)
-    return outs[:count], outs[count:]
-
-
-def head_back(means, head_rows, head_in, rows, skip, counted, final_norm, count_total):
+    return (outs, None) if last else (outs[:count], outs[count:])
+
+
+def head_rows_of(middle, own, other, vectors, core, cuts):
+    scored, width = middle.shape
+    core_rows = scored // 2
+    sizes = [b - a for a, b in zip(cuts[:-1], cuts[1:])]
+
+    def body(core_ref, middle_ref, own_ref, other_ref, vec_ref, rows_ref, in_ref, *parts):
+        both = own_ref[...].astype(F32) + other_ref[...].astype(F32)
+        rows = middle_ref[...] + (both + vec_ref[0:1, :])
+        rows_ref[...] = rows
+        xhat, unused = norm_rows(rows)
+        normed = xhat * vec_ref[1:2, :] + vec_ref[2:3, :]
+        in_ref[...] = normed.astype(B16)
+        mine = jnp.where(core_ref[0] == 0, normed[:core_rows], normed[core_rows:]).astype(B16)
+        for ref, first, last in zip(parts, cuts[:-1], cuts[1:]):
+            ref[...] = mine[first:last]
+
+    outs = pl.pallas_call(
+        body,
+        in_specs=[pl.BlockSpec(memory_space=pltpu.SMEM)] + [VMEM] * 4,
+        out_specs=[VMEM] * (2 + len(sizes)),
+        out_shape=[shape((scored, width), F32), shape((scored, width), B16)]
+        + [shape((size, width), B16) for size in sizes],
+        cost_estimate=cost(3),
+        name="head_rows",
+    )(core, middle, own, other, vectors)
+    return outs[0], outs[1], outs[2:]
+
+
+def head_back(own, other, head_rows, head_in, rows, skip, counted, final_norm, core, count_total):
     scored, width = head_rows.shape
 
-    def body(mean_ref, rows_ref, in_ref, target_ref, counted_ref, norm_ref, grad_ref, loss_ref):
-        lse = joined_lse(mean_ref[...], width)
+    def body(core_ref, own_ref, other_ref, rows_ref, in_ref, target_ref, counted_ref, norm_ref,
+             grad_ref, loss_ref):
+        own_mean, other_mean = own_ref[...].astype(F32), other_ref[...].astype(F32)
+        first = core_ref[0] == 0
+        mean = jnp.concatenate(
+            [jnp.where(first, own_mean, other_mean), jnp.where(first, other_mean, own_mean)], 0
+        )
+        lse = joined_lse(mean, width)
         target = target_ref[...]
         logit = jnp.sum(in_ref[...].astype(F32) * target, -1, keepdims=True)
         seen = counted_ref[...]
-        loss_ref[...] = jnp.broadcast_to((lse - logit) * seen, (BLOCK, LANES))
-        d_head = (mean_ref[:, :width].astype(F32) - target) * (seen / count_total)
+        loss_ref[...] = jnp.broadcast_to((lse - logit) * seen, (scored, LANES))
+        d_head = (mean[:, :width] - target) * (seen / count_total)
         grad_ref[...] = norm_rows_back(d_head, rows_ref[...], norm_ref[0:1, :])
 
     return pl.pallas_call(
         body,
-        grid=(scored // BLOCK,),
-        in_specs=[
-            rows_spec(width + LANES),
-            rows_spec(width),
-            rows_spec(width),
-            pl.BlockSpec((BLOCK, width), lambda i: (i + skip // BLOCK, 0)),
-            rows_spec(1),
-            whole_spec(final_norm.shape),
-        ],
-        out_specs=[rows_spec(width), rows_spec(LANES)],
+        grid_spec=pltpu.PrefetchScalarGridSpec(
+            num_scalar_prefetch=1,
+            grid=(1,),
+            in_specs=[
+                whole_spec(own.shape),
+                whole_spec(other.shape),
+                whole_spec(head_rows.shape),
+                whole_spec(head_in.shape),
+                pl.BlockSpec((scored, width), lambda i, *refs: (skip // scored, 0)),
+                whole_spec(counted.shape),
+                whole_spec(final_norm.shape),
+            ],
+            out_specs=[whole_spec((scored, width)), whole_spec((scored, LANES))],
+        ),
         out_shape=[shape((scored, width), F32), shape((scored, LANES), F32)],
         compiler_params=params(),
         cost_estimate=cost(4),
         name="head_back",
-    )(means, head_rows, head_in, rows, counted, final_norm)
+    )(core, own, other, head_rows, head_in, rows, counted, final_norm)
 
 
 def mlp_back(gradient, slope, me, w_up, w_down, residual=None):
@@ -757,7 +804,7 @@
 
 
 def last_attention_back(gradient, own, other, middle, gain, q, k, v, lse, prefix, layout, picks,
-                        picks_column, me, weight, plen):
+                        me, weight, plen):
     scored, width = gradient.shape
     row_count, half = k.shape
     prefix_rows = prefix.shape[1]
@@ -766,9 +813,9 @@
     stacks = len(weight.operands)
 
     def body(me_ref, layout_ref, picks_ref, grad_ref, own_ref, other_ref, middle_ref, gain_ref,
-             q_ref, k_ref, v_ref, lse_ref, prefix_ref, column_ref, *refs):
+             q_ref, k_ref, v_ref, lse_ref, prefix_ref, picks_row_ref, *refs):
         (part_ref, spread_ref, dprefix_ref, full, sems,
-         dmix_s, dq_s, dk_s, dv_s, sum_s, rows_s) = refs[stacks:]
+         dmix_s, lse_s, dq_s, dkv_s, sum_s, rows_s) = refs[stacks:]
         refs = (me_ref[0], refs[:stacks], full, sems)
         weight.start(*refs)
         incoming = own_ref[...].astype(F32) + other_ref[...].astype(F32)
@@ -783,9 +830,11 @@
         lax.fori_loop(0, scored, put, 0, unroll=8)
         weight.wait(*refs)
         dmix_s[...] = dot_nn(grad_mid.astype(B16), full[:, 3 * half :]).astype(B16)
-        bias = key_bias(layout_ref, column_ref[...], row_count)
-        bias_prefix = prefix_bias(scored, prefix_rows, plen)
-        lane = lax.broadcasted_iota(jnp.int32, (scored, LANES), 1)
+        bias = jnp.transpose(key_bias(layout_ref, jnp.transpose(picks_row_ref[...]), row_count))
+        bias_prefix = jnp.where(
+            lax.broadcasted_iota(jnp.int32, (prefix_rows, scored), 0) < plen, 0.0, NEG_BIG
+        )
+        lse_s[...] = jnp.transpose(lse_ref[...])
 
         def pair(index, carry):
             columns = pl.ds(pl.multiple_of(index * LANES, LANES), LANES)
@@ -795,41 +844,34 @@
             found = [[], [], [], [], []]
             for side in range(2):
                 cut = slice(side * HEAD_DIM, (side + 1) * HEAD_DIM)
-                log_total = jnp.sum(
-                    jnp.where(lane == prefix_rows * (2 * index + side), lse_ref[...], 0.0),
-                    -1,
-                    keepdims=True,
-                )
-                qh, dh = query[:, cut], d_mixed[:, cut]
-                shares = jnp.exp(dot_nt(qh, key[:, cut]) + bias - log_total)
-                shares_p = jnp.exp(dot_nt(qh, key_p[:, cut]) + bias_prefix - log_total)
-                d_shares = dot_nt(dh, value[:, cut]).astype(B16).astype(F32)
-                d_shares_p = dot_nt(dh, value_p[:, cut]).astype(B16).astype(F32)
-                inner = jnp.sum(shares * d_shares, -1, keepdims=True) + jnp.sum(
-                    shares_p * d_shares_p, -1, keepdims=True
+                place = pl.multiple_of(prefix_rows * (2 * index + side), prefix_rows)
+                log_total = lse_s[pl.ds(place, 1), :]
+                qh, dh, kh, kp = query[:, cut], d_mixed[:, cut], key[:, cut], key_p[:, cut]
+                shares = jnp.exp(dot_nt(kh, qh) + bias - log_total)
+                shares_p = jnp.exp(dot_nt(kp, qh) + bias_prefix - log_total)
+                d_shares = dot_nt(value[:, cut], dh).astype(B16).astype(F32)
+                d_shares_p = dot_nt(value_p[:, cut], dh).astype(B16).astype(F32)
+                inner = jnp.sum(shares * d_shares, 0, keepdims=True) + jnp.sum(
+                    shares_p * d_shares_p, 0, keepdims=True
                 )
                 d_scores = (shares * (d_shares - inner)).astype(B16)
                 d_scores_p = (shares_p * (d_shares_p - inner)).astype(B16)
-                found[0].append(
-                    (dot_nn(d_scores, key[:, cut]) + dot_nn(d_scores_p, key_p[:, cut])) * scale
-                )
-                found[1].append(dot_tn(d_scores, qh))
-                found[2].append(dot_tn(shares.astype(B16), dh))
-                found[3].append(dot_tn(d_scores_p, qh))
-                found[4].append(dot_tn(shares_p.astype(B16), dh))
-            joined = [jnp.concatenate(f, 1) for f in found]
-            dq_s[:, columns] = joined[0].astype(B16)
-            dk_s[:, columns] = joined[1].astype(B16)
-            dv_s[:, columns] = joined[2].astype(B16)
-            dprefix_ref[0, :, columns] = joined[3]
-            dprefix_ref[1, :, columns] = joined[4]
+                found[0].append((dot_tn(kh, d_scores) + dot_tn(kp, d_scores_p)) * scale)
+                found[1].append(dot_nn(d_scores, qh))
+                found[2].append(dot_nn(shares.astype(B16), dh))
+                found[3].append(dot_nn(d_scores_p, qh))
+                found[4].append(dot_nn(shares_p.astype(B16), dh))
+            dq_s[columns, :] = jnp.concatenate(found[0], 0)
+            joined = [jnp.concatenate(f, 1) for f in found[1:]]
+            dkv_s[:, columns] = joined[0].astype(B16)
+            dkv_s[:, pl.ds(pl.multiple_of(half + index * LANES, LANES), LANES)] = joined[1].astype(B16)
+            dprefix_ref[0, :, columns] = joined[2]
+            dprefix_ref[1, :, columns] = joined[3]
             return carry
 
         lax.fori_loop(0, half // LANES, pair, 0)
-        sum_s[...] = dot_nt(dk_s[...], full[:, half : 2 * half]) + dot_nt(
-            dv_s[...], full[:, 2 * half : 3 * half]
-        )
-        rows_s[...] = dot_nt(dq_s[...], full[:, :half])
+        sum_s[...] = dot_nt(dkv_s[...], full[:, half : 3 * half])
+        rows_s[...] = dot_nt(jnp.transpose(dq_s[...]).astype(B16), full[:, :half])
 
         def add(index, carry):
             place = pl.ds(picks_ref[index], 1)
@@ -839,7 +881,7 @@
         lax.fori_loop(0, scored, add, 0, unroll=8)
         part_ref[...] = sum_s[...].astype(B16)
 
-    inputs = [gradient, own, other, middle, gain, q, k, v, lse, prefix, picks_column]
+    inputs = [gradient, own, other, middle, gain, q, k, v, lse, prefix, picks.reshape(1, scored)]
     return pl.pallas_call(
         body,
         grid_spec=pltpu.PrefetchScalarGridSpec(
@@ -854,9 +896,9 @@
             scratch_shapes=weight.scratch
             + [
                 pltpu.VMEM((scored, half), B16),
-                pltpu.VMEM((scored, half), B16),
-                pltpu.VMEM((row_count, half), B16),
-                pltpu.VMEM((row_count, half), B16),
+                pltpu.VMEM((LANES, scored), F32),
+                pltpu.VMEM((half, scored), F32),
+                pltpu.VMEM((row_count, 2 * half), B16),
                 pltpu.VMEM((row_count, width), F32),
                 pltpu.VMEM((scored, width), F32),
             ],
@@ -1228,18 +1270,20 @@
         me,
         *mlp_weights(1),
     )
-    both = part_two.astype(F32) + partner(part_two).astype(F32)
-    head_rows = middle1 + (both + vec_last[8])
-    center = head_rows - jnp.mean(head_rows, -1, keepdims=True)
-    spread = jnp.mean(center * center, -1, keepdims=True)
-    head_in = (center * lax.rsqrt(spread + EPS_NORM) * final_norm[0] + final_norm[1]).astype(B16)
-
-    core_rows = scored // 2
-    mine = lax.dynamic_slice_in_dim(head_in, own_index * core_rows, core_rows, 0)
-    cuts_head = (0, 48, 96, core_rows)
+    core = own_index.astype(jnp.int32).reshape(1)
+    cuts_head = (0, 48, 96, scored // 2)
+    head_rows, head_in, mine = head_rows_of(
+        middle1,
+        part_two,
+        partner(part_two),
+        jnp.stack([vec_last[8], final_norm[0], final_norm[1]]),
+        core,
+        cuts_head,
+    )
+
     head_order = bit_orders(size, 3)
     head = Rounds()
-    head.add(0, head_order, [mine[a:b] for a, b in zip(cuts_head[:-1], cuts_head[1:])])
+    head.add(0, head_order, mine)
     for stage in range(stages):
         head.step(0, stage)
     near, far = [
@@ -1253,13 +1297,8 @@
     for stage in reversed(range(stages)):
         got = [flip(array, head_order[p][stage]) for p, array in enumerate(send)]
         keep, send = merge(keep, got, stage == 0)
-    own_means = jnp.concatenate(keep, 0)
+    (own_means,) = keep
     other_means = partner(own_means)
-    means = jnp.where(
-        own_index == 0,
-        jnp.concatenate([own_means, other_means], 0),
-        jnp.concatenate([other_means, own_means], 0),
-    )
     place = loss_pos % bucket_width
     slot = loss_pos // bucket_width
     lengths = jnp.sum(
@@ -1273,7 +1312,16 @@
     counted = (place < lengths).astype(F32).reshape(scored, 1)
     count_total = float(scored * size)
     grad_rows, loss_terms = head_back(
-        means, head_rows, head_in, stream, row_count, counted, final_norm, count_total
+        own_means,
+        other_means,
+        head_rows,
+        head_in,
+        stream,
+        row_count,
+        counted,
+        final_norm,
+        core,
+        count_total,
     )
     loss_part = jnp.sum(loss_terms[:, 0])
 
@@ -1291,7 +1339,6 @@
         prefix_kv[1],
         layout,
         loss_pos,
-        picks_column,
         me,
         attention_weight(1),
         plen,
@@ -1352,6 +1399,7 @@
     ibias_out = adamw_update(
         inner_bias, moment_inner_bias, square_inner_bias, factor * d_inner_bias, corr_one, corr_two
     )
+    d_outer = with_layout_constraint(d_outer, Layout(major_to_minor=(0, 1, 2, 3)))
     outer_out = adamw_update(
         outer_weight, moment_outer, square_outer, factor * d_outer, corr_one, corr_two
     )

time: 661 us -> 658 us (level)
    pallas_call x5 -> x6, Pallas kernels: 15.7 us -> 18.8 us  [the longest x4 12 us: merge(): pl.pallas_call(body, in_specs=[VMEM] * (2 * count), out_specs=[VMEM] * (1...]
    unnamed x212 -> x202, local copies, waits for them, and re-layouts: 26.5 us -> 24.5 us
where the time goes in v4:
time: 658 us; the launch traced here: 651 us
  Pallas kernels  247 us (38%)
  waiting for transfers between devices  205 us (31%)
  starting transfers between devices  104 us (16%)
  local copies, waits for them, and re-layouts  38.1 us (6%)
  other arithmetic  25.5 us (4%)
  matrix products  18.4 us (3%)
  between operations  13.6 us (2%)
    ppermute x75, waiting for transfers between devices, flip(): return lax.ppermute(array, 'dev', [(i, i ^ bit) for i in range(size)])  190 us
    ppermute x75, starting transfers between devices, flip(): return lax.ppermute(array, 'dev', [(i, i ^ bit) for i in range(size)])  92.9 us
    pallas_call x3, Pallas kernels, vocabulary(): pl.pallas_call(body, in_specs=[VMEM] * (len(stacks) + 1), out_specs=[VMEM...  47.6 us
    pallas_call x11, Pallas kernels, pack(): pl.pallas_call(body, in_specs=[pl.BlockSpec(memory_space=pl.ANY)] * len(a...  34.3 us
    pallas_call x2, Pallas kernels, mlp(): pl.pallas_call(body, grid_spec=pltpu.PrefetchScalarGridSpec(num_scalar_pr...  31.7 us
    pallas_call x1, Pallas kernels, first_attention(): pl.pallas_call(body, grid_spec=pltpu.PrefetchScalarGridSpec(num_scalar_pr...  31.3 us
    pallas_call x2, Pallas kernels, mlp_back(): pl.pallas_call(body, grid_spec=pltpu.PrefetchScalarGridSpec(num_scalar_pr...  27.3 us
    unnamed x202, local copies, waits for them, and re-layouts  24.5 us
  transfers between devices with their start and end apart: 89, of which 51 were waited for; matrix products, arithmetic and copies ran while one was open for 6% of the time, Pallas kernels for 18%

profile of v4, /device:TPU:0, one launch (start us, length us, event | category | flops | bytes accessed | tf_op | source)
XLA Modules:
  0.0 651.4 jit_solution(12357324331543507833)
XLA Ops:
  4.7 3.0 collective-permute-start.1
  7.7 2.6 collective-permute-start.5
  21.4 4.9 all-to-all-start.2
  26.4 7.0 %collective-permute-done.3.refs_1_ = bf16[1,64,1920]{2,1,0:T(8,128)(2,1)S(1)} collective-permute-done((bf16[1,64,1920]{2,1,0:T(8,128)(2,1)S(1)}, bf16[1,64,1920]{2,1,0:T(8,128)(2,1)S(1)}, u32[]{:S(2)}, u32[]{:S(2)}) %collective-permute-start.3) | collective-permute-done | bytes 245792 | tf_op jit(solution)/shard_map/ppermute | solution.py:51
  34.8 2.6 pack.11
  39.6 4.1 collective-permute-start.6
  43.8 6.2 fusion.18
  52.2 10.6 %collective-permute-done.8.refs_3_ = bf16[2,64,2048]{2,1,0:T(8,128)(2,1)S(1)} collective-permute-done((bf16[2,64,2048]{2,1,0:T(8,128)(2,1)}, bf16[2,64,2048]{2,1,0:T(8,128)(2,1)S(1)}, u32[]{:S(2)}, u32[]{:S(2)}) %collective-permute-start.8) | collective-permute-done | bytes 524320 | tf_op jit(solution)/shard_map/ppermute | solution.py:51
  64.5 3.5 pack.12
  68.0 4.8 all-to-all-start.3
  77.9 2.4 collective-permute-start.10
  80.4 41.9 %collective-permute-done.10 = f32[2,2,10,512]{3,2,1,0:T(8,128)S(1)} collective-permute-done((f32[2,2,10,512]{3,2,1,0:T(8,128)S(1)}, f32[2,2,10,512]{3,2,1,0:T(8,128)S(1)}, u32[]{:S(2)}, u32[]{:S(2)}) %collective-permute-start.10) | collective-permute-done | bytes 81952 | tf_op jit(solution)/shard_map/ppermute | solution.py:51
  124.5 3.0 pack.13
  132.2 4.3 pack.14
  139.3 2.4 collective-permute-start.18
  147.2 9.3 %convert_add_fusion = f32[1280,1024]{1,0:T(8,128)} fusion(s32[1280]{0:T(1024)S(1)} %add_select_fusion.5, bf16[768,1024]{1,0:T(8,128)(2,1)} %collective-permute-done.14, bf16[768,1024]{1,0:T(8,128)(2,1)} %bitcast.31, bf16[1024,1024]{1,0:T(8,128)(2,1)} %bitcast_select_fusion), kind=kOutput, calls=%fused_computation.22 | convolution fusion | flops 4037410816 | bytes 10490880 | tf_op jit(solution)/shard_map/dot_general | solution.py:1049
  166.2 31.3 %first_attention.1 = (bf16[1024,1024]{1,0:T(8,128)(2,1)}, bf16[1024,512]{1,0:T(8,128)(2,1)}, bf16[1024,512]{1,0:T(8,128)(2,1)}, f32[1024,128]{1,0:T(8,128)}) custom-call(s32[1]{0:T(128)} %bitcast.4.me_ref, s32[6]{0:T(128)} %pad_add_fusion.layout_ref, f32[1280,1024]{1,0:T(8,128)} %get-tuple-element.290.stream_ref.base_ref.target_ref, f32[2,1024]{1,0:T(2,128)} %bitcast.174, ...), custom_call_target="tpu_custom_call" | custom-call | flops 34500001792 | bytes 1024 | tf_op jit(solution)/shard_map/first_attention/pallas_call | solution.py:348
  202.8 5.4 collective-permute-done.23.refs_1_
  208.1 3.7 collective-permute-done.25.refs_5_
  212.5 2.7 collective-permute-done.26.refs_7_
  215.9 2.7 pack.15
  222.6 22.2 %mlp.2 = (bf16[1024,1024]{1,0:T(8,128)(2,1)}, f32[1024,1024]{1,0:T(8,128)}, bf16[1024,2048]{1,0:T(8,128)(2,1)}) custom-call(s32[1]{0:T(128)} %bitcast.4.me_ref, f32[1280,1024]{1,0:T(8,128)} %get-tuple-element.290.stream_ref.base_ref.target_ref, bf16[1024,1024]{1,0:T(8,128)(2,1)} %get-tuple-element.309.own_ref, bf16[1024,1024]{1,0:T(8,128)(2,1)} %copy-done.47, ...), custom_call_target="tpu_custom_call" | custom-call | flops 26449999872 | bytes 1024 | tf_op jit(solution)/shard_map/mlp/pallas_call | solution.py:425
  246.5 3.7 pack.16
  254.6 2.3 pad.13
  256.9 17.3 %collective-permute-done.32.refs_1_ = bf16[4,64,896]{2,1,0:T(8,128)(2,1)} collective-permute-done((bf16[4,64,896]{2,1,0:T(8,128)(2,1)}, bf16[4,64,896]{2,1,0:T(8,128)(2,1)}, u32[]{:S(2)}, u32[]{:S(2)}) %collective-permute-start.32) | collective-permute-done | bytes 458784 | tf_op jit(solution)/shard_map/ppermute | solution.py:51
  274.2 3.8 collective-permute-done.33.refs_3_
  277.9 3.0 pack.17
  284.2 4.3 pack.18
  290.1 2.6 collective-permute-start.37
  292.7 5.4 pad_maximum_fusion.refs_1_.refs_2_.refs_3_
  298.1 6.6 %collective-permute-done.37.refs_1_ = bf16[8,64,256]{2,1,0:T(8,128)(2,1)S(1)} collective-permute-done((bf16[8,64,256]{2,1,0:T(8,128)(2,1)}, bf16[8,64,256]{2,1,0:T(8,128)(2,1)S(1)}, u32[]{:S(2)}, u32[]{:S(2)}) %collective-permute-start.37) | collective-permute-done | bytes 262176 | tf_op jit(solution)/shard_map/ppermute | solution.py:51
  312.0 20.6 %last_attention.1 = (f32[1024,1024]{1,0:T(8,128)}, bf16[256,1024]{1,0:T(8,128)(2,1)}, bf16[1024,512]{1,0:T(8,128)(2,1)}, bf16[1024,512]{1,0:T(8,128)(2,1)}, bf16...) custom-call(s32[1]{0:T(128)} %bitcast.4.me_ref, ...), custom_call_target="tpu_custom_call" | custom-call | flops 25300000768 | bytes 1024 | tf_op jit(solution)/shard_map/last_attention/pallas_call | solution.py:510
  334.8 5.1 collective-permute-done.42.refs_1_.refs_3_
  342.3 9.5 %mlp.3 = (bf16[256,1024]{1,0:T(8,128)(2,1)}, f32[256,1024]{1,0:T(8,128)}, bf16[256,2048]{1,0:T(8,128)(2,1)}) custom-call(s32[1]{0:T(128)} %bitcast.4.me_ref, f32[256,1024]{1,0:T(8,128)} %get-tuple-element.344.base_ref, bf16[256,1024]{1,0:T(8,128)(2,1)} %get-tuple-element.345.own_ref, bf16[256,1024]{1,0:T(8,128)(2,1)} %copy-done.66, ...), custom_call_target="tpu_custom_call" | custom-call | flops 5750000128 | bytes 1024 | tf_op jit(solution)/shard_map/mlp/pallas_call | solution.py:425
  354.8 3.0 head_rows.1
  361.9 6.8 %collective-permute-done.49.refs_5_ = bf16[1,32,1024]{2,1,0:T(8,128)(2,1)S(1)} collective-permute-done((bf16[1,32,1024]{2,1,0:T(8,128)(2,1)}, bf16[1,32,1024]{2,1,0:T(8,128)(2,1)S(1)}, u32[]{:S(2)}, u32[]{:S(2)}) %collective-permute-start.49) | collective-permute-done | bytes 65568 | tf_op jit(solution)/shard_map/ppermute | solution.py:51
  374.5 4.0 collective-permute-done.52.refs_5_
  378.6 5.2 collective-permute-done.51.refs_3_
  384.4 2.4 pack.20
  388.9 7.4 %collective-permute-done.55.refs_5_ = bf16[4,32,1024]{2,1,0:T(8,128)(2,1)S(1)} collective-permute-done((bf16[4,32,1024]{2,1,0:T(8,128)(2,1)}, bf16[4,32,1024]{2,1,0:T(8,128)(2,1)S(1)}, u32[]{:S(2)}, u32[]{:S(2)}) %collective-permute-start.55) | collective-permute-done | bytes 262176 | tf_op jit(solution)/shard_map/ppermute | solution.py:51
  399.2 2.9 pack.21
  405.5 10.3 %vocabulary.3.refs_0_ = bf16[384,1152]{1,0:T(8,128)(2,1)} custom-call(bf16[384,1024]{1,0:T(8,128)(2,1)} %bitcast.181, bf16[3200,1024]{1,0:T(8,128)(2,1)} %pad_maximum_fusion.refs_1_.refs_2_.refs_3_), custom_call_target="tpu_custom_call" | custom-call | flops 11500000256 | bytes 1024 | tf_op jit(solution)/shard_map/vocabulary/pallas_call | solution.py:606
  417.2 3.7 collective-permute-done.56
  423.3 22.1 %vocabulary.5 = (bf16[384,1152]{1,0:T(8,128)(2,1)}, bf16[384,1152]{1,0:T(8,128)(2,1)}, bf16[256,1152]{1,0:T(8,128)(2,1)}) custom-call(bf16[384,1024]{1,0:T(8,128)(2,1)} %bitcast.182, bf16[384,1024]{1,0:T(8,128)(2,1)} %bitcast.183, bf16[256,1024]{1,0:T(8,128)(2,1)} %bitcast.185, bf16[3200,1024]{1,0:T(8,128)(2,1)} %pad_maximum_fusion.refs_1_.refs_2_.refs_3_), custom_call_target="tpu_custom_call" | custom-call | flops 29899999232 | bytes 1024 | tf_op jit(solution)/shard_map/vocabulary/pallas_call | solution.py:606
  447.3 15.2 %vocabulary.4 = (bf16[384,1152]{1,0:T(8,128)(2,1)}, bf16[256,1152]{1,0:T(8,128)(2,1)}) custom-call(bf16[384,1024]{1,0:T(8,128)(2,1)} %bitcast.180, bf16[256,1024]{1,0:T(8,128)(2,1)} %bitcast.184, bf16[3200,1024]{1,0:T(8,128)(2,1)} %pad_maximum_fusion.refs_1_.refs_2_.refs_3_), custom_call_target="tpu_custom_call" | custom-call | flops 18400000000 | bytes 1024 | tf_op jit(solution)/shard_map/vocabulary/pallas_call | solution.py:606
  462.5 2.6 collective-permute-done.59.refs_3_
  466.6 4.4 merge.4
  473.3 6.2 collective-permute-done.64.refs_5_
  481.3 3.0 merge.5
  488.2 4.4 collective-permute-done.67.refs_5_
  495.3 2.4 merge.6
  497.6 2.5 collective-permute-start.69
  500.7 5.7 collective-permute-done.70.refs_5_
  511.8 3.9 head_back.1
  515.7 8.2 %mlp_back.2.own_ref = bf16[256,1024]{1,0:T(8,128)(2,1)} custom-call(s32[1]{0:T(128)} %bitcast.4.me_ref, f32[256,1024]{1,0:T(8,128)} %get-tuple-element.408.refs_0_.grad_ref, bf16[256,2048]{1,0:T(8,128)(2,1)} %get-tuple-element.409.refs_1_, bf16[8,64,640]{2,1,0:T(8,128)(2,1)} %get-tuple-element.346.refs_0_.refs_2_, ...), custom_call_target="tpu_custom_call" | custom-call | flops 5750000128 | bytes 1024 | tf_op jit(solution)/shard_map/mlp_back/pallas_call | solution.py:789
  526.9 23.6 %last_attention_back.1 = (bf16[1024,1024]{1,0:T(8,128)(2,1)}, f32[1024,1024]{1,0:T(8,128)}, f32[2,16,512]{2,1,0:T(8,128)}) custom-call(s32[1]{0:T(128)} %bitcast.4.me_ref, s32[6]{0:T(128)} %pad_add_fusion.layout_ref, s32[256]{0:T(256)} %picks_ref.3, f32[256,1024]{1,0:T(8,128)} %get-tuple-element.408.refs_0_.grad_ref, bf16[256,1024]{1,0:T(8,128)(2,1)} %mlp_back.2.own_ref, ...), custom_call_target="tpu_custom_call" | custom-call | flops 27599998976 | bytes 1024 | tf_op jit(solution)/shard_map/last_attention_back/pallas_call | solution.py:885
  550.7 4.2 collective-permute-done.73.refs_5_
  556.3 19.1 %mlp_back.3 = (bf16[1024,1024]{1,0:T(8,128)(2,1)}, f32[1024,1024]{1,0:T(8,128)}) custom-call(s32[1]{0:T(128)} %bitcast.4.me_ref, f32[1024,1024]{1,0:T(8,128)} %get-tuple-element.414.refs_0_, bf16[1024,2048]{1,0:T(8,128)(2,1)} %get-tuple-element.415.refs_1_, f32[1024,1024]{1,0:T(8,128)} %get-tuple-element.416.refs_2_, f32[1,1024]{1,0:T(1,128)} %copy-done.31, ...), custom_call_target="tpu_custom_call" | custom-call | flops 23000000512 | bytes 1024 | tf_op jit(solution)/shard_map/mlp_back/pallas_call | solution.py:789
  575.6 4.2 collective-permute-done.74.other_ref
  581.3 11.6 %first_prefix_back.1 = f32[2,16,512]{2,1,0:T(8,128)} custom-call(s32[1]{0:T(128)} %bitcast.4.me_ref, f32[1024,1024]{1,0:T(8,128)} %get-tuple-element.418.grad_ref, bf16[1024,1024]{1,0:T(8,128)(2,1)} %get-tuple-element.419.own_ref, bf16[1024,1024]{1,0:T(8,128)(2,1)} %copy-done.49, f32[1024,1024]{1,0:T(8,128)} %get-tuple-element.311.base_ref.middle_ref, ...), custom_call_target="tpu_custom_call" | custom-call | flops 12650000384 | bytes 1024 | tf_op jit(solution)/shard_map/first_prefix_back/pallas_call | solution.py:975
  597.6 2.9 collective-permute-done.75
  604.1 2.3 collective-permute-start.79
  610.5 6.3 collective-permute-done.79
  637.4 2.4 collective-permute-done.86
  (431 shorter events, 170.1 us)
Async XLA Ops:
  4.7 11.7 %collective-permute-start.1 = (f32[2,2,10,512]{3,2,1,0:T(8,128)S(1)}, f32[2,2,10,512]{3,2,1,0:T(8,128)S(1)}, u32[]{:S(2)}, u32[]{:S(2)}) collective-permute-start(f32[2,2,10,512]{3,2,1,0:T(8,128)S(1)} %convolution_bitcast_fusion), channel_id=1, source_target_pairs={{0,2},{2,0},{4,6},{6,4},{8,10},{10,8},{12,14},{14,12},{16,18},{18,... | collective-permute-start | bytes 245768 | tf_op jit(solution)/shard_map/ppermute | solution.py:51
  7.7 25.7 %collective-permute-start.5 = (bf16[1,64,2176]{2,1,0:T(8,128)(2,1)S(1)}, bf16[1,64,2176]{2,1,0:T(8,128)(2,1)S(1)}, u32[]{:S(2)}, u32[]{:S(2)}) collective-permute-start(bf16[1,64,2176]{2,1,0:T(8,128)(2,1)S(1)} %fusion.28.refs_4_), channel_id=1, source_target_pairs={{0,16},{2,18},{4,20},{6,22},{8,24},{10,26},{12,28},{14,30},{16,0},... | collective-permute-start | bytes 835592 | tf_op jit(solution)/shard_map/ppermute | solution.py:51
  10.3 23.1 %collective-permute-start.4 = (bf16[1,64,2048]{2,1,0:T(8,128)(2,1)S(1)}, bf16[1,64,2048]{2,1,0:T(8,128)(2,1)S(1)}, u32[]{:S(2)}, u32[]{:S(2)}) collective-permute-start(bf16[1,64,2048]{2,1,0:T(8,128)(2,1)S(1)} %fusion.32.refs_2_), channel_id=1, source_target_pairs={{0,8},{2,10},{4,12},{6,14},{8,0},{10,2},{12,4},{14,6},{16,24},{18,... | collective-permute-start | bytes 786440 | tf_op jit(solution)/shard_map/ppermute | solution.py:51
  11.9 21.5 %collective-permute-start.3 = (bf16[1,64,1920]{2,1,0:T(8,128)(2,1)S(1)}, bf16[1,64,1920]{2,1,0:T(8,128)(2,1)S(1)}, u32[]{:S(2)}, u32[]{:S(2)}) collective-permute-start(bf16[1,64,1920]{2,1,0:T(8,128)(2,1)S(1)} %fusion.43.refs_0_), channel_id=1, source_target_pairs={{0,16},{2,18},{4,20},{6,22},{8,24},{10,26},{12,28},{14,30},{16,0},... | collective-permute-start | bytes 737288 | tf_op jit(solution)/shard_map/ppermute | solution.py:51
  21.4 16.1 %all-to-all-start.2 = ((s32[16,1,49]{2,1,0:T(1,128)}), s32[16,1,49]{2,1,0:T(1,128)S(1)}, u32[]{:S(2)}, u32[]{:S(2)}) async-start(s32[16,1,49]{2,1,0:T(1,128)} %bitcast.21), calls=%async_computation.2 | async-start | bytes 16384 | tf_op jit(solution)/shard_map/all_to_all | solution.py:1033
  37.5 25.3 %collective-permute-start.9 = (bf16[2,64,2176]{2,1,0:T(8,128)(2,1)}, bf16[2,64,2176]{2,1,0:T(8,128)(2,1)S(1)}, u32[]{:S(2)}, u32[]{:S(2)}) collective-permute-start(bf16[2,64,2176]{2,1,0:T(8,128)(2,1)} %get-tuple-element.263.refs_4_), channel_id=1, source_target_pairs={{0,2},{2,0},{4,6},{6,4},{8,10},{10,8},{12,14},{14,12},{16,18},{18,... | collective-permute-start | bytes 1671176 | tf_op jit(solution)/shard_map/ppermute | solution.py:51
  38.1 24.8 %collective-permute-start.8 = (bf16[2,64,2048]{2,1,0:T(8,128)(2,1)}, bf16[2,64,2048]{2,1,0:T(8,128)(2,1)S(1)}, u32[]{:S(2)}, u32[]{:S(2)}) collective-permute-start(bf16[2,64,2048]{2,1,0:T(8,128)(2,1)} %get-tuple-element.262.refs_2_), channel_id=1, source_target_pairs={{0,16},{2,18},{4,20},{6,22},{8,24},{10,26},{12,28},{14,30},{16,0},... | collective-permute-start | bytes 1572872 | tf_op jit(solution)/shard_map/ppermute | solution.py:51
  38.3 13.9 %collective-permute-start.7 = (bf16[2,64,1920]{2,1,0:T(8,128)(2,1)}, bf16[2,64,1920]{2,1,0:T(8,128)(2,1)S(1)}, u32[]{:S(2)}, u32[]{:S(2)}) collective-permute-start(bf16[2,64,1920]{2,1,0:T(8,128)(2,1)} %get-tuple-element.261.refs_0_), channel_id=1, source_target_pairs={{0,4},{2,6},{4,0},{6,2},{8,12},{10,14},{12,8},{14,10},{16,20},{18,... | collective-permute-start | bytes 1474568 | tf_op jit(solution)/shard_map/ppermute | solution.py:51
  39.6 12.5 %collective-permute-start.6 = (f32[2,2,10,512]{3,2,1,0:T(8,128)S(1)}, f32[2,2,10,512]{3,2,1,0:T(8,128)S(1)}, u32[]{:S(2)}, u32[]{:S(2)}) collective-permute-start(f32[2,2,10,512]{3,2,1,0:T(8,128)S(1)} %add.295), channel_id=1, source_target_pairs={{0,8},{2,10},{4,12},{6,14},{8,0},{10,2},{12,4},{14,6},{16,24},{18,... | collective-permute-start | bytes 245768 | tf_op jit(solution)/shard_map/ppermute | solution.py:51
  68.0 59.5 %all-to-all-start.3 = ((bf16[16,48,1024]{2,1,0:T(8,128)(2,1)}), bf16[16,48,1024]{2,1,0:T(8,128)(2,1)}, u32[]{:S(2)}, u32[]{:S(2)}) async-start(bf16[16,48,1024]{2,1,0:T(8,128)(2,1)} %bitcast.26), calls=%async_computation.3 | async-start | bytes 3145728 | tf_op jit(solution)/shard_map/all_to_all | solution.py:1042
  72.8 51.7 %collective-permute-start.13 = (bf16[4,64,2176]{2,1,0:T(8,128)(2,1)}, bf16[4,64,2176]{2,1,0:T(8,128)(2,1)}, u32[]{:S(2)}, u32[]{:S(2)}) collective-permute-start(bf16[4,64,2176]{2,1,0:T(8,128)(2,1)} %get-tuple-element.276.refs_4_), channel_id=1, source_target_pairs={{0,4},{2,6},{4,0},{6,2},{8,12},{10,14},{12,8},{14,10},{16,20},{18,... | collective-permute-start | bytes 3342344 | tf_op jit(solution)/shard_map/ppermute | solution.py:51
  74.9 49.6 %collective-permute-start.12 = (bf16[4,64,2048]{2,1,0:T(8,128)(2,1)}, bf16[4,64,2048]{2,1,0:T(8,128)(2,1)}, u32[]{:S(2)}, u32[]{:S(2)}) collective-permute-start(bf16[4,64,2048]{2,1,0:T(8,128)(2,1)} %get-tuple-element.275.refs_2_), channel_id=1, source_target_pairs={{0,2},{2,0},{4,6},{6,4},{8,10},{10,8},{12,14},{14,12},{16,18},{18,... | collective-permute-start | bytes 3145736 | tf_op jit(solution)/shard_map/ppermute | solution.py:51
  76.3 48.1 %collective-permute-start.11 = (bf16[4,64,1920]{2,1,0:T(8,128)(2,1)}, bf16[4,64,1920]{2,1,0:T(8,128)(2,1)}, u32[]{:S(2)}, u32[]{:S(2)}) collective-permute-start(bf16[4,64,1920]{2,1,0:T(8,128)(2,1)} %get-tuple-element.274.refs_0_), channel_id=1, source_target_pairs={{0,8},{2,10},{4,12},{6,14},{8,0},{10,2},{12,4},{14,6},{16,24},{18,... | collective-permute-start | bytes 2949128 | tf_op jit(solution)/shard_map/ppermute | solution.py:51
  77.9 44.5 %collective-permute-start.10 = (f32[2,2,10,512]{3,2,1,0:T(8,128)S(1)}, f32[2,2,10,512]{3,2,1,0:T(8,128)S(1)}, u32[]{:S(2)}, u32[]{:S(2)}) collective-permute-start(f32[2,2,10,512]{3,2,1,0:T(8,128)S(1)} %add.296), channel_id=1, source_target_pairs={{0,16},{2,18},{4,20},{6,22},{8,24},{10,26},{12,28},{14,30},{16,0},... | collective-permute-start | bytes 245768 | tf_op jit(solution)/shard_map/ppermute | solution.py:51
  127.5 19.8 %collective-permute-start.14 = (bf16[768,1024]{1,0:T(8,128)(2,1)}, bf16[768,1024]{1,0:T(8,128)(2,1)}, u32[]{:S(2)}, u32[]{:S(2)}) collective-permute-start(bf16[768,1024]{1,0:T(8,128)(2,1)} %bitcast.31), channel_id=1, source_target_pairs={{0,1},{1,0},{2,3},{3,2},{4,5},{5,4},{6,7},{7,6},{8,9},{9,8},{10,11... | collective-permute-start | bytes 4718600 | tf_op jit(solution)/shard_map/ppermute | solution.py:55
  137.2 8.8 %collective-permute-start.15 = (s32[1,1]{1,0:T(1,128)}, s32[1,1]{1,0:T(1,128)}, u32[]{:S(2)}, u32[]{:S(2)}) collective-permute-start(s32[1,1]{1,0:T(1,128)} %bitcast.42), channel_id=1, source_target_pairs={{0,1},{1,0},{2,3},{3,2},{4,5},{5,4},{6,7},{7,6},{8,9},{9,8},{10,11... | collective-permute-start | bytes 20 | tf_op jit(solution)/shard_map/ppermute | solution.py:55
  139.3 21.3 %collective-permute-start.18 = (bf16[8,64,768]{2,1,0:T(8,128)(2,1)}, bf16[8,64,768]{2,1,0:T(8,128)(2,1)S(1)}, u32[]{:S(2)}, u32[]{:S(2)}) collective-permute-start(bf16[8,64,768]{2,1,0:T(8,128)(2,1)} %get-tuple-element.289.refs_4_.refs_0_), channel_id=1, source_target_pairs={{0,8},{2,10},{4,12},{6,14},{8,0},{10,2},{12,4},{14,6},{16,24},{18,... | collective-permute-start | bytes 2359304 | tf_op jit(solution)/shard_map/ppermute | solution.py:51
  141.7 16.6 %collective-permute-start.16 = (bf16[8,64,640]{2,1,0:T(8,128)(2,1)}, bf16[8,64,640]{2,1,0:T(8,128)(2,1)S(1)}, u32[]{:S(2)}, u32[]{:S(2)}) collective-permute-start(bf16[8,64,640]{2,1,0:T(8,128)(2,1)} %get-tuple-element.287.refs_0_), channel_id=1, source_target_pairs={{0,2},{2,0},{4,6},{6,4},{8,10},{10,8},{12,14},{14,12},{16,18},{18,... | collective-permute-start | bytes 1966088 | tf_op jit(solution)/shard_map/ppermute | solution.py:51
  143.8 16.7 %collective-permute-start.17 = (bf16[8,64,640]{2,1,0:T(8,128)(2,1)}, bf16[8,64,640]{2,1,0:T(8,128)(2,1)S(1)}, u32[]{:S(2)}, u32[]{:S(2)}) collective-permute-start(bf16[8,64,640]{2,1,0:T(8,128)(2,1)} %get-tuple-element.288.refs_2_), channel_id=1, source_target_pairs={{0,4},{2,6},{4,0},{6,2},{8,12},{10,14},{12,8},{14,10},{16,20},{18,... | collective-permute-start | bytes 1966088 | tf_op jit(solution)/shard_map/ppermute | solution.py:51
  161.9 35.6 %collective-permute-start.20 = (bf16[8,64,1408]{2,1,0:T(8,128)(2,1)}, bf16[8,64,1408]{2,1,0:T(8,128)(2,1)S(1)}, u32[]{:S(2)}, u32[]{:S(2)}) collective-permute-start(bf16[8,64,1408]{2,1,0:T(8,128)(2,1)} %get-tuple-element.298.refs_2_.refs_4_.refs_8_.refs_10_), channel_id=1, source_target_pairs={{0,4},{2,6},{4,0},{6,2},{8,12},{10,14},{12,8},{14,10},{16,20},{18,... | collective-permute-start | bytes 4325384 | tf_op jit(solution)/shard_map/ppermute | solution.py:51
  163.7 33.8 %collective-permute-start.21 = (bf16[8,64,1408]{2,1,0:T(8,128)(2,1)}, bf16[8,64,1408]{2,1,0:T(8,128)(2,1)}, u32[]{:S(2)}, u32[]{:S(2)}) collective-permute-start(bf16[8,64,1408]{2,1,0:T(8,128)(2,1)} %get-tuple-element.299.refs_6_.refs_12_), channel_id=1, source_target_pairs={{0,8},{2,10},{4,12},{6,14},{8,0},{10,2},{12,4},{14,6},{16,24},{18,... | collective-permute-start | bytes 4325384 | tf_op jit(solution)/shard_map/ppermute | solution.py:51
  165.3 32.2 %collective-permute-start.19 = (bf16[8,64,1280]{2,1,0:T(8,128)(2,1)}, bf16[8,64,1280]{2,1,0:T(8,128)(2,1)}, u32[]{:S(2)}, u32[]{:S(2)}) collective-permute-start(bf16[8,64,1280]{2,1,0:T(8,128)(2,1)} %get-tuple-element.297.refs_0_.refs_6_), channel_id=1, source_target_pairs={{0,2},{2,0},{4,6},{6,4},{8,10},{10,8},{12,14},{14,12},{16,18},{18,... | collective-permute-start | bytes 3932168 | tf_op jit(solution)/shard_map/ppermute | solution.py:51
  198.7 20.0 %collective-permute-start.22 = (bf16[1024,1024]{1,0:T(8,128)(2,1)}, bf16[1024,1024]{1,0:T(8,128)(2,1)S(1)}, u32[]{:S(2)}, u32[]{:S(2)}) collective-permute-start(bf16[1024,1024]{1,0:T(8,128)(2,1)} %get-tuple-element.309.own_ref), channel_id=1, source_target_pairs={{0,1},{1,0},{2,3},{3,2},{4,5},{5,4},{6,7},{7,6},{8,9},{9,8},{10,11... | collective-permute-start | bytes 6291464 | tf_op jit(solution)/shard_map/ppermute | solution.py:55
  199.3 15.9 %collective-permute-start.26 = (bf16[1,64,2176]{2,1,0:T(8,128)(2,1)S(1)}, bf16[1,64,2176]{2,1,0:T(8,128)(2,1)S(1)}, u32[]{:S(2)}, u32[]{:S(2)}) collective-permute-start(bf16[1,64,2176]{2,1,0:T(8,128)(2,1)S(1)} %fusion.26.refs_6_), channel_id=1, source_target_pairs={{0,16},{2,18},{4,20},{6,22},{8,24},{10,26},{12,28},{14,30},{16,0},... | collective-permute-start | bytes 835592 | tf_op jit(solution)/shard_map/ppermute | solution.py:51
  199.3 12.5 %collective-permute-start.25 = (bf16[1,64,2048]{2,1,0:T(8,128)(2,1)S(1)}, bf16[1,64,2048]{2,1,0:T(8,128)(2,1)S(1)}, u32[]{:S(2)}, u32[]{:S(2)}) collective-permute-start(bf16[1,64,2048]{2,1,0:T(8,128)(2,1)S(1)} %fusion.35.refs_4_), channel_id=1, source_target_pairs={{0,8},{2,10},{4,12},{6,14},{8,0},{10,2},{12,4},{14,6},{16,24},{18,... | collective-permute-start | bytes 786440 | tf_op jit(solution)/shard_map/ppermute | solution.py:51
  218.6 26.2 %collective-permute-start.30 = (bf16[2,64,2176]{2,1,0:T(8,128)(2,1)}, bf16[2,64,2176]{2,1,0:T(8,128)(2,1)S(1)}, u32[]{:S(2)}, u32[]{:S(2)}) collective-permute-start(bf16[2,64,2176]{2,1,0:T(8,128)(2,1)} %get-tuple-element.316.refs_6_), channel_id=1, source_target_pairs={{0,8},{2,10},{4,12},{6,14},{8,0},{10,2},{12,4},{14,6},{16,24},{18,... | collective-permute-start | bytes 1671176 | tf_op jit(solution)/shard_map/ppermute | solution.py:51
  218.7 26.1 %collective-permute-start.29 = (bf16[2,64,2048]{2,1,0:T(8,128)(2,1)}, bf16[2,64,2048]{2,1,0:T(8,128)(2,1)S(1)}, u32[]{:S(2)}, u32[]{:S(2)}) collective-permute-start(bf16[2,64,2048]{2,1,0:T(8,128)(2,1)} %get-tuple-element.315.refs_4_), channel_id=1, source_target_pairs={{0,16},{2,18},{4,20},{6,22},{8,24},{10,26},{12,28},{14,30},{16,0},... | collective-permute-start | bytes 1572872 | tf_op jit(solution)/shard_map/ppermute | solution.py:51
  220.6 24.3 %collective-permute-start.28 = (bf16[2,64,1024]{2,1,0:T(8,128)(2,1)}, bf16[2,64,1024]{2,1,0:T(8,128)(2,1)}, u32[]{:S(2)}, u32[]{:S(2)}) collective-permute-start(bf16[2,64,1024]{2,1,0:T(8,128)(2,1)} %get-tuple-element.314.refs_2_), channel_id=1, source_target_pairs={{0,4},{2,6},{4,0},{6,2},{8,12},{10,14},{12,8},{14,10},{16,20},{18,... | collective-permute-start | bytes 786440 | tf_op jit(solution)/shard_map/ppermute | solution.py:51
  221.1 23.7 %collective-permute-start.27 = (bf16[2,64,896]{2,1,0:T(8,128)(2,1)}, bf16[2,64,896]{2,1,0:T(8,128)(2,1)S(1)}, u32[]{:S(2)}, u32[]{:S(2)}) collective-permute-start(bf16[2,64,896]{2,1,0:T(8,128)(2,1)} %get-tuple-element.313.refs_0_), channel_id=1, source_target_pairs={{0,4},{2,6},{4,0},{6,2},{8,12},{10,14},{12,8},{14,10},{16,20},{18,... | collective-permute-start | bytes 688136 | tf_op jit(solution)/shard_map/ppermute | solution.py:51
  250.2 30.8 %collective-permute-start.31 = (bf16[1024,1024]{1,0:T(8,128)(2,1)}, bf16[1024,1024]{1,0:T(8,128)(2,1)}, u32[]{:S(2)}, u32[]{:S(2)}) collective-permute-start(bf16[1024,1024]{1,0:T(8,128)(2,1)} %get-tuple-element.342.own_ref), channel_id=1, source_target_pairs={{0,1},{1,0},{2,3},{3,2},{4,5},{5,4},{6,7},{7,6},{8,9},{9,8},{10,11... | collective-permute-start | bytes 6291464 | tf_op jit(solution)/shard_map/ppermute | solution.py:55
  250.3 27.7 %collective-permute-start.35 = (bf16[4,64,2176]{2,1,0:T(8,128)(2,1)}, bf16[4,64,2176]{2,1,0:T(8,128)(2,1)}, u32[]{:S(2)}, u32[]{:S(2)}) collective-permute-start(bf16[4,64,2176]{2,1,0:T(8,128)(2,1)} %get-tuple-element.326.refs_6_), channel_id=1, source_target_pairs={{0,4},{2,6},{4,0},{6,2},{8,12},{10,14},{12,8},{14,10},{16,20},{18,... | collective-permute-start | bytes 3342344 | tf_op jit(solution)/shard_map/ppermute | solution.py:51
  250.8 27.1 %collective-permute-start.34 = (bf16[4,64,2048]{2,1,0:T(8,128)(2,1)}, bf16[4,64,2048]{2,1,0:T(8,128)(2,1)}, u32[]{:S(2)}, u32[]{:S(2)}) collective-permute-start(bf16[4,64,2048]{2,1,0:T(8,128)(2,1)} %get-tuple-element.325.refs_4_), channel_id=1, source_target_pairs={{0,2},{2,0},{4,6},{6,4},{8,10},{10,8},{12,14},{14,12},{16,18},{18,... | collective-permute-start | bytes 3145736 | tf_op jit(solution)/shard_map/ppermute | solution.py:51
  251.6 26.4 %collective-permute-start.33 = (bf16[4,64,1024]{2,1,0:T(8,128)(2,1)}, bf16[4,64,1024]{2,1,0:T(8,128)(2,1)}, u32[]{:S(2)}, u32[]{:S(2)}) collective-permute-start(bf16[4,64,1024]{2,1,0:T(8,128)(2,1)} %get-tuple-element.324.refs_2_), channel_id=1, source_target_pairs={{0,16},{2,18},{4,20},{6,22},{8,24},{10,26},{12,28},{14,30},{16,0},... | collective-permute-start | bytes 1572872 | tf_op jit(solution)/shard_map/ppermute | solution.py:51
  252.7 21.5 %collective-permute-start.32 = (bf16[4,64,896]{2,1,0:T(8,128)(2,1)}, bf16[4,64,896]{2,1,0:T(8,128)(2,1)}, u32[]{:S(2)}, u32[]{:S(2)}) collective-permute-start(bf16[4,64,896]{2,1,0:T(8,128)(2,1)} %get-tuple-element.323.refs_0_), channel_id=1, source_target_pairs={{0,8},{2,10},{4,12},{6,14},{8,0},{10,2},{12,4},{14,6},{16,24},{18,... | collective-permute-start | bytes 1376264 | tf_op jit(solution)/shard_map/ppermute | solution.py:51
  281.0 11.7 %collective-permute-start.36 = (bf16[1600,1024]{1,0:T(8,128)(2,1)S(1)}, bf16[1600,1024]{1,0:T(8,128)(2,1)}, u32[]{:S(2)}, u32[]{:S(2)}) collective-permute-start(bf16[1600,1024]{1,0:T(8,128)(2,1)S(1)} %pad.13), channel_id=1, source_target_pairs={{0,1},{1,0},{2,3},{3,2},{4,5},{5,4},{6,7},{7,6},{8,9},{9,8},{10,11... | collective-permute-start | bytes 9830408 | tf_op jit(solution)/shard_map/ppermute | solution.py:55
  283.1 23.7 %collective-permute-start.40 = (bf16[8,64,768]{2,1,0:T(8,128)(2,1)}, bf16[8,64,768]{2,1,0:T(8,128)(2,1)}, u32[]{:S(2)}, u32[]{:S(2)}) collective-permute-start(bf16[8,64,768]{2,1,0:T(8,128)(2,1)} %get-tuple-element.341.refs_6_), channel_id=1, source_target_pairs={{0,2},{2,0},{4,6},{6,4},{8,10},{10,8},{12,14},{14,12},{16,18},{18,... | collective-permute-start | bytes 2359304 | tf_op jit(solution)/shard_map/ppermute | solution.py:51
  288.5 18.4 %collective-permute-start.39 = (bf16[8,64,640]{2,1,0:T(8,128)(2,1)}, bf16[8,64,640]{2,1,0:T(8,128)(2,1)S(1)}, u32[]{:S(2)}, u32[]{:S(2)}) collective-permute-start(bf16[8,64,640]{2,1,0:T(8,128)(2,1)} %get-tuple-element.340.refs_4_), channel_id=1, source_target_pairs={{0,4},{2,6},{4,0},{6,2},{8,12},{10,14},{12,8},{14,10},{16,20},{18,... | collective-permute-start | bytes 1966088 | tf_op jit(solution)/shard_map/ppermute | solution.py:51
  290.1 16.8 %collective-permute-start.38 = (bf16[8,64,384]{2,1,0:T(8,128)(2,1)}, bf16[8,64,384]{2,1,0:T(8,128)(2,1)S(1)}, u32[]{:S(2)}, u32[]{:S(2)}) collective-permute-start(bf16[8,64,384]{2,1,0:T(8,128)(2,1)} %get-tuple-element.339.refs_2_), channel_id=1, source_target_pairs={{0,8},{2,10},{4,12},{6,14},{8,0},{10,2},{12,4},{14,6},{16,24},{18,... | collective-permute-start | bytes 1179656 | tf_op jit(solution)/shard_map/ppermute | solution.py:51
  290.1 14.7 %collective-permute-start.37 = (bf16[8,64,256]{2,1,0:T(8,128)(2,1)}, bf16[8,64,256]{2,1,0:T(8,128)(2,1)S(1)}, u32[]{:S(2)}, u32[]{:S(2)}) collective-permute-start(bf16[8,64,256]{2,1,0:T(8,128)(2,1)} %get-tuple-element.338.refs_0_), channel_id=1, source_target_pairs={{0,16},{2,18},{4,20},{6,22},{8,24},{10,26},{12,28},{14,30},{16,0},... | collective-permute-start | bytes 786440 | tf_op jit(solution)/shard_map/ppermute | solution.py:51
  307.8 32.8 %collective-permute-start.44 = (bf16[8,64,1408]{2,1,0:T(8,128)(2,1)}, bf16[8,64,1408]{2,1,0:T(8,128)(2,1)S(1)}, u32[]{:S(2)}, u32[]{:S(2)}) collective-permute-start(bf16[8,64,1408]{2,1,0:T(8,128)(2,1)} %get-tuple-element.348.refs_4_.refs_6_.refs_8_), channel_id=1, source_target_pairs={{0,4},{2,6},{4,0},{6,2},{8,12},{10,14},{12,8},{14,10},{16,20},{18,... | collective-permute-start | bytes 4325384 | tf_op jit(solution)/shard_map/ppermute | solution.py:51
  308.4 32.5 %collective-permute-start.45 = (bf16[8,64,1408]{2,1,0:T(8,128)(2,1)}, bf16[8,64,1408]{2,1,0:T(8,128)(2,1)S(1)}, u32[]{:S(2)}, u32[]{:S(2)}) collective-permute-start(bf16[8,64,1408]{2,1,0:T(8,128)(2,1)} %get-tuple-element.349.refs_8_.refs_10_), channel_id=1, source_target_pairs={{0,2},{2,0},{4,6},{6,4},{8,10},{10,8},{12,14},{14,12},{16,18},{18,... | collective-permute-start | bytes 4325384 | tf_op jit(solution)/shard_map/ppermute | solution.py:51
  309.4 30.5 %collective-permute-start.42 = (bf16[8,64,640]{2,1,0:T(8,128)(2,1)}, bf16[8,64,640]{2,1,0:T(8,128)(2,1)}, u32[]{:S(2)}, u32[]{:S(2)}) collective-permute-start(bf16[8,64,640]{2,1,0:T(8,128)(2,1)} %get-tuple-element.346.refs_0_.refs_2_), channel_id=1, source_target_pairs={{0,16},{2,18},{4,20},{6,22},{8,24},{10,26},{12,28},{14,30},{16,0},... | collective-permute-start | bytes 1966088 | tf_op jit(solution)/shard_map/ppermute | solution.py:51
  311.0 28.9 %collective-permute-start.43 = (bf16[8,64,640]{2,1,0:T(8,128)(2,1)}, bf16[8,64,640]{2,1,0:T(8,128)(2,1)}, u32[]{:S(2)}, u32[]{:S(2)}) collective-permute-start(bf16[8,64,640]{2,1,0:T(8,128)(2,1)} %get-tuple-element.347.refs_2_.refs_4_), channel_id=1, source_target_pairs={{0,8},{2,10},{4,12},{6,14},{8,0},{10,2},{12,4},{14,6},{16,24},{18,... | collective-permute-start | bytes 1966088 | tf_op jit(solution)/shard_map/ppermute | solution.py:51
  357.8 10.9 %collective-permute-start.47 = (bf16[1,48,1024]{2,1,0:T(8,128)(2,1)}, bf16[1,48,1024]{2,1,0:T(8,128)(2,1)S(1)}, u32[]{:S(2)}, u32[]{:S(2)}) collective-permute-start(bf16[1,48,1024]{2,1,0:T(8,128)(2,1)} %bitcast.186), channel_id=1, source_target_pairs={{0,16},{2,18},{4,20},{6,22},{8,24},{10,26},{12,28},{14,30},{16,0},... | collective-permute-start | bytes 294920 | tf_op jit(solution)/shard_map/ppermute | solution.py:51
  359.3 9.4 %collective-permute-start.48 = (bf16[1,48,1024]{2,1,0:T(8,128)(2,1)}, bf16[1,48,1024]{2,1,0:T(8,128)(2,1)S(1)}, u32[]{:S(2)}, u32[]{:S(2)}) collective-permute-start(bf16[1,48,1024]{2,1,0:T(8,128)(2,1)} %bitcast.188), channel_id=1, source_target_pairs={{0,8},{2,10},{4,12},{6,14},{8,0},{10,2},{12,4},{14,6},{16,24},{18,... | collective-permute-start | bytes 294920 | tf_op jit(solution)/shard_map/ppermute | solution.py:51
  360.4 8.2 %collective-permute-start.49 = (bf16[1,32,1024]{2,1,0:T(8,128)(2,1)}, bf16[1,32,1024]{2,1,0:T(8,128)(2,1)S(1)}, u32[]{:S(2)}, u32[]{:S(2)}) collective-permute-start(bf16[1,32,1024]{2,1,0:T(8,128)(2,1)} %bitcast.190), channel_id=1, source_target_pairs={{0,16},{2,18},{4,20},{6,22},{8,24},{10,26},{12,28},{14,30},{16,0},... | collective-permute-start | bytes 196616 | tf_op jit(solution)/shard_map/ppermute | solution.py:51
  373.2 10.6 %collective-permute-start.51 = (bf16[2,48,1024]{2,1,0:T(8,128)(2,1)}, bf16[2,48,1024]{2,1,0:T(8,128)(2,1)S(1)}, u32[]{:S(2)}, u32[]{:S(2)}) collective-permute-start(bf16[2,48,1024]{2,1,0:T(8,128)(2,1)} %get-tuple-element.362.refs_2_), channel_id=1, source_target_pairs={{0,16},{2,18},{4,20},{6,22},{8,24},{10,26},{12,28},{14,30},{16,0},... | collective-permute-start | bytes 589832 | tf_op jit(solution)/shard_map/ppermute | solution.py:51
  386.8 10.9 %collective-permute-start.53 = (bf16[4,48,1024]{2,1,0:T(8,128)(2,1)}, bf16[4,48,1024]{2,1,0:T(8,128)(2,1)S(1)}, u32[]{:S(2)}, u32[]{:S(2)}) collective-permute-start(bf16[4,48,1024]{2,1,0:T(8,128)(2,1)} %get-tuple-element.367.refs_0_), channel_id=1, source_target_pairs={{0,8},{2,10},{4,12},{6,14},{8,0},{10,2},{12,4},{14,6},{16,24},{18,... | collective-permute-start | bytes 1179656 | tf_op jit(solution)/shard_map/ppermute | solution.py:51
  386.9 10.9 %collective-permute-start.54 = (bf16[4,48,1024]{2,1,0:T(8,128)(2,1)}, bf16[4,48,1024]{2,1,0:T(8,128)(2,1)S(1)}, u32[]{:S(2)}, u32[]{:S(2)}) collective-permute-start(bf16[4,48,1024]{2,1,0:T(8,128)(2,1)} %get-tuple-element.368.refs_2_), channel_id=1, source_target_pairs={{0,2},{2,0},{4,6},{6,4},{8,10},{10,8},{12,14},{14,12},{16,18},{18,... | collective-permute-start | bytes 1179656 | tf_op jit(solution)/shard_map/ppermute | solution.py:51
  388.1 8.2 %collective-permute-start.55 = (bf16[4,32,1024]{2,1,0:T(8,128)(2,1)}, bf16[4,32,1024]{2,1,0:T(8,128)(2,1)S(1)}, u32[]{:S(2)}, u32[]{:S(2)}) collective-permute-start(bf16[4,32,1024]{2,1,0:T(8,128)(2,1)} %get-tuple-element.369.refs_4_), channel_id=1, source_target_pairs={{0,4},{2,6},{4,0},{6,2},{8,12},{10,14},{12,8},{14,10},{16,20},{18,... | collective-permute-start | bytes 786440 | tf_op jit(solution)/shard_map/ppermute | solution.py:51
  402.1 18.8 %collective-permute-start.56 = (bf16[8,48,1024]{2,1,0:T(8,128)(2,1)}, bf16[8,48,1024]{2,1,0:T(8,128)(2,1)S(1)}, u32[]{:S(2)}, u32[]{:S(2)}) collective-permute-start(bf16[8,48,1024]{2,1,0:T(8,128)(2,1)} %get-tuple-element.373), channel_id=1, source_target_pairs={{0,2},{2,0},{4,6},{6,4},{8,10},{10,8},{12,14},{14,12},{16,18},{18,... | collective-permute-start | bytes 2359304 | tf_op jit(solution)/shard_map/ppermute | solution.py:51
  403.8 18.5 %collective-permute-start.57 = (bf16[8,48,1024]{2,1,0:T(8,128)(2,1)}, bf16[8,48,1024]{2,1,0:T(8,128)(2,1)S(1)}, u32[]{:S(2)}, u32[]{:S(2)}) collective-permute-start(bf16[8,48,1024]{2,1,0:T(8,128)(2,1)} %get-tuple-element.374), channel_id=1, source_target_pairs={{0,4},{2,6},{4,0},{6,2},{8,12},{10,14},{12,8},{14,10},{16,20},{18,... | collective-permute-start | bytes 2359304 | tf_op jit(solution)/shard_map/ppermute | solution.py:51
  404.6 12.7 %collective-permute-start.58 = (bf16[8,32,1024]{2,1,0:T(8,128)(2,1)}, bf16[8,32,1024]{2,1,0:T(8,128)(2,1)S(1)}, u32[]{:S(2)}, u32[]{:S(2)}) collective-permute-start(bf16[8,32,1024]{2,1,0:T(8,128)(2,1)} %get-tuple-element.375), channel_id=1, source_target_pairs={{0,8},{2,10},{4,12},{6,14},{8,0},{10,2},{12,4},{14,6},{16,24},{18,... | collective-permute-start | bytes 1572872 | tf_op jit(solution)/shard_map/ppermute | solution.py:51
  445.4 19.7 %collective-permute-start.59 = (bf16[384,1152]{1,0:T(8,128)(2,1)}, bf16[384,1152]{1,0:T(8,128)(2,1)S(1)}, u32[]{:S(2)}, u32[]{:S(2)}) collective-permute-start(bf16[384,1152]{1,0:T(8,128)(2,1)} %get-tuple-element.385), channel_id=1, source_target_pairs={{0,2},{2,0},{4,6},{6,4},{8,10},{10,8},{12,14},{14,12},{16,18},{18,... | collective-permute-start | bytes 2654216 | tf_op jit(solution)/shard_map/ppermute | solution.py:51
  446.0 19.7 %collective-permute-start.60 = (bf16[384,1152]{1,0:T(8,128)(2,1)}, bf16[384,1152]{1,0:T(8,128)(2,1)S(1)}, u32[]{:S(2)}, u32[]{:S(2)}) collective-permute-start(bf16[384,1152]{1,0:T(8,128)(2,1)} %get-tuple-element.386), channel_id=1, source_target_pairs={{0,4},{2,6},{4,0},{6,2},{8,12},{10,14},{12,8},{14,10},{16,20},{18,... | collective-permute-start | bytes 2654216 | tf_op jit(solution)/shard_map/ppermute | solution.py:51
  446.7 15.8 %collective-permute-start.61 = (bf16[256,1152]{1,0:T(8,128)(2,1)}, bf16[256,1152]{1,0:T(8,128)(2,1)S(1)}, u32[]{:S(2)}, u32[]{:S(2)}) collective-permute-start(bf16[256,1152]{1,0:T(8,128)(2,1)} %get-tuple-element.387), channel_id=1, source_target_pairs={{0,8},{2,10},{4,12},{6,14},{8,0},{10,2},{12,4},{14,6},{16,24},{18,... | collective-permute-start | bytes 1769480 | tf_op jit(solution)/shard_map/ppermute | solution.py:51
  471.0 9.3 %collective-permute-start.62 = (bf16[192,1152]{1,0:T(8,128)(2,1)}, bf16[192,1152]{1,0:T(8,128)(2,1)S(1)}, u32[]{:S(2)}, u32[]{:S(2)}) collective-permute-start(bf16[192,1152]{1,0:T(8,128)(2,1)} %get-tuple-element.391), channel_id=1, source_target_pairs={{0,8},{2,10},{4,12},{6,14},{8,0},{10,2},{12,4},{14,6},{16,24},{18,... | collective-permute-start | bytes 1327112 | tf_op jit(solution)/shard_map/ppermute | solution.py:51
  471.3 9.0 %collective-permute-start.63 = (bf16[192,1152]{1,0:T(8,128)(2,1)}, bf16[192,1152]{1,0:T(8,128)(2,1)S(1)}, u32[]{:S(2)}, u32[]{:S(2)}) collective-permute-start(bf16[192,1152]{1,0:T(8,128)(2,1)} %get-tuple-element.392), channel_id=1, source_target_pairs={{0,2},{2,0},{4,6},{6,4},{8,10},{10,8},{12,14},{14,12},{16,18},{18,... | collective-permute-start | bytes 1327112 | tf_op jit(solution)/shard_map/ppermute | solution.py:51
  484.3 8.3 %collective-permute-start.65 = (bf16[96,1152]{1,0:T(8,128)(2,1)}, bf16[96,1152]{1,0:T(8,128)(2,1)S(1)}, u32[]{:S(2)}, u32[]{:S(2)}) collective-permute-start(bf16[96,1152]{1,0:T(8,128)(2,1)} %get-tuple-element.397), channel_id=1, source_target_pairs={{0,4},{2,6},{4,0},{6,2},{8,12},{10,14},{12,8},{14,10},{16,20},{18,... | collective-permute-start | bytes 663560 | tf_op jit(solution)/shard_map/ppermute | solution.py:51
  485.1 9.4 %collective-permute-start.66 = (bf16[96,1152]{1,0:T(8,128)(2,1)}, bf16[96,1152]{1,0:T(8,128)(2,1)S(1)}, u32[]{:S(2)}, u32[]{:S(2)}) collective-permute-start(bf16[96,1152]{1,0:T(8,128)(2,1)} %get-tuple-element.398), channel_id=1, source_target_pairs={{0,16},{2,18},{4,20},{6,22},{8,24},{10,26},{12,28},{14,30},{16,0},... | collective-permute-start | bytes 663560 | tf_op jit(solution)/shard_map/ppermute | solution.py:51
  497.6 8.8 %collective-permute-start.68 = (bf16[48,1152]{1,0:T(8,128)(2,1)}, bf16[48,1152]{1,0:T(8,128)(2,1)S(1)}, u32[]{:S(2)}, u32[]{:S(2)}) collective-permute-start(bf16[48,1152]{1,0:T(8,128)(2,1)} %get-tuple-element.403), channel_id=1, source_target_pairs={{0,16},{2,18},{4,20},{6,22},{8,24},{10,26},{12,28},{14,30},{16,0},... | collective-permute-start | bytes 331784 | tf_op jit(solution)/shard_map/ppermute | solution.py:51
  497.6 8.8 %collective-permute-start.69 = (bf16[48,1152]{1,0:T(8,128)(2,1)}, bf16[48,1152]{1,0:T(8,128)(2,1)S(1)}, u32[]{:S(2)}, u32[]{:S(2)}) collective-permute-start(bf16[48,1152]{1,0:T(8,128)(2,1)} %get-tuple-element.404), channel_id=1, source_target_pairs={{0,8},{2,10},{4,12},{6,14},{8,0},{10,2},{12,4},{14,6},{16,24},{18,... | collective-permute-start | bytes 331784 | tf_op jit(solution)/shard_map/ppermute | solution.py:51
  604.1 12.7 %collective-permute-start.79 = (f32[2,2,10,512]{3,2,1,0:T(8,128)S(1)}, f32[2,2,10,512]{3,2,1,0:T(8,128)S(1)}, u32[]{:S(2)}, u32[]{:S(2)}) collective-permute-start(f32[2,2,10,512]{3,2,1,0:T(8,128)S(1)} %add_add_fusion.1), channel_id=1, source_target_pairs={{0,16},{2,18},{4,20},{6,22},{8,24},{10,26},{12,28},{14,30},{16,0},... | collective-permute-start | bytes 245768 | tf_op jit(solution)/shard_map/ppermute | solution.py:51
  606.4 10.4 %collective-permute-start.80 = (f32[2,2,10,512]{3,2,1,0:T(8,128)S(1)}, f32[2,2,10,512]{3,2,1,0:T(8,128)S(1)}, u32[]{:S(2)}, u32[]{:S(2)}) collective-permute-start(f32[2,2,10,512]{3,2,1,0:T(8,128)S(1)} %add_add_fusion.1), channel_id=1, source_target_pairs={{0,24},{2,26},{4,28},{6,30},{8,16},{10,18},{12,20},{14,22},{16,8},... | collective-permute-start | bytes 245768 | tf_op jit(solution)/shard_map/ppermute | solution.py:51
  (126 other events, 2114.6 us)

commit v5 on v4

--- a/solution.py
+++ b/solution.py
@@ -36,8 +36,10 @@
     return jax.ShapeDtypeStruct(dims, dtype)
 
 
-def params(**more):
-    return pltpu.CompilerParams(dimension_semantics=("arbitrary",), **more)
+def params(mebibytes, grid=True):
+    return pltpu.CompilerParams(
+        dimension_semantics=("arbitrary",) if grid else None, vmem_limit_bytes=mebibytes << 20
+    )
 
 
 def cost(microseconds):
@@ -107,6 +109,7 @@
         out_specs=[pl.BlockSpec(memory_space=pltpu.VMEM)] * len(outs),
         out_shape=outs,
         scratch_shapes=[pltpu.SemaphoreType.DMA((len(arrays),))],
+        compiler_params=params(20, False),
         cost_estimate=cost(2),
         name="pack",
     )(*arrays)
@@ -368,7 +371,7 @@
             shape((row_count, half), B16),
             shape((row_count, LANES), F32),
         ],
-        compiler_params=params(),
+        compiler_params=params(32),
         cost_estimate=cost(30 * row_count // 1024),
         name="first_attention",
     )(me, layout, stream, vectors, bias_qkv, prefix, *weight.operands)
@@ -444,7 +447,7 @@
             shape((row_count, width), F32),
             shape((row_count, hidden), B16),
         ],
-        compiler_params=params(),
+        compiler_params=params(36),
         cost_estimate=cost(23 * row_count // 1024),
         name="mlp",
     )(me, base, own, other, vectors, bias_up, *w_up.operands, *w_down.operands)
@@ -546,7 +549,7 @@
             shape((scored, LANES), F32),
             shape((scored, width), F32),
         ],
-        compiler_params=params(),
+        compiler_params=params(36),
         cost_estimate=cost(22),
         name="last_attention",
     )(me, layout, picks, base, own, other, vectors, bias_qkv, prefix, picks_column, *weight.operands)
@@ -612,6 +615,7 @@
             pltpu.VMEM((ends[-1], width), B16),
             pltpu.VMEM((ends[-1], width + LANES), B16),
         ],
+        compiler_params=params(32, False),
         cost_estimate=cost(10 * ends[-1] // 384),
         name="vocabulary",
     )(*stacks, table)
@@ -658,6 +662,7 @@
         out_shape=[shape((begins[-1], wide), B16)]
         if last
         else [shape((a.shape[0] // 2, wide), B16) for a in firsts] * 2,
+        compiler_params=params(20, False),
         cost_estimate=cost(3),
         name="merge",
     )(*firsts, *seconds)
@@ -686,6 +691,7 @@
         out_specs=[VMEM] * (2 + len(sizes)),
         out_shape=[shape((scored, width), F32), shape((scored, width), B16)]
         + [shape((size, width), B16) for size in sizes],
+        compiler_params=params(16, False),
         cost_estimate=cost(3),
         name="head_rows",
     )(core, middle, own, other, vectors)
@@ -727,7 +733,7 @@
             out_specs=[whole_spec((scored, width)), whole_spec((scored, LANES))],
         ),
         out_shape=[shape((scored, width), F32), shape((scored, LANES), F32)],
-        compiler_params=params(),
+        compiler_params=params(24),
         cost_estimate=cost(4),
         name="head_back",
     )(core, own, other, head_rows, head_in, rows, counted, final_norm)
@@ -797,7 +803,7 @@
         ),
         out_shape=[shape((row_count, width), B16)]
         + ([shape((row_count, width), F32)] if extra else []),
-        compiler_params=params(),
+        compiler_params=params(36),
         cost_estimate=cost(20 * row_count // 1024),
         name="mlp_back",
     )(me, gradient, slope, *extra, *w_up.operands, *w_down.operands)
@@ -908,7 +914,7 @@
             shape((row_count, width), F32),
             shape(prefix.shape, F32),
         ],
-        compiler_params=params(),
+        compiler_params=params(48),
         cost_estimate=cost(24),
         name="last_attention_back",
     )(me, layout, picks, *inputs, *weight.operands)
@@ -994,7 +1000,7 @@
             + [pltpu.VMEM((3, lanes, half), B16), pltpu.VMEM((2, lanes, half), F32)],
         ),
         out_shape=shape(prefix.shape, F32),
-        compiler_params=params(),
+        compiler_params=params(24),
         cost_estimate=cost(11),
         name="first_prefix_back",
     )(me, gradient, own, other, middle, gain, q, mixed, lse, prefix, *weight.operands)

time: 658 us -> 637 us (0.968)
  Pallas kernels: 247 us -> 185 us
  local copies, waits for them, and re-layouts: 38.1 us -> 73.8 us
  starting transfers between devices: 104 us -> 112 us
    unnamed x202 -> x304, local copies, waits for them, and re-layouts: 24.5 us -> 62.1 us
    pallas_call x11, Pallas kernels: 34.3 us -> 10.7 us  [pack(): pl.pallas_call(body, in_specs=[pl.BlockSpec(memory_space=pl.ANY)] * len(a...]
    pallas_call x3, Pallas kernels: 47.6 us -> 34.3 us  [vocabulary(): pl.pallas_call(body, in_specs=[VMEM] * (len(stacks) + 1), out_specs=[VMEM...]
    pallas_call x4, Pallas kernels: 12 us -> 2.83 us  [merge(): pl.pallas_call(body, in_specs=[VMEM] * (2 * count), out_specs=[VMEM] * (1...]
    ppermute x75, starting transfers between devices: 92.9 us -> 99.8 us  [flip(): return lax.ppermute(array, 'dev', [(i, i ^ bit) for i in range(size)])]
  transfers between devices with their start and end apart: 89 -> 89, of which waited for: 51 -> 53; matrix products, arithmetic and copies ran while one was open for 6% -> 6% of each run, Pallas kernels for 18% -> 15%
where the time goes in v5:
time: 637 us; the launch traced here: 630 us
  waiting for transfers between devices  206 us (32%)
  Pallas kernels  185 us (29%)
  starting transfers between devices  112 us (18%)
  local copies, waits for them, and re-layouts  73.8 us (12%)
  other arithmetic  21.2 us (3%)
  matrix products  18.4 us (3%)
  between operations  14.4 us (2%)
    ppermute x75, waiting for transfers between devices, flip(): return lax.ppermute(array, 'dev', [(i, i ^ bit) for i in range(size)])  190 us
    ppermute x75, starting transfers between devices, flip(): return lax.ppermute(array, 'dev', [(i, i ^ bit) for i in range(size)])  99.8 us
    unnamed x304, local copies, waits for them, and re-layouts  62.1 us
    pallas_call x3, Pallas kernels, vocabulary(): pl.pallas_call(body, in_specs=[VMEM] * (len(stacks) + 1), out_specs=[VMEM...  34.3 us
    pallas_call x1, Pallas kernels, first_attention(): pl.pallas_call(body, grid_spec=pltpu.PrefetchScalarGridSpec(num_scalar_pr...  30.6 us
    pallas_call x2, Pallas kernels, mlp(): pl.pallas_call(body, grid_spec=pltpu.PrefetchScalarGridSpec(num_scalar_pr...  28.4 us
    pallas_call x2, Pallas kernels, mlp_back(): pl.pallas_call(body, grid_spec=pltpu.PrefetchScalarGridSpec(num_scalar_pr...  25.3 us
    pallas_call x1, Pallas kernels, last_attention_back(): pl.pallas_call(body, grid_spec=pltpu.PrefetchScalarGridSpec(num_scalar_pr...  23.7 us
  transfers between devices with their start and end apart: 89, of which 53 were waited for; matrix products, arithmetic and copies ran while one was open for 6% of the time, Pallas kernels for 15%

profile of v5, /device:TPU:0, one launch (start us, length us, event | category | flops | bytes accessed | tf_op | source)
XLA Modules:
  0.0 629.9 jit_solution(11060123272371316552)
XLA Ops:
  6.1 3.0 collective-permute-start.1
  9.1 2.6 collective-permute-start.5
  15.5 2.2 convert_reduce_fusion
  24.1 4.9 all-to-all-start.2
  29.0 5.7 collective-permute-done.3.refs_1_
  37.1 2.6 collective-permute-start.8
  41.8 6.3 fusion.18
  48.1 5.3 collective-permute-done.6
  55.8 6.6 %collective-permute-done.8.refs_3_ = bf16[2,64,2048]{2,1,0:T(8,128)(2,1)S(1)} collective-permute-done((bf16[2,64,2048]{2,1,0:T(8,128)(2,1)S(1)}, bf16[2,64,2048]{2,1,0:T(8,128)(2,1)S(1)}, u32[]{:S(2)}, u32[]{:S(2)}) %collective-permute-start.8) | collective-permute-done | bytes 524320 | tf_op jit(solution)/shard_map/ppermute | solution.py:53
  70.5 5.3 all-to-all-start.3
  80.9 2.4 collective-permute-start.10
  83.5 41.9 %collective-permute-done.10 = f32[2,2,10,512]{3,2,1,0:T(8,128)S(1)} collective-permute-done((f32[2,2,10,512]{3,2,1,0:T(8,128)S(1)}, f32[2,2,10,512]{3,2,1,0:T(8,128)S(1)}, u32[]{:S(2)}, u32[]{:S(2)}) %collective-permute-start.10) | collective-permute-done | bytes 81952 | tf_op jit(solution)/shard_map/ppermute | solution.py:53
  147.1 2.6 collective-permute-start.18
  151.1 2.2 collective-permute-start.17
  154.6 9.2 %convert_add_fusion = f32[1280,1024]{1,0:T(8,128)} fusion(s32[1280]{0:T(1024)S(1)} %add_select_fusion.5, bf16[768,1024]{1,0:T(8,128)(2,1)} %collective-permute-done.14, bf16[768,1024]{1,0:T(8,128)(2,1)} %bitcast.31, bf16[1024,1024]{1,0:T(8,128)(2,1)} %bitcast_select_fusion), kind=kOutput, calls=%fused_computation.22 | convolution fusion | flops 4037410816 | bytes 10490880 | tf_op jit(solution)/shard_map/dot_general | solution.py:1055
  163.8 2.5 collective-permute-done.16.refs_1_
  168.0 2.2 collective-permute-start.20
  172.9 30.6 %first_attention.1 = (bf16[1024,1024]{1,0:T(8,128)(2,1)S(1)}, bf16[1024,512]{1,0:T(8,128)(2,1)S(1)}, bf16[1024,512]{1,0:T(8,128)(2,1)S(1)}, f32[1024,128]{1,0:T(8,128)S(1)}) custom-call(s32[1]{0:T(128)} %bitcast.4.me_ref, s32[6]{0:T(128)S(1)} %pad_add_fusion.layout_ref, f32[1280,1024]{1,0:T(8,128)} %get-tuple-element.290.stream_ref.base_ref.target_ref, ...), custom_call_target="tpu_custom_call" | custom-call | flops 34500001792 | bytes 1024 | tf_op jit(solution)/shard_map/first_attention/pallas_call | solution.py:351
  208.9 6.0 collective-permute-done.23.refs_1_
  214.9 4.0 collective-permute-done.25.refs_5_
  218.9 3.1 collective-permute-done.26.refs_7_
  225.8 20.6 %mlp.2 = (bf16[1024,1024]{1,0:T(8,128)(2,1)S(1)}, f32[1024,1024]{1,0:T(8,128)}, bf16[1024,2048]{1,0:T(8,128)(2,1)}) custom-call(s32[1]{0:T(128)} %bitcast.4.me_ref, f32[1280,1024]{1,0:T(8,128)S(1)} %copy-done.150, bf16[1024,1024]{1,0:T(8,128)(2,1)S(1)} %get-tuple-element.309.own_ref, bf16[1024,1024]{1,0:T(8,128)(2,1)S(1)} %collective-permute-done.22.other_ref, ...), custom_call_target="tpu_custom_call" | custom-call | flops 26449999872 | bytes 1024 | tf_op jit(solution)/shard_map/mlp/pallas_call | solution.py:428
  252.1 2.2 collective-permute-start.33
  258.2 17.4 %collective-permute-done.32.refs_1_ = bf16[4,64,896]{2,1,0:T(8,128)(2,1)S(1)} collective-permute-done((bf16[4,64,896]{2,1,0:T(8,128)(2,1)S(1)}, bf16[4,64,896]{2,1,0:T(8,128)(2,1)S(1)}, u32[]{:S(2)}, u32[]{:S(2)}) %collective-permute-start.32) | collective-permute-done | bytes 458784 | tf_op jit(solution)/shard_map/ppermute | solution.py:53
  275.5 2.6 collective-permute-done.33.refs_3_
  298.7 3.4 collective-permute-start.37
  302.1 3.7 pad_maximum_fusion.refs_1_.refs_2_.refs_3_
  305.8 7.2 %collective-permute-done.37.refs_1_ = bf16[8,64,256]{2,1,0:T(8,128)(2,1)S(1)} collective-permute-done((bf16[8,64,256]{2,1,0:T(8,128)(2,1)}, bf16[8,64,256]{2,1,0:T(8,128)(2,1)S(1)}, u32[]{:S(2)}, u32[]{:S(2)}) %collective-permute-start.37) | collective-permute-done | bytes 262176 | tf_op jit(solution)/shard_map/ppermute | solution.py:53
  318.1 2.5 collective-permute-start.42
  327.5 17.8 %last_attention.1 = (f32[1024,1024]{1,0:T(8,128)S(1)}, bf16[256,1024]{1,0:T(8,128)(2,1)S(1)}, bf16[1024,512]{1,0:T(8,128)(2,1)S(1)}, bf16[1024,512]{1,0:T(8,128)...) custom-call(s32[1]{0:T(128)} %bitcast.4.me_ref, ...), custom_call_target="tpu_custom_call" | custom-call | flops 25300000768 | bytes 1024 | tf_op jit(solution)/shard_map/last_attention/pallas_call | solution.py:513
  352.2 7.9 %mlp.3 = (bf16[256,1024]{1,0:T(8,128)(2,1)S(1)}, f32[256,1024]{1,0:T(8,128)S(1)}, bf16[256,2048]{1,0:T(8,128)(2,1)S(1)}) custom-call(s32[1]{0:T(128)} %bitcast.4.me_ref, f32[256,1024]{1,0:T(8,128)S(1)} %get-tuple-element.344.base_ref, bf16[256,1024]{1,0:T(8,128)(2,1)S(1)} %get-tuple-element.345.own_ref, ...), custom_call_target="tpu_custom_call" | custom-call | flops 5750000128 | bytes 1024 | tf_op jit(solution)/shard_map/mlp/pallas_call | solution.py:428
  363.7 2.3 collective-permute-start.47
  367.3 2.2 collective-permute-start.49
  369.5 3.7 collective-permute-done.49.refs_5_
  375.4 2.2 collective-permute-start.51
  378.5 4.1 collective-permute-done.52.refs_5_
  382.6 3.8 collective-permute-done.51.refs_3_
  390.0 6.5 %collective-permute-done.55.refs_5_ = bf16[4,32,1024]{2,1,0:T(8,128)(2,1)S(1)} collective-permute-done((bf16[4,32,1024]{2,1,0:T(8,128)(2,1)S(1)}, bf16[4,32,1024]{2,1,0:T(8,128)(2,1)S(1)}, u32[]{:S(2)}, u32[]{:S(2)}) %collective-permute-start.55) | collective-permute-done | bytes 262176 | tf_op jit(solution)/shard_map/ppermute | solution.py:53
  402.1 6.2 vocabulary.3.refs_0_
  408.3 4.5 collective-permute-done.58
  412.8 5.2 collective-permute-done.56
  418.2 17.3 %vocabulary.5 = (bf16[384,1152]{1,0:T(8,128)(2,1)S(1)}, bf16[384,1152]{1,0:T(8,128)(2,1)S(1)}, bf16[256,1152]{1,0:T(8,128)(2,1)S(1)}) custom-call(bf16[384,1024]{1,0:T(8,128)(2,1)S(1)} %bitcast.169, bf16[384,1024]{1,0:T(8,128)(2,1)S(1)} %bitcast.170, bf16[256,1024]{1,0:T(8,128)(2,1)S(1)} %bitcast.172, ...), custom_call_target="tpu_custom_call" | custom-call | flops 29899999232 | bytes 1024 | tf_op jit(solution)/shard_map/vocabulary/pallas_call | solution.py:609
  438.1 10.8 %vocabulary.4 = (bf16[384,1152]{1,0:T(8,128)(2,1)S(1)}, bf16[256,1152]{1,0:T(8,128)(2,1)S(1)}) custom-call(bf16[384,1024]{1,0:T(8,128)(2,1)S(1)} %bitcast.167, bf16[256,1024]{1,0:T(8,128)(2,1)S(1)} %bitcast.171, bf16[3200,1024]{1,0:T(8,128)(2,1)S(1)} %pad_maximum_fusion.refs_1_.refs_2_.refs_3_), custom_call_target="tpu_custom_call" | custom-call | flops 18400000000 | bytes 1024 | tf_op jit(solution)/shard_map/vocabulary/pallas_call | solution.py:609
  449.8 5.1 collective-permute-done.59.refs_3_
  459.3 6.4 %collective-permute-done.64.refs_5_ = bf16[128,1152]{1,0:T(8,128)(2,1)S(1)} collective-permute-done((bf16[128,1152]{1,0:T(8,128)(2,1)S(1)}, bf16[128,1152]{1,0:T(8,128)(2,1)S(1)}, u32[]{:S(2)}, u32[]{:S(2)}) %collective-permute-start.64) | collective-permute-done | bytes 294944 | tf_op jit(solution)/shard_map/ppermute | solution.py:53
  468.0 4.2 collective-permute-start.66
  473.0 4.5 collective-permute-done.67.refs_5_
  477.4 4.9 collective-permute-done.66.refs_4_
  482.8 3.7 collective-permute-start.69
  486.8 5.3 collective-permute-done.70.refs_5_
  495.1 2.4 head_back.1
  498.3 6.3 %mlp_back.2.own_ref = bf16[256,1024]{1,0:T(8,128)(2,1)S(1)} custom-call(s32[1]{0:T(128)} %bitcast.4.me_ref, f32[256,1024]{1,0:T(8,128)S(1)} %get-tuple-element.408.refs_0_.grad_ref, bf16[256,2048]{1,0:T(8,128)(2,1)S(1)} %copy-done.90, bf16[8,64,640]{2,1,0:T(8,128)(2,1)S(1)} %copy-done.60, bf16[8,64,640]{2,1,0:T(8,128)(2,1)} %collective-permute-done.42.refs_1_.refs_3_, ...), custom_call_target="tpu_custom_call" | custom-call | flops 5750000128 | bytes 1024 | tf_op jit(solution)/shard_map/mlp_back/pallas_call | solution.py:795
  506.7 23.7 %last_attention_back.1 = (bf16[1024,1024]{1,0:T(8,128)(2,1)}, f32[1024,1024]{1,0:T(8,128)}, f32[2,16,512]{2,1,0:T(8,128)S(1)}) custom-call(s32[1]{0:T(128)} %bitcast.4.me_ref, s32[6]{0:T(128)S(1)} %pad_add_fusion.layout_ref, s32[256]{0:T(256)S(1)} %copy-done.2, f32[256,1024]{1,0:T(8,128)} %copy-done.91, bf16[256,1024]{1,0:T(8,128)(2,1)S(1)} %mlp_back.2.own_ref, ...), custom_call_target="tpu_custom_call" | custom-call | flops 27599998976 | bytes 1024 | tf_op jit(solution)/shard_map/last_attention_back/pallas_call | solution.py:891
  530.6 4.2 collective-permute-done.73.refs_5_
  536.5 19.0 %mlp_back.3 = (bf16[1024,1024]{1,0:T(8,128)(2,1)S(1)}, f32[1024,1024]{1,0:T(8,128)}) custom-call(s32[1]{0:T(128)} %bitcast.4.me_ref, f32[1024,1024]{1,0:T(8,128)} %get-tuple-element.414.refs_0_, bf16[1024,2048]{1,0:T(8,128)(2,1)} %get-tuple-element.415.refs_1_, f32[1024,1024]{1,0:T(8,128)} %copy-done.99, f32[1,1024]{1,0:T(1,128)S(1)} %get-tuple-element.487.refs_3_, ...), custom_call_target="tpu_custom_call" | custom-call | flops 23000000512 | bytes 1024 | tf_op jit(solution)/shard_map/mlp_back/pallas_call | solution.py:795
  555.7 4.0 collective-permute-done.74.other_ref
  559.8 2.2 copy-done.98
  563.2 8.3 %first_prefix_back.1 = f32[2,16,512]{2,1,0:T(8,128)S(1)} custom-call(s32[1]{0:T(128)} %bitcast.4.me_ref, f32[1024,1024]{1,0:T(8,128)S(1)} %copy-done.98, bf16[1024,1024]{1,0:T(8,128)(2,1)S(1)} %get-tuple-element.419.own_ref, bf16[1024,1024]{1,0:T(8,128)(2,1)S(1)} %collective-permute-done.74.other_ref, f32[1024,1024]{1,0:T(8,128)S(1)} %copy-done.97, ...), custom_call_target="tpu_custom_call" | custom-call | flops 12650000384 | bytes 1024 | tf_op jit(solution)/shard_map/first_prefix_back/pallas_call | solution.py:981
  575.4 2.7 collective-permute-done.75
  583.1 3.1 collective-permute-start.80
  586.2 2.2 collective-permute-done.78
  588.4 6.1 collective-permute-done.79
  608.2 2.8 collective-permute-done.84
  615.5 2.4 collective-permute-done.86
  (533 shorter events, 186.8 us)
Async XLA Ops:
  6.1 12.3 %collective-permute-start.1 = (f32[2,2,10,512]{3,2,1,0:T(8,128)S(1)}, f32[2,2,10,512]{3,2,1,0:T(8,128)S(1)}, u32[]{:S(2)}, u32[]{:S(2)}) collective-permute-start(f32[2,2,10,512]{3,2,1,0:T(8,128)S(1)} %convolution_bitcast_fusion), channel_id=1, source_target_pairs={{0,2},{2,0},{4,6},{6,4},{8,10},{10,8},{12,14},{14,12},{16,18},{18,... | collective-permute-start | bytes 245768 | tf_op jit(solution)/shard_map/ppermute | solution.py:53
  9.1 25.7 %collective-permute-start.5 = (bf16[1,64,2176]{2,1,0:T(8,128)(2,1)S(1)}, bf16[1,64,2176]{2,1,0:T(8,128)(2,1)S(1)}, u32[]{:S(2)}, u32[]{:S(2)}) collective-permute-start(bf16[1,64,2176]{2,1,0:T(8,128)(2,1)S(1)} %fusion.28.refs_4_), channel_id=1, source_target_pairs={{0,16},{2,18},{4,20},{6,22},{8,24},{10,26},{12,28},{14,30},{16,0},... | collective-permute-start | bytes 835592 | tf_op jit(solution)/shard_map/ppermute | solution.py:53
  11.6 23.1 %collective-permute-start.4 = (bf16[1,64,2048]{2,1,0:T(8,128)(2,1)S(1)}, bf16[1,64,2048]{2,1,0:T(8,128)(2,1)S(1)}, u32[]{:S(2)}, u32[]{:S(2)}) collective-permute-start(bf16[1,64,2048]{2,1,0:T(8,128)(2,1)S(1)} %fusion.32.refs_2_), channel_id=1, source_target_pairs={{0,8},{2,10},{4,12},{6,14},{8,0},{10,2},{12,4},{14,6},{16,24},{18,... | collective-permute-start | bytes 786440 | tf_op jit(solution)/shard_map/ppermute | solution.py:53
  13.2 21.5 %collective-permute-start.3 = (bf16[1,64,1920]{2,1,0:T(8,128)(2,1)S(1)}, bf16[1,64,1920]{2,1,0:T(8,128)(2,1)S(1)}, u32[]{:S(2)}, u32[]{:S(2)}) collective-permute-start(bf16[1,64,1920]{2,1,0:T(8,128)(2,1)S(1)} %fusion.43.refs_0_), channel_id=1, source_target_pairs={{0,16},{2,18},{4,20},{6,22},{8,24},{10,26},{12,28},{14,30},{16,0},... | collective-permute-start | bytes 737288 | tf_op jit(solution)/shard_map/ppermute | solution.py:53
  24.1 12.1 %all-to-all-start.2 = ((s32[16,1,49]{2,1,0:T(1,128)}), s32[16,1,49]{2,1,0:T(1,128)S(1)}, u32[]{:S(2)}, u32[]{:S(2)}) async-start(s32[16,1,49]{2,1,0:T(1,128)} %bitcast.21), calls=%async_computation.2 | async-start | bytes 16384 | tf_op jit(solution)/shard_map/all_to_all | solution.py:1039
  36.2 27.0 %collective-permute-start.9 = (bf16[2,64,2176]{2,1,0:T(8,128)(2,1)S(1)}, bf16[2,64,2176]{2,1,0:T(8,128)(2,1)S(1)}, u32[]{:S(2)}, u32[]{:S(2)}) collective-permute-start(bf16[2,64,2176]{2,1,0:T(8,128)(2,1)S(1)} %get-tuple-element.263.refs_4_), channel_id=1, source_target_pairs={{0,2},{2,0},{4,6},{6,4},{8,10},{10,8},{12,14},{14,12},{16,18},{18,... | collective-permute-start | bytes 1671176 | tf_op jit(solution)/shard_map/ppermute | solution.py:53
  37.1 25.3 %collective-permute-start.8 = (bf16[2,64,2048]{2,1,0:T(8,128)(2,1)S(1)}, bf16[2,64,2048]{2,1,0:T(8,128)(2,1)S(1)}, u32[]{:S(2)}, u32[]{:S(2)}) collective-permute-start(bf16[2,64,2048]{2,1,0:T(8,128)(2,1)S(1)} %get-tuple-element.262.refs_2_), channel_id=1, source_target_pairs={{0,16},{2,18},{4,20},{6,22},{8,24},{10,26},{12,28},{14,30},{16,0},... | collective-permute-start | bytes 1572872 | tf_op jit(solution)/shard_map/ppermute | solution.py:53
  39.7 15.3 %collective-permute-start.7 = (bf16[2,64,1920]{2,1,0:T(8,128)(2,1)S(1)}, bf16[2,64,1920]{2,1,0:T(8,128)(2,1)S(1)}, u32[]{:S(2)}, u32[]{:S(2)}) collective-permute-start(bf16[2,64,1920]{2,1,0:T(8,128)(2,1)S(1)} %get-tuple-element.261.refs_0_), channel_id=1, source_target_pairs={{0,4},{2,6},{4,0},{6,2},{8,12},{10,14},{12,8},{14,10},{16,20},{18,... | collective-permute-start | bytes 1474568 | tf_op jit(solution)/shard_map/ppermute | solution.py:53
  40.3 13.2 %collective-permute-start.6 = (f32[2,2,10,512]{3,2,1,0:T(8,128)}, f32[2,2,10,512]{3,2,1,0:T(8,128)}, u32[]{:S(2)}, u32[]{:S(2)}) collective-permute-start(f32[2,2,10,512]{3,2,1,0:T(8,128)} %add.295), channel_id=1, source_target_pairs={{0,8},{2,10},{4,12},{6,14},{8,0},{10,2},{12,4},{14,6},{16,24},{18,... | collective-permute-start | bytes 245768 | tf_op jit(solution)/shard_map/ppermute | solution.py:53
  70.5 62.3 %all-to-all-start.3 = ((bf16[16,48,1024]{2,1,0:T(8,128)(2,1)}), bf16[16,48,1024]{2,1,0:T(8,128)(2,1)}, u32[]{:S(2)}, u32[]{:S(2)}) async-start(bf16[16,48,1024]{2,1,0:T(8,128)(2,1)} %bitcast.182), calls=%async_computation.3 | async-start | bytes 3145728 | tf_op jit(solution)/shard_map/all_to_all | solution.py:1048
  75.8 51.6 %collective-permute-start.13 = (bf16[4,64,2176]{2,1,0:T(8,128)(2,1)S(1)}, bf16[4,64,2176]{2,1,0:T(8,128)(2,1)S(1)}, u32[]{:S(2)}, u32[]{:S(2)}) collective-permute-start(bf16[4,64,2176]{2,1,0:T(8,128)(2,1)S(1)} %get-tuple-element.276.refs_4_), channel_id=1, source_target_pairs={{0,4},{2,6},{4,0},{6,2},{8,12},{10,14},{12,8},{14,10},{16,20},{18,... | collective-permute-start | bytes 3342344 | tf_op jit(solution)/shard_map/ppermute | solution.py:53
  77.9 49.5 %collective-permute-start.12 = (bf16[4,64,2048]{2,1,0:T(8,128)(2,1)S(1)}, bf16[4,64,2048]{2,1,0:T(8,128)(2,1)S(1)}, u32[]{:S(2)}, u32[]{:S(2)}) collective-permute-start(bf16[4,64,2048]{2,1,0:T(8,128)(2,1)S(1)} %get-tuple-element.275.refs_2_), channel_id=1, source_target_pairs={{0,2},{2,0},{4,6},{6,4},{8,10},{10,8},{12,14},{14,12},{16,18},{18,... | collective-permute-start | bytes 3145736 | tf_op jit(solution)/shard_map/ppermute | solution.py:53
  79.4 48.0 %collective-permute-start.11 = (bf16[4,64,1920]{2,1,0:T(8,128)(2,1)}, bf16[4,64,1920]{2,1,0:T(8,128)(2,1)S(1)}, u32[]{:S(2)}, u32[]{:S(2)}) collective-permute-start(bf16[4,64,1920]{2,1,0:T(8,128)(2,1)} %copy-done.44), channel_id=1, source_target_pairs={{0,8},{2,10},{4,12},{6,14},{8,0},{10,2},{12,4},{14,6},{16,24},{18,... | collective-permute-start | bytes 2949128 | tf_op jit(solution)/shard_map/ppermute | solution.py:53
  80.9 44.4 %collective-permute-start.10 = (f32[2,2,10,512]{3,2,1,0:T(8,128)S(1)}, f32[2,2,10,512]{3,2,1,0:T(8,128)S(1)}, u32[]{:S(2)}, u32[]{:S(2)}) collective-permute-start(f32[2,2,10,512]{3,2,1,0:T(8,128)S(1)} %copy-done.122), channel_id=1, source_target_pairs={{0,16},{2,18},{4,20},{6,22},{8,24},{10,26},{12,28},{14,30},{16,0},... | collective-permute-start | bytes 245768 | tf_op jit(solution)/shard_map/ppermute | solution.py:53
  132.8 21.8 %collective-permute-start.14 = (bf16[768,1024]{1,0:T(8,128)(2,1)}, bf16[768,1024]{1,0:T(8,128)(2,1)}, u32[]{:S(2)}, u32[]{:S(2)}) collective-permute-start(bf16[768,1024]{1,0:T(8,128)(2,1)} %bitcast.31), channel_id=1, source_target_pairs={{0,1},{1,0},{2,3},{3,2},{4,5},{5,4},{6,7},{7,6},{8,9},{9,8},{10,11... | collective-permute-start | bytes 4718600 | tf_op jit(solution)/shard_map/ppermute | solution.py:57
  145.1 8.2 %collective-permute-start.15 = (s32[1,1]{1,0:T(1,128)}, s32[1,1]{1,0:T(1,128)}, u32[]{:S(2)}, u32[]{:S(2)}) collective-permute-start(s32[1,1]{1,0:T(1,128)} %bitcast.42), channel_id=1, source_target_pairs={{0,1},{1,0},{2,3},{3,2},{4,5},{5,4},{6,7},{7,6},{8,9},{9,8},{10,11... | collective-permute-start | bytes 20 | tf_op jit(solution)/shard_map/ppermute | solution.py:57
  147.1 20.8 %collective-permute-start.18 = (bf16[8,64,768]{2,1,0:T(8,128)(2,1)S(1)}, bf16[8,64,768]{2,1,0:T(8,128)(2,1)}, u32[]{:S(2)}, u32[]{:S(2)}) collective-permute-start(bf16[8,64,768]{2,1,0:T(8,128)(2,1)S(1)} %copy-done.50), channel_id=1, source_target_pairs={{0,8},{2,10},{4,12},{6,14},{8,0},{10,2},{12,4},{14,6},{16,24},{18,... | collective-permute-start | bytes 2359304 | tf_op jit(solution)/shard_map/ppermute | solution.py:53
  149.7 16.7 %collective-permute-start.16 = (bf16[8,64,640]{2,1,0:T(8,128)(2,1)}, bf16[8,64,640]{2,1,0:T(8,128)(2,1)}, u32[]{:S(2)}, u32[]{:S(2)}) collective-permute-start(bf16[8,64,640]{2,1,0:T(8,128)(2,1)} %get-tuple-element.287.refs_0_), channel_id=1, source_target_pairs={{0,2},{2,0},{4,6},{6,4},{8,10},{10,8},{12,14},{14,12},{16,18},{18,... | collective-permute-start | bytes 1966088 | tf_op jit(solution)/shard_map/ppermute | solution.py:53
  151.1 16.8 %collective-permute-start.17 = (bf16[8,64,640]{2,1,0:T(8,128)(2,1)}, bf16[8,64,640]{2,1,0:T(8,128)(2,1)}, u32[]{:S(2)}, u32[]{:S(2)}) collective-permute-start(bf16[8,64,640]{2,1,0:T(8,128)(2,1)} %get-tuple-element.288.refs_2_), channel_id=1, source_target_pairs={{0,4},{2,6},{4,0},{6,2},{8,12},{10,14},{12,8},{14,10},{16,20},{18,... | collective-permute-start | bytes 1966088 | tf_op jit(solution)/shard_map/ppermute | solution.py:53
  168.0 38.3 %collective-permute-start.20 = (bf16[8,64,1408]{2,1,0:T(8,128)(2,1)S(1)}, bf16[8,64,1408]{2,1,0:T(8,128)(2,1)S(1)}, u32[]{:S(2)}, u32[]{:S(2)}) collective-permute-start(bf16[8,64,1408]{2,1,0:T(8,128)(2,1)S(1)} %get-tuple-element.298.refs_2_.refs_4_.refs_8_.refs_10_), channel_id=1, source_target_pairs={{0,4},{2,6},{4,0},{6,2},{8,12},{10,14},{12,8},{14,10},{16,20},{18,... | collective-permute-start | bytes 4325384 | tf_op jit(solution)/shard_map/ppermute | solution.py:53
  170.2 36.0 %collective-permute-start.21 = (bf16[8,64,1408]{2,1,0:T(8,128)(2,1)}, bf16[8,64,1408]{2,1,0:T(8,128)(2,1)S(1)}, u32[]{:S(2)}, u32[]{:S(2)}) collective-permute-start(bf16[8,64,1408]{2,1,0:T(8,128)(2,1)} %copy-done.10), channel_id=1, source_target_pairs={{0,8},{2,10},{4,12},{6,14},{8,0},{10,2},{12,4},{14,6},{16,24},{18,... | collective-permute-start | bytes 4325384 | tf_op jit(solution)/shard_map/ppermute | solution.py:53
  171.9 34.3 %collective-permute-start.19 = (bf16[8,64,1280]{2,1,0:T(8,128)(2,1)}, bf16[8,64,1280]{2,1,0:T(8,128)(2,1)S(1)}, u32[]{:S(2)}, u32[]{:S(2)}) collective-permute-start(bf16[8,64,1280]{2,1,0:T(8,128)(2,1)} %copy-done.25), channel_id=1, source_target_pairs={{0,2},{2,0},{4,6},{6,4},{8,10},{10,8},{12,14},{14,12},{16,18},{18,... | collective-permute-start | bytes 3932168 | tf_op jit(solution)/shard_map/ppermute | solution.py:53
  206.2 16.6 %collective-permute-start.22 = (bf16[1024,1024]{1,0:T(8,128)(2,1)S(1)}, bf16[1024,1024]{1,0:T(8,128)(2,1)S(1)}, u32[]{:S(2)}, u32[]{:S(2)}) collective-permute-start(bf16[1024,1024]{1,0:T(8,128)(2,1)S(1)} %get-tuple-element.309.own_ref), channel_id=1, source_target_pairs={{0,1},{1,0},{2,3},{3,2},{4,5},{5,4},{6,7},{7,6},{8,9},{9,8},{10,11... | collective-permute-start | bytes 6291464 | tf_op jit(solution)/shard_map/ppermute | solution.py:57
  206.3 15.7 %collective-permute-start.26 = (bf16[1,64,2176]{2,1,0:T(8,128)(2,1)S(1)}, bf16[1,64,2176]{2,1,0:T(8,128)(2,1)S(1)}, u32[]{:S(2)}, u32[]{:S(2)}) collective-permute-start(bf16[1,64,2176]{2,1,0:T(8,128)(2,1)S(1)} %fusion.26.refs_6_), channel_id=1, source_target_pairs={{0,16},{2,18},{4,20},{6,22},{8,24},{10,26},{12,28},{14,30},{16,0},... | collective-permute-start | bytes 835592 | tf_op jit(solution)/shard_map/ppermute | solution.py:53
  206.4 12.5 %collective-permute-start.25 = (bf16[1,64,2048]{2,1,0:T(8,128)(2,1)S(1)}, bf16[1,64,2048]{2,1,0:T(8,128)(2,1)S(1)}, u32[]{:S(2)}, u32[]{:S(2)}) collective-permute-start(bf16[1,64,2048]{2,1,0:T(8,128)(2,1)S(1)} %fusion.35.refs_4_), channel_id=1, source_target_pairs={{0,8},{2,10},{4,12},{6,14},{8,0},{10,2},{12,4},{14,6},{16,24},{18,... | collective-permute-start | bytes 786440 | tf_op jit(solution)/shard_map/ppermute | solution.py:53
  206.8 8.1 %collective-permute-start.24 = (bf16[1,64,1024]{2,1,0:T(8,128)(2,1)S(1)}, bf16[1,64,1024]{2,1,0:T(8,128)(2,1)S(1)}, u32[]{:S(2)}, u32[]{:S(2)}) collective-permute-start(bf16[1,64,1024]{2,1,0:T(8,128)(2,1)S(1)} %fusion.46.refs_2_), channel_id=1, source_target_pairs={{0,2},{2,0},{4,6},{6,4},{8,10},{10,8},{12,14},{14,12},{16,18},{18,... | collective-permute-start | bytes 393224 | tf_op jit(solution)/shard_map/ppermute | solution.py:53
  222.8 26.9 %collective-permute-start.30 = (bf16[2,64,2176]{2,1,0:T(8,128)(2,1)S(1)}, bf16[2,64,2176]{2,1,0:T(8,128)(2,1)S(1)}, u32[]{:S(2)}, u32[]{:S(2)}) collective-permute-start(bf16[2,64,2176]{2,1,0:T(8,128)(2,1)S(1)} %get-tuple-element.316.refs_6_), channel_id=1, source_target_pairs={{0,8},{2,10},{4,12},{6,14},{8,0},{10,2},{12,4},{14,6},{16,24},{18,... | collective-permute-start | bytes 1671176 | tf_op jit(solution)/shard_map/ppermute | solution.py:53
  222.9 26.8 %collective-permute-start.29 = (bf16[2,64,2048]{2,1,0:T(8,128)(2,1)S(1)}, bf16[2,64,2048]{2,1,0:T(8,128)(2,1)S(1)}, u32[]{:S(2)}, u32[]{:S(2)}) collective-permute-start(bf16[2,64,2048]{2,1,0:T(8,128)(2,1)S(1)} %get-tuple-element.315.refs_4_), channel_id=1, source_target_pairs={{0,16},{2,18},{4,20},{6,22},{8,24},{10,26},{12,28},{14,30},{16,0},... | collective-permute-start | bytes 1572872 | tf_op jit(solution)/shard_map/ppermute | solution.py:53
  223.8 26.0 %collective-permute-start.28 = (bf16[2,64,1024]{2,1,0:T(8,128)(2,1)S(1)}, bf16[2,64,1024]{2,1,0:T(8,128)(2,1)S(1)}, u32[]{:S(2)}, u32[]{:S(2)}) collective-permute-start(bf16[2,64,1024]{2,1,0:T(8,128)(2,1)S(1)} %get-tuple-element.314.refs_2_), channel_id=1, source_target_pairs={{0,4},{2,6},{4,0},{6,2},{8,12},{10,14},{12,8},{14,10},{16,20},{18,... | collective-permute-start | bytes 786440 | tf_op jit(solution)/shard_map/ppermute | solution.py:53
  224.2 25.6 %collective-permute-start.27 = (bf16[2,64,896]{2,1,0:T(8,128)(2,1)S(1)}, bf16[2,64,896]{2,1,0:T(8,128)(2,1)S(1)}, u32[]{:S(2)}, u32[]{:S(2)}) collective-permute-start(bf16[2,64,896]{2,1,0:T(8,128)(2,1)S(1)} %get-tuple-element.313.refs_0_), channel_id=1, source_target_pairs={{0,4},{2,6},{4,0},{6,2},{8,12},{10,14},{12,8},{14,10},{16,20},{18,... | collective-permute-start | bytes 688136 | tf_op jit(solution)/shard_map/ppermute | solution.py:53
  250.8 30.9 %collective-permute-start.31 = (bf16[1024,1024]{1,0:T(8,128)(2,1)S(1)}, bf16[1024,1024]{1,0:T(8,128)(2,1)S(1)}, u32[]{:S(2)}, u32[]{:S(2)}) collective-permute-start(bf16[1024,1024]{1,0:T(8,128)(2,1)S(1)} %get-tuple-element.342.own_ref), channel_id=1, source_target_pairs={{0,1},{1,0},{2,3},{3,2},{4,5},{5,4},{6,7},{7,6},{8,9},{9,8},{10,11... | collective-permute-start | bytes 6291464 | tf_op jit(solution)/shard_map/ppermute | solution.py:57
  250.8 27.3 %collective-permute-start.35 = (bf16[4,64,2176]{2,1,0:T(8,128)(2,1)S(1)}, bf16[4,64,2176]{2,1,0:T(8,128)(2,1)S(1)}, u32[]{:S(2)}, u32[]{:S(2)}) collective-permute-start(bf16[4,64,2176]{2,1,0:T(8,128)(2,1)S(1)} %get-tuple-element.326.refs_6_), channel_id=1, source_target_pairs={{0,4},{2,6},{4,0},{6,2},{8,12},{10,14},{12,8},{14,10},{16,20},{18,... | collective-permute-start | bytes 3342344 | tf_op jit(solution)/shard_map/ppermute | solution.py:53
  251.3 26.8 %collective-permute-start.34 = (bf16[4,64,2048]{2,1,0:T(8,128)(2,1)S(1)}, bf16[4,64,2048]{2,1,0:T(8,128)(2,1)S(1)}, u32[]{:S(2)}, u32[]{:S(2)}) collective-permute-start(bf16[4,64,2048]{2,1,0:T(8,128)(2,1)S(1)} %get-tuple-element.325.refs_4_), channel_id=1, source_target_pairs={{0,2},{2,0},{4,6},{6,4},{8,10},{10,8},{12,14},{14,12},{16,18},{18,... | collective-permute-start | bytes 3145736 | tf_op jit(solution)/shard_map/ppermute | solution.py:53
  252.1 26.0 %collective-permute-start.33 = (bf16[4,64,1024]{2,1,0:T(8,128)(2,1)S(1)}, bf16[4,64,1024]{2,1,0:T(8,128)(2,1)S(1)}, u32[]{:S(2)}, u32[]{:S(2)}) collective-permute-start(bf16[4,64,1024]{2,1,0:T(8,128)(2,1)S(1)} %get-tuple-element.324.refs_2_), channel_id=1, source_target_pairs={{0,16},{2,18},{4,20},{6,22},{8,24},{10,26},{12,28},{14,30},{16,0},... | collective-permute-start | bytes 1572872 | tf_op jit(solution)/shard_map/ppermute | solution.py:53
  254.2 21.3 %collective-permute-start.32 = (bf16[4,64,896]{2,1,0:T(8,128)(2,1)S(1)}, bf16[4,64,896]{2,1,0:T(8,128)(2,1)S(1)}, u32[]{:S(2)}, u32[]{:S(2)}) collective-permute-start(bf16[4,64,896]{2,1,0:T(8,128)(2,1)S(1)} %get-tuple-element.323.refs_0_), channel_id=1, source_target_pairs={{0,8},{2,10},{4,12},{6,14},{8,0},{10,2},{12,4},{14,6},{16,24},{18,... | collective-permute-start | bytes 1376264 | tf_op jit(solution)/shard_map/ppermute | solution.py:53
  283.1 19.0 %collective-permute-start.36 = (bf16[1600,1024]{1,0:T(8,128)(2,1)}, bf16[1600,1024]{1,0:T(8,128)(2,1)}, u32[]{:S(2)}, u32[]{:S(2)}) collective-permute-start(bf16[1600,1024]{1,0:T(8,128)(2,1)} %pad.13), channel_id=1, source_target_pairs={{0,1},{1,0},{2,3},{3,2},{4,5},{5,4},{6,7},{7,6},{8,9},{9,8},{10,11... | collective-permute-start | bytes 9830408 | tf_op jit(solution)/shard_map/ppermute | solution.py:57
  283.3 32.5 %collective-permute-start.40 = (bf16[8,64,768]{2,1,0:T(8,128)(2,1)}, bf16[8,64,768]{2,1,0:T(8,128)(2,1)S(1)}, u32[]{:S(2)}, u32[]{:S(2)}) collective-permute-start(bf16[8,64,768]{2,1,0:T(8,128)(2,1)} %copy-done.52), channel_id=1, source_target_pairs={{0,2},{2,0},{4,6},{6,4},{8,10},{10,8},{12,14},{14,12},{16,18},{18,... | collective-permute-start | bytes 2359304 | tf_op jit(solution)/shard_map/ppermute | solution.py:53
  296.9 18.9 %collective-permute-start.39 = (bf16[8,64,640]{2,1,0:T(8,128)(2,1)}, bf16[8,64,640]{2,1,0:T(8,128)(2,1)}, u32[]{:S(2)}, u32[]{:S(2)}) collective-permute-start(bf16[8,64,640]{2,1,0:T(8,128)(2,1)} %get-tuple-element.340.refs_4_), channel_id=1, source_target_pairs={{0,4},{2,6},{4,0},{6,2},{8,12},{10,14},{12,8},{14,10},{16,20},{18,... | collective-permute-start | bytes 1966088 | tf_op jit(solution)/shard_map/ppermute | solution.py:53
  298.5 16.6 %collective-permute-start.38 = (bf16[8,64,384]{2,1,0:T(8,128)(2,1)S(1)}, bf16[8,64,384]{2,1,0:T(8,128)(2,1)S(1)}, u32[]{:S(2)}, u32[]{:S(2)}) collective-permute-start(bf16[8,64,384]{2,1,0:T(8,128)(2,1)S(1)} %copy-done.81), channel_id=1, source_target_pairs={{0,8},{2,10},{4,12},{6,14},{8,0},{10,2},{12,4},{14,6},{16,24},{18,... | collective-permute-start | bytes 1179656 | tf_op jit(solution)/shard_map/ppermute | solution.py:53
  298.7 14.2 %collective-permute-start.37 = (bf16[8,64,256]{2,1,0:T(8,128)(2,1)}, bf16[8,64,256]{2,1,0:T(8,128)(2,1)S(1)}, u32[]{:S(2)}, u32[]{:S(2)}) collective-permute-start(bf16[8,64,256]{2,1,0:T(8,128)(2,1)} %get-tuple-element.338.refs_0_), channel_id=1, source_target_pairs={{0,16},{2,18},{4,20},{6,22},{8,24},{10,26},{12,28},{14,30},{16,0},... | collective-permute-start | bytes 786440 | tf_op jit(solution)/shard_map/ppermute | solution.py:53
  316.7 32.8 %collective-permute-start.44 = (bf16[8,64,1408]{2,1,0:T(8,128)(2,1)}, bf16[8,64,1408]{2,1,0:T(8,128)(2,1)S(1)}, u32[]{:S(2)}, u32[]{:S(2)}) collective-permute-start(bf16[8,64,1408]{2,1,0:T(8,128)(2,1)} %copy-done.17), channel_id=1, source_target_pairs={{0,4},{2,6},{4,0},{6,2},{8,12},{10,14},{12,8},{14,10},{16,20},{18,... | collective-permute-start | bytes 4325384 | tf_op jit(solution)/shard_map/ppermute | solution.py:53
  317.2 32.7 %collective-permute-start.45 = (bf16[8,64,1408]{2,1,0:T(8,128)(2,1)}, bf16[8,64,1408]{2,1,0:T(8,128)(2,1)}, u32[]{:S(2)}, u32[]{:S(2)}) collective-permute-start(bf16[8,64,1408]{2,1,0:T(8,128)(2,1)} %copy-done.20), channel_id=1, source_target_pairs={{0,2},{2,0},{4,6},{6,4},{8,10},{10,8},{12,14},{14,12},{16,18},{18,... | collective-permute-start | bytes 4325384 | tf_op jit(solution)/shard_map/ppermute | solution.py:53
  318.1 31.2 %collective-permute-start.42 = (bf16[8,64,640]{2,1,0:T(8,128)(2,1)}, bf16[8,64,640]{2,1,0:T(8,128)(2,1)}, u32[]{:S(2)}, u32[]{:S(2)}) collective-permute-start(bf16[8,64,640]{2,1,0:T(8,128)(2,1)} %copy-done.58), channel_id=1, source_target_pairs={{0,16},{2,18},{4,20},{6,22},{8,24},{10,26},{12,28},{14,30},{16,0},... | collective-permute-start | bytes 1966088 | tf_op jit(solution)/shard_map/ppermute | solution.py:53
  320.6 28.7 %collective-permute-start.43 = (bf16[8,64,640]{2,1,0:T(8,128)(2,1)}, bf16[8,64,640]{2,1,0:T(8,128)(2,1)}, u32[]{:S(2)}, u32[]{:S(2)}) collective-permute-start(bf16[8,64,640]{2,1,0:T(8,128)(2,1)} %copy-done.61), channel_id=1, source_target_pairs={{0,8},{2,10},{4,12},{6,14},{8,0},{10,2},{12,4},{14,6},{16,24},{18,... | collective-permute-start | bytes 1966088 | tf_op jit(solution)/shard_map/ppermute | solution.py:53
  363.7 9.6 %collective-permute-start.47 = (bf16[1,48,1024]{2,1,0:T(8,128)(2,1)S(1)}, bf16[1,48,1024]{2,1,0:T(8,128)(2,1)S(1)}, u32[]{:S(2)}, u32[]{:S(2)}) collective-permute-start(bf16[1,48,1024]{2,1,0:T(8,128)(2,1)S(1)} %bitcast.173), channel_id=1, source_target_pairs={{0,16},{2,18},{4,20},{6,22},{8,24},{10,26},{12,28},{14,30},{16,0},... | collective-permute-start | bytes 294920 | tf_op jit(solution)/shard_map/ppermute | solution.py:53
  374.0 8.5 %collective-permute-start.50 = (bf16[2,48,1024]{2,1,0:T(8,128)(2,1)S(1)}, bf16[2,48,1024]{2,1,0:T(8,128)(2,1)S(1)}, u32[]{:S(2)}, u32[]{:S(2)}) collective-permute-start(bf16[2,48,1024]{2,1,0:T(8,128)(2,1)S(1)} %get-tuple-element.361.refs_0_), channel_id=1, source_target_pairs={{0,4},{2,6},{4,0},{6,2},{8,12},{10,14},{12,8},{14,10},{16,20},{18,... | collective-permute-start | bytes 589832 | tf_op jit(solution)/shard_map/ppermute | solution.py:53
  375.4 10.9 %collective-permute-start.51 = (bf16[2,48,1024]{2,1,0:T(8,128)(2,1)S(1)}, bf16[2,48,1024]{2,1,0:T(8,128)(2,1)S(1)}, u32[]{:S(2)}, u32[]{:S(2)}) collective-permute-start(bf16[2,48,1024]{2,1,0:T(8,128)(2,1)S(1)} %get-tuple-element.362.refs_2_), channel_id=1, source_target_pairs={{0,16},{2,18},{4,20},{6,22},{8,24},{10,26},{12,28},{14,30},{16,0},... | collective-permute-start | bytes 589832 | tf_op jit(solution)/shard_map/ppermute | solution.py:53
  387.7 9.5 %collective-permute-start.53 = (bf16[4,48,1024]{2,1,0:T(8,128)(2,1)S(1)}, bf16[4,48,1024]{2,1,0:T(8,128)(2,1)S(1)}, u32[]{:S(2)}, u32[]{:S(2)}) collective-permute-start(bf16[4,48,1024]{2,1,0:T(8,128)(2,1)S(1)} %get-tuple-element.367.refs_0_), channel_id=1, source_target_pairs={{0,8},{2,10},{4,12},{6,14},{8,0},{10,2},{12,4},{14,6},{16,24},{18,... | collective-permute-start | bytes 1179656 | tf_op jit(solution)/shard_map/ppermute | solution.py:53
  387.9 10.8 %collective-permute-start.54 = (bf16[4,48,1024]{2,1,0:T(8,128)(2,1)S(1)}, bf16[4,48,1024]{2,1,0:T(8,128)(2,1)S(1)}, u32[]{:S(2)}, u32[]{:S(2)}) collective-permute-start(bf16[4,48,1024]{2,1,0:T(8,128)(2,1)S(1)} %get-tuple-element.368.refs_2_), channel_id=1, source_target_pairs={{0,2},{2,0},{4,6},{6,4},{8,10},{10,8},{12,14},{14,12},{16,18},{18,... | collective-permute-start | bytes 1179656 | tf_op jit(solution)/shard_map/ppermute | solution.py:53
  399.7 18.4 %collective-permute-start.56 = (bf16[8,48,1024]{2,1,0:T(8,128)(2,1)S(1)}, bf16[8,48,1024]{2,1,0:T(8,128)(2,1)S(1)}, u32[]{:S(2)}, u32[]{:S(2)}) collective-permute-start(bf16[8,48,1024]{2,1,0:T(8,128)(2,1)S(1)} %get-tuple-element.373), channel_id=1, source_target_pairs={{0,2},{2,0},{4,6},{6,4},{8,10},{10,8},{12,14},{14,12},{16,18},{18,... | collective-permute-start | bytes 2359304 | tf_op jit(solution)/shard_map/ppermute | solution.py:53
  400.6 17.6 %collective-permute-start.57 = (bf16[8,48,1024]{2,1,0:T(8,128)(2,1)S(1)}, bf16[8,48,1024]{2,1,0:T(8,128)(2,1)S(1)}, u32[]{:S(2)}, u32[]{:S(2)}) collective-permute-start(bf16[8,48,1024]{2,1,0:T(8,128)(2,1)S(1)} %get-tuple-element.374), channel_id=1, source_target_pairs={{0,4},{2,6},{4,0},{6,2},{8,12},{10,14},{12,8},{14,10},{16,20},{18,... | collective-permute-start | bytes 2359304 | tf_op jit(solution)/shard_map/ppermute | solution.py:53
  401.3 11.5 %collective-permute-start.58 = (bf16[8,32,1024]{2,1,0:T(8,128)(2,1)S(1)}, bf16[8,32,1024]{2,1,0:T(8,128)(2,1)S(1)}, u32[]{:S(2)}, u32[]{:S(2)}) collective-permute-start(bf16[8,32,1024]{2,1,0:T(8,128)(2,1)S(1)} %get-tuple-element.375), channel_id=1, source_target_pairs={{0,8},{2,10},{4,12},{6,14},{8,0},{10,2},{12,4},{14,6},{16,24},{18,... | collective-permute-start | bytes 1572872 | tf_op jit(solution)/shard_map/ppermute | solution.py:53
  435.6 19.4 %collective-permute-start.59 = (bf16[384,1152]{1,0:T(8,128)(2,1)S(1)}, bf16[384,1152]{1,0:T(8,128)(2,1)S(1)}, u32[]{:S(2)}, u32[]{:S(2)}) collective-permute-start(bf16[384,1152]{1,0:T(8,128)(2,1)S(1)} %get-tuple-element.385), channel_id=1, source_target_pairs={{0,2},{2,0},{4,6},{6,4},{8,10},{10,8},{12,14},{14,12},{16,18},{18,... | collective-permute-start | bytes 2654216 | tf_op jit(solution)/shard_map/ppermute | solution.py:53
  437.2 18.9 %collective-permute-start.60 = (bf16[384,1152]{1,0:T(8,128)(2,1)S(1)}, bf16[384,1152]{1,0:T(8,128)(2,1)S(1)}, u32[]{:S(2)}, u32[]{:S(2)}) collective-permute-start(bf16[384,1152]{1,0:T(8,128)(2,1)S(1)} %get-tuple-element.386), channel_id=1, source_target_pairs={{0,4},{2,6},{4,0},{6,2},{8,12},{10,14},{12,8},{14,10},{16,20},{18,... | collective-permute-start | bytes 2654216 | tf_op jit(solution)/shard_map/ppermute | solution.py:53
  437.5 12.4 %collective-permute-start.61 = (bf16[256,1152]{1,0:T(8,128)(2,1)S(1)}, bf16[256,1152]{1,0:T(8,128)(2,1)S(1)}, u32[]{:S(2)}, u32[]{:S(2)}) collective-permute-start(bf16[256,1152]{1,0:T(8,128)(2,1)S(1)} %get-tuple-element.387), channel_id=1, source_target_pairs={{0,8},{2,10},{4,12},{6,14},{8,0},{10,2},{12,4},{14,6},{16,24},{18,... | collective-permute-start | bytes 1769480 | tf_op jit(solution)/shard_map/ppermute | solution.py:53
  457.6 8.6 %collective-permute-start.62 = (bf16[192,1152]{1,0:T(8,128)(2,1)S(1)}, bf16[192,1152]{1,0:T(8,128)(2,1)S(1)}, u32[]{:S(2)}, u32[]{:S(2)}) collective-permute-start(bf16[192,1152]{1,0:T(8,128)(2,1)S(1)} %get-tuple-element.391), channel_id=1, source_target_pairs={{0,8},{2,10},{4,12},{6,14},{8,0},{10,2},{12,4},{14,6},{16,24},{18,... | collective-permute-start | bytes 1327112 | tf_op jit(solution)/shard_map/ppermute | solution.py:53
  458.5 8.5 %collective-permute-start.63 = (bf16[192,1152]{1,0:T(8,128)(2,1)S(1)}, bf16[192,1152]{1,0:T(8,128)(2,1)S(1)}, u32[]{:S(2)}, u32[]{:S(2)}) collective-permute-start(bf16[192,1152]{1,0:T(8,128)(2,1)S(1)} %get-tuple-element.392), channel_id=1, source_target_pairs={{0,2},{2,0},{4,6},{6,4},{8,10},{10,8},{12,14},{14,12},{16,18},{18,... | collective-permute-start | bytes 1327112 | tf_op jit(solution)/shard_map/ppermute | solution.py:53
  467.7 9.7 %collective-permute-start.65 = (bf16[96,1152]{1,0:T(8,128)(2,1)S(1)}, bf16[96,1152]{1,0:T(8,128)(2,1)S(1)}, u32[]{:S(2)}, u32[]{:S(2)}) collective-permute-start(bf16[96,1152]{1,0:T(8,128)(2,1)S(1)} %get-tuple-element.397), channel_id=1, source_target_pairs={{0,4},{2,6},{4,0},{6,2},{8,12},{10,14},{12,8},{14,10},{16,20},{18,... | collective-permute-start | bytes 663560 | tf_op jit(solution)/shard_map/ppermute | solution.py:53
  468.0 14.3 %collective-permute-start.66 = (bf16[96,1152]{1,0:T(8,128)(2,1)S(1)}, bf16[96,1152]{1,0:T(8,128)(2,1)S(1)}, u32[]{:S(2)}, u32[]{:S(2)}) collective-permute-start(bf16[96,1152]{1,0:T(8,128)(2,1)S(1)} %get-tuple-element.398), channel_id=1, source_target_pairs={{0,16},{2,18},{4,20},{6,22},{8,24},{10,26},{12,28},{14,30},{16,0},... | collective-permute-start | bytes 663560 | tf_op jit(solution)/shard_map/ppermute | solution.py:53
  482.8 9.3 %collective-permute-start.68 = (bf16[48,1152]{1,0:T(8,128)(2,1)S(1)}, bf16[48,1152]{1,0:T(8,128)(2,1)S(1)}, u32[]{:S(2)}, u32[]{:S(2)}) collective-permute-start(bf16[48,1152]{1,0:T(8,128)(2,1)S(1)} %get-tuple-element.403), channel_id=1, source_target_pairs={{0,16},{2,18},{4,20},{6,22},{8,24},{10,26},{12,28},{14,30},{16,0},... | collective-permute-start | bytes 331784 | tf_op jit(solution)/shard_map/ppermute | solution.py:53
  482.8 9.2 %collective-permute-start.69 = (bf16[48,1152]{1,0:T(8,128)(2,1)S(1)}, bf16[48,1152]{1,0:T(8,128)(2,1)S(1)}, u32[]{:S(2)}, u32[]{:S(2)}) collective-permute-start(bf16[48,1152]{1,0:T(8,128)(2,1)S(1)} %get-tuple-element.404), channel_id=1, source_target_pairs={{0,8},{2,10},{4,12},{6,14},{8,0},{10,2},{12,4},{14,6},{16,24},{18,... | collective-permute-start | bytes 331784 | tf_op jit(solution)/shard_map/ppermute | solution.py:53
  572.4 7.6 %collective-permute-start.76 = (f32[2,2,10,512]{3,2,1,0:T(8,128)S(1)}, f32[2,2,10,512]{3,2,1,0:T(8,128)S(1)}, u32[]{:S(2)}, u32[]{:S(2)}) collective-permute-start(f32[2,2,10,512]{3,2,1,0:T(8,128)S(1)} %pad_maximum_fusion.3), channel_id=1, source_target_pairs={{0,4},{2,6},{4,0},{6,2},{8,12},{10,14},{12,8},{14,10},{16,20},{18,... | collective-permute-start | bytes 245768 | tf_op jit(solution)/shard_map/ppermute | solution.py:53
  581.8 12.7 %collective-permute-start.79 = (f32[2,2,10,512]{3,2,1,0:T(8,128)S(1)}, f32[2,2,10,512]{3,2,1,0:T(8,128)S(1)}, u32[]{:S(2)}, u32[]{:S(2)}) collective-permute-start(f32[2,2,10,512]{3,2,1,0:T(8,128)S(1)} %add_add_fusion.1), channel_id=1, source_target_pairs={{0,16},{2,18},{4,20},{6,22},{8,24},{10,26},{12,28},{14,30},{16,0},... | collective-permute-start | bytes 245768 | tf_op jit(solution)/shard_map/ppermute | solution.py:53
  583.1 11.5 %collective-permute-start.80 = (f32[2,2,10,512]{3,2,1,0:T(8,128)S(1)}, f32[2,2,10,512]{3,2,1,0:T(8,128)S(1)}, u32[]{:S(2)}, u32[]{:S(2)}) collective-permute-start(f32[2,2,10,512]{3,2,1,0:T(8,128)S(1)} %add_add_fusion.1), channel_id=1, source_target_pairs={{0,24},{2,26},{4,28},{6,30},{8,16},{10,18},{12,20},{14,22},{16,8},... | collective-permute-start | bytes 245768 | tf_op jit(solution)/shard_map/ppermute | solution.py:53
  (177 other events, 2169.7 us)
